TPU v7x, 32 devices: a whole 2x2x4 slice. The times are simulated.
32 devices in a mesh: dp: 2 (over x), context: 8 (over z, core), tensor: 2 (over y).
Axes of the slice: x: 2, y: 2, z: 4, core: 2. Of those that a mesh axis runs over, the one named last changes fastest.
Arguments:
- tokens: bfloat16 [4, 4096, 768], P('dp', 'context'), may hold values from -6 to 6
- documents: int32 [4, 4096], P('dp', 'context'), may hold values from 0 to 15, never falling along the last dimension, each value on 1 to 1024 neighbouring positions
- norm_gain: float32 [768], P(('dp', 'context')), may hold values from 0.5 to 1.5
- entry_weight: float32 [768, 2, 1536], P(('dp', 'context'), None, 'tensor'), may hold values from -0.21875 to 0.21875
- state_weight: float32 [768, 256], P(('dp', 'context')), may hold values from -0.21875 to 0.21875
- step_weight: float32 [768, 24], P(('dp', 'context'), 'tensor'), may hold values from -0.109375 to 0.109375
- inner_kernel: float32 [5, 1536], P(None, 'tensor'), may hold values from -0.5 to 0.5
- state_filter: float32 [5, 256], replicated, may hold values from -0.5 to 0.5
- step_bias: float32 [24], P('tensor'), may hold values from -7 to -3
- decay_log: float32 [24], P('tensor'), may hold values from -1 to 1.5
- skip_gain: float32 [24], P('tensor'), may hold values from 0.25 to 1
- gate_gain: float32 [1536], P('tensor'), may hold values from 0.5 to 1.5
- exit_weight: float32 [768, 1536], P(('dp', 'context'), 'tensor'), may hold values from -0.15625 to 0.15625
- cotangent: bfloat16 [4, 4096, 768], P('dp', 'context'), may hold values from -6 to 6
Outputs:
- block_out: bfloat16 [4, 4096, 768], P('dp', 'context')
- token_grad: float32 [4, 4096, 768], P('dp', 'context')
- norm_grad: float32 [768], P(('dp', 'context'))
- entry_grad: float32 [768, 2, 1536], P(('dp', 'context'), None, 'tensor')
- state_weight_gradient: float32 [768, 256], P(('dp', 'context'))
- step_weight_gradient: float32 [768, 24], P(('dp', 'context'), 'tensor')
- kernel_grad: float32 [5, 1536], P(None, 'tensor')
- filter_grad: float32 [5, 256], replicated
- bias_grad: float32 [24], P('tensor')
- decay_grad: float32 [24], P('tensor')
- skip_grad: float32 [24], P('tensor')
- gate_grad: float32 [1536], P('tensor')
- exit_weight_gradient: float32 [768, 1536], P(('dp', 'context'), 'tensor')
Inputs may be any that keep to these rules, and one draw needn't show every extreme that they name: `documents`: in each sequence the document numbers start at 0, never fall, every one of 0 to 15 occurs, each document has 1 to 1024 positions, and one has exactly 1024.
All inputs are finite; a program needn't handle non-finite values.
Results may differ from a plain program's by a relative error of at most 0.012.
The roundings to bfloat16 on the way count: a program that leaves them out, or rounds other values in their place, can miss the bound.
Values may be sent and summed in bfloat16 or wider, within the bound.
A program may use at most 256 MiB of HBM per device.

v0:
```python
import jax
import jax.numpy as jnp
from jax import lax
from jax.sharding import PartitionSpec as P

HEAD = 64
NSTATE = 128
CONV = 4
SPAN = 256


EPSILON = 1e-05
PRECISION_HIGH = lax.Precision.HIGHEST


def passed_along(x, axis, by):
    count = lax.axis_size(axis)
    pairs = [(i, i + by) for i in range(count) if 0 <= i + by < count]
    return lax.ppermute(x, axis, pairs)


def carried_in(value, axis, join, neutral, backward):
    count, mine = (lax.axis_size(axis), lax.axis_index(axis))
    pieces = jax.tree.map(lambda part: lax.all_gather(part, axis), value)
    if backward:
        pieces = jax.tree.map(lambda part: part[::-1], pieces)
        mine = count - 1 - mine
    so_far = jax.tree.map(
        lambda part, zero: jnp.full_like(part, 0) + jnp.asarray(zero, part.dtype), value, neutral
    )

    def hop(position, so_far):
        longer = join(so_far, jax.tree.map(lambda part: part[position], pieces))
        return jax.tree.map(lambda new, old: jnp.where(position < mine, new, old), longer, so_far)

    return lax.fori_loop(0, count - 1, hop, so_far)


def prepare(extended, step_unactivated, kernel, step_bias, decay_log, ids_before, documents):
    width = documents.shape[1]
    ids_extended = jnp.concatenate([ids_before, documents], axis=1)
    preact = kernel[CONV]
    for offset in range(CONV):
        match = (ids_extended[:, offset : offset + width] == documents).astype(jnp.float32)
        preact = preact + kernel[offset] * extended[:, offset : offset + width] * match[:, :, None]
    mixed = jax.nn.silu(preact)
    inner_width = mixed.shape[2] - 2 * NSTATE
    steps = jax.nn.softplus(step_unactivated + step_bias)
    return (
        mixed[:, :, :inner_width],
        mixed[:, :, inner_width : inner_width + NSTATE],
        mixed[:, :, inner_width + NSTATE :],
        -steps * jnp.exp(decay_log),
        steps,
    )


def span_summary(inner, writer, log_decay, steps, documents, before):
    seqs, width = documents.shape
    heads = steps.shape[2]
    cumulative = jnp.cumsum(log_decay, axis=1)
    final = cumulative[:, -1]
    tail = (
        (documents == documents[:, -1:]).astype(jnp.float32)[:, :, None]
        * jnp.exp(final[:, None, :] - cumulative)
        * steps
    )
    values = inner.reshape(seqs, width, heads, HEAD)
    local = jnp.einsum("suh,suhp,sun->shpn", tail, values, writer, precision=PRECISION_HIGH)
    keep = (documents[:, -1] == before).astype(jnp.float32)
    return (local, keep[:, None] * jnp.exp(final))


def span_output(inner, writer, reader, log_decay, steps, carry_in, documents, before):
    seqs, width = documents.shape
    heads = steps.shape[2]
    cumulative = jnp.cumsum(jnp.swapaxes(log_decay, 1, 2), axis=2)
    places = jnp.arange(width)
    same = (places[:, None] >= places[None, :])[None] & (
        documents[:, :, None] == documents[:, None, :]
    )
    spread = cumulative[:, :, :, None] - cumulative[:, :, None, :]
    decay = jnp.exp(jnp.where(same[:, None], spread, 0.0)) * same[:, None].astype(jnp.float32)
    scores = jnp.einsum("stn,sun->stu", reader, writer, precision=PRECISION_HIGH)
    weights = decay * scores[:, None] * jnp.swapaxes(steps, 1, 2)[:, :, None, :]
    values = inner.reshape(seqs, width, heads, HEAD)
    local = jnp.einsum("shtu,suhp->sthp", weights, values, precision=PRECISION_HIGH)
    opened = (documents == before[:, None]).astype(jnp.float32)
    carried = jnp.einsum("stn,shpn->sthp", reader, carry_in, precision=PRECISION_HIGH)
    growth = opened[:, :, None] * jnp.exp(jnp.swapaxes(cumulative, 1, 2))
    result = local + growth[:, :, :, None] * carried
    return result.reshape(seqs, width, heads * HEAD)


def span_bounds(documents, before):
    width = documents.shape[1]
    length = min(SPAN, width)
    bounds = []
    for index in range(width // length):
        first = index * length
        entry = before if index == 0 else documents[:, first - 1]
        bounds.append((first, first + length, entry))
    return bounds


def block_state(inner, writer, log_decay, steps, documents, before):
    state = None
    gain = None
    for first, last, entry in span_bounds(documents, before):
        local, factor = span_summary(
            inner[:, first:last],
            writer[:, first:last],
            log_decay[:, first:last],
            steps[:, first:last],
            documents[:, first:last],
            entry,
        )
        if state is None:
            state, gain = (local, factor)
        else:
            state = factor[:, :, None, None] * state + local
            gain = gain * factor
    return (state, gain)


def block_output(inner, writer, reader, log_decay, steps, carry_in, documents, before):
    pieces = []
    entering = carry_in
    for first, last, entry in span_bounds(documents, before):
        part_docs = documents[:, first:last]
        pieces.append(
            span_output(
                inner[:, first:last],
                writer[:, first:last],
                reader[:, first:last],
                log_decay[:, first:last],
                steps[:, first:last],
                entering,
                part_docs,
                entry,
            )
        )
        if last < documents.shape[1]:
            local, factor = span_summary(
                inner[:, first:last],
                writer[:, first:last],
                log_decay[:, first:last],
                steps[:, first:last],
                part_docs,
                entry,
            )
            entering = factor[:, :, None, None] * entering + local
    return jnp.concatenate(pieces, axis=1)


def combine(earlier, later):
    return (earlier[0] * later[0], later[0][:, :, None, None] * earlier[1] + later[1])


def body(
    tokens,
    documents,
    norm_gain,
    entry_weight,
    state_weight,
    step_weight,
    inner_kernel,
    state_filter,
    step_bias,
    decay_log,
    skip_gain,
    gate_gain,
    exit_weight,
    cotangent,
):
    position = lax.axis_index("context")
    inputs = tokens.astype(jnp.float32)
    masters = (
        norm_gain.astype(jnp.bfloat16),
        entry_weight.astype(jnp.bfloat16),
        state_weight.astype(jnp.bfloat16),
        step_weight.astype(jnp.bfloat16),
        exit_weight.astype(jnp.bfloat16),
    )
    gain_low, entry_reduced, state_low, step_reduced, exit_reduced = (
        lax.all_gather(masters[0], ("dp", "context"), axis=0, tiled=True),
        lax.all_gather(masters[1], ("dp", "context"), axis=0, tiled=True),
        lax.all_gather(masters[2], ("dp", "context"), axis=0, tiled=True),
        lax.all_gather(masters[3], ("dp", "context"), axis=0, tiled=True),
        lax.all_gather(masters[4], ("dp", "context"), axis=0, tiled=True),
    )
    scale = lax.rsqrt(jnp.mean(inputs * inputs, axis=-1, keepdims=True) + EPSILON)
    hidden_activation = (inputs * scale * gain_low.astype(jnp.float32)).astype(jnp.bfloat16)
    gate_preactivation = jnp.einsum(
        "bqm,mj->bqj", hidden_activation, entry_reduced[:, 0], preferred_element_type=jnp.float32
    )
    convolution_weight = jnp.concatenate([entry_reduced[:, 1], state_low], axis=1)
    convolution_input = jnp.einsum(
        "bqm,mj->bqj", hidden_activation, convolution_weight, preferred_element_type=jnp.float32
    ).astype(jnp.bfloat16)
    step_unactivated = jnp.einsum(
        "wje,en->wjn", hidden_activation, step_reduced, preferred_element_type=jnp.float32
    )
    edge_ids = passed_along(documents[:, -(CONV - 1) :], "context", 1)
    ids_before = jnp.where(position == 0, -1, edge_ids)
    before = ids_before[:, -1]
    edge_rows = passed_along(convolution_input[:, -(CONV - 1) :], "context", 1)
    extended = jnp.concatenate([edge_rows, convolution_input], axis=1).astype(jnp.float32)
    kernel = jnp.concatenate([inner_kernel, state_filter], axis=1)

    def prepare_local(extended, step_unactivated, kernel, step_bias, decay_log):
        return prepare(
            extended, step_unactivated, kernel, step_bias, decay_log, ids_before, documents
        )

    (inner, writer, reader, log_decay, steps), prepare_back = jax.vjp(
        prepare_local, extended, step_unactivated, kernel, step_bias, decay_log
    )

    def state_local(inner, writer, log_decay, steps):
        return block_state(inner, writer, log_decay, steps, documents, before)

    (state_here, carry_gain), state_back = jax.vjp(state_local, inner, writer, log_decay, steps)
    ones = jnp.ones_like(carry_gain)
    zeros = jnp.zeros_like(state_here)
    gain_in, carry_in = carried_in(
        (carry_gain, state_here), "context", combine, (ones, zeros), False
    )

    def output_local(inner, writer, reader, log_decay, steps, carry_in):
        return block_output(inner, writer, reader, log_decay, steps, carry_in, documents, before)

    scanned, output_back = jax.vjp(output_local, inner, writer, reader, log_decay, steps, carry_in)
    heads = steps.shape[2]
    skip_wide = jnp.repeat(skip_gain, HEAD)
    output = scanned + skip_wide * inner
    gate_act = jax.nn.silu(gate_preactivation)
    gated = output * gate_act
    square_sum = lax.psum(jnp.sum(gated * gated, axis=-1), "tensor")
    inner_total = gated.shape[-1] * lax.axis_size("tensor")
    normal = lax.rsqrt(square_sum / inner_total + EPSILON)[:, :, None]
    unit_activation = (gated * normal * gate_gain).astype(jnp.bfloat16)
    partial_value_sum = jnp.einsum(
        "yjr,pr->yjp", unit_activation, exit_reduced, preferred_element_type=jnp.float32
    )
    branch_path = lax.psum(partial_value_sum, "tensor")
    block_out = (inputs + branch_path).astype(jnp.bfloat16)
    gain_back, entry_backward, state_backward_weight, step_backward, exit_backward = (
        lax.all_gather(masters[0], ("dp", "context"), axis=0, tiled=True),
        lax.all_gather(masters[1], ("dp", "context"), axis=0, tiled=True),
        lax.all_gather(masters[2], ("dp", "context"), axis=0, tiled=True),
        lax.all_gather(masters[3], ("dp", "context"), axis=0, tiled=True),
        lax.all_gather(masters[4], ("dp", "context"), axis=0, tiled=True),
    )
    exit_weight_gradient = jnp.einsum(
        "yqr,yqj->rj", cotangent, unit_activation, preferred_element_type=jnp.float32
    )
    unit_activation_gradient = jnp.einsum(
        "bqm,mj->bqj", cotangent, exit_backward, preferred_element_type=jnp.float32
    )
    gate_grad = jnp.sum(unit_activation_gradient * gated * normal, axis=(0, 1))
    scaled = unit_activation_gradient * gate_gain
    cross = lax.psum(jnp.sum(scaled * gated, axis=-1), "tensor")[:, :, None]
    gated_grad = normal * scaled - normal * normal * normal * gated * cross / inner_total
    output_grad = gated_grad * gate_act
    sigma = jax.nn.sigmoid(gate_preactivation)
    gate_preactivation_gradient = (
        gated_grad * output * sigma * (1.0 + gate_preactivation * (1.0 - sigma))
    ).astype(jnp.bfloat16)
    seqs, width = documents.shape
    skip_grad = jnp.sum((output_grad * inner).reshape(seqs, width, heads, HEAD), axis=(0, 1, 3))
    inner_one, writer_one, reader_one, decay_one, steps_one, entering = output_back(output_grad)
    gain_out, adjoint = carried_in((carry_gain, entering), "context", combine, (ones, zeros), True)
    gain_cot = jnp.sum(adjoint * carry_in, axis=(2, 3))
    inner_two, writer_two, decay_two, steps_two = state_back((adjoint, gain_cot))
    writer_sum, reader_sum = lax.psum((writer_one + writer_two, reader_one), "tensor")
    extended_grad, step_raw_full, kernel_full, bias_grad, decay_grad = prepare_back(
        (
            inner_one + inner_two + skip_wide * output_grad,
            writer_sum,
            reader_sum,
            decay_one + decay_two,
            steps_one + steps_two,
        )
    )
    edge_grad = passed_along(extended_grad[:, : CONV - 1], "context", -1)
    conv_part = extended_grad[:, CONV - 1 :]
    conv_grad = jnp.concatenate(
        [conv_part[:, : -(CONV - 1)], conv_part[:, -(CONV - 1) :] + edge_grad], axis=1
    )
    conv_low = conv_grad.astype(jnp.bfloat16)
    step_unactivated_gradient = step_raw_full.astype(jnp.bfloat16)
    inner_width = gate_preactivation.shape[-1]
    inner_convolved = conv_low[:, :, :inner_width]
    state_convolved = conv_low[:, :, inner_width:]
    gate_row_values = jnp.einsum(
        "yqr,yqj->rj",
        hidden_activation,
        gate_preactivation_gradient,
        preferred_element_type=jnp.float32,
    )
    inner_row_values = jnp.einsum(
        "yqr,yqj->rj", hidden_activation, inner_convolved, preferred_element_type=jnp.float32
    )
    entry_grad = jnp.stack([gate_row_values, inner_row_values], axis=1)
    state_weight_gradient = jnp.einsum(
        "yqr,yqj->rj", hidden_activation, state_convolved, preferred_element_type=jnp.float32
    )
    step_weight_gradient = jnp.einsum(
        "yfm,yfc->mc",
        hidden_activation,
        step_unactivated_gradient,
        preferred_element_type=jnp.float32,
    )
    hidden_part = jnp.einsum(
        "yjr,pr->yjp",
        gate_preactivation_gradient,
        entry_backward[:, 0],
        preferred_element_type=jnp.float32,
    )
    hidden_part = hidden_part + jnp.einsum(
        "yjr,pr->yjp", inner_convolved, entry_backward[:, 1], preferred_element_type=jnp.float32
    )
    hidden_part = hidden_part + jnp.einsum(
        "imr,vr->imv", step_unactivated_gradient, step_backward, preferred_element_type=jnp.float32
    )
    hidden_grad = lax.psum(hidden_part, "tensor")
    hidden_grad = hidden_grad + jnp.einsum(
        "yjr,pr->yjp", state_convolved, state_backward_weight, preferred_element_type=jnp.float32
    )
    norm_grad = jnp.sum(hidden_grad * inputs * scale, axis=(0, 1))
    normed_grad = hidden_grad * gain_back.astype(jnp.float32)
    token_grad = (
        cotangent.astype(jnp.float32)
        + scale * normed_grad
        - scale
        * scale
        * scale
        * inputs
        * jnp.sum(normed_grad * inputs, axis=-1, keepdims=True)
        / inputs.shape[-1]
    )
    shards = (
        lax.psum_scatter(norm_grad, ("dp", "context"), scatter_dimension=0, tiled=True),
        lax.psum_scatter(entry_grad, ("dp", "context"), scatter_dimension=0, tiled=True),
        lax.psum_scatter(state_weight_gradient, ("dp", "context"), scatter_dimension=0, tiled=True),
        lax.psum_scatter(step_weight_gradient, ("dp", "context"), scatter_dimension=0, tiled=True),
        lax.psum_scatter(exit_weight_gradient, ("dp", "context"), scatter_dimension=0, tiled=True),
    )
    smalls = lax.psum(
        (
            kernel_full[:, :inner_width],
            kernel_full[:, inner_width:],
            bias_grad,
            decay_grad,
            skip_grad,
            gate_grad,
        ),
        ("dp", "context"),
    )
    return (
        block_out,
        token_grad,
        shards[0],
        shards[1],
        shards[2],
        shards[3],
        smalls[0],
        smalls[1],
        smalls[2],
        smalls[3],
        smalls[4],
        smalls[5],
        shards[4],
    )


def solution(mesh):
    in_specs = (
        P("dp", "context", None),
        P("dp", "context"),
        P(("dp", "context")),
        P(("dp", "context"), None, "tensor"),
        P(("dp", "context"), None),
        P(("dp", "context"), "tensor"),
        P(None, "tensor"),
        P(),
        P("tensor"),
        P("tensor"),
        P("tensor"),
        P("tensor"),
        P(("dp", "context"), "tensor"),
        P("dp", "context", None),
    )
    out_specs = (
        P("dp", "context", None),
        P("dp", "context", None),
        P(("dp", "context")),
        P(("dp", "context"), None, "tensor"),
        P(("dp", "context"), None),
        P(("dp", "context"), "tensor"),
        P(None, "tensor"),
        P(),
        P("tensor"),
        P("tensor"),
        P("tensor"),
        P("tensor"),
        P(("dp", "context"), "tensor"),
    )
    return jax.shard_map(body, mesh=mesh, in_specs=in_specs, out_specs=out_specs, check_vma=False)
```

profile of v0, /device:TPU:0, one launch (start us, length us, event | category | flops | bytes accessed | tf_op | source)
XLA Modules:
  0.0 956.8 jit_solution(13679648080346581622)
XLA Ops:
  16.3 34.1 %all-reduce.37 = bf16[768]{0:T(1024)(128)(2,1)S(1)} all-reduce(bf16[768]{0:T(1024)(128)(2,1)S(1)} %dynamic-update-slice), channel_id=1, replica_groups=mesh['dp'=2,'context'=8,'tensor'=2] {'dp','context'}, use_global_device_ids=true, to_apply=%add.37 | all-reduce | flops 768 | bytes 3072
  51.2 17.4 %all-gather.2 = bf16[16,48,12]{1,2,0:T(8,128)(2,1)S(1)} all-gather(bf16[1,48,12]{1,2,0:T(8,128)(2,1)S(1)} %convert_bitcast_fusion), channel_id=1, replica_groups=mesh['dp'=2,'context'=8,'tensor'=2] {'dp','context'}, dimensions={0}, use_global_device_ids=true | all-gather | bytes 19584 | tf_op jit(solution)/shard_map/all_gather | solution.py:189
  78.7 20.7 %all_gather.40 = bf16[768,256]{1,0:T(8,128)(2,1)S(1)} all-gather(bf16[48,256]{1,0:T(8,128)(2,1)S(1)} %convert_element_type.95), channel_id=1, replica_groups=mesh['dp'=2,'context'=8,'tensor'=2] {'dp','context'}, dimensions={0}, use_global_device_ids=true | all-gather | bytes 417792 | tf_op jit(solution)/shard_map/all_gather | solution.py:188
  148.0 9.9 %all_gather.42 = f32[8,2,12]{2,1,0:T(2,128)} all-gather(f32[1,2,12]{2,1,0:T(2,128)S(1)} %fusion.186), channel_id=1, replica_groups=mesh['dp'=2,'context'=8,'tensor'=2] {'context'}, dimensions={0}, use_global_device_ids=true | all-gather | bytes 864 | tf_op jit(solution)/shard_map/all_gather | solution.py:24
  166.0 32.1 %all-gather.12.cloned.1.call-done = f32[16,12,64,128]{3,2,1,0:T(8,128)} async-done(((f32[2,12,64,128]{3,2,1,0:T(8,128)}), f32[16,12,64,128]{3,2,1,0:T(8,128)}) %all-gather.12.cloned.1.call-update) | async-done | bytes 6291472 | tf_op jit(solution)/shard_map/all_gather | solution.py:24
  198.2 14.1 %while.28 = (s32[]{:T(128)}, f32[2,12,64,128]{3,2,1,0:T(8,128)S(1)}, s32[]{:T(128)}, f32[8,2,12]{2,1,0:T(2,128)}, f32[8,2,12,64,128]{4,3,2,1,0:T(8,128)}, /*index=5*/s32[]{:T(128)}, s32[]{:T(128)}) while((s32[]{:T(128)}, f32[2,12,64,128]{3,2,1,0:T(8,128)S(1)}, s32[]{:T(128)}, f32[8,2,12]{2,1,0:T(2,128)}, ...), condition=%wide.region_6.7_spmd.clone, body=%wide.region_5.6_spmd.clone.sunk | while | flops 786436 | bytes 2359697 | solution.py:36
  214.8 9.6 %bitcast_add_fusion.3 = f32[2,256,12,64]{1,3,2,0:T(8,128)} fusion(f32[2,256,12,64]{1,3,2,0:T(8,128)S(1)} %fusion.151, f32[2,256,12,64]{1,3,2,0:T(8,128)S(1)} %bitcast.305, f32[2,12,256]{2,1,0:T(8,128)S(1)} %copy-done.82, f32[2,256,256]{2,1,0:T(8,128)} %fusion.169, f32[2,256,256]{2,1,0:T(8,128)S(1)} %copy-done.57, f32[2,12,256]{2,1,0:T(8,128)S(1)} %copy-done.84, ...), kind=kOutput, calls=%fused_computation.118 | convolution fusion | flops 1216610304 | bytes 5971968 | tf_op jit(solution)/shard_map/jvp(shtu,suhp->sthp)/dot_general | solution.py:87
  230.1 8.4 bitcast_add_fusion.2
  241.7 8.3 multiply_reduce_fusion.11
  255.2 6.6 multiply_reduce_fusion.8
  266.7 8.3 multiply_reduce_fusion.9
  292.9 12.6 %fusion.23 = (f32[2,12,256]{2,1,0:T(8,128)}, f32[2,12,256]{2,1,0:T(8,128)}, f32[2,12,256]{2,1,0:T(8,128)}, f32[2,256,256]{2,1,0:T(8,128)}) fusion(f32[2,12,256]{2,1,0:T(8,128)} %copy.340, f32[2,256,256]{2,1,0:T(8,128)} %fusion.169, f32[2,256,256]{2,1,0:T(8,128)} %get-tuple-element.429, f32[2,12,256]{2,1,0:T(8,128)} %copy.338, ...), kind=kOutput, calls=%fused_computation.50 | convolution fusion | flops 1231403008 | bytes 4972544 | tf_op jit(solution)/shard_map/transpose(jvp(shtu,suhp->sthp))/dot_general | solution.py:87
  310.4 8.3 fusion.13
  345.2 13.0 %fusion.21 = (f32[2,12,256]{2,1,0:T(8,128)}, f32[2,12,256]{2,1,0:T(8,128)}, f32[2,12,256]{2,1,0:T(8,128)}, f32[2,256,256]{2,1,0:T(8,128)}) fusion(f32[2,12,256]{2,1,0:T(8,128)} %copy.355, f32[2,256,256]{2,1,0:T(8,128)} %fusion.159, f32[2,256,256]{2,1,0:T(8,128)} %get-tuple-element.432, f32[2,12,256]{2,1,0:T(8,128)} %copy.353, ...), kind=kOutput, calls=%fused_computation.48 | convolution fusion | flops 1231403008 | bytes 4972544 | tf_op jit(solution)/shard_map/transpose(jvp(shtu,suhp->sthp))/dot_general | solution.py:87
  379.6 8.6 fusion.6
  425.2 14.0 %while.29 = (s32[]{:T(128)}, f32[2,12,64,128]{3,2,1,0:T(8,128)S(1)}, s32[]{:T(128)}, f32[8,2,12]{2,1,0:T(2,128)}, f32[8,2,12,64,128]{4,3,2,1,0:T(8,128)}, /*index=5*/s32[]{:T(128)}, s32[]{:T(128)}) while((s32[]{:T(128)}, f32[2,12,64,128]{3,2,1,0:T(8,128)S(1)}, s32[]{:T(128)}, f32[8,2,12]{2,1,0:T(2,128)}, ...), condition=%wide.region_16.17_spmd.clone, body=%wide.region_15.16_spmd.clone.sunk | while | flops 786436 | bytes 2359697 | solution.py:36
  514.0 14.7 %all-reduce.47.cloned.1.call-done = (f32[2,512,128]{2,1,0:T(8,128)}, f32[2,512,128]{2,1,0:T(8,128)}) async-done(((f32[2,512,128]{2,1,0:T(8,128)}, f32[2,512,128]{2,1,0:T(8,128)}), (f32[2,512,128]{2,1,0:T(8,128)}, f32[2,512,128]{2,1,0:T(8,128)})) %all-reduce.47.cloned.1.call-update) | async-done | bytes 1048592 | tf_op jit(solution)/shard_map/psum | solution.py:276
  528.7 12.0 %multiply_reduce_fusion.7 = (f32[1024]{0:T(1024)S(1)}, f32[1024]{0:T(1024)S(1)}, f32[1024]{0:T(1024)S(1)}, f32[1024]{0:T(1024)S(1)}, f32[1024]{0:T(1024)S(1)}, /*index=5*/f32[2,512,1024]{2,1,0:T(8,128)S(1)}) fusion(f32[2,515,1024]{2,1,0:T(8,128)} %copy-done, f32[2,512]{1,0:T(2,128)S(1)} %get-tuple-element.440, f32[2,512]{1,0:T(2,128)S(1)} %get-tuple-element.441, ...), kind=kLoop, calls=%fused_computation.40 | loop fusion | flops 24112128 | bytes 29392896 | tf_op jit(solution)/shard_map/transpose(jvp())/reduce_sum | solution.py:45
  578.9 9.1 reduce-scatter.13.cloned.1.call-done
  592.9 150.3 %all-reduce.45.cloned.1.call-done = (f32[2,512,768]{2,1,0:T(8,128)}, f32[2,512,768]{2,1,0:T(8,128)}) async-done(((f32[2,512,768]{2,1,0:T(8,128)}, f32[2,512,768]{2,1,0:T(8,128)}), (f32[2,512,768]{2,1,0:T(8,128)}, f32[2,512,768]{2,1,0:T(8,128)})) %all-reduce.45.cloned.1.call-update) | async-done | bytes 6291472 | tf_op jit(solution)/shard_map/psum | solution.py:246
  749.1 63.3 %all-reduce.39 = (f32[768]{0:T(1024)S(1)}, f32[5,768]{1,0:T(8,128)}, f32[5,256]{1,0:T(8,128)}, f32[12]{0:T(128)}, f32[12]{0:T(128)}, /*index=5*/f32[12]{0:T(128)}, f32[768]{0:T(1024)}) all-reduce(f32[768]{0:T(1024)S(1)} %get-tuple-element.400, ...), channel_id=4, replica_groups=mesh['dp'=2,'context'=8,'tensor'=2] {'dp','context'}, use_global_device_ids=true, to_apply=%region_45.46.clone | all-reduce | flops 6692 | bytes 53536
  813.0 7.0 fusion.30
  825.3 64.4 %reduce-scatter.15.cloned.1.call-done = f32[48,768]{1,0:T(8,128)} async-done(((f32[768,768]{1,0:T(8,128)}), f32[48,768]{1,0:T(8,128)}) %reduce-scatter.15.cloned.1.call-update) | async-done | bytes 147472
  889.7 60.0 %reduce-scatter.11.cloned.1.call-done = f32[48,256]{1,0:T(8,128)} async-done(((f32[768,256]{1,0:T(8,128)}), f32[48,256]{1,0:T(8,128)}) %reduce-scatter.11.cloned.1.call-update) | async-done | bytes 49168 | tf_op jit(solution)/shard_map/reduce_scatter | solution.py:346
  (496 shorter events, 360.5 us)
Async XLA Ops:
  7.2 66.3 %copy-start.112 = (f32[12]{0:T(128)S(1)}, f32[12]{0:T(128)}, u32[]{:S(2)}) copy-start(f32[12]{0:T(128)} %param.26) | copy-start | bytes 148
  7.2 100.6 %all-gather.8.cloned.1.call-start = ((), (), s32[]{:S(2)}) async-start(), calls=%async_computation.4 | async-start | bytes 2506752 | tf_op jit(solution)/shard_map/all_gather | solution.py:187
  8.0 93.2 %collective-permute-start.1 = (s32[2,3]{1,0:T(2,128)S(1)}, s32[2,3]{1,0:T(2,128)S(1)}, u32[]{:S(2)}, u32[]{:S(2)}) collective-permute-start(s32[2,3]{1,0:T(2,128)S(1)} %slice.211), channel_id=1, source_target_pairs={{0,2},{2,4},{4,6},{6,8},{8,10},{10,12},{12,14},{1,3},{3,5},{5,7},{... | collective-permute-start | bytes 80 | tf_op jit(solution)/shard_map/ppermute | solution.py:19
  12.0 186.1 %all-gather.12.cloned.1.call-start = ((), (), s32[]{:S(2)}) async-start(), calls=%async_computation.8 | async-start | bytes 7077888 | tf_op jit(solution)/shard_map/all_gather | solution.py:24
  13.4 61.3 %copy-start.114 = (f32[12]{0:T(128)}, f32[12]{0:T(128)S(1)}, u32[]{:S(2)}) copy-start(f32[12]{0:T(128)S(1)} %exp.91) | copy-start | bytes 148
  74.8 33.0 %copy-start.20 = (f32[2,512,12]{2,0,1:T(2,128)}, f32[2,512,12]{2,0,1:T(2,128)S(1)}, u32[]{:S(2)}) copy-start(f32[2,512,12]{2,0,1:T(2,128)S(1)} %get-tuple-element.388) | copy-start | bytes 147460
  78.4 36.2 %copy-start.34 = (f32[2,12,256]{1,0,2:T(2,128)}, f32[2,12,256]{1,0,2:T(2,128)S(1)}, u32[]{:S(2)}) copy-start(f32[2,12,256]{1,0,2:T(2,128)S(1)} %copy.347) | copy-start | bytes 73732
  111.8 4.9 collective-permute-start
  135.9 24.4 %copy-start.49 = (f32[2,256,12]{2,0,1:T(2,128)S(1)}, f32[2,256,12]{2,0,1:T(2,128)}, u32[]{:S(2)}) copy-start(f32[2,256,12]{2,0,1:T(2,128)} %get-tuple-element.426) | copy-start | bytes 73732
  135.9 24.5 %copy-start.48 = (f32[2,256,12]{2,0,1:T(2,128)S(1)}, f32[2,256,12]{2,0,1:T(2,128)}, u32[]{:S(2)}) copy-start(f32[2,256,12]{2,0,1:T(2,128)} %get-tuple-element.427) | copy-start | bytes 73732
  135.9 119.3 %all-gather.10.cloned.1.call-start = ((), (), s32[]{:S(2)}) async-start(), calls=%async_computation.5 | async-start | bytes 1253376 | tf_op jit(solution)/shard_map/all_gather | solution.py:190
  137.6 281.0 %all-gather.14.cloned.1.call-start = ((), (), s32[]{:S(2)}) async-start(), calls=%async_computation.9 | async-start | bytes 7077888 | tf_op jit(solution)/shard_map/all_gather | solution.py:24
  143.7 98.0 %copy-start.78 = (f32[768]{0:T(1024)}, f32[768]{0:T(1024)S(1)}, u32[]{:S(2)}) copy-start(f32[768]{0:T(1024)S(1)} %mul.876) | copy-start | bytes 9220
  160.4 54.3 %copy-start.60 = (f32[2,256,12]{1,2,0:T(8,128)}, f32[2,256,12]{1,2,0:T(8,128)S(1)}, u32[]{:S(2)}) copy-start(f32[2,256,12]{1,2,0:T(8,128)S(1)} %copy.343) | copy-start | bytes 73732
  291.2 237.5 %all-reduce.47.cloned.1.call-start = ((), (), s32[]{:S(2)}) async-start(), calls=%async_computation.13 | async-start | bytes 2097152 | tf_op jit(solution)/shard_map/psum | solution.py:276
  489.7 98.3 %reduce-scatter.13.cloned.1.call-start = ((), (), s32[]{:S(2)}) async-start(), calls=%async_computation.10 | async-start | bytes 417792
  508.2 235.0 %all-reduce.45.cloned.1.call-start = ((), (), s32[]{:S(2)}) async-start(), calls=%async_computation.12 | async-start | bytes 12582912 | tf_op jit(solution)/shard_map/psum | solution.py:246
  544.0 9.4 collective-permute-start.2
  561.0 262.5 %reduce-scatter.9.cloned.1.call-start = ((), (), s32[]{:S(2)}) async-start(), calls=%async_computation.6 | async-start | bytes 5013504 | tf_op jit(solution)/shard_map/reduce_scatter | solution.py:345
  568.8 320.9 %reduce-scatter.15.cloned.1.call-start = ((), (), s32[]{:S(2)}) async-start(), calls=%async_computation.11 | async-start | bytes 2506752
  578.0 371.7 %reduce-scatter.11.cloned.1.call-start = ((), (), s32[]{:S(2)}) async-start(), calls=%async_computation.7 | async-start | bytes 835584 | tf_op jit(solution)/shard_map/reduce_scatter | solution.py:346
  589.5 153.6 %copy-start.31 = (bf16[2,512,768]{2,1,0:T(8,128)(2,1)S(1)}, bf16[2,512,768]{2,1,0:T(8,128)(2,1)}, u32[]{:S(2)}) copy-start(bf16[2,512,768]{2,1,0:T(8,128)(2,1)} %param.18) | copy-start | bytes 4718596
  589.6 153.6 %copy-start.43 = (bf16[768,256]{1,0:T(8,128)(2,1)S(1)}, bf16[768,256]{1,0:T(8,128)(2,1)}, u32[]{:S(2)}) copy-start(bf16[768,256]{1,0:T(8,128)(2,1)} %copy-done.42) | copy-start | bytes 1179652
  743.2 69.8 %copy-start.107 = (f32[2,512]{1,0:T(2,128)S(1)}, f32[2,512]{1,0:T(2,128)}, u32[]{:S(2)}) copy-start(f32[2,512]{1,0:T(2,128)} %get-tuple-element.444) | copy-start | bytes 12292
  (107 other events, 639.4 us)
Sparse Core Ops, SparseCore 0:
  12.1 45.0 all-gather.7
  136.0 62.0 all-gather.11
  200.5 37.0 all-gather.9
  291.3 63.4 all-gather.13
  489.8 38.8 all-reduce.46
  532.4 55.5 reduce-scatter.12
  590.5 152.6 all-reduce.44
  747.5 75.8 reduce-scatter.8
  827.8 61.9 reduce-scatter.14
  894.1 55.5 reduce-scatter.10
where the time goes:
time: 967 us; the launch traced here: 957 us
  waiting for transfers between devices  334 us (35%)
  matrix products  177 us (18%)
  blocking collectives  155 us (16%)
  other arithmetic  143 us (15%)
  local copies, waits for them, and re-layouts  122 us (13%)
  between operations  17.2 us (2%)
    psum x1, waiting for transfers between devices, body(): branch_path = lax.psum(partial_value_sum, 'tensor')  150 us
    unnamed x2, blocking collectives  97.4 us
    unnamed x12, waiting for transfers between devices  73.7 us
    dot_general x6, matrix products, span_output(): jnp.einsum('shtu,suhp->sthp', weights, values, precision=PRECISION_HIGH)  60.5 us
    reduce_scatter x1, waiting for transfers between devices, body(): lax.psum_scatter(state_weight_gradient, ('dp', 'context'), scatter_dimens...  60 us
    another operation x22, other arithmetic  36 us
    all_gather x2, waiting for transfers between devices, carried_in(): pieces = jax.tree.map(lambda part: lax.all_gather(part, axis), value)  32.1 us
    dot_general x8, matrix products, span_summary(): jnp.einsum('suh,suhp,sun->shpn', tail, values, writer, precision=PRECISIO...  29.6 us
  transfers between devices with their start and end apart: 13, of which 7 were waited for; matrix products, arithmetic and copies ran while one was open for 32% of the time, Pallas kernels for 0%

commit v1 on v0

v1 whole, which is shorter than its diff:
```python
import functools
import jax
import jax.numpy as jnp
from jax import lax
from jax.experimental import pallas as pl
from jax.experimental.pallas import tpu as pltpu
from jax.sharding import PartitionSpec as P

HEAD = 64
NSTATE = 128
CONV = 4
EPSILON = 1e-05
Q = 128
HALO = 16
LANES = 128
WIDE = 256
LOG2E = 1.4426950408889634
FAR = -1e30
LOW = jnp.bfloat16
F32 = jnp.float32
VMEM_LIMIT = 60 * 1024 * 1024


def mm(a, b):
    return lax.dot_general(a, b, (((1,), (0,)), ((), ())), preferred_element_type=F32)


def mm_nt(a, b):
    return lax.dot_general(a, b, (((1,), (1,)), ((), ())), preferred_element_type=F32)


def mm_tn(a, b):
    return lax.dot_general(a, b, (((0,), (0,)), ((), ())), preferred_element_type=F32)


def mm_exact(a, b):
    return lax.dot_general(
        a, b, (((1,), (0,)), ((), ())), precision=lax.Precision.HIGHEST, preferred_element_type=F32
    )


def split3(v):
    high = v.astype(LOW).astype(F32)
    rest = v - high
    mid = rest.astype(LOW).astype(F32)
    low = rest - mid
    return (high + pltpu.roll(mid, 32, 1) + pltpu.roll(low, 64, 1)).astype(LOW)


def iota(shape, dim):
    return lax.broadcasted_iota(jnp.int32, shape, dim)


def spreader(first_head, width, count):
    k = iota((LANES, width * count), 0)
    lane = iota((LANES, width * count), 1)
    hit = ((k & 31) == first_head + lane // width) & (k < 96)
    return hit.astype(F32).astype(LOW)


def gatherer(first_head, width, count):
    lane = iota((width * count, LANES), 0)
    k = iota((width * count, LANES), 1)
    return (k == first_head + lane // width).astype(F32).astype(LOW)


def head_sums(v, collect):
    high = v.astype(LOW)
    rest = (v - high.astype(F32)).astype(LOW)
    return mm(high, collect) + mm(rest, collect)


def sigmoid(v):
    return 1.0 / (1.0 + jnp.exp(-v))


def twice(v):
    return jnp.concatenate([v, v], axis=1)


def conv_forward(cin, taps, masks):
    rows = cin.shape[0] - HALO
    out = taps[CONV : CONV + 1] + taps[CONV - 1 : CONV] * cin[HALO:]
    for back in range(1, CONV):
        part = cin[HALO - back : HALO - back + rows]
        out = out + taps[CONV - 1 - back : CONV - back] * (part * twice(masks[back - 1]))
    return out


def conv_backward(pg, cin, taps, masks):
    rows, width = pg.shape
    sums = [None] * (CONV + 1)
    sums[CONV] = jnp.sum(pg, axis=0, keepdims=True)
    sums[CONV - 1] = jnp.sum(pg * cin[HALO:], axis=0, keepdims=True)
    pad = jnp.zeros((HALO, width), F32)
    grad = jnp.concatenate([pad, pg * taps[CONV - 1 : CONV]], axis=0)
    for back in range(1, CONV):
        masked = pg * twice(masks[back - 1])
        part = cin[HALO - back : HALO - back + rows]
        sums[CONV - 1 - back] = jnp.sum(masked * part, axis=0, keepdims=True)
        padded = jnp.concatenate([pad, masked * taps[CONV - 1 - back : CONV - back], pad], axis=0)
        grad = grad + padded[back : back + rows + HALO]
    return sums, grad


def front_body(
    which, tokens, halo, halo_docs, doc_col, doc_row, w_gate, w_inner, w_small, par, par_heads,
    state_filter, hidden_out, cin_out, gate_out, pre_out, loc_out, fold_out, gain_out,
    cin_state_out, pre_state_out, bc_out, bct_out, score_out, mask_out, zst_out, dt_out, sp_out,
    cumt_out, fac_out, match_out, hidden, sp_tail, facs
):
    step = pl.program_id(0)
    rows = tokens.shape[1]
    spans = rows // Q

    @pl.when(step == 0)
    def _():
        gain_t = jnp.transpose(w_small[0, :, LANES : 2 * LANES].astype(F32))
        gain = gain_t[24:25]
        for ref, first, count in ((halo, 0, HALO), (tokens, HALO, rows)):
            value = (ref[...] if ref is halo else ref[0]).astype(F32)
            scale = lax.rsqrt(jnp.mean(value * value, axis=1, keepdims=True) + EPSILON)
            hidden[first : first + count] = (value * scale * gain).astype(LOW)
        hidden_out[...] = hidden[HALO:]
        both = [mm(hidden[...], w_small[index]) for index in range(2)]
        cin = jnp.concatenate([both[0][:, :LANES], both[1][:, :LANES]], axis=1).astype(LOW)
        cin_state_out[...] = cin
        docs = jnp.concatenate([halo_docs[...], doc_col[...]], axis=0)
        masks = []
        for back in range(1, CONV):
            match = (docs[HALO - back : HALO - back + rows] == docs[HALO:]).astype(F32)
            match_out[back - 1] = match
            masks.append(match)
        pre = conv_forward(cin.astype(F32), state_filter[...], masks)
        pre_state_out[...] = pre
        mixed = (pre * sigmoid(pre)).astype(LOW)
        bc_out[...] = mixed
        turned = jnp.transpose(mixed.astype(F32)).astype(LOW)
        bct_out[...] = turned
        heads = par_heads[...]
        used = iota((rows, LANES), 1) < 24
        raw = both[0][HALO:, LANES:] + both[1][HALO:, LANES:]
        zst = jnp.where(used, raw, 0.0) + heads[0:1]
        zst_out[...] = zst
        dt = jnp.where(used, jnp.maximum(zst, 0.0) + jnp.log1p(jnp.exp(-jnp.abs(zst))), 0.0)
        dt_out[...] = dt
        decay = -dt * jnp.exp(heads[1:2])
        t_at, u_at = iota((Q, Q), 0), iota((Q, Q), 1)
        lower = (t_at >= u_at).astype(F32)
        fac_rows = []
        for index in range(spans):
            at = slice(index * Q, (index + 1) * Q)
            cum = mm_exact(lower, decay[at])
            final = cum[Q - 1 : Q]
            before = docs[HALO + index * Q - 1 : HALO + index * Q]
            here = doc_col[at]
            last = here[Q - 1 : Q]
            opened = (here == before).astype(F32)
            tail = (here == last).astype(F32) * jnp.exp(final - cum)
            fac_rows.append((last == before).astype(F32) * jnp.exp(final))
            cum2 = cum * LOG2E
            turned_cum = jnp.transpose(cum2)
            for group in range(6):
                cumt_out[group, 0:4, at] = turned_cum[4 * group : 4 * group + 4]
            sp_out[0, at] = split3(dt[at])
            sp_out[1, at] = split3(cum2)
            lanes_used = iota((Q, LANES), 1) < 24
            sp_out[2, at] = split3(jnp.where(lanes_used, opened * jnp.exp(cum), 0.0))
            sp_out[3, at] = split3(jnp.where(lanes_used, tail, 0.0))
            sp_tail[at] = split3(jnp.where(lanes_used, tail * dt[at], 0.0))
            same = (t_at >= u_at) & (here == doc_row[0:1, at])
            mask_out[at] = jnp.where(same, 0.0, FAR)
            score_out[at] = mm_nt(mixed[at, LANES:], mixed[at, :LANES])
        gain_total = fac_rows[0]
        for row in fac_rows[1:]:
            gain_total = gain_total * row
        rows8 = jnp.concatenate(
            fac_rows + [gain_total] + [jnp.zeros((1, LANES), F32)] * (7 - spans), axis=0
        )
        rows8 = jnp.where(iota((8, LANES), 1) < 24, rows8, 0.0)
        fac_out[...] = rows8
        facs[...] = split3(rows8)

    cin = mm(hidden[...], w_inner[0]).astype(LOW)
    cin_out[...] = cin
    gate_out[...] = mm(hidden[HALO:], w_gate[0])
    masks = [match_out[back] for back in range(CONV - 1)]
    pre = conv_forward(cin.astype(F32), par[0], masks)
    pre_out[...] = pre
    spread = spreader(4 * step, HEAD, 4)
    value = (pre * sigmoid(pre) * mm(sp_tail[...], spread)).astype(LOW)
    facx = mm(facs[...], spread)
    fold = jnp.zeros((NSTATE, WIDE), F32)
    for index in range(spans):
        at = slice(index * Q, (index + 1) * Q)
        loc = mm(bct_out[:NSTATE, at], value[at])
        loc_out[at] = loc
        fold = facx[index : index + 1] * fold + loc
    fold_out[...] = fold
    gain_out[...] = jnp.broadcast_to(facx[spans : spans + 1], (8, WIDE))


def const(shape):
    zeros = (0,) * len(shape)
    return pl.BlockSpec(shape, lambda *_: zeros)


def params(**extra):
    return pltpu.CompilerParams(vmem_limit_bytes=VMEM_LIMIT, **extra)


def front(which, tokens, halo, halo_docs, doc_col, doc_row, weights, par, par_heads, state_filter):
    rows, model = tokens.shape[1:]
    wide = 2 * 3 * WIDE
    ext = rows + HALO
    shape = jax.ShapeDtypeStruct
    outs = (
        (shape((rows, model), LOW), const((rows, model))),
        (shape((ext, wide), LOW), pl.BlockSpec((ext, WIDE), lambda s, w: (0, s))),
        (shape((rows, wide), F32), pl.BlockSpec((rows, WIDE), lambda s, w: (0, s))),
        (shape((rows, wide), F32), pl.BlockSpec((rows, WIDE), lambda s, w: (0, s))),
        (shape((rows, wide), F32), pl.BlockSpec((rows, WIDE), lambda s, w: (0, s))),
        (shape((NSTATE, wide), F32), pl.BlockSpec((NSTATE, WIDE), lambda s, w: (0, s))),
        (shape((8, wide), F32), pl.BlockSpec((8, WIDE), lambda s, w: (0, s))),
        (shape((ext, WIDE), LOW), const((ext, WIDE))),
        (shape((rows, WIDE), F32), const((rows, WIDE))),
        (shape((rows, WIDE), LOW), const((rows, WIDE))),
        (shape((WIDE, rows), LOW), const((WIDE, rows))),
        (shape((rows, Q), F32), const((rows, Q))),
        (shape((rows, Q), F32), const((rows, Q))),
        (shape((rows, LANES), F32), const((rows, LANES))),
        (shape((rows, LANES), F32), const((rows, LANES))),
        (shape((4, rows, LANES), LOW), const((4, rows, LANES))),
        (shape((6, 8, rows), F32), const((6, 8, rows))),
        (shape((8, LANES), F32), const((8, LANES))),
        (shape((CONV - 1, rows, LANES), F32), const((CONV - 1, rows, LANES))),
    )
    return pl.pallas_call(
        front_body,
        out_shape=[out[0] for out in outs],
        grid_spec=pltpu.PrefetchScalarGridSpec(
            num_scalar_prefetch=1,
            grid=(6,),
            in_specs=[
                pl.BlockSpec((1, rows, model), lambda s, w: (w[0], 0, 0)),
                const((HALO, model)),
                const((HALO, LANES)),
                const((rows, LANES)),
                const((8, rows)),
                pl.BlockSpec((1, model, WIDE), lambda s, w: (s // 3, 0, s % 3)),
                pl.BlockSpec((1, model, WIDE), lambda s, w: (s // 3, 0, 3 + s % 3)),
                pl.BlockSpec((2, model, WIDE), lambda s, w: (0, 0, 9)),
                pl.BlockSpec((1, 8, WIDE), lambda s, w: (s // 3, 0, s % 3)),
                const((8, LANES)),
                const((8, WIDE)),
            ],
            out_specs=[out[1] for out in outs],
            scratch_shapes=[
                pltpu.VMEM((ext, model), LOW),
                pltpu.VMEM((rows, LANES), LOW),
                pltpu.VMEM((8, LANES), LOW),
            ],
        ),
        compiler_params=params(),
        name="front",
    )(
        which, tokens, halo, halo_docs, doc_col, doc_row, weights, weights, weights, par, par_heads,
        state_filter,
    )


def middle_body(
    which, tokens, cot, cot_t, pre_ref, gate_ref, loc_ref, carry_ref, w_exit, par, par_heads, bc,
    bct, score, mask, sp, cumt, fac, block_out, exit_out, dy_out, gpg_out, enter_out, row_out,
    skip_out, outputs, gates, unit_grads, mixes, sums, total
):
    step = pl.program_id(0)
    rows = pre_ref.shape[0]
    spans = rows // Q
    wide = 6 * WIDE

    @pl.when(step == 0)
    def _():
        sums[...] = jnp.zeros_like(sums)
        total[...] = jnp.zeros_like(total)
        skip_out[...] = jnp.zeros_like(skip_out)

    @pl.when(step < 6)
    def _():
        group = step
        spread = spreader(4 * group, HEAD, 4)
        pre = pre_ref[...]
        mix = pre * sigmoid(pre)
        mixes[group] = mix
        value = mix * mm(sp[0], spread)
        growth = mm(sp[2], spread)
        facx = mm(split3(fac[...]), spread)
        cums = mm(sp[1], spreader(4 * group, LANES, 4))
        skipx = mm(split3(par_heads[...]), spread)[2:3]
        state = carry_ref[...].astype(F32)
        half = iota((Q, LANES), 1) < HEAD
        for index in range(spans):
            at = slice(index * Q, (index + 1) * Q)
            carried = mm(bc[at, LANES:], state.astype(LOW)) * growth[at]
            parts = []
            for pair in range(2):
                lanes = slice(pair * LANES, (pair + 1) * LANES)
                local = None
                for side in range(2):
                    head = 2 * pair + side
                    across = cumt[group, head : head + 1, at]
                    spread_at = cums[at, head * LANES : (head + 1) * LANES] - across + mask[at]
                    weight = (jnp.exp2(spread_at) * score[at]).astype(LOW)
                    keep = half if side == 0 else jnp.logical_not(half)
                    seen = jnp.where(keep, value[at, lanes], 0.0).astype(LOW)
                    part = mm(weight, seen)
                    local = part if local is None else local + part
                parts.append(local)
            out = jnp.concatenate(parts, axis=1) + carried + skipx * mix[at]
            outputs[group, at] = out
            state = facx[index : index + 1] * state + loc_ref[at]
        gate = gate_ref[...]
        gates[group] = gate
        gated = outputs[group] * (gate * sigmoid(gate))
        unit_grad = mm(cot[0], w_exit[0])
        unit_grads[group] = unit_grad
        square = gated * gated
        cross = unit_grad * par[0, 5:6] * gated
        sums[0] += square[:, :LANES] + square[:, LANES:]
        sums[1] += cross[:, :LANES] + cross[:, LANES:]

    @pl.when(step == 5)
    def _():
        square = jnp.sum(sums[0], axis=1, keepdims=True)
        cross = jnp.sum(sums[1], axis=1, keepdims=True)
        normal = lax.rsqrt(square / wide + EPSILON)
        sums[0] = jnp.broadcast_to(normal, (rows, LANES))
        sums[1] = jnp.broadcast_to(normal * normal * normal * cross / wide, (rows, LANES))

    @pl.when(step >= 6)
    def _():
        group = step - 6
        spread = spreader(4 * group, HEAD, 4)
        normal = twice(sums[0])
        pull = twice(sums[1])
        gain = par[0, 5:6]
        gate = gates[group]
        out = outputs[group]
        unit_grad = unit_grads[group]
        sigma = sigmoid(gate)
        act = gate * sigma
        gated = out * act
        scaled_in = gated * normal
        unit = (scaled_in * gain).astype(LOW)
        total[...] += mm_nt(unit, w_exit[0])
        exit_out[0] = mm(cot_t[...], unit).astype(LOW)
        gate_sum = jnp.sum(unit_grad * scaled_in, axis=0, keepdims=True)
        gated_grad = normal * (unit_grad * gain) - pull * gated
        dy = gated_grad * act
        dy_out[...] = dy
        gpg_out[...] = (gated_grad * out * sigma * (1.0 + gate * (1.0 - sigma))).astype(LOW)
        skip_sum = jnp.sum(dy * mixes[group], axis=0, keepdims=True)
        row_out[...] = jnp.broadcast_to(gate_sum, (8, WIDE))
        skip_out[...] += head_sums(
            jnp.broadcast_to(skip_sum, (8, WIDE)), gatherer(4 * group, HEAD, 4)
        )
        facx = mm(split3(fac[...]), spread)
        pushed = (dy * mm(sp[2], spread)).astype(LOW)
        enter = jnp.zeros((NSTATE, WIDE), F32)
        for index in reversed(range(spans)):
            at = slice(index * Q, (index + 1) * Q)
            enter = facx[index : index + 1] * enter + mm(bct[NSTATE:, at], pushed[at])
        enter_out[...] = enter

    @pl.when(step == 11)
    def _():
        block_out[...] = (tokens[0].astype(F32) + total[...]).astype(LOW)


def middle(
    which, tokens, cot, cot_t, pre, gate, loc, carry, weights, par, par_heads, bc, bct, score, mask,
    sp, cumt, fac
):
    rows, model = tokens.shape[1:]
    wide = 6 * WIDE
    shape = jax.ShapeDtypeStruct

    def early(s):
        return jnp.minimum(s, 5)

    def late(s):
        return jnp.maximum(s - 6, 0)

    def group(s):
        return s % 6

    outs = (
        (shape((rows, model), LOW), const((rows, model))),
        (
            shape((2, model, 3 * WIDE), LOW),
            pl.BlockSpec((1, model, WIDE), lambda s, w: (late(s) // 3, 0, late(s) % 3)),
        ),
        (shape((rows, wide), F32), pl.BlockSpec((rows, WIDE), lambda s, w: (0, late(s)))),
        (shape((rows, wide), LOW), pl.BlockSpec((rows, WIDE), lambda s, w: (0, late(s)))),
        (shape((NSTATE, wide), F32), pl.BlockSpec((NSTATE, WIDE), lambda s, w: (0, late(s)))),
        (shape((8, wide), F32), pl.BlockSpec((8, WIDE), lambda s, w: (0, late(s)))),
        (shape((8, LANES), F32), const((8, LANES))),
    )
    return pl.pallas_call(
        middle_body,
        out_shape=[out[0] for out in outs],
        grid_spec=pltpu.PrefetchScalarGridSpec(
            num_scalar_prefetch=1,
            grid=(12,),
            in_specs=[
                pl.BlockSpec((1, rows, model), lambda s, w: (w[0], 0, 0)),
                pl.BlockSpec((1, rows, model), lambda s, w: (w[0], 0, 0)),
                const((model, rows)),
                pl.BlockSpec((rows, WIDE), lambda s, w: (0, early(s))),
                pl.BlockSpec((rows, WIDE), lambda s, w: (0, early(s))),
                pl.BlockSpec((rows, WIDE), lambda s, w: (0, early(s))),
                pl.BlockSpec((NSTATE, WIDE), lambda s, w: (0, early(s))),
                pl.BlockSpec((1, model, WIDE), lambda s, w: (group(s) // 3, 0, 6 + group(s) % 3)),
                pl.BlockSpec((1, 8, WIDE), lambda s, w: (group(s) // 3, 0, group(s) % 3)),
                const((8, LANES)),
                const((rows, WIDE)),
                const((WIDE, rows)),
                const((rows, Q)),
                const((rows, Q)),
                const((4, rows, LANES)),
                const((6, 8, rows)),
                const((8, LANES)),
            ],
            out_specs=[out[1] for out in outs],
            scratch_shapes=[
                pltpu.VMEM((6, rows, WIDE), F32),
                pltpu.VMEM((6, rows, WIDE), F32),
                pltpu.VMEM((6, rows, WIDE), F32),
                pltpu.VMEM((6, rows, WIDE), F32),
                pltpu.VMEM((2, rows, LANES), F32),
                pltpu.VMEM((rows, model), F32),
            ],
        ),
        compiler_params=params(),
        name="middle",
    )(
        which, tokens, cot, cot_t, pre, gate, loc, carry, weights, par, par_heads, bc, bct, score,
        mask, sp, cumt, fac,
    )


def scan_back_body(
    pre_ref, dy_ref, loc_ref, carry_ref, adj_ref, cin_ref, par, par_heads, state_filter, cin_state,
    pre_state, bc, bct, score, mask, sp, cumt, fac, match, zst, dt_ref, cg_out, edge_out, tap_out,
    cg_state_out, edge_state_out, tap_state_out, srg_out, small_out, d_bc, d_score, d_cum, heads
):
    group = pl.program_id(0)
    rows = pre_ref.shape[0]
    spans = rows // Q

    @pl.when(group == 0)
    def _():
        d_bc[...] = jnp.zeros_like(d_bc)
        d_score[...] = jnp.zeros_like(d_score)
        d_cum[...] = jnp.zeros_like(d_cum)
        heads[...] = jnp.zeros_like(heads)

    spread = spreader(4 * group, HEAD, 4)
    collect = gatherer(4 * group, HEAD, 4)
    pre = pre_ref[...]
    sigma = sigmoid(pre)
    mix = pre * sigma
    dtx = mm(sp[0], spread)
    growth = mm(sp[2], spread)
    tails = mm(sp[3], spread)
    facx = mm(split3(fac[...]), spread)
    cums = mm(sp[1], spreader(4 * group, LANES, 4))
    skipx = mm(split3(par_heads[...]), spread)[2:3]
    states = [carry_ref[...].astype(F32)]
    for index in range(spans - 1):
        at = slice(index * Q, (index + 1) * Q)
        states.append(facx[index : index + 1] * states[-1] + loc_ref[at])
    adjoint = adj_ref[...].astype(F32)
    half = iota((Q, LANES), 1) < HEAD
    ones = jnp.ones((8, Q), F32).astype(LOW)
    masks = [match[back] for back in range(CONV - 1)]
    pgs = [None] * spans
    for index in reversed(range(spans)):
        at = slice(index * Q, (index + 1) * Q)
        dy = dy_ref[at]
        value = mix[at] * dtx[at]
        state_low, adj_low = states[index].astype(LOW), adjoint.astype(LOW)
        pushed = dy * growth[at]
        pushed_low = pushed.astype(LOW)
        reached = mm(bc[at, :LANES], adj_low) * tails[at]
        carried = mm(bc[at, LANES:], state_low)
        d_bc[at, :LANES] += mm_nt((value * tails[at]).astype(LOW), adj_low)
        d_bc[at, LANES:] += mm_nt(pushed_low, state_low)
        heads[0, at] += head_sums(value * reached, collect)
        heads[1, at] += head_sums(pushed * carried, collect)
        fac_part = jnp.sum(adjoint * states[index], axis=0, keepdims=True)
        heads[3, index * 8 : index * 8 + 8] += head_sums(
            jnp.broadcast_to(fac_part, (8, WIDE)), collect
        )
        adjoint = facx[index : index + 1] * adjoint + mm(bct[NSTATE:, at], pushed_low)
        parts = []
        sum_score = None
        for pair in range(2):
            lanes = slice(pair * LANES, (pair + 1) * LANES)
            value_low = value[:, lanes].astype(LOW)
            local = None
            for side in range(2):
                head = 2 * pair + side
                across = cumt[group, head : head + 1, at]
                spread_at = cums[at, head * LANES : (head + 1) * LANES] - across + mask[at]
                decay = jnp.exp2(spread_at)
                keep = half if side == 0 else jnp.logical_not(half)
                dy_low = jnp.where(keep, dy[:, lanes], 0.0).astype(LOW)
                inner = decay * mm_nt(dy_low, value_low)
                sum_score = inner if sum_score is None else sum_score + inner
                moved = (inner * score[at]).astype(LOW)
                turn = mm_nt(ones, moved) - mm(ones, moved)
                d_cum[group, head : head + 1, at] = turn[0:1]
                part = mm_tn((decay * score[at]).astype(LOW), dy_low)
                local = part if local is None else local + part
            parts.append(local)
        d_score[at] += sum_score
        d_value = jnp.concatenate(parts, axis=1) + reached
        heads[2, at] += head_sums(mix[at] * d_value, collect)
        d_mix = dtx[at] * d_value + skipx * dy
        s = sigma[at]
        pgs[index] = d_mix * s * (1.0 + pre[at] * (1.0 - s))
    pg = jnp.concatenate(pgs, axis=0)
    sums, grad = conv_backward(pg, cin_ref[...].astype(F32), par[0], masks)
    tap_out[...] = jnp.concatenate(sums + [jnp.zeros((3, WIDE), F32)], axis=0)
    cg_out[...] = grad[HALO:]
    edge_out[...] = grad[:HALO]

    @pl.when(group == 5)
    def _():
        t_at, u_at = iota((Q, Q), 0), iota((Q, Q), 1)
        onward = (t_at <= u_at).astype(F32)
        earlier = (t_at > u_at).astype(F32)
        rate = jnp.exp(par_heads[1:2])
        bias_sum = jnp.zeros((1, LANES), F32)
        decay_sum = jnp.zeros((1, LANES), F32)
        used = iota((Q, LANES), 1) < 24
        for index in range(spans):
            at = slice(index * Q, (index + 1) * Q)
            pieces = [d_cum[piece, 0:4, at] for piece in range(6)]
            pieces.append(jnp.zeros((LANES - 24, Q), F32))
            cum_col = jnp.transpose(jnp.concatenate(pieces, axis=0))
            fac_row = fac[index : index + 1] * heads[3, index * 8 : index * 8 + 1]
            d_decay = (
                mm_exact(onward, cum_col + heads[1, at]) + mm_exact(earlier, heads[0, at]) + fac_row
            )
            dt = dt_ref[at]
            raw = (heads[2, at] - d_decay * rate) * sigmoid(zst[at])
            raw = jnp.where(used, raw, 0.0)
            srg_out[at] = raw.astype(LOW)
            bias_sum += jnp.sum(raw, axis=0, keepdims=True)
            decay_sum -= jnp.sum(
                jnp.where(used, d_decay * dt * rate, 0.0), axis=0, keepdims=True
            )
            score_low = d_score[at].astype(LOW)
            d_bc[at, :LANES] += mm_tn(score_low, bc[at, LANES:])
            d_bc[at, LANES:] += mm(score_low, bc[at, :LANES])
        small_out[...] = jnp.concatenate(
            [bias_sum, decay_sum, jnp.zeros((6, LANES), F32)], axis=0
        )
        pre = pre_state[...]
        s = sigmoid(pre)
        pg = d_bc[...] * s * (1.0 + pre * (1.0 - s))
        sums, grad = conv_backward(pg, cin_state[...].astype(F32), state_filter[...], masks)
        tap_state_out[...] = jnp.concatenate(sums + [jnp.zeros((3, WIDE), F32)], axis=0)
        cg_state_out[...] = grad[HALO:]
        edge_state_out[...] = grad[:HALO]


def scan_back(
    pre, dy, loc, carry, adj, cin, par, par_heads, state_filter, cin_state, pre_state, bc, bct,
    score, mask, sp, cumt, fac, match, zst, dt
):
    rows, wide = pre.shape
    ext = rows + HALO
    shape = jax.ShapeDtypeStruct
    column = lambda count: pl.BlockSpec((count, WIDE), lambda s: (0, s))
    outs = (
        (shape((rows, wide), F32), column(rows)),
        (shape((HALO, wide), F32), column(HALO)),
        (shape((8, wide), F32), column(8)),
        (shape((rows, WIDE), F32), const((rows, WIDE))),
        (shape((HALO, WIDE), F32), const((HALO, WIDE))),
        (shape((8, WIDE), F32), const((8, WIDE))),
        (shape((rows, LANES), LOW), const((rows, LANES))),
        (shape((8, LANES), F32), const((8, LANES))),
    )
    return pl.pallas_call(
        scan_back_body,
        out_shape=[out[0] for out in outs],
        grid=(6,),
        in_specs=[
            column(rows),
            column(rows),
            column(rows),
            column(NSTATE),
            column(NSTATE),
            column(ext),
            pl.BlockSpec((1, 8, WIDE), lambda s: (s // 3, 0, s % 3)),
            const((8, LANES)),
            const((8, WIDE)),
            const((ext, WIDE)),
            const((rows, WIDE)),
            const((rows, WIDE)),
            const((WIDE, rows)),
            const((rows, Q)),
            const((rows, Q)),
            const((4, rows, LANES)),
            const((6, 8, rows)),
            const((8, LANES)),
            const((CONV - 1, rows, LANES)),
            const((rows, LANES)),
            const((rows, LANES)),
        ],
        out_specs=[out[1] for out in outs],
        scratch_shapes=[
            pltpu.VMEM((rows, WIDE), F32),
            pltpu.VMEM((rows, Q), F32),
            pltpu.VMEM((6, 8, rows), F32),
            pltpu.VMEM((4, rows, LANES), F32),
        ],
        compiler_params=params(),
        name="scan_back",
    )(
        pre, dy, loc, carry, adj, cin, par, par_heads, state_filter, cin_state, pre_state, bc, bct,
        score, mask, sp, cumt, fac, match, zst, dt,
    )


def tail_body(
    which, tokens, cot, hidden_t, gpg, cg, edge, cg_state, edge_state, srg, w_gate, w_inner, w_small,
    gate_out, inner_out, small_out, token_out, norm_out, total
):
    step = pl.program_id(0)
    rows = gpg.shape[0]

    def joined(grad, arrived):
        return jnp.concatenate(
            [grad[: rows - HALO], grad[rows - HALO :] + arrived[...]], axis=0
        ).astype(LOW)

    @pl.when(step == 0)
    def _():
        state = joined(cg_state, edge_state)
        steps = srg[...]
        turned = hidden_t[...]
        small_out[:, :WIDE] = mm(turned, state).astype(LOW)
        small_out[:, WIDE:] = mm(turned, steps).astype(LOW)
        acc = mm_nt(state[:, :LANES], w_small[0, :, :LANES])
        acc += mm_nt(state[:, LANES:], w_small[1, :, :LANES])
        acc += mm_nt(steps, w_small[0, :, LANES:])
        acc += mm_nt(steps, w_small[1, :, LANES:])
        total[...] = acc

    grad = joined(cg, edge)
    gate_grad = gpg[...]
    turned = hidden_t[...]
    gate_out[0] = mm(turned, gate_grad).astype(LOW)
    inner_out[0] = mm(turned, grad).astype(LOW)
    total[...] += mm_nt(gate_grad, w_gate[0]) + mm_nt(grad, w_inner[0])

    @pl.when(step == 5)
    def _():
        value = tokens[0].astype(F32)
        scale = lax.rsqrt(jnp.mean(value * value, axis=1, keepdims=True) + EPSILON)
        hidden_grad = total[...]
        norm_sum = jnp.sum(hidden_grad * (value * scale), axis=0, keepdims=True)
        norm_out[...] = jnp.broadcast_to(norm_sum, norm_out.shape)
        gain = jnp.transpose(w_small[0, :, LANES : 2 * LANES].astype(F32))[24:25]
        normed = hidden_grad * gain
        pull = jnp.sum(normed * value, axis=1, keepdims=True) / value.shape[1]
        token_out[...] = (
            cot[0].astype(F32) + scale * normed - (scale * scale * scale) * value * pull
        )


def tail(which, tokens, cot, hidden_t, gpg, cg, edge, cg_state, edge_state, srg, weights):
    rows, model = tokens.shape[1:]
    shape = jax.ShapeDtypeStruct
    column = lambda count: pl.BlockSpec((count, WIDE), lambda s, w: (0, s))
    parts = pl.BlockSpec((1, model, WIDE), lambda s, w: (s // 3, 0, s % 3))
    outs = (
        (shape((2, model, 3 * WIDE), LOW), parts),
        (shape((2, model, 3 * WIDE), LOW), parts),
        (shape((model, WIDE + LANES), LOW), const((model, WIDE + LANES))),
        (shape((rows, model), F32), const((rows, model))),
        (shape((8, model), F32), const((8, model))),
    )
    return pl.pallas_call(
        tail_body,
        out_shape=[out[0] for out in outs],
        grid_spec=pltpu.PrefetchScalarGridSpec(
            num_scalar_prefetch=1,
            grid=(6,),
            in_specs=[
                pl.BlockSpec((1, rows, model), lambda s, w: (w[0], 0, 0)),
                pl.BlockSpec((1, rows, model), lambda s, w: (w[0], 0, 0)),
                const((model, rows)),
                column(rows),
                column(rows),
                column(HALO),
                const((rows, WIDE)),
                const((HALO, WIDE)),
                const((rows, LANES)),
                pl.BlockSpec((1, model, WIDE), lambda s, w: (s // 3, 0, s % 3)),
                pl.BlockSpec((1, model, WIDE), lambda s, w: (s // 3, 0, 3 + s % 3)),
                pl.BlockSpec((2, model, WIDE), lambda s, w: (0, 0, 9)),
            ],
            out_specs=[out[1] for out in outs],
            scratch_shapes=[pltpu.VMEM((rows, model), F32)],
        ),
        compiler_params=params(),
        name="tail",
    )(
        which, tokens, cot, hidden_t, gpg, cg, edge, cg_state, edge_state, srg, weights, weights,
        weights,
    )


def chained(fold, gain, hops, backward):
    count = lax.axis_size("context")
    by = -1 if backward else 1
    pairs = [(i, i + by) for i in range(count) if 0 <= i + by < count]
    carry = jnp.zeros_like(fold)
    for _ in range(hops):
        carry = lax.ppermute(fold + gain[0:1] * carry, "context", pairs)
    return carry


def body(
    tokens, documents, norm_gain, entry_weight, state_weight, step_weight, inner_kernel,
    state_filter, step_bias, decay_log, skip_gain, gate_gain, exit_weight, cotangent,
):
    every = ("tensor", "dp", "context")
    seqs, rows, model = tokens.shape
    count = lax.axis_size("context")
    position, side = lax.axis_index("context"), lax.axis_index("tensor")
    group_count = lax.axis_size("dp") * count
    own_rows = norm_gain.shape[0]
    which = jnp.reshape(side, (1,)).astype(jnp.int32)
    longest = rows * count // 4
    hops = min(count - 1, -(-(longest - 1) // rows))

    first = (side == 0).astype(F32)
    state_half = jnp.where(side == 0, state_weight[:, :NSTATE], state_weight[:, NSTATE:])
    packed = jnp.concatenate(
        [
            entry_weight[:, 0],
            entry_weight[:, 1],
            exit_weight,
            state_half,
            step_weight * first,
            step_weight * (1.0 - first),
            norm_gain[:, None],
            jnp.zeros((own_rows, LANES - 25), F32),
        ],
        axis=1,
    ).astype(LOW)
    weights = lax.all_gather(packed, every, axis=0, tiled=True).reshape(2, model, -1)

    def placed(v):
        return jnp.concatenate([v * first, v * (1.0 - first), jnp.zeros((LANES - 24,), F32)])

    row6 = jnp.concatenate(
        [placed(step_bias), placed(decay_log), placed(skip_gain), jnp.zeros((model - 3 * LANES,))]
    )
    par_own = jnp.concatenate(
        [inner_kernel, gate_gain[None], row6[None], jnp.zeros((1, model), F32)], axis=0
    )
    par = lax.all_gather(par_own, "tensor", axis=0)
    par_heads = jnp.concatenate(
        [(par[0, 6] + par[1, 6])[: 3 * LANES].reshape(3, LANES), jnp.zeros((5, LANES), F32)], axis=0
    )
    filt = jnp.concatenate([state_filter, jnp.zeros((3, WIDE), F32)], axis=0)

    docs = lax.dynamic_index_in_dim(documents, side, 0, keepdims=False).astype(F32)
    doc_col = jnp.broadcast_to(docs[:, None], (rows, LANES))
    doc_row = jnp.broadcast_to(docs[None], (8, rows))
    forward = [(i, i + 1) for i in range(count - 1)]
    own_tokens = lax.dynamic_index_in_dim(tokens, side, 0, keepdims=False)
    halo = lax.ppermute(own_tokens[-HALO:], "context", forward)
    halo_docs = lax.ppermute(doc_col[-HALO:], "context", forward)
    halo_docs = jnp.where(position == 0, -1.0, halo_docs)

    (
        hidden, cin, gate, pre, loc, fold, gain, cin_state, pre_state, bc, bct, score, mask, zst, dt,
        sp, cumt, fac, match,
    ) = front(which, tokens, halo, halo_docs, doc_col, doc_row, weights, par, par_heads, filt)
    carry = chained(fold, gain, hops, False)
    cot_t = lax.dynamic_index_in_dim(cotangent, side, 0, keepdims=False).T
    block_own, exit_part, dy, gpg, enter, gate_row, skip_row = middle(
        which, tokens, cotangent, cot_t, pre, gate, loc, carry, weights, par, par_heads, bc, bct,
        score, mask, sp, cumt, fac,
    )
    adj = chained(enter, gain, hops, True)
    cg, edge, taps, cg_state, edge_state, taps_state, srg, head_rows = scan_back(
        pre, dy, loc, carry, adj, cin, par, par_heads, filt, cin_state, pre_state, bc, bct, score,
        mask, sp, cumt, fac, match, zst, dt,
    )
    back = [(i + 1, i) for i in range(count - 1)]
    edge, edge_state = lax.ppermute((edge, edge_state), "context", back)
    gate_part, inner_part, small_part, token_own, norm_row = tail(
        which, tokens, cotangent, hidden.T, gpg, cg, edge, cg_state, edge_state, srg, weights
    )

    small_both = jnp.stack([small_part, small_part])
    parts = jnp.concatenate([gate_part, inner_part, exit_part, small_both], axis=2)
    mine = lax.psum_scatter(
        parts.reshape(2 * model, -1).astype(F32), every, scatter_dimension=0, tiled=True
    )
    smalls = lax.psum((taps, taps_state, gate_row, skip_row, head_rows, norm_row), every)
    taps, taps_state, gate_row, skip_row, head_rows, norm_row = smalls
    block_out = lax.all_gather(block_own, "tensor", axis=0)
    token_grad = lax.all_gather(token_own, "tensor", axis=0)
    wide = 3 * WIDE
    at = lax.axis_index("dp") * count + position
    half = lambda v: lax.dynamic_slice_in_dim(v, side * wide, wide, axis=-1)
    twelve = lambda v: lax.dynamic_slice_in_dim(v[:24], side * 12, 12, axis=0)
    step_grad = lax.dynamic_slice_in_dim(mine[:, 9 * WIDE + WIDE : 9 * WIDE + WIDE + 24], side * 12, 12, axis=1)
    return (
        block_out,
        token_grad,
        lax.dynamic_slice_in_dim(norm_row[0], at * own_rows, own_rows, axis=0),
        jnp.stack([mine[:, :wide], mine[:, wide : 2 * wide]], axis=1),
        mine[:, 9 * WIDE : 10 * WIDE],
        step_grad,
        half(taps[: CONV + 1]),
        taps_state[: CONV + 1],
        twelve(head_rows[0]),
        twelve(head_rows[1]),
        twelve(skip_row[0]),
        half(gate_row[0]),
        mine[:, 2 * wide : 3 * wide],
    )


def solution(mesh):
    in_specs = (
        P("dp", "context", None),
        P("dp", "context"),
        P(("dp", "context")),
        P(("dp", "context"), None, "tensor"),
        P(("dp", "context"), None),
        P(("dp", "context"), "tensor"),
        P(None, "tensor"),
        P(),
        P("tensor"),
        P("tensor"),
        P("tensor"),
        P("tensor"),
        P(("dp", "context"), "tensor"),
        P("dp", "context", None),
    )
    out_specs = (
        P("dp", "context", None),
        P("dp", "context", None),
        P(("dp", "context")),
        P(("dp", "context"), None, "tensor"),
        P(("dp", "context"), None),
        P(("dp", "context"), "tensor"),
        P(None, "tensor"),
        P(),
        P("tensor"),
        P("tensor"),
        P("tensor"),
        P("tensor"),
        P(("dp", "context"), "tensor"),
    )
    return jax.shard_map(body, mesh=mesh, in_specs=in_specs, out_specs=out_specs, check_vma=False)
```

time: 967 us -> 636 us (0.66)
  matrix products: 177 us -> 0 us
  blocking collectives: 155 us -> 4.79 us
  other arithmetic: 143 us -> 27.8 us
  waiting for transfers between devices: 334 us -> 444 us
  local copies, waits for them, and re-layouts: 122 us -> 30.8 us
  Pallas kernels: 0 us -> 88.2 us
  starting transfers between devices: 7.47 us -> 25 us
    dot_general x40 -> x0, matrix products: 177 us -> none  [the longest x6 60.5 us: span_output(): jnp.einsum('shtu,suhp->sthp', weights, values, precision=PRECISION_HIGH)]
    reduce_scatter x2 -> x1, waiting for transfers between devices: 63.4 us -> 197 us  [body(): lax.psum_scatter(parts.reshape(2 * model, -1).astype(F32), every, scatter...]
    unnamed x2 -> x0, blocking collectives: 97.4 us -> none
    pallas_call x0 -> x4, Pallas kernels: none -> 88.2 us  [the longest x1 38.2 us: scan_back(): pl.pallas_call(scan_back_body, out_shape=[out[0] for out in outs], grid=(...]
    unnamed x12 -> x5, waiting for transfers between devices: 73.7 us -> 0.59 us
    all_gather x4 -> x3, waiting for transfers between devices: 32.2 us -> 102 us  [the longest x1 59.7 us: body(): lax.all_gather(packed, every, axis=0, tiled=True).reshape(2, model, -1)]
    psum x2 -> x1, waiting for transfers between devices: 165 us -> 107 us  [body(): lax.psum((taps, taps_state, gate_row, skip_row, head_rows, norm_row), every)]
    all_gather x3 -> x1, blocking collectives: 48 us -> 4.79 us  [body(): par = lax.all_gather(par_own, 'tensor', axis=0)]
  transfers between devices with their start and end apart: 13 -> 13, of which waited for: 7 -> 9; matrix products, arithmetic and copies ran while one was open for 32% -> 5% of each run, Pallas kernels for 0% -> 8%
where the time goes in v1:
time: 636 us; the launch traced here: 634 us
  waiting for transfers between devices  444 us (70%)
  Pallas kernels  88.2 us (14%)
  local copies, waits for them, and re-layouts  30.8 us (5%)
  other arithmetic  27.8 us (4%)
  starting transfers between devices  25 us (4%)
  between operations  14 us (2%)
    reduce_scatter x1, waiting for transfers between devices, body(): lax.psum_scatter(parts.reshape(2 * model, -1).astype(F32), every, scatter...  197 us
    psum x1, waiting for transfers between devices, body(): lax.psum((taps, taps_state, gate_row, skip_row, head_rows, norm_row), every)  107 us
    all_gather x1, waiting for transfers between devices, body(): lax.all_gather(packed, every, axis=0, tiled=True).reshape(2, model, -1)  59.7 us
    all_gather x1, waiting for transfers between devices, body(): token_grad = lax.all_gather(token_own, 'tensor', axis=0)  42.1 us
    pallas_call x1, Pallas kernels, scan_back(): pl.pallas_call(scan_back_body, out_shape=[out[0] for out in outs], grid=(...  38.2 us
    ppermute x4, waiting for transfers between devices, chained(): carry = lax.ppermute(fold + gain[0:1] * carry, 'context', pairs)  27.2 us
    pallas_call x1, Pallas kernels, middle(): pl.pallas_call(middle_body, out_shape=[out[0] for out in outs], grid_spec...  21.4 us
    ppermute x4, starting transfers between devices, chained(): carry = lax.ppermute(fold + gain[0:1] * carry, 'context', pairs)  15.3 us
  transfers between devices with their start and end apart: 13, of which 9 were waited for; matrix products, arithmetic and copies ran while one was open for 5% of the time, Pallas kernels for 8%

profile of v1, /device:TPU:0, one launch (start us, length us, event | category | flops | bytes accessed | tf_op | source)
XLA Modules:
  0.0 634.4 jit_solution(15587013312237436245)
XLA Ops:
  13.3 2.3 collective-permute-start.1
  16.4 4.6 collective-permute-start
  24.0 4.8 all-gather
  31.4 59.7 %all-gather.7.cloned.1.call-done = bf16[1536,2560]{1,0:T(8,128)(2,1)} async-done(((bf16[48,2560]{1,0:T(8,128)(2,1)}), bf16[1536,2560]{1,0:T(8,128)(2,1)}) %all-gather.7.cloned.1.call-update) | async-done | bytes 7864336 | tf_op jit(solution)/shard_map/all_gather | solution.py:769
  92.5 14.1 %front.1 = (bf16[512,768]{1,0:T(8,128)(2,1)}, bf16[528,1536]{1,0:T(8,128)(2,1)}, f32[512,1536]{1,0:T(8,128)}, f32[512,1536]{1,0:T(8,128)}, f32[512,1536]{1,0:T(8...) custom-call(s32[1]{0:T(128)} %bitcast.which, ...), custom_call_target="tpu_custom_call" | custom-call | tf_op jit(solution)/shard_map/front/pallas_call | solution.py:238
  108.9 2.2 collective-permute-start.2
  111.1 1.8 collective-permute-done.2
  114.2 10.3 %collective-permute-start.3 = (f32[128,1536]{1,0:T(8,128)S(1)}, f32[128,1536]{1,0:T(8,128)S(1)}, u32[]{:S(2)}, u32[]{:S(2)}) collective-permute-start(f32[128,1536]{1,0:T(8,128)S(1)} %multiply_add_fusion.1), channel_id=1, source_target_pairs={{0,2},{2,4},{4,6},{6,8},{8,10},{10,12},{12,14},{1,3},{3,5},{5,7},{... | collective-permute-start | bytes 2359304 | tf_op jit(solution)/shard_map/ppermute | solution.py:736
  127.3 21.4 %middle.1 = (bf16[512,768]{1,0:T(8,128)(2,1)}, bf16[2,768,768]{2,1,0:T(8,128)(2,1)}, f32[512,1536]{1,0:T(8,128)}, bf16[512,1536]{1,0:T(8,128)(2,1)}, f32[128,153...) custom-call(s32[1]{0:T(128)} %bitcast.which, bf16[2,512,768]{2,1,0:T(8,128)(2,1)} %tokens.5, ...), custom_call_target="tpu_custom_call" | custom-call | tf_op jit(solution)/shard_map/middle/pallas_call | solution.py:409
  151.3 11.8 %collective-permute-done.4 = f32[128,1536]{1,0:T(8,128)S(1)} collective-permute-done((f32[128,1536]{1,0:T(8,128)S(1)}, f32[128,1536]{1,0:T(8,128)S(1)}, u32[]{:S(2)}, u32[]{:S(2)}) %collective-permute-start.4) | collective-permute-done | bytes 786464 | tf_op jit(solution)/shard_map/ppermute | solution.py:736
  164.3 1.5 collective-permute-start.5
  165.8 13.0 %collective-permute-done.5.adj_ref = f32[128,1536]{1,0:T(8,128)S(1)} collective-permute-done((f32[128,1536]{1,0:T(8,128)S(1)}, f32[128,1536]{1,0:T(8,128)S(1)}, u32[]{:S(2)}, u32[]{:S(2)}) %collective-permute-start.5) | collective-permute-done | bytes 786464 | tf_op jit(solution)/shard_map/ppermute | solution.py:736
  179.7 38.2 %scan_back.1 = (f32[512,1536]{1,0:T(8,128)}, f32[16,1536]{1,0:T(8,128)}, f32[8,1536]{1,0:T(8,128)}, f32[512,256]{1,0:T(8,128)}, f32[16,256]{1,0:T(8,128)}, /*ind...) custom-call(f32[512,1536]{1,0:T(8,128)} %get-tuple-element.52.pre_ref, ...), custom_call_target="tpu_custom_call" | custom-call | tf_op jit(solution)/shard_map/scan_back/pallas_call | solution.py:598
  221.7 10.5 %collective-permute-done.7.edge_state = f32[16,256]{1,0:T(8,128)S(1)} collective-permute-done((f32[16,256]{1,0:T(8,128)}, f32[16,256]{1,0:T(8,128)S(1)}, u32[]{:S(2)}, u32[]{:S(2)}) %collective-permute-start.7) | collective-permute-done | bytes 16416 | tf_op jit(solution)/shard_map/ppermute | solution.py:811
  232.8 14.5 %tail.1 = (bf16[2,768,768]{2,1,0:T(8,128)(2,1)}, bf16[2,768,768]{2,1,0:T(8,128)(2,1)}, bf16[768,384]{1,0:T(8,128)(2,1)}, f32[512,768]{1,0:T(8,128)}, f32[8,768]{1,0:T(8,128)}) custom-call(s32[1]{0:T(128)} %bitcast.which, bf16[2,512,768]{2,1,0:T(8,128)(2,1)} %tokens.5, bf16[2,512,768]{2,1,0:T(8,128)(2,1)} %cot.3, bf16[768,512]{1,0:T(8,128)(2,1)} %bitcast.49, ...), custom_call_target="tpu_custom_call" | custom-call | tf_op jit(solution)/shard_map/tail/pallas_call | solution.py:699
  248.0 6.3 maximum_maximum_fusion
  254.4 10.1 %bitcast_convert_fusion = f32[1536,2688]{1,0:T(8,128)} fusion(bf16[2,768,2688]{2,1,0:T(8,128)(2,1)} %maximum_maximum_fusion), kind=kLoop, calls=%fused_computation.1 | loop fusion | flops 4128768 | bytes 24772608 | tf_op jit(solution)/shard_map/convert_element_type | solution.py:819
  264.5 106.5 %all-reduce.5.cloned.1.call-done = (f32[8,768]{1,0:T(8,128)}, f32[8,1536]{1,0:T(8,128)}, f32[8,256]{1,0:T(8,128)}, f32[8,128]{1,0:T(8,128)}, f32[8,128]{1,0:T(8,128)}, /*index=5*/f32[8,1536]{1,0:T(8,128)}) async-done(((f32[8,768]{1,0:T(8,128)}, f32[8,1536]{1,0:T(8,128)}, f32[8,256]{1,0:T(8,128)}, f32[8,128]{1,0:T(8,128)}, f32[8,128]{1,0:T(8,128)}, /*index=5*/f32[8,1536]{1,0:T(8,128)}), (f32[8,768]{1,0:T(8,128)}, ...) | async-done | bytes 139280 | tf_op jit(solution)/shard_map/psum | solution.py:821
  378.3 42.1 %all-gather.11.cloned.1.call-done = f32[1024,768]{1,0:T(8,128)} async-done(((f32[512,768]{1,0:T(8,128)}), f32[1024,768]{1,0:T(8,128)}) %all-gather.11.cloned.1.call-update) | async-done | bytes 3145744 | tf_op jit(solution)/shard_map/all_gather | solution.py:824
  420.4 197.0 %reduce-scatter.2.cloned.1.call-done = f32[48,2688]{1,0:T(8,128)} async-done(((f32[1536,2688]{1,0:T(8,128)}), f32[48,2688]{1,0:T(8,128)}) %reduce-scatter.2.cloned.1.call-update) | async-done | bytes 516112 | tf_op jit(solution)/shard_map/reduce_scatter | solution.py:818
  617.4 1.7 fusion.6
  621.6 1.4 slice.127
  623.0 2.7 copy.53
  625.6 1.7 copy.54
  (96 shorter events, 40.0 us)
Async XLA Ops:
  7.2 83.9 %all-gather.7.cloned.1.call-start = ((), (), s32[]{:S(2)}) async-start(), calls=%async_computation.1 | async-start | bytes 8110080 | tf_op jit(solution)/shard_map/all_gather | solution.py:769
  12.4 252.1 %all-gather.9.cloned.1.call-start = ((), (), s32[]{:S(2)}) async-start(), calls=%async_computation.3 | async-start | bytes 2359296 | tf_op jit(solution)/shard_map/all_gather | solution.py:823
  13.3 17.4 %collective-permute-start.1 = (f32[16,128]{1,0:T(8,128)S(1)}, f32[16,128]{1,0:T(8,128)S(1)}, u32[]{:S(2)}, u32[]{:S(2)}) collective-permute-start(f32[16,128]{1,0:T(8,128)S(1)} %broadcast_in_dim.40), channel_id=1, source_target_pairs={{0,2},{2,4},{4,6},{6,8},{8,10},{10,12},{12,14},{1,3},{3,5},{5,7},{... | collective-permute-start | bytes 24584 | tf_op jit(solution)/shard_map/ppermute | solution.py:792
  16.4 14.9 %collective-permute-start = (bf16[16,768]{1,0:T(8,128)(2,1)S(1)}, bf16[16,768]{1,0:T(8,128)(2,1)S(1)}, u32[]{:S(2)}, u32[]{:S(2)}) collective-permute-start(bf16[16,768]{1,0:T(8,128)(2,1)S(1)} %dynamic-slice_bitcast_fusion), channel_id=1, source_target_pairs={{0,2},{2,4},{4,6},{6,8},{8,10},{10,12},{12,14},{1,3},{3,5},{5,7},{... | collective-permute-start | bytes 73736 | tf_op jit(solution)/shard_map/ppermute | solution.py:791
  28.8 63.7 %copy-start.4 = (f32[16,768]{1,0:T(8,128)}, f32[16,768]{1,0:T(8,128)S(1)}, u32[]{:S(2)}) copy-start(f32[16,768]{1,0:T(8,128)S(1)} %all-gather) | copy-start | bytes 147460
  31.4 61.2 %copy-start.8 = (bf16[16,768]{1,0:T(8,128)(2,1)}, bf16[16,768]{1,0:T(8,128)(2,1)S(1)}, u32[]{:S(2)}) copy-start(bf16[16,768]{1,0:T(8,128)(2,1)S(1)} %collective-permute-done.halo) | copy-start | bytes 73732
  106.7 17.8 %copy-start = (bf16[2,512,768]{2,1,0:T(8,128)(2,1)S(1)}, bf16[2,512,768]{2,1,0:T(8,128)(2,1)}, u32[]{:S(2)}) copy-start(bf16[2,512,768]{2,1,0:T(8,128)(2,1)} %cot.3) | copy-start | bytes 4718596
  108.9 4.1 collective-permute-start.2
  114.2 12.2 %collective-permute-start.3 = (f32[128,1536]{1,0:T(8,128)S(1)}, f32[128,1536]{1,0:T(8,128)S(1)}, u32[]{:S(2)}, u32[]{:S(2)}) collective-permute-start(f32[128,1536]{1,0:T(8,128)S(1)} %multiply_add_fusion.1), channel_id=1, source_target_pairs={{0,2},{2,4},{4,6},{6,8},{8,10},{10,12},{12,14},{1,3},{3,5},{5,7},{... | collective-permute-start | bytes 2359304 | tf_op jit(solution)/shard_map/ppermute | solution.py:736
  126.4 0.9 copy-start.1
  149.9 13.2 %collective-permute-start.4 = (f32[128,1536]{1,0:T(8,128)S(1)}, f32[128,1536]{1,0:T(8,128)S(1)}, u32[]{:S(2)}, u32[]{:S(2)}) collective-permute-start(f32[128,1536]{1,0:T(8,128)S(1)} %broadcast_add_fusion), channel_id=1, source_target_pairs={{2,0},{4,2},{6,4},{8,6},{10,8},{12,10},{14,12},{3,1},{5,3},{7,5},{... | collective-permute-start | bytes 2359304 | tf_op jit(solution)/shard_map/ppermute | solution.py:736
  151.2 219.9 %all-reduce.5.cloned.1.call-start = ((), (), s32[]{:S(2)}) async-start(), calls=%async_computation.5 | async-start | bytes 278528 | tf_op jit(solution)/shard_map/psum | solution.py:821
  164.3 14.5 %collective-permute-start.5 = (f32[128,1536]{1,0:T(8,128)S(1)}, f32[128,1536]{1,0:T(8,128)S(1)}, u32[]{:S(2)}, u32[]{:S(2)}) collective-permute-start(f32[128,1536]{1,0:T(8,128)S(1)} %multiply_add_fusion), channel_id=1, source_target_pairs={{2,0},{4,2},{6,4},{8,6},{10,8},{12,10},{14,12},{3,1},{5,3},{7,5},{... | collective-permute-start | bytes 2359304 | tf_op jit(solution)/shard_map/ppermute | solution.py:736
  178.8 0.9 copy-start.5
  179.7 40.8 %copy-start.6 = (bf16[512,768]{1,0:T(8,128)(2,1)S(1)}, bf16[512,768]{1,0:T(8,128)(2,1)}, u32[]{:S(2)}) copy-start(bf16[512,768]{1,0:T(8,128)(2,1)} %get-tuple-element.65) | copy-start | bytes 2359300
  217.8 14.4 %collective-permute-start.6 = (f32[16,1536]{1,0:T(8,128)}, f32[16,1536]{1,0:T(8,128)S(1)}, u32[]{:S(2)}, u32[]{:S(2)}) collective-permute-start(f32[16,1536]{1,0:T(8,128)} %get-tuple-element.76), channel_id=1, source_target_pairs={{2,0},{4,2},{6,4},{8,6},{10,8},{12,10},{14,12},{3,1},{5,3},{7,5},{... | collective-permute-start | bytes 294920 | tf_op jit(solution)/shard_map/ppermute | solution.py:811
  219.1 13.0 %collective-permute-start.7 = (f32[16,256]{1,0:T(8,128)}, f32[16,256]{1,0:T(8,128)S(1)}, u32[]{:S(2)}, u32[]{:S(2)}) collective-permute-start(f32[16,256]{1,0:T(8,128)} %get-tuple-element.78), channel_id=1, source_target_pairs={{2,0},{4,2},{6,4},{8,6},{10,8},{12,10},{14,12},{3,1},{5,3},{7,5},{... | collective-permute-start | bytes 49160 | tf_op jit(solution)/shard_map/ppermute | solution.py:811
  232.2 0.6 copy-start.9
  232.2 0.6 copy-start.7
  232.8 15.2 %copy-start.3 = (bf16[2,768,768]{2,1,0:T(8,128)(2,1)S(1)}, bf16[2,768,768]{2,1,0:T(8,128)(2,1)}, u32[]{:S(2)}) copy-start(bf16[2,768,768]{2,1,0:T(8,128)(2,1)} %get-tuple-element.84) | copy-start | bytes 7077892
  247.4 173.0 %all-gather.11.cloned.1.call-start = ((), (), s32[]{:S(2)}) async-start(), calls=%async_computation.4 | async-start | bytes 4718592 | tf_op jit(solution)/shard_map/all_gather | solution.py:824
  248.0 369.4 %reduce-scatter.2.cloned.1.call-start = ((), (), s32[]{:S(2)}) async-start(), calls=%async_computation.2 | async-start | bytes 17031168 | tf_op jit(solution)/shard_map/reduce_scatter | solution.py:818
  420.4 205.2 %copy-start.2 = (f32[1024,768]{1,0:T(8,128)S(1)}, f32[1024,768]{1,0:T(8,128)}, u32[]{:S(2)}) copy-start(f32[1024,768]{1,0:T(8,128)} %all-gather.11.cloned.1.call-done) | copy-start | bytes 9437188
  625.6 1.7 copy-start.10
Sparse Core Ops, SparseCore 0:
  12.6 78.5 all-gather.6
  151.3 36.9 all-gather.8
  247.5 123.4 all-reduce.4
  372.5 47.8 all-gather.10
  426.6 190.7 reduce-scatter.1

commit v2 on v1

--- a/solution.py
+++ b/solution.py
@@ -654,8 +654,11 @@
         state = joined(cg_state, edge_state)
         steps = srg[...]
         turned = hidden_t[...]
-        small_out[:, :WIDE] = mm(turned, state).astype(LOW)
-        small_out[:, WIDE:] = mm(turned, steps).astype(LOW)
+        state_part = mm(turned, state).astype(LOW)
+        step_part = mm(turned, steps).astype(LOW)
+        for part in range(2):
+            small_out[part, :, :LANES] = state_part[:, part * LANES : (part + 1) * LANES]
+            small_out[part, :, LANES:] = step_part
         acc = mm_nt(state[:, :LANES], w_small[0, :, :LANES])
         acc += mm_nt(state[:, LANES:], w_small[1, :, :LANES])
         acc += mm_nt(steps, w_small[0, :, LANES:])
@@ -681,7 +684,7 @@
         pull = jnp.sum(normed * value, axis=1, keepdims=True) / value.shape[1]
         token_out[...] = (
             cot[0].astype(F32) + scale * normed - (scale * scale * scale) * value * pull
-        )
+        ).astype(LOW)
 
 
 def tail(which, tokens, cot, hidden_t, gpg, cg, edge, cg_state, edge_state, srg, weights):
@@ -692,8 +695,8 @@
     outs = (
         (shape((2, model, 3 * WIDE), LOW), parts),
         (shape((2, model, 3 * WIDE), LOW), parts),
-        (shape((model, WIDE + LANES), LOW), const((model, WIDE + LANES))),
-        (shape((rows, model), F32), const((rows, model))),
+        (shape((2, model, WIDE), LOW), const((2, model, WIDE))),
+        (shape((rows, model), LOW), const((rows, model))),
         (shape((8, model), F32), const((8, model))),
     )
     return pl.pallas_call(
@@ -727,29 +730,657 @@
     )
 
 
-def chained(fold, gain, hops, backward):
+def ring_place():
+    position = lax.axis_index("context")
+    return {
+        "x": lax.axis_index("dp"),
+        "y": lax.axis_index("tensor"),
+        "z": position // 2,
+        "c": position % 2,
+    }
+
+
+def device(x, y, z, c):
+    return {"dp": x, "context": z * 2 + c, "tensor": y}
+
+
+def remote(src, dst, send_sem, recv_sem, target):
+    return pltpu.make_async_remote_copy(
+        src_ref=src,
+        dst_ref=dst,
+        send_sem=send_sem,
+        recv_sem=recv_sem,
+        device_id=target,
+        device_id_type=pl.DeviceIdType.MESH,
+    )
+
+
+def greet(targets, depth):
+    barrier = pltpu.get_barrier_semaphore()
+    for target in targets:
+        pl.semaphore_signal(barrier, inc=1, device_id=target, device_id_type=pl.DeviceIdType.MESH)
+    if depth > 1:
+        here = ring_place()
+
+        def one(step, carry):
+            away = lax.rem(here["z"] + step, depth)
+            pl.semaphore_signal(
+                barrier,
+                inc=1,
+                device_id=device(here["x"], here["y"], away, here["c"]),
+                device_id_type=pl.DeviceIdType.MESH,
+            )
+            return carry
+
+        lax.fori_loop(1, depth, one, 0)
+    pl.semaphore_wait(barrier, len(targets) + max(depth - 1, 0))
+
+
+def each(count, run, first=0):
+    def one(step, carry):
+        run(step)
+        return carry
+
+    lax.fori_loop(first, count, one, 0)
+
+
+def gather_body(
+    depth, packed, par_own, edge_own, docs_own, weights, par, edge, docs, docs_in, sends, lands,
+    side_send, side_land, local
+):
+    here = ring_place()
+    x, y, z, c = here["x"], here["y"], here["z"], here["c"]
+    count = 2 * depth
+    position = z * 2 + c
+    onward, behind = lax.rem(position + 1, count), lax.rem(position + count - 1, count)
+    other = 1 - c
+    x1, y1 = x + (1 - c) * (1 - 2 * x), y + c * (1 - 2 * y)
+    x2, y2 = x + c * (1 - 2 * x), y + (1 - c) * (1 - 2 * y)
+    partner = device(x, y, z, other)
+    first_peer, second_peer = device(x1, y1, z, c), device(x2, y2, z, c)
+    y_peer = device(x, 1 - y, z, c)
+    next_one = {"dp": x, "context": onward, "tensor": y}
+    last_one = {"dp": x, "context": behind, "tensor": y}
+    greet([partner, device(1 - x, y, z, c), y_peer, next_one, last_one], depth)
+
+    def chunk(cx, cy, cz, cc):
+        return weights.at[cy, cx, cz * 2 + cc]
+
+    def landed(cx, cy, cz, cc):
+        return lands.at[((cy * 2 + cx) * depth + cz) * 2 + cc]
+
+    def moved(kind, index, cx, cy, cz, cc, target, own=False):
+        return remote(
+            packed if own else chunk(cx, cy, cz, cc),
+            chunk(cx, cy, cz, cc),
+            sends.at[kind, index],
+            landed(cx, cy, cz, cc),
+            target,
+        )
+
+    def arrive(cx, cy, cz, cc):
+        moved(0, 0, cx, cy, cz, cc, partner).wait_recv()
+
+    sides = [
+        remote(edge_own, edge, side_send.at[0], side_land.at[0], next_one),
+        remote(docs_own, docs_in, side_send.at[1], side_land.at[1], next_one),
+        remote(par_own, par.at[y], side_send.at[2], side_land.at[2], y_peer),
+    ]
+    keep = pltpu.make_async_copy(packed, chunk(x, y, z, c), local.at[0])
+    keep_par = pltpu.make_async_copy(par_own, par.at[y], local.at[1])
+    keep.start()
+    keep_par.start()
+
+    def to_depth(step):
+        away = lax.rem(z + step, depth)
+        return moved(3, step, x, y, z, c, device(x, y, away, c), True)
+
+    own_first = moved(1, 0, x, y, z, c, first_peer, True)
+    own_second = moved(2, 0, x, y, z, c, second_peer, True)
+    own_core = moved(0, 0, x, y, z, c, partner, True)
+    own_first.start()
+    own_second.start()
+    each(depth, lambda step: to_depth(step).start(), 1)
+    own_core.start()
+    for copy in sides:
+        copy.start()
+
+    def near(step):
+        away = lax.rem(z + depth - step, depth)
+        arrive(x, y, away, c)
+        moved(1, step, x, y, away, c, first_peer).start()
+        moved(2, step, x, y, away, c, second_peer).start()
+        moved(0, step, x, y, away, c, partner).start()
+
+    each(depth, near, 1)
+
+    def across(step):
+        away = lax.rem(z + depth - step, depth)
+        arrive(x1, y1, away, c)
+        moved(2, depth + step, x1, y1, away, c, second_peer).start()
+        moved(0, depth + step, x1, y1, away, c, partner).start()
+
+    each(depth, across)
+
+    def far(step):
+        away = lax.rem(z + depth - step, depth)
+        arrive(x2, y2, away, c)
+        moved(0, 2 * depth + step, x2, y2, away, c, partner).start()
+        arrive(1 - x, 1 - y, away, c)
+        moved(0, 3 * depth + step, 1 - x, 1 - y, away, c, partner).start()
+
+    each(depth, far)
+
+    def from_core(step):
+        arrive(x, y, step, other)
+        arrive(1 - x, y, step, other)
+        arrive(x, 1 - y, step, other)
+        arrive(1 - x, 1 - y, step, other)
+
+    each(depth, from_core)
+    for copy in sides:
+        copy.wait_recv()
+    docs[...] = jnp.where(position == 0, -1.0, docs_in[...])
+    each(4 * depth, lambda step: moved(0, step, x, y, z, c, partner).wait_send())
+    each(depth, lambda step: moved(1, step, x, y, z, c, partner).wait_send())
+    each(2 * depth, lambda step: moved(2, step, x, y, z, c, partner).wait_send())
+    each(depth, lambda step: moved(3, step, x, y, z, c, partner).wait_send(), 1)
+    for copy in sides:
+        copy.wait_send()
+    keep.wait()
+    keep_par.wait()
+
+
+def gather(packed, par_own, edge_own, docs_own):
     count = lax.axis_size("context")
+    depth = count // 2
+    shape = jax.ShapeDtypeStruct
+    vmem = pl.BlockSpec(memory_space=pltpu.VMEM)
+    return pl.pallas_call(
+        functools.partial(gather_body, depth),
+        out_shape=(
+            shape((2, 2, count) + packed.shape, LOW),
+            shape((2,) + par_own.shape, F32),
+            shape(edge_own.shape, LOW),
+            shape(docs_own.shape, F32),
+        ),
+        in_specs=[vmem] * 4,
+        out_specs=[pl.BlockSpec(memory_space=pl.ANY), vmem, vmem, vmem],
+        scratch_shapes=[
+            pltpu.VMEM(docs_own.shape, F32),
+            pltpu.SemaphoreType.DMA((4, 4 * depth)),
+            pltpu.SemaphoreType.DMA((8 * depth,)),
+            pltpu.SemaphoreType.DMA((3,)),
+            pltpu.SemaphoreType.DMA((3,)),
+            pltpu.SemaphoreType.DMA((2,)),
+        ],
+        compiler_params=params(collective_id=0, has_side_effects=True),
+        name="gather",
+    )(packed, par_own, edge_own, docs_own)
+
+
+CUTS = 4
+
+
+def chain_body(
+    depth, rounds, backward, fold, gain, out, from_mate, from_chip, to_mate, to_chip, mate_send,
+    mate_land, chip_send, chip_land
+):
+    here = ring_place()
+    x, y, z, c = here["x"], here["y"], here["z"], here["c"]
+    first = 1 if backward else 0
+    order = depth - 1 - z if backward else z
     by = -1 if backward else 1
-    pairs = [(i, i + by) for i in range(count) if 0 <= i + by < count]
-    carry = jnp.zeros_like(fold)
-    for _ in range(hops):
-        carry = lax.ppermute(fold + gain[0:1] * carry, "context", pairs)
-    return carry
+    width = fold.shape[1] // CUTS
+    mate = device(x, y, z, 1 - c)
+    after = device(x, y, z + by, first)
+    before = device(x, y, z - by, 1 - first)
+    leads = c == first
+    barrier = pltpu.get_barrier_semaphore()
+
+    def signal(target):
+        pl.semaphore_signal(barrier, inc=1, device_id=target, device_id_type=pl.DeviceIdType.MESH)
+
+    signal(mate)
+
+    linked_before = leads & (order > 0)
+    linked_after = jnp.logical_not(leads) & (order < depth - 1)
+
+    @pl.when(linked_before)
+    def _():
+        signal(before)
+
+    @pl.when(linked_after)
+    def _():
+        signal(after)
+
+    pl.semaphore_wait(
+        barrier, 1 + linked_before.astype(jnp.int32) + linked_after.astype(jnp.int32)
+    )
+
+    def mate_copy(turn, cut):
+        return remote(
+            to_mate.at[turn, cut], from_mate.at[turn, cut], mate_send.at[turn, cut],
+            mate_land.at[turn, cut], mate,
+        )
+
+    def chip_copy(turn, cut):
+        return remote(
+            to_chip.at[turn, cut], from_chip.at[turn, cut], chip_send.at[turn, cut],
+            chip_land.at[turn, cut], after,
+        )
+
+    def lanes(cut):
+        return slice(cut * width, (cut + 1) * width)
+
+    def joined(cut, arrived):
+        at = lanes(cut)
+        return (fold[:, at] + gain[0:1, at] * arrived.astype(F32)).astype(LOW)
+
+    @pl.when(leads)
+    def _():
+        for cut in range(CUTS):
+            to_mate[0, cut] = fold[:, lanes(cut)].astype(LOW)
+            mate_copy(0, cut).start()
+
+        @pl.when(order > 0)
+        def _():
+            for turn in range(rounds):
+                for cut in range(CUTS):
+                    chip_copy(turn, cut).wait_recv()
+                    to_mate[turn + 1, cut] = joined(cut, from_chip[turn, cut])
+                    mate_copy(turn + 1, cut).start()
+            for cut in range(CUTS):
+                out[:, lanes(cut)] = from_chip[rounds - 1, cut]
+
+        @pl.when(order == 0)
+        def _():
+            for turn in range(rounds):
+                for cut in range(CUTS):
+                    to_mate[turn + 1, cut] = fold[:, lanes(cut)].astype(LOW)
+                    mate_copy(turn + 1, cut).start()
+            out[...] = jnp.zeros_like(out)
+
+        for turn in range(rounds + 1):
+            for cut in range(CUTS):
+                mate_copy(turn, cut).wait_send()
+
+    @pl.when(jnp.logical_not(leads))
+    def _():
+        for turn in range(rounds):
+            for cut in range(CUTS):
+                mate_copy(turn, cut).wait_recv()
+
+                @pl.when(order < depth - 1)
+                def _():
+                    to_chip[turn, cut] = joined(cut, from_mate[turn, cut])
+                    chip_copy(turn, cut).start()
+
+        for cut in range(CUTS):
+            mate_copy(rounds, cut).wait_recv()
+            out[:, lanes(cut)] = from_mate[rounds, cut]
+
+        @pl.when(order < depth - 1)
+        def _():
+            for turn in range(rounds):
+                for cut in range(CUTS):
+                    chip_copy(turn, cut).wait_send()
+
+
+def chain(fold, gain, rounds, backward, number):
+    depth = lax.axis_size("context") // 2
+    states, wide = fold.shape
+    vmem = pl.BlockSpec(memory_space=pltpu.VMEM)
+    slots = lambda turns: pltpu.VMEM((turns, CUTS, states, wide // CUTS), LOW)
+    marks = lambda turns: pltpu.SemaphoreType.DMA((turns, CUTS))
+    return pl.pallas_call(
+        functools.partial(chain_body, depth, rounds, backward),
+        out_shape=jax.ShapeDtypeStruct(fold.shape, LOW),
+        in_specs=[vmem] * 2,
+        out_specs=vmem,
+        scratch_shapes=[
+            slots(rounds + 1),
+            slots(rounds),
+            slots(rounds + 1),
+            slots(rounds),
+            marks(rounds + 1),
+            marks(rounds + 1),
+            marks(rounds),
+            marks(rounds),
+        ],
+        compiler_params=params(collective_id=number, has_side_effects=True),
+        name="chain_back" if backward else "chain",
+    )(fold, gain)
+
+
+def edges_body(count, own, own_state, out, out_state, send, land):
+    position = lax.axis_index("context")
+    before, after = {"context": position - 1}, {"context": position + 1}
+    barrier = pltpu.get_barrier_semaphore()
+
+    def signal(target):
+        pl.semaphore_signal(barrier, inc=1, device_id=target, device_id_type=pl.DeviceIdType.MESH)
+
+    @pl.when(position > 0)
+    def _():
+        signal(before)
+
+    @pl.when(position < count - 1)
+    def _():
+        signal(after)
+
+    has_before = (position > 0).astype(jnp.int32)
+    has_after = (position < count - 1).astype(jnp.int32)
+    pl.semaphore_wait(barrier, has_before + has_after)
+
+    copies = [
+        remote(own, out, send.at[0], land.at[0], before),
+        remote(own_state, out_state, send.at[1], land.at[1], before),
+    ]
+
+    @pl.when(position > 0)
+    def _():
+        for copy in copies:
+            copy.start()
+
+    @pl.when(position == count - 1)
+    def _():
+        out[...] = jnp.zeros_like(out)
+        out_state[...] = jnp.zeros_like(out_state)
+
+    @pl.when(position < count - 1)
+    def _():
+        for copy in copies:
+            copy.wait_recv()
+
+    @pl.when(position > 0)
+    def _():
+        for copy in copies:
+            copy.wait_send()
+
+
+def edges(own, own_state):
+    vmem = pl.BlockSpec(memory_space=pltpu.VMEM)
+    return pl.pallas_call(
+        functools.partial(edges_body, lax.axis_size("context")),
+        out_shape=(
+            jax.ShapeDtypeStruct(own.shape, F32),
+            jax.ShapeDtypeStruct(own_state.shape, F32),
+        ),
+        in_specs=[vmem] * 2,
+        out_specs=[vmem] * 2,
+        scratch_shapes=[pltpu.SemaphoreType.DMA((2,)), pltpu.SemaphoreType.DMA((2,))],
+        compiler_params=params(collective_id=3, has_side_effects=True),
+        name="edges",
+    )(own, own_state)
+
+
+def reduce_body(
+    depth, gate, inner, exits, small, token, vector, out, state_out, vector_out, token_out, own, core,
+    send1, land1, send2, land2, send3, land3, state_own, vec_send, vec_land, own_sem, core_send,
+    core_land, s1, l1, s2, l2, s3, l3, vs, vl, ts, tl, keep_sem
+):
+    here = ring_place()
+    x, y, z, c = here["x"], here["y"], here["z"], here["c"]
+    other = 1 - c
+    x1, y1 = x + (1 - c) * (1 - 2 * x), y + c * (1 - 2 * y)
+    x2, y2 = x + c * (1 - 2 * x), y + (1 - c) * (1 - 2 * y)
+    partner = device(x, y, z, other)
+    first_peer, second_peer = device(x1, y1, z, c), device(x2, y2, z, c)
+    x_peer, y_peer = device(1 - x, y, z, c), device(x, 1 - y, z, c)
+    wide = gate.shape[-1]
+    tall = 3 * wide
+    greet([partner, x_peer, y_peer], depth)
+    pieces = [
+        (gate, slice(0, wide)),
+        (inner, slice(wide, 2 * wide)),
+        (exits, slice(2 * wide, tall)),
+        (small, slice(tall, tall + WIDE)),
+    ]
+
+    token_copy = remote(token, token_out.at[y], ts.at[0], tl.at[0], y_peer)
+    token_keep = pltpu.make_async_copy(token, token_out.at[y], keep_sem.at[0])
+    token_keep.start()
+
+    def spot(step):
+        return lax.rem(z + 1 + step, depth)
+
+    def core_pieces(cx, cy, cz):
+        for ref, cols in pieces:
+            yield remote(
+                ref.at[cy, cx, cz * 2 + other],
+                core.at[cy, cx, cz, :, cols],
+                core_send.at[cy, cx, cz],
+                core_land.at[cy, cx, cz],
+                partner,
+            )
+
+    def core_whole(cx, cy, cz):
+        return remote(
+            core.at[cy, cx, cz], core.at[cy, cx, cz], core_send.at[cy, cx, cz],
+            core_land.at[cy, cx, cz], partner,
+        )
+
+    def own_pieces(cx, cy, cz):
+        for ref, cols in pieces:
+            yield pltpu.make_async_copy(
+                ref.at[cy, cx, cz * 2 + c], own.at[cy, cx, cz, :, cols], own_sem.at[cy, cx, cz]
+            )
+
+    def own_whole(cx, cy, cz):
+        return pltpu.make_async_copy(
+            own.at[cy, cx, cz], own.at[cy, cx, cz], own_sem.at[cy, cx, cz]
+        )
+
+    def start(step):
+        cz = spot(step)
+        for cy in range(2):
+            for cx in range(2):
+                for copy in core_pieces(cx, cy, cz):
+                    copy.start()
+                for copy in own_pieces(cx, cy, cz):
+                    copy.start()
+
+    vec_send[0] = vector[...]
+    vec_targets = [partner, x_peer, y_peer]
+
+    def vec_copy(turn):
+        return remote(vec_send.at[turn], vec_land.at[turn], vs.at[turn], vl.at[turn], vec_targets[turn])
+
+    def vec_far(step):
+        away = lax.rem(z + step, depth)
+        return remote(
+            vec_send.at[3], vec_land.at[3 + z], vs.at[2 + step], vl.at[3 + z],
+            device(x, y, away, c),
+        )
+
+    vec_copy(0).start()
+    each(depth, start)
+    token_copy.start()
+    for turn in range(3):
+        vec_copy(turn).wait_recv()
+        vec_send[turn + 1] = vec_send[turn] + vec_land[turn]
+        if turn < 2:
+            vec_copy(turn + 1).start()
+    each(depth, lambda step: vec_far(step).start(), 1)
+    vec_land[3 + z] = vec_send[3]
+
+    def base(cx, cy, cz):
+        return own[cy, cx, cz].astype(F32) + core[cy, cx, cz].astype(F32)
+
+    def first_copy(cz):
+        return remote(send1.at[cz], land1.at[cz], s1.at[cz], l1.at[cz], first_peer)
+
+    def second_copy(cz):
+        return remote(send2.at[cz], land2.at[cz], s2.at[cz], l2.at[cz], second_peer)
+
+    def third_copy(cz):
+        return remote(
+            send3.at[cz], land3.at[z], s3.at[cz], l3.at[z], device(x, y, cz, c)
+        )
+
+    def third_arrival(cz):
+        return remote(
+            send3.at[cz], land3.at[cz], s3.at[cz], l3.at[cz], device(x, y, cz, c)
+        )
+
+    mine = y + c * (x - y)
+
+    def other_axis(index):
+        return x + c * (index - x), y + (1 - c) * (index - y)
+
+    def stage1(step):
+        cz = spot(step)
+        for cy in range(2):
+            for cx in range(2):
+                core_whole(cx, cy, cz).wait_recv()
+                own_whole(cx, cy, cz).wait()
+        for index in range(2):
+            kx, ky = other_axis(index)
+            cx, cy = kx + (1 - c) * (1 - 2 * kx), ky + c * (1 - 2 * ky)
+            send1[cz, index] = base(cx, cy, cz).astype(LOW)
+        first_copy(cz).start()
+
+    def stage2(step):
+        cz = spot(step)
+        first_copy(cz).wait_recv()
+        kx, ky = other_axis(1 - mine)
+        send2[cz] = (base(kx, ky, cz) + land1[cz, 1 - mine].astype(F32)).astype(LOW)
+        second_copy(cz).start()
+
+    def final(cz):
+        second_copy(cz).wait_recv()
+        return base(x, y, cz) + land1[cz, mine].astype(F32) + land2[cz].astype(F32)
+
+    def stage3(step):
+        cz = spot(step)
+        send3[cz] = final(cz).astype(LOW)
+        third_copy(cz).start()
+
+    def turn(step):
+        @pl.when(step < depth)
+        def _():
+            stage1(step)
+
+        @pl.when((step >= 1) & (step <= depth))
+        def _():
+            stage2(step - 1)
+
+        @pl.when((step >= 2) & (step <= depth))
+        def _():
+            stage3(step - 2)
+
+    each(depth + 1, turn)
+    out[...] = final(z)
+
+    def add(step):
+        cz = lax.rem(z + step, depth)
+        third_arrival(cz).wait_recv()
+        out[...] += land3[cz].astype(F32)
+
+    each(depth, add, 1)
+    state_own[...] = out[:, tall : tall + NSTATE]
+    state_copy = remote(state_own, state_out.at[y], ts.at[1], tl.at[1], y_peer)
+    state_copy.start()
+    state_out[y] = state_own[...]
+
+    def vec_sum(step):
+        away = lax.rem(z + step, depth)
+        remote(
+            vec_send.at[3], vec_land.at[3 + away], vs.at[2 + step], vl.at[3 + away],
+            device(x, y, away, c),
+        ).wait_recv()
+
+    each(depth, vec_sum, 1)
+    vector_out[...] = vec_land[3]
+
+    def vec_add(step):
+        vector_out[...] += vec_land[3 + step]
+
+    each(depth, vec_add, 1)
+
+    for step in range(3):
+        vec_copy(step).wait_send()
+    each(depth, lambda step: vec_far(step).wait_send(), 1)
+
+    def sent(cz):
+        for cy in range(2):
+            for cx in range(2):
+                core_whole(cx, cy, cz).wait_send()
+        first_copy(cz).wait_send()
+        second_copy(cz).wait_send()
+
+    each(depth, sent)
+    each(depth, lambda step: third_copy(lax.rem(z + step, depth)).wait_send(), 1)
+    token_copy.wait()
+    state_copy.wait()
+    token_keep.wait()
+
+
+def reduce_all(gate, inner, exits, small, token, vector):
+    count = lax.axis_size("context")
+    depth = count // 2
+    own_rows = gate.shape[3]
+    tall = 3 * gate.shape[-1] + WIDE
+    shape = jax.ShapeDtypeStruct
+    vmem = pl.BlockSpec(memory_space=pltpu.VMEM)
+    anywhere = pl.BlockSpec(memory_space=pl.ANY)
+    buffer = lambda *lead: pltpu.VMEM(lead + (own_rows, tall), LOW)
+    sem = lambda *lead: pltpu.SemaphoreType.DMA(lead)
+    return pl.pallas_call(
+        functools.partial(reduce_body, depth),
+        out_shape=(
+            shape((own_rows, tall), F32),
+            shape((2, own_rows, NSTATE), F32),
+            shape(vector.shape, F32),
+            shape((2,) + token.shape, LOW),
+        ),
+        in_specs=[anywhere] * 4 + [vmem] * 2,
+        out_specs=[vmem, vmem, vmem, anywhere],
+        scratch_shapes=[
+            buffer(2, 2, depth),
+            buffer(2, 2, depth),
+            buffer(depth, 2),
+            buffer(depth, 2),
+            buffer(depth),
+            buffer(depth),
+            buffer(depth),
+            buffer(depth),
+            pltpu.VMEM((own_rows, NSTATE), F32),
+            pltpu.VMEM((4,) + vector.shape, F32),
+            pltpu.VMEM((3 + depth,) + vector.shape, F32),
+            sem(2, 2, depth),
+            sem(2, 2, depth),
+            sem(2, 2, depth),
+            sem(depth),
+            sem(depth),
+            sem(depth),
+            sem(depth),
+            sem(depth),
+            sem(depth),
+            sem(2 + depth),
+            sem(3 + depth),
+            sem(2),
+            sem(2),
+            sem(1),
+        ],
+        compiler_params=params(collective_id=4, has_side_effects=True),
+        name="reduce_all",
+    )(gate, inner, exits, small, token, vector)
 
 
 def body(
     tokens, documents, norm_gain, entry_weight, state_weight, step_weight, inner_kernel,
     state_filter, step_bias, decay_log, skip_gain, gate_gain, exit_weight, cotangent,
 ):
-    every = ("tensor", "dp", "context")
     seqs, rows, model = tokens.shape
     count = lax.axis_size("context")
     position, side = lax.axis_index("context"), lax.axis_index("tensor")
-    group_count = lax.axis_size("dp") * count
     own_rows = norm_gain.shape[0]
+    wide = 3 * WIDE
     which = jnp.reshape(side, (1,)).astype(jnp.int32)
     longest = rows * count // 4
-    hops = min(count - 1, -(-(longest - 1) // rows))
+    rounds = min(count // 2 - 1, -(-(longest - 1) // (2 * rows)))
 
     first = (side == 0).astype(F32)
     state_half = jnp.where(side == 0, state_weight[:, :NSTATE], state_weight[:, NSTATE:])
@@ -766,7 +1397,6 @@
         ],
         axis=1,
     ).astype(LOW)
-    weights = lax.all_gather(packed, every, axis=0, tiled=True).reshape(2, model, -1)
 
     def placed(v):
         return jnp.concatenate([v * first, v * (1.0 - first), jnp.zeros((LANES - 24,), F32)])
@@ -777,69 +1407,71 @@
     par_own = jnp.concatenate(
         [inner_kernel, gate_gain[None], row6[None], jnp.zeros((1, model), F32)], axis=0
     )
-    par = lax.all_gather(par_own, "tensor", axis=0)
-    par_heads = jnp.concatenate(
-        [(par[0, 6] + par[1, 6])[: 3 * LANES].reshape(3, LANES), jnp.zeros((5, LANES), F32)], axis=0
-    )
-    filt = jnp.concatenate([state_filter, jnp.zeros((3, WIDE), F32)], axis=0)
-
     docs = lax.dynamic_index_in_dim(documents, side, 0, keepdims=False).astype(F32)
     doc_col = jnp.broadcast_to(docs[:, None], (rows, LANES))
     doc_row = jnp.broadcast_to(docs[None], (8, rows))
-    forward = [(i, i + 1) for i in range(count - 1)]
-    own_tokens = lax.dynamic_index_in_dim(tokens, side, 0, keepdims=False)
-    halo = lax.ppermute(own_tokens[-HALO:], "context", forward)
-    halo_docs = lax.ppermute(doc_col[-HALO:], "context", forward)
-    halo_docs = jnp.where(position == 0, -1.0, halo_docs)
+    edge_own = lax.dynamic_index_in_dim(tokens[:, -HALO:], side, 0, keepdims=False)
+    weights, par, halo, halo_docs = gather(packed, par_own, edge_own, doc_col[-HALO:])
+    weights = weights.reshape(2, model, -1)
+    par_heads = jnp.concatenate(
+        [(par[0, 6] + par[1, 6])[: 3 * LANES].reshape(3, LANES), jnp.zeros((5, LANES), F32)], axis=0
+    )
+    filt = jnp.concatenate([state_filter, jnp.zeros((3, WIDE), F32)], axis=0)
 
     (
         hidden, cin, gate, pre, loc, fold, gain, cin_state, pre_state, bc, bct, score, mask, zst, dt,
         sp, cumt, fac, match,
     ) = front(which, tokens, halo, halo_docs, doc_col, doc_row, weights, par, par_heads, filt)
-    carry = chained(fold, gain, hops, False)
+    carry = chain(fold, gain, rounds, False, 1)
     cot_t = lax.dynamic_index_in_dim(cotangent, side, 0, keepdims=False).T
     block_own, exit_part, dy, gpg, enter, gate_row, skip_row = middle(
         which, tokens, cotangent, cot_t, pre, gate, loc, carry, weights, par, par_heads, bc, bct,
         score, mask, sp, cumt, fac,
     )
-    adj = chained(enter, gain, hops, True)
+    block_other = lax.ppermute(block_own, "tensor", [(0, 1), (1, 0)])
+    adj = chain(enter, gain, rounds, True, 2)
     cg, edge, taps, cg_state, edge_state, taps_state, srg, head_rows = scan_back(
         pre, dy, loc, carry, adj, cin, par, par_heads, filt, cin_state, pre_state, bc, bct, score,
         mask, sp, cumt, fac, match, zst, dt,
     )
-    back = [(i + 1, i) for i in range(count - 1)]
-    edge, edge_state = lax.ppermute((edge, edge_state), "context", back)
+    edge, edge_state = edges(edge, edge_state)
     gate_part, inner_part, small_part, token_own, norm_row = tail(
         which, tokens, cotangent, hidden.T, gpg, cg, edge, cg_state, edge_state, srg, weights
     )
-
-    small_both = jnp.stack([small_part, small_part])
-    parts = jnp.concatenate([gate_part, inner_part, exit_part, small_both], axis=2)
-    mine = lax.psum_scatter(
-        parts.reshape(2 * model, -1).astype(F32), every, scatter_dimension=0, tiled=True
-    )
-    smalls = lax.psum((taps, taps_state, gate_row, skip_row, head_rows, norm_row), every)
-    taps, taps_state, gate_row, skip_row, head_rows, norm_row = smalls
-    block_out = lax.all_gather(block_own, "tensor", axis=0)
-    token_grad = lax.all_gather(token_own, "tensor", axis=0)
-    wide = 3 * WIDE
+    row5 = jnp.concatenate([gate_row[0], head_rows[0], skip_row[0]])
+    row6 = jnp.concatenate([norm_row[0], head_rows[1], jnp.zeros((2 * wide + WIDE - model - LANES,))])
+    vector = jnp.concatenate(
+        [
+            jnp.concatenate([taps[: CONV + 1], taps_state[: CONV + 1]], axis=1),
+            row5[None],
+            row6[None],
+            jnp.zeros((1, 2 * wide + WIDE), F32),
+        ],
+        axis=0,
+    )
+    cut = lambda v: v.reshape(2, 2, count, own_rows, v.shape[-1])
+    mine, state_both, vector, token_both = reduce_all(
+        cut(gate_part), cut(inner_part), cut(exit_part), cut(small_part), token_own, vector
+    )
+    block_out = jnp.where(
+        (jnp.arange(2) == side)[:, None, None], block_own[None], block_other[None]
+    )
     at = lax.axis_index("dp") * count + position
     half = lambda v: lax.dynamic_slice_in_dim(v, side * wide, wide, axis=-1)
-    twelve = lambda v: lax.dynamic_slice_in_dim(v[:24], side * 12, 12, axis=0)
-    step_grad = lax.dynamic_slice_in_dim(mine[:, 9 * WIDE + WIDE : 9 * WIDE + WIDE + 24], side * 12, 12, axis=1)
+    twelve = lambda v: lax.dynamic_slice_in_dim(v[..., :24], side * 12, 12, axis=-1)
     return (
         block_out,
-        token_grad,
-        lax.dynamic_slice_in_dim(norm_row[0], at * own_rows, own_rows, axis=0),
+        token_both.astype(F32),
+        lax.dynamic_slice_in_dim(vector[6], at * own_rows, own_rows, axis=0),
         jnp.stack([mine[:, :wide], mine[:, wide : 2 * wide]], axis=1),
-        mine[:, 9 * WIDE : 10 * WIDE],
-        step_grad,
-        half(taps[: CONV + 1]),
-        taps_state[: CONV + 1],
-        twelve(head_rows[0]),
-        twelve(head_rows[1]),
-        twelve(skip_row[0]),
-        half(gate_row[0]),
+        jnp.concatenate([state_both[0], state_both[1]], axis=1),
+        twelve(mine[:, 3 * wide + NSTATE :]),
+        half(vector[: CONV + 1, : 2 * wide]),
+        vector[: CONV + 1, 2 * wide :],
+        twelve(vector[5, 2 * wide : 2 * wide + LANES]),
+        twelve(vector[6, model : model + LANES]),
+        twelve(vector[5, 2 * wide + LANES :]),
+        half(vector[5, : 2 * wide]),
         mine[:, 2 * wide : 3 * wide],
     )
 

time: 636 us -> 281 us (0.44)
  waiting for transfers between devices: 444 us -> 0.01 us
  Pallas kernels: 88.2 us -> 239 us
  starting transfers between devices: 25 us -> 1.16 us
  other arithmetic: 27.8 us -> 10.6 us
  between operations: 14 us -> 0.86 us
    reduce_scatter x1 -> x0, waiting for transfers between devices: 197 us -> none  [body(): lax.psum_scatter(parts.reshape(2 * model, -1).astype(F32), every, scatter...]
    pallas_call x0 -> x5, Pallas kernels: none -> 151 us  [the longest x1 70.2 us: reduce_all(): pl.pallas_call(functools.partial(reduce_body, depth), out_shape=(shape((o...]
    psum x1 -> x0, waiting for transfers between devices: 107 us -> none  [body(): lax.psum((taps, taps_state, gate_row, skip_row, head_rows, norm_row), every)]
    all_gather x3 -> x0, waiting for transfers between devices: 102 us -> none  [the longest x1 59.7 us: body(): lax.all_gather(packed, every, axis=0, tiled=True).reshape(2, model, -1)]
    ppermute x8 -> x1, waiting for transfers between devices: 37.8 us -> 0.01 us  [body(): block_other = lax.ppermute(block_own, 'tensor', [(0, 1), (1, 0)])]
    ppermute x8 -> x1, starting transfers between devices: 24.8 us -> 1.16 us  [body(): block_other = lax.ppermute(block_own, 'tensor', [(0, 1), (1, 0)])]
    convert_element_type x1, other arithmetic: 10.1 us -> 1.9 us  [body(): token_both.astype(F32)]
    unnamed x28 -> x18, local copies, waits for them, and re-layouts: 9.99 us -> 3.41 us
  transfers between devices with their start and end apart: 13 -> 1, of which waited for: 9 -> 0; matrix products, arithmetic and copies ran while one was open for 5% -> 7% of each run, Pallas kernels for 8% -> 53%
where the time goes in v2:
time: 281 us; the launch traced here: 279 us
  Pallas kernels  239 us (85%)
  local copies, waits for them, and re-layouts  27.6 us (10%)
  other arithmetic  10.6 us (4%)
    pallas_call x1, Pallas kernels, reduce_all(): pl.pallas_call(functools.partial(reduce_body, depth), out_shape=(shape((o...  70.2 us
    pallas_call x1, Pallas kernels, gather(): pl.pallas_call(functools.partial(gather_body, depth), out_shape=(shape((2...  50.4 us
    pallas_call x1, Pallas kernels, scan_back(): pl.pallas_call(scan_back_body, out_shape=[out[0] for out in outs], grid=(...  38.2 us
    pallas_call x2, Pallas kernels, chain(): pl.pallas_call(functools.partial(chain_body, depth, rounds, backward), ou...  23 us
    pallas_call x1, Pallas kernels, middle(): pl.pallas_call(middle_body, out_shape=[out[0] for out in outs], grid_spec...  21.5 us
    pallas_call x1, Pallas kernels, tail(): pl.pallas_call(tail_body, out_shape=[out[0] for out in outs], grid_spec=p...  14.3 us
    pallas_call x1, Pallas kernels, front(): pl.pallas_call(front_body, out_shape=[out[0] for out in outs], grid_spec=...  14.1 us
    pallas_call x1, Pallas kernels, edges(): pl.pallas_call(functools.partial(edges_body, lax.axis_size('context')), o...  7.1 us
  transfers between devices with their start and end apart: 1, of which 0 were waited for; matrix products, arithmetic and copies ran while one was open for 7% of the time, Pallas kernels for 53%

profile of v2, /device:TPU:0, one launch (start us, length us, event | category | flops | bytes accessed | tf_op | source)
XLA Modules:
  0.0 279.0 jit_solution(4325223108545688803)
XLA Ops:
  4.5 1.0 copy.47
  5.5 0.9 convert.27
  9.4 1.4 maximum_maximum_fusion.1.par_own
  12.3 50.4 %gather.1 = (bf16[2,2,8,48,2560]{4,3,2,1,0:T(8,128)(2,1)}, f32[2,8,768]{2,1,0:T(8,128)}, bf16[16,768]{1,0:T(8,128)(2,1)}, f32[16,128]{1,0:T(8,128)}) custom-call(bf16[48,2560]{1,0:T(8,128)(2,1)} %concatenate.31.packed, f32[8,768]{1,0:T(8,128)} %maximum_maximum_fusion.1.par_own, bf16[16,768]{1,0:T(8,128)(2,1)} %dynamic-slice_bitcast_fusion.edge_own, ...), custom_call_target="tpu_custom_call" | custom-call | tf_op jit(solution)/shard_map/gather/pallas_call | solution.py:899
  64.1 1.3 concatenate.35.state_filter
  65.4 1.2 copy.35
  66.6 0.8 broadcast_in_dim.82.doc_col
  68.1 14.1 %front.1 = (bf16[512,768]{1,0:T(8,128)(2,1)}, bf16[528,1536]{1,0:T(8,128)(2,1)}, f32[512,1536]{1,0:T(8,128)}, f32[512,1536]{1,0:T(8,128)}, f32[512,1536]{1,0:T(8...) custom-call(s32[1]{0:T(128)} %bitcast.which, ...), custom_call_target="tpu_custom_call" | custom-call | tf_op jit(solution)/shard_map/front/pallas_call | solution.py:238
  82.2 4.5 %chain.1.carry_ref = bf16[128,1536]{1,0:T(8,128)(2,1)} custom-call(f32[128,1536]{1,0:T(8,128)} %get-tuple-element.69.fold, f32[8,1536]{1,0:T(8,128)} %get-tuple-element.70.gain), custom_call_target="tpu_custom_call" | custom-call | tf_op jit(solution)/shard_map/chain/pallas_call | solution.py:1036
  86.7 21.5 %middle.1 = (bf16[512,768]{1,0:T(8,128)(2,1)}, bf16[2,768,768]{2,1,0:T(8,128)(2,1)}, f32[512,1536]{1,0:T(8,128)}, bf16[512,1536]{1,0:T(8,128)(2,1)}, f32[128,153...) custom-call(s32[1]{0:T(128)} %bitcast.which, bf16[2,512,768]{2,1,0:T(8,128)(2,1)} %tokens.5, ...), custom_call_target="tpu_custom_call" | custom-call | tf_op jit(solution)/shard_map/middle/pallas_call | solution.py:409
  108.2 1.2 collective-permute-start
  109.3 18.5 %chain_back.1.adj_ref = bf16[128,1536]{1,0:T(8,128)(2,1)} custom-call(f32[128,1536]{1,0:T(8,128)} %get-tuple-element.82.fold, f32[8,1536]{1,0:T(8,128)} %get-tuple-element.70.gain), custom_call_target="tpu_custom_call" | custom-call | tf_op jit(solution)/shard_map/chain_back/pallas_call | solution.py:1036
  127.8 38.2 %scan_back.1 = (f32[512,1536]{1,0:T(8,128)}, f32[16,1536]{1,0:T(8,128)}, f32[8,1536]{1,0:T(8,128)}, f32[512,256]{1,0:T(8,128)}, f32[16,256]{1,0:T(8,128)}, /*ind...) custom-call(f32[512,1536]{1,0:T(8,128)} %get-tuple-element.66.pre_ref, ...), custom_call_target="tpu_custom_call" | custom-call | tf_op jit(solution)/shard_map/scan_back/pallas_call | solution.py:598
  166.9 0.8 slice_reduce_fusion
  168.4 1.2 copy.42
  169.6 7.1 %edges.1 = (f32[16,1536]{1,0:T(8,128)}, f32[16,256]{1,0:T(8,128)}) custom-call(f32[16,1536]{1,0:T(8,128)} %get-tuple-element.90.own, f32[16,256]{1,0:T(8,128)} %get-tuple-element.91.own_state), custom_call_target="tpu_custom_call" | custom-call | tf_op jit(solution)/shard_map/edges/pallas_call | solution.py:1104
  176.8 14.3 %tail.1 = (bf16[2,768,768]{2,1,0:T(8,128)(2,1)}, bf16[2,768,768]{2,1,0:T(8,128)(2,1)}, bf16[2,768,256]{2,1,0:T(8,128)(2,1)}, bf16[512,768]{1,0:T(8,128)(2,1)}, f32[8,768]{1,0:T(8,128)}) custom-call(s32[1]{0:T(128)} %bitcast.which, bf16[2,512,768]{2,1,0:T(8,128)(2,1)} %tokens.5, bf16[2,512,768]{2,1,0:T(8,128)(2,1)} %cot.3, bf16[768,512]{1,0:T(8,128)(2,1)} %bitcast.56, ...), custom_call_target="tpu_custom_call" | custom-call | tf_op jit(solution)/shard_map/tail/pallas_call | solution.py:702
  192.6 70.2 %reduce_all.1 = (f32[48,2560]{1,0:T(8,128)}, f32[2,48,128]{2,1,0:T(8,128)}, f32[8,1792]{1,0:T(8,128)}, bf16[2,512,768]{2,1,0:T(8,128)(2,1)}) custom-call(bf16[2,2,8,48,768]{4,3,2,1,0:T(8,128)(2,1)} %bitcast.58, bf16[2,2,8,48,768]{4,3,2,1,0:T(8,128)(2,1)} %bitcast.59, bf16[2,2,8,48,768]{4,3,2,1,0:T(8,128)(2,1)} %bitcast.57, ...), custom_call_target="tpu_custom_call" | custom-call | tf_op jit(solution)/shard_map/reduce_all/pallas_call | solution.py:1330
  262.8 1.9 fusion.6
  266.2 0.8 slice.127
  268.5 1.3 slice.134
  269.9 0.9 copy.43
  270.8 1.9 convert_element_type.26
  277.7 1.4 broadcast_select_fusion
  (66 shorter events, 21.3 us)
Async XLA Ops:
  0.6 64.8 %copy-start = (bf16[2,512,768]{2,1,0:T(8,128)(2,1)S(1)}, bf16[2,512,768]{2,1,0:T(8,128)(2,1)}, u32[]{:S(2)}) copy-start(bf16[2,512,768]{2,1,0:T(8,128)(2,1)} %cot.3) | copy-start | bytes 4718596
  108.2 169.5 %collective-permute-start = (bf16[512,768]{1,0:T(8,128)(2,1)}, bf16[512,768]{1,0:T(8,128)(2,1)S(1)}, u32[]{:S(2)}, u32[]{:S(2)}) collective-permute-start(bf16[512,768]{1,0:T(8,128)(2,1)} %get-tuple-element.78), channel_id=1, source_target_pairs={{0,1},{1,0},{2,3},{3,2},{4,5},{5,4},{6,7},{7,6},{8,9},{9,8},{10,11... | collective-permute-start | bytes 2359304 | tf_op jit(solution)/shard_map/ppermute | solution.py:1431
  127.8 40.6 %copy-start.2 = (bf16[512,768]{1,0:T(8,128)(2,1)S(1)}, bf16[512,768]{1,0:T(8,128)(2,1)}, u32[]{:S(2)}) copy-start(bf16[512,768]{1,0:T(8,128)(2,1)} %get-tuple-element.79) | copy-start | bytes 2359300
  176.7 15.1 %copy-start.5 = (f32[8,1536]{1,0:T(8,128)S(1)}, f32[8,1536]{1,0:T(8,128)}, u32[]{:S(2)}) copy-start(f32[8,1536]{1,0:T(8,128)} %get-tuple-element.101) | copy-start | bytes 147460
  176.8 15.1 %copy-start.6 = (f32[8,256]{1,0:T(8,128)S(1)}, f32[8,256]{1,0:T(8,128)}, u32[]{:S(2)}) copy-start(f32[8,256]{1,0:T(8,128)} %get-tuple-element.102) | copy-start | bytes 24580
  262.8 8.0 %copy-start.1 = (bf16[2,512,768]{2,1,0:T(8,128)(2,1)S(1)}, bf16[2,512,768]{2,1,0:T(8,128)(2,1)}, u32[]{:S(2)}) copy-start(bf16[2,512,768]{2,1,0:T(8,128)(2,1)} %get-tuple-element.107) | copy-start | bytes 4718596
  270.8 6.2 %copy-start.4 = (f32[2,48,128]{2,1,0:T(8,128)S(1)}, f32[2,48,128]{2,1,0:T(8,128)}, u32[]{:S(2)}) copy-start(f32[2,48,128]{2,1,0:T(8,128)} %get-tuple-element.110) | copy-start | bytes 147460
  270.8 6.8 %copy-start.3 = (bf16[512,768]{1,0:T(8,128)(2,1)S(1)}, bf16[512,768]{1,0:T(8,128)(2,1)}, u32[]{:S(2)}) copy-start(bf16[512,768]{1,0:T(8,128)(2,1)} %get-tuple-element.78) | copy-start | bytes 2359300

commit v3 on v1

--- a/solution.py
+++ b/solution.py
@@ -12,6 +12,7 @@
 EPSILON = 1e-05
 Q = 128
 HALO = 16
+EDGE = 8
 LANES = 128
 WIDE = 256
 LOG2E = 1.4426950408889634
@@ -121,7 +122,7 @@
             value = (ref[...] if ref is halo else ref[0]).astype(F32)
             scale = lax.rsqrt(jnp.mean(value * value, axis=1, keepdims=True) + EPSILON)
             hidden[first : first + count] = (value * scale * gain).astype(LOW)
-        hidden_out[...] = hidden[HALO:]
+        hidden_out[...] = jnp.transpose(hidden[HALO:])
         both = [mm(hidden[...], w_small[index]) for index in range(2)]
         cin = jnp.concatenate([both[0][:, :LANES], both[1][:, :LANES]], axis=1).astype(LOW)
         cin_state_out[...] = cin
@@ -215,7 +216,7 @@
     ext = rows + HALO
     shape = jax.ShapeDtypeStruct
     outs = (
-        (shape((rows, model), LOW), const((rows, model))),
+        (shape((model, rows), LOW), const((model, rows))),
         (shape((ext, wide), LOW), pl.BlockSpec((ext, WIDE), lambda s, w: (0, s))),
         (shape((rows, wide), F32), pl.BlockSpec((rows, WIDE), lambda s, w: (0, s))),
         (shape((rows, wide), F32), pl.BlockSpec((rows, WIDE), lambda s, w: (0, s))),
@@ -249,10 +250,10 @@
                 const((8, rows)),
                 pl.BlockSpec((1, model, WIDE), lambda s, w: (s // 3, 0, s % 3)),
                 pl.BlockSpec((1, model, WIDE), lambda s, w: (s // 3, 0, 3 + s % 3)),
-                pl.BlockSpec((2, model, WIDE), lambda s, w: (0, 0, 9)),
+                pl.BlockSpec((2, model, WIDE), lambda s, w: (0, 0, 6)),
                 pl.BlockSpec((1, 8, WIDE), lambda s, w: (s // 3, 0, s % 3)),
                 const((8, LANES)),
-                const((8, WIDE)),
+                const((CONV + 1, WIDE)),
             ],
             out_specs=[out[1] for out in outs],
             scratch_shapes=[
@@ -420,7 +421,7 @@
                 pl.BlockSpec((rows, WIDE), lambda s, w: (0, early(s))),
                 pl.BlockSpec((rows, WIDE), lambda s, w: (0, early(s))),
                 pl.BlockSpec((NSTATE, WIDE), lambda s, w: (0, early(s))),
-                pl.BlockSpec((1, model, WIDE), lambda s, w: (group(s) // 3, 0, 6 + group(s) % 3)),
+                pl.BlockSpec((1, model, WIDE), lambda s, w: (group(s) // 3, 0, group(s) % 3)),
                 pl.BlockSpec((1, 8, WIDE), lambda s, w: (group(s) // 3, 0, group(s) % 3)),
                 const((8, LANES)),
                 const((rows, WIDE)),
@@ -534,7 +535,7 @@
     sums, grad = conv_backward(pg, cin_ref[...].astype(F32), par[0], masks)
     tap_out[...] = jnp.concatenate(sums + [jnp.zeros((3, WIDE), F32)], axis=0)
     cg_out[...] = grad[HALO:]
-    edge_out[...] = grad[:HALO]
+    edge_out[...] = grad[HALO - EDGE : HALO]
 
     @pl.when(group == 5)
     def _():
@@ -574,7 +575,7 @@
         sums, grad = conv_backward(pg, cin_state[...].astype(F32), state_filter[...], masks)
         tap_state_out[...] = jnp.concatenate(sums + [jnp.zeros((3, WIDE), F32)], axis=0)
         cg_state_out[...] = grad[HALO:]
-        edge_state_out[...] = grad[:HALO]
+        edge_state_out[...] = grad[HALO - EDGE : HALO]
 
 
 def scan_back(
@@ -587,10 +588,10 @@
     column = lambda count: pl.BlockSpec((count, WIDE), lambda s: (0, s))
     outs = (
         (shape((rows, wide), F32), column(rows)),
-        (shape((HALO, wide), F32), column(HALO)),
+        (shape((EDGE, wide), F32), column(EDGE)),
         (shape((8, wide), F32), column(8)),
         (shape((rows, WIDE), F32), const((rows, WIDE))),
-        (shape((HALO, WIDE), F32), const((HALO, WIDE))),
+        (shape((EDGE, WIDE), F32), const((EDGE, WIDE))),
         (shape((8, WIDE), F32), const((8, WIDE))),
         (shape((rows, LANES), LOW), const((rows, LANES))),
         (shape((8, LANES), F32), const((8, LANES))),
@@ -608,7 +609,7 @@
             column(ext),
             pl.BlockSpec((1, 8, WIDE), lambda s: (s // 3, 0, s % 3)),
             const((8, LANES)),
-            const((8, WIDE)),
+            const((CONV + 1, WIDE)),
             const((ext, WIDE)),
             const((rows, WIDE)),
             const((rows, WIDE)),
@@ -646,7 +647,7 @@
 
     def joined(grad, arrived):
         return jnp.concatenate(
-            [grad[: rows - HALO], grad[rows - HALO :] + arrived[...]], axis=0
+            [grad[: rows - EDGE], grad[rows - EDGE :] + arrived[...]], axis=0
         ).astype(LOW)
 
     @pl.when(step == 0)
@@ -654,8 +655,11 @@
         state = joined(cg_state, edge_state)
         steps = srg[...]
         turned = hidden_t[...]
-        small_out[:, :WIDE] = mm(turned, state).astype(LOW)
-        small_out[:, WIDE:] = mm(turned, steps).astype(LOW)
+        state_part = mm(turned, state).astype(LOW)
+        step_part = mm(turned, steps).astype(LOW)
+        for part in range(2):
+            small_out[part, :, :LANES] = state_part[:, part * LANES : (part + 1) * LANES]
+            small_out[part, :, LANES:] = step_part
         acc = mm_nt(state[:, :LANES], w_small[0, :, :LANES])
         acc += mm_nt(state[:, LANES:], w_small[1, :, :LANES])
         acc += mm_nt(steps, w_small[0, :, LANES:])
@@ -681,7 +685,7 @@
         pull = jnp.sum(normed * value, axis=1, keepdims=True) / value.shape[1]
         token_out[...] = (
             cot[0].astype(F32) + scale * normed - (scale * scale * scale) * value * pull
-        )
+        ).astype(LOW)
 
 
 def tail(which, tokens, cot, hidden_t, gpg, cg, edge, cg_state, edge_state, srg, weights):
@@ -692,8 +696,8 @@
     outs = (
         (shape((2, model, 3 * WIDE), LOW), parts),
         (shape((2, model, 3 * WIDE), LOW), parts),
-        (shape((model, WIDE + LANES), LOW), const((model, WIDE + LANES))),
-        (shape((rows, model), F32), const((rows, model))),
+        (shape((2, model, WIDE), LOW), const((2, model, WIDE))),
+        (shape((rows, model), LOW), const((rows, model))),
         (shape((8, model), F32), const((8, model))),
     )
     return pl.pallas_call(
@@ -708,13 +712,13 @@
                 const((model, rows)),
                 column(rows),
                 column(rows),
-                column(HALO),
+                column(EDGE),
                 const((rows, WIDE)),
-                const((HALO, WIDE)),
+                const((EDGE, WIDE)),
                 const((rows, LANES)),
                 pl.BlockSpec((1, model, WIDE), lambda s, w: (s // 3, 0, s % 3)),
                 pl.BlockSpec((1, model, WIDE), lambda s, w: (s // 3, 0, 3 + s % 3)),
-                pl.BlockSpec((2, model, WIDE), lambda s, w: (0, 0, 9)),
+                pl.BlockSpec((2, model, WIDE), lambda s, w: (0, 0, 6)),
             ],
             out_specs=[out[1] for out in outs],
             scratch_shapes=[pltpu.VMEM((rows, model), F32)],
@@ -727,121 +731,998 @@
     )
 
 
-def chained(fold, gain, hops, backward):
+def remote(src, dst, send_sem, recv_sem, target):
+    return pltpu.make_async_remote_copy(
+        src_ref=src,
+        dst_ref=dst,
+        send_sem=send_sem,
+        recv_sem=recv_sem,
+        device_id=target,
+        device_id_type=pl.DeviceIdType.MESH,
+    )
+
+
+def each(count, run, first=0):
+    def one(step, carry):
+        run(step)
+        return carry
+
+    lax.fori_loop(first, count, one, 0)
+
+
+class Place:
+    def __init__(self, depth):
+        position = lax.axis_index("context")
+        self.depth = depth
+        self.position = position
+        self.x, self.y = lax.axis_index("dp"), lax.axis_index("tensor")
+        self.z, self.c = position // 2, position % 2
+        self.mate = self.at(self.x, self.y, self.z, 1 - self.c)
+        self.x_peer = self.at(1 - self.x, self.y, self.z, self.c)
+        self.y_peer = self.at(self.x, 1 - self.y, self.z, self.c)
+
+    def at(self, x, y, z, c):
+        return {"dp": x, "context": z * 2 + c, "tensor": y}
+
+    def up(self):
+        return self.at(self.x, self.y, self.z + 1, self.c)
+
+    def down(self):
+        return self.at(self.x, self.y, self.z - 1, self.c)
+
+    def away(self, z):
+        return self.at(self.x, self.y, z, self.c)
+
+    def axes(self, turned):
+        x, y, z, c = self.x, self.y, self.z, self.c
+        x1, y1 = x + (1 - turned) * (1 - 2 * x), y + turned * (1 - 2 * y)
+        x2, y2 = x + turned * (1 - 2 * x), y + (1 - turned) * (1 - 2 * y)
+        return (x1, y1), (x2, y2)
+
+    def around(self, run, first=0):
+        z, depth = self.z, self.depth
+        if first == 0:
+            run(z)
+
+        def step(away):
+            @pl.when(z - away >= 0)
+            def _():
+                run(z - away)
+
+            @pl.when(z + away < depth)
+            def _():
+                run(z + away)
+
+        each(depth, step, 1)
+
+    def greet(self, always, sometimes=(), column=False):
+        barrier = pltpu.get_barrier_semaphore()
+        kind = pl.DeviceIdType.MESH
+        total = len(always)
+        for target in always:
+            pl.semaphore_signal(barrier, inc=1, device_id=target, device_id_type=kind)
+        for holds, target in sometimes:
+
+            @pl.when(holds)
+            def _():
+                pl.semaphore_signal(barrier, inc=1, device_id=target, device_id_type=kind)
+
+            total = total + holds.astype(jnp.int32)
+        if column:
+            for_all = lambda step: pl.semaphore_signal(
+                barrier,
+                inc=1,
+                device_id=self.away(lax.rem(self.z + step, self.depth)),
+                device_id_type=kind,
+            )
+            each(self.depth, for_all, 1)
+            total = total + (self.depth - 1)
+        pl.semaphore_wait(barrier, total)
+
+
+class Gathering:
+    def __init__(self, place, own, full, sends, lands, local):
+        self.place, self.own_ref, self.full = place, own, full
+        self.sends, self.lands, self.local = sends, lands, local
+        (self.x1, self.y1), (self.x2, self.y2) = place.axes(place.c)
+        self.first = place.at(self.x1, self.y1, place.z, place.c)
+        self.second = place.at(self.x2, self.y2, place.z, place.c)
+
+    @staticmethod
+    def scratch(depth):
+        sem = pltpu.SemaphoreType.DMA
+        return [sem((5, 4 * depth)), sem((8 * depth,)), sem((1,))]
+
+    def copy(self, kind, index, x, y, z, c, target, own=False):
+        chunk = self.full.at[y, x, z * 2 + c]
+        mark = ((y * 2 + x) * self.place.depth + z) * 2 + c
+        return remote(
+            self.own_ref if own else chunk, chunk, self.sends.at[kind, index], self.lands.at[mark],
+            target,
+        )
+
+    def arrive(self, x, y, z, c):
+        self.copy(0, 0, x, y, z, c, self.place.mate).wait_recv()
+
+    def kept(self):
+        p = self.place
+        return pltpu.make_async_copy(
+            self.own_ref, self.full.at[p.y, p.x, p.z * 2 + p.c], self.local.at[0]
+        )
+
+    def own(self):
+        p = self.place
+        mine = (p.x, p.y, p.z, p.c)
+
+        @pl.when(p.z + 1 < p.depth)
+        def _():
+            self.copy(3, p.z, *mine, p.up(), True).start()
+
+        @pl.when(p.z > 0)
+        def _():
+            self.copy(4, p.z, *mine, p.down(), True).start()
+
+        self.copy(1, p.z, *mine, self.first, True).start()
+        self.copy(2, p.z, *mine, self.second, True).start()
+        self.copy(0, p.z, *mine, p.mate, True).start()
+        self.kept().start()
+
+    def near(self):
+        p = self.place
+
+        def run(z):
+            chunk = (p.x, p.y, z, p.c)
+            self.arrive(*chunk)
+
+            @pl.when((z < p.z) & (p.z + 1 < p.depth))
+            def _():
+                self.copy(3, z, *chunk, p.up()).start()
+
+            @pl.when((z > p.z) & (p.z > 0))
+            def _():
+                self.copy(4, z, *chunk, p.down()).start()
+
+            self.copy(1, z, *chunk, self.first).start()
+            self.copy(2, z, *chunk, self.second).start()
+            self.copy(0, z, *chunk, p.mate).start()
+
+        p.around(run, 1)
+
+    def across(self):
+        p = self.place
+
+        def run(z):
+            chunk = (self.x1, self.y1, z, p.c)
+            self.arrive(*chunk)
+            self.copy(2, p.depth + z, *chunk, self.second).start()
+            self.copy(0, p.depth + z, *chunk, p.mate).start()
+
+        p.around(run)
+
+    def far(self):
+        p = self.place
+
+        def near_row(z):
+            self.arrive(self.x2, self.y2, z, p.c)
+            self.copy(0, 2 * p.depth + z, self.x2, self.y2, z, p.c, p.mate).start()
+
+        def far_row(z):
+            self.arrive(1 - p.x, 1 - p.y, z, p.c)
+            self.copy(0, 3 * p.depth + z, 1 - p.x, 1 - p.y, z, p.c, p.mate).start()
+
+        p.around(near_row)
+        p.around(far_row)
+
+    def finish(self):
+        p = self.place
+
+        def from_mate(z):
+            for y in range(2):
+                for x in range(2):
+                    self.arrive(x, y, z, 1 - p.c)
+
+        each(p.depth, from_mate)
+
+        def sent(kind, index, target):
+            self.copy(kind, index, p.x, p.y, p.z, p.c, target).wait_send()
+
+        each(4 * p.depth, lambda step: sent(0, step, p.mate))
+        each(p.depth, lambda step: sent(1, step, p.mate))
+        each(2 * p.depth, lambda step: sent(2, step, p.mate))
+
+        def chained(z):
+            @pl.when((z <= p.z) & (p.z + 1 < p.depth))
+            def _():
+                sent(3, z, p.mate)
+
+            @pl.when((z >= p.z) & (p.z > 0))
+            def _():
+                sent(4, z, p.mate)
+
+        each(p.depth, chained)
+        self.kept().wait()
+
+
+class Reducing:
+    def __init__(self, place, turned, parts, total, bufs, sems):
+        self.place, self.parts, self.total = place, parts, total
+        self.own, self.core, self.send1, self.land1 = bufs[:4]
+        self.send2, self.land2, self.send3, self.land3 = bufs[4:]
+        self.own_sem, self.core_send, self.core_land = sems[:3]
+        self.s1, self.l1, self.s2, self.l2, self.s3, self.l3 = sems[3:]
+        self.turned = turned
+        (x1, y1), (x2, y2) = place.axes(turned)
+        self.first = place.at(x1, y1, place.z, place.c)
+        self.second = place.at(x2, y2, place.z, place.c)
+        self.mine = place.y + turned * (place.x - place.y)
+
+    @staticmethod
+    def scratch(depth, rows, tall):
+        buffer = lambda *lead: pltpu.VMEM(lead + (rows, tall), LOW)
+        sem = lambda *lead: pltpu.SemaphoreType.DMA(lead)
+        bufs = [
+            buffer(2, 2, depth), buffer(2, 2, depth), buffer(depth, 2), buffer(depth, 2),
+            buffer(depth), buffer(depth), buffer(depth), buffer(depth),
+        ]
+        return bufs + [sem(2, 2, depth)] * 3 + [sem(depth)] * 6
+
+    def spot(self, step):
+        return lax.rem(self.place.z + 1 + step, self.place.depth)
+
+    def whole(self, y, x, z):
+        return remote(
+            self.core.at[y, x, z], self.core.at[y, x, z], self.core_send.at[y, x, z],
+            self.core_land.at[y, x, z], self.place.mate,
+        )
+
+    def own_whole(self, y, x, z):
+        return pltpu.make_async_copy(
+            self.own.at[y, x, z], self.own.at[y, x, z], self.own_sem.at[y, x, z]
+        )
+
+    def start(self, step):
+        p = self.place
+        z = self.spot(step)
+        for y in range(2):
+            for x in range(2):
+                for ref, cols in self.parts:
+                    remote(
+                        ref.at[y, x, z * 2 + 1 - p.c], self.core.at[y, x, z, :, cols],
+                        self.core_send.at[y, x, z], self.core_land.at[y, x, z], p.mate,
+                    ).start()
+                    pltpu.make_async_copy(
+                        ref.at[y, x, z * 2 + p.c], self.own.at[y, x, z, :, cols],
+                        self.own_sem.at[y, x, z],
+                    ).start()
+
+    def base(self, y, x, z):
+        return self.own[y, x, z].astype(F32) + self.core[y, x, z].astype(F32)
+
+    def copy1(self, z):
+        return remote(
+            self.send1.at[z], self.land1.at[z], self.s1.at[z], self.l1.at[z], self.first
+        )
+
+    def copy2(self, z):
+        return remote(
+            self.send2.at[z], self.land2.at[z], self.s2.at[z], self.l2.at[z], self.second
+        )
+
+    def copy3(self, z, lands_at):
+        return remote(
+            self.send3.at[z], self.land3.at[lands_at], self.s3.at[z], self.l3.at[lands_at],
+            self.place.away(z),
+        )
+
+    def stage1(self, step):
+        p, turned = self.place, self.turned
+        z = self.spot(step)
+        for y in range(2):
+            for x in range(2):
+                self.whole(y, x, z).wait_recv()
+                self.own_whole(y, x, z).wait()
+        for index in range(2):
+            x = (1 - turned) * (1 - p.x) + turned * index
+            y = turned * (1 - p.y) + (1 - turned) * index
+            self.send1[z, index] = self.base(y, x, z).astype(LOW)
+        self.copy1(z).start()
+
+    def stage2(self, step):
+        p, turned = self.place, self.turned
+        z = self.spot(step)
+        self.copy1(z).wait_recv()
+        other = 1 - self.mine
+        x = (1 - turned) * p.x + turned * other
+        y = turned * p.y + (1 - turned) * other
+        self.send2[z] = (self.base(y, x, z) + self.land1[z, other].astype(F32)).astype(LOW)
+        self.copy2(z).start()
+
+    def final(self, z):
+        p = self.place
+        self.copy2(z).wait_recv()
+        return (
+            self.base(p.y, p.x, z)
+            + self.land1[z, self.mine].astype(F32)
+            + self.land2[z].astype(F32)
+        )
+
+    def stage3(self, step):
+        z = self.spot(step)
+        self.send3[z] = self.final(z).astype(LOW)
+        self.copy3(z, self.place.z).start()
+
+    def turn(self, step):
+        depth = self.place.depth
+
+        @pl.when(step < depth)
+        def _():
+            self.stage1(step)
+
+        @pl.when((step >= 1) & (step <= depth))
+        def _():
+            self.stage2(step - 1)
+
+        @pl.when((step >= 2) & (step <= depth))
+        def _():
+            self.stage3(step - 2)
+
+    def close(self):
+        p = self.place
+        self.total[...] = self.final(p.z)
+
+        def add(step):
+            z = lax.rem(p.z + step, p.depth)
+            self.copy3(z, z).wait_recv()
+            self.total[...] += self.land3[z].astype(F32)
+
+        each(p.depth, add, 1)
+
+    def finish(self):
+        p = self.place
+
+        def sent(z):
+            for y in range(2):
+                for x in range(2):
+                    self.whole(y, x, z).wait_send()
+            self.copy1(z).wait_send()
+            self.copy2(z).wait_send()
+
+        each(p.depth, sent)
+        each(p.depth, lambda step: self.copy3(lax.rem(p.z + step, p.depth), p.z).wait_send(), 1)
+
+
+CUTS = 4
+
+
+class Chaining:
+    def __init__(self, place, rounds, backward, fold, gain, out, bufs, sems):
+        self.place, self.rounds = place, rounds
+        self.fold, self.gain, self.out = fold, gain, out
+        self.from_mate, self.from_chip, self.to_mate, self.to_chip = bufs
+        self.mate_send, self.mate_land, self.chip_send, self.chip_land = sems
+        first = 1 if backward else 0
+        by = -1 if backward else 1
+        self.order = place.depth - 1 - place.z if backward else place.z
+        self.leads = place.c == first
+        self.after = place.at(place.x, place.y, place.z + by, first)
+        self.before = place.at(place.x, place.y, place.z - by, 1 - first)
+        self.linked_before = self.leads & (self.order > 0)
+        self.linked_after = jnp.logical_not(self.leads) & (self.order < place.depth - 1)
+        self.width = fold.shape[1] // CUTS
+
+    @staticmethod
+    def scratch(rounds, states, wide):
+        slots = lambda turns: pltpu.VMEM((turns, CUTS, states, wide // CUTS), LOW)
+        marks = lambda turns: pltpu.SemaphoreType.DMA((turns, CUTS))
+        return [
+            slots(rounds + 1), slots(rounds), slots(rounds + 1), slots(rounds),
+            marks(rounds + 1), marks(rounds + 1), marks(rounds), marks(rounds),
+        ]
+
+    def sometimes(self):
+        return [(self.linked_before, self.before), (self.linked_after, self.after)]
+
+    def mate_copy(self, turn, cut):
+        return remote(
+            self.to_mate.at[turn, cut], self.from_mate.at[turn, cut], self.mate_send.at[turn, cut],
+            self.mate_land.at[turn, cut], self.place.mate,
+        )
+
+    def chip_copy(self, turn, cut):
+        return remote(
+            self.to_chip.at[turn, cut], self.from_chip.at[turn, cut], self.chip_send.at[turn, cut],
+            self.chip_land.at[turn, cut], self.after,
+        )
+
+    def lanes(self, cut):
+        return slice(cut * self.width, (cut + 1) * self.width)
+
+    def joined(self, cut, arrived):
+        at = self.lanes(cut)
+        return (self.fold[:, at] + self.gain[0:1, at] * arrived.astype(F32)).astype(LOW)
+
+    def open(self):
+        @pl.when(self.leads)
+        def _():
+            for cut in range(CUTS):
+                self.to_mate[0, cut] = self.fold[:, self.lanes(cut)].astype(LOW)
+                self.mate_copy(0, cut).start()
+
+        @pl.when(jnp.logical_not(self.leads))
+        def _():
+            self.pass_on(0)
+
+    def pass_on(self, turn):
+        for cut in range(CUTS):
+            self.mate_copy(turn, cut).wait_recv()
+
+            @pl.when(self.linked_after)
+            def _():
+                self.to_chip[turn, cut] = self.joined(cut, self.from_mate[turn, cut])
+                self.chip_copy(turn, cut).start()
+
+    def relay(self):
+        @pl.when(self.linked_before)
+        def _():
+            for turn in range(self.rounds):
+                for cut in range(CUTS):
+                    self.chip_copy(turn, cut).wait_recv()
+                    self.to_mate[turn + 1, cut] = self.joined(cut, self.from_chip[turn, cut])
+                    self.mate_copy(turn + 1, cut).start()
+            for cut in range(CUTS):
+                self.out[:, self.lanes(cut)] = self.from_chip[self.rounds - 1, cut]
+
+        @pl.when(self.leads & (self.order == 0))
+        def _():
+            for turn in range(self.rounds):
+                for cut in range(CUTS):
+                    self.to_mate[turn + 1, cut] = self.fold[:, self.lanes(cut)].astype(LOW)
+                    self.mate_copy(turn + 1, cut).start()
+            self.out[...] = jnp.zeros_like(self.out)
+
+    def close(self):
+        @pl.when(self.leads)
+        def _():
+            for turn in range(self.rounds + 1):
+                for cut in range(CUTS):
+                    self.mate_copy(turn, cut).wait_send()
+
+        @pl.when(jnp.logical_not(self.leads))
+        def _():
+            for turn in range(1, self.rounds):
+                self.pass_on(turn)
+            for cut in range(CUTS):
+                self.mate_copy(self.rounds, cut).wait_recv()
+                self.out[:, self.lanes(cut)] = self.from_mate[self.rounds, cut]
+
+        @pl.when(self.linked_after)
+        def _():
+            for turn in range(self.rounds):
+                for cut in range(CUTS):
+                    self.chip_copy(turn, cut).wait_send()
+
+
+VMEM_SPEC = pl.BlockSpec(memory_space=pltpu.VMEM)
+ANY_SPEC = pl.BlockSpec(memory_space=pl.ANY)
+
+
+def pack_body(
+    side_ref, entry, exits, state, steps, gain, inner_kernel, gate_gain, bias, decay, skip, docs,
+    tail_tokens, packed, packed_exit, par, doc_col, doc_row, edge
+):
+    side = side_ref[0]
+    rows = entry.shape[0]
+    wide = entry.shape[2]
+
+    def placed(value):
+        filled = jnp.concatenate(
+            [value, jnp.zeros((value.shape[0], LANES - value.shape[1]), F32)], axis=1
+        )
+        return jnp.where(side == 0, filled, pltpu.roll(filled, value.shape[1], 1))
+
+    packed[:, :wide] = entry[:, 0].astype(LOW)
+    packed[:, wide : 2 * wide] = entry[:, 1].astype(LOW)
+    half = jnp.where(side == 0, state[:, :NSTATE], state[:, NSTATE:])
+    packed[:, 2 * wide : 2 * wide + NSTATE] = half.astype(LOW)
+    gain_row = jnp.concatenate([gain[...], jnp.zeros((1, LANES - rows), F32)], axis=1)
+    gain_col = jnp.transpose(jnp.broadcast_to(gain_row, (LANES, LANES)))[:rows]
+    lane = iota((rows, LANES), 1)
+    small = jnp.where(lane == 24, gain_col, placed(steps[...]))
+    packed[:, 2 * wide + NSTATE :] = small.astype(LOW)
+    packed_exit[...] = exits[...].astype(LOW)
+    par[0 : CONV + 1] = inner_kernel[...]
+    par[CONV + 1 : CONV + 2] = gate_gain[...]
+    par[CONV + 2 : CONV + 4] = jnp.zeros((2, wide), F32)
+    for index, ref in enumerate((bias, decay, skip)):
+        par[CONV + 2 : CONV + 3, index * LANES : (index + 1) * LANES] = placed(ref[...])
+    own = jnp.where(side == 0, docs[0:1], docs[1:2]).astype(F32)
+    doc_row[...] = jnp.broadcast_to(own, doc_row.shape)
+    doc_col[...] = jnp.transpose(jnp.broadcast_to(own, (LANES, own.shape[1])))
+    edge[...] = tail_tokens[0]
+
+
+def pack(
+    which, entry, exits, state, steps, gain, inner_kernel, gate_gain, bias, decay, skip, docs, tokens
+):
+    own_rows, _, wide = entry.shape
+    rows, model = tokens.shape[1:]
+    shape = jax.ShapeDtypeStruct
+    arrays = (
+        entry, exits, state, steps, gain[None], inner_kernel, gate_gain[None], bias[None],
+        decay[None], skip[None], docs,
+    )
+    outs = (
+        shape((own_rows, 2 * wide + WIDE), LOW),
+        shape((own_rows, wide), LOW),
+        shape((8, wide), F32),
+        shape((rows, LANES), F32),
+        shape((8, rows), F32),
+        shape((HALO, model), LOW),
+    )
+    return pl.pallas_call(
+        pack_body,
+        out_shape=outs,
+        grid_spec=pltpu.PrefetchScalarGridSpec(
+            num_scalar_prefetch=1,
+            grid=(1,),
+            in_specs=[const(array.shape) for array in arrays]
+            + [pl.BlockSpec((1, HALO, model), lambda s, w: (w[0], rows // HALO - 1, 0))],
+            out_specs=[const(out.shape) for out in outs],
+        ),
+        compiler_params=params(),
+        name="pack",
+    )(which, *arrays, tokens)
+
+
+def gather_body(
+    depth, packed, par_own, edge_own, docs_own, cot, weights, par, heads, edge, docs, cot_t, docs_in,
+    cot_in, side_send, side_land, local, *scratch
+):
+    place = Place(depth)
+    count = 2 * depth
+    onward = {"context": lax.rem(place.position + 1, count)}
+    behind = {"context": lax.rem(place.position + count - 1, count)}
+    x, y, z, c = place.x, place.y, place.z, place.c
+    place.greet(
+        [place.mate, place.x_peer, place.y_peer, onward, behind],
+        [(z + 1 < depth, place.up()), (z > 0, place.down())],
+    )
+    gathering = Gathering(place, packed, weights, *scratch)
+    sides = [
+        remote(edge_own, edge, side_send.at[0], side_land.at[0], onward),
+        remote(docs_own, docs_in, side_send.at[1], side_land.at[1], onward),
+        remote(par_own, par.at[y], side_send.at[2], side_land.at[2], place.y_peer),
+    ]
+    for copy in sides:
+        copy.start()
+    gathering.own()
+    cot_copy = pltpu.make_async_copy(cot.at[y], cot_in, local.at[1])
+    cot_copy.start()
+    par_keep = pltpu.make_async_copy(par_own, par.at[y], local.at[0])
+    par_keep.start()
+    cot_copy.wait()
+    cot_t[...] = jnp.transpose(cot_in[...])
+    gathering.near()
+    gathering.across()
+    for copy in sides:
+        copy.wait()
+    docs[...] = jnp.where(place.position == 0, -1.0, docs_in[...])
+    par_keep.wait()
+    both = par[0, CONV + 2 : CONV + 3] + par[1, CONV + 2 : CONV + 3]
+    heads[...] = jnp.zeros_like(heads)
+    for index in range(3):
+        heads[index : index + 1] = both[:, index * LANES : (index + 1) * LANES]
+    gathering.far()
+    gathering.finish()
+
+
+def gather(packed, par_own, edge_own, docs_own, cot):
     count = lax.axis_size("context")
-    by = -1 if backward else 1
-    pairs = [(i, i + by) for i in range(count) if 0 <= i + by < count]
-    carry = jnp.zeros_like(fold)
-    for _ in range(hops):
-        carry = lax.ppermute(fold + gain[0:1] * carry, "context", pairs)
-    return carry
+    depth = count // 2
+    rows, model = cot.shape[1:]
+    shape = jax.ShapeDtypeStruct
+    return pl.pallas_call(
+        functools.partial(gather_body, depth),
+        out_shape=(
+            shape((2, 2, count) + packed.shape, LOW),
+            shape((2,) + par_own.shape, F32),
+            shape((8, LANES), F32),
+            shape(edge_own.shape, LOW),
+            shape(docs_own.shape, F32),
+            shape((model, rows), LOW),
+        ),
+        in_specs=[VMEM_SPEC] * 4 + [ANY_SPEC],
+        out_specs=[ANY_SPEC] + [VMEM_SPEC] * 5,
+        scratch_shapes=[
+            pltpu.VMEM(docs_own.shape, F32),
+            pltpu.VMEM((rows, model), LOW),
+            pltpu.SemaphoreType.DMA((3,)),
+            pltpu.SemaphoreType.DMA((3,)),
+            pltpu.SemaphoreType.DMA((2,)),
+        ]
+        + Gathering.scratch(depth),
+        compiler_params=params(collective_id=0, has_side_effects=True),
+        name="gather",
+    )(packed, par_own, edge_own, docs_own, cot)
+
+
+def chain_body(depth, rounds, fold, gain, packed, carry, weights, *scratch):
+    place = Place(depth)
+    chaining = Chaining(place, rounds, False, fold, gain, carry, scratch[:4], scratch[4:8])
+    gathering = Gathering(place, packed, weights, *scratch[8:])
+    place.greet(
+        [place.mate, place.x_peer, place.y_peer],
+        [(place.z + 1 < depth, place.up()), (place.z > 0, place.down())] + chaining.sometimes(),
+    )
+    chaining.open()
+    gathering.own()
+    gathering.near()
+    chaining.relay()
+    gathering.across()
+    gathering.far()
+    chaining.close()
+    gathering.finish()
+
+
+def chain(fold, gain, packed, rounds):
+    count = lax.axis_size("context")
+    depth = count // 2
+    states, wide = fold.shape
+    shape = jax.ShapeDtypeStruct
+    return pl.pallas_call(
+        functools.partial(chain_body, depth, rounds),
+        out_shape=(shape(fold.shape, LOW), shape((2, 2, count) + packed.shape, LOW)),
+        in_specs=[VMEM_SPEC] * 3,
+        out_specs=[VMEM_SPEC, ANY_SPEC],
+        scratch_shapes=Chaining.scratch(rounds, states, wide) + Gathering.scratch(depth),
+        compiler_params=params(collective_id=1, has_side_effects=True),
+        name="chain",
+    )(fold, gain, packed)
+
+
+def chain_back_body(depth, rounds, fold, gain, exits, carry, total, *scratch):
+    place = Place(depth)
+    chaining = Chaining(place, rounds, True, fold, gain, carry, scratch[:4], scratch[4:8])
+    reducing = Reducing(
+        place, place.c, [(exits, slice(0, exits.shape[-1]))], total, scratch[8:16], scratch[16:]
+    )
+    place.greet([place.mate, place.x_peer, place.y_peer], chaining.sometimes(), True)
+    chaining.open()
+    each(depth, reducing.start)
+    for step in range(2):
+        reducing.turn(step)
+    chaining.relay()
+    each(depth + 1, reducing.turn, 2)
+    reducing.close()
+    chaining.close()
+    reducing.finish()
+
+
+def chain_back(fold, gain, exits, rounds):
+    count = lax.axis_size("context")
+    depth = count // 2
+    states, wide = fold.shape
+    own_rows, tall = exits.shape[3:]
+    shape = jax.ShapeDtypeStruct
+    return pl.pallas_call(
+        functools.partial(chain_back_body, depth, rounds),
+        out_shape=(shape(fold.shape, LOW), shape((own_rows, tall), F32)),
+        in_specs=[VMEM_SPEC] * 2 + [ANY_SPEC],
+        out_specs=[VMEM_SPEC] * 2,
+        scratch_shapes=Chaining.scratch(rounds, states, wide)
+        + Reducing.scratch(depth, own_rows, tall),
+        compiler_params=params(collective_id=2, has_side_effects=True),
+        name="chain_back",
+    )(fold, gain, exits)
+
+
+def edges_body(depth, own, own_state, out, out_state, send, land):
+    place = Place(depth)
+    position, count = place.position, 2 * depth
+    before, after = {"context": position - 1}, {"context": position + 1}
+    place.greet([], [(position > 0, before), (position < count - 1, after)])
+    copies = [
+        remote(own, out, send.at[0], land.at[0], before),
+        remote(own_state, out_state, send.at[1], land.at[1], before),
+    ]
+
+    @pl.when(position > 0)
+    def _():
+        for copy in copies:
+            copy.start()
+
+    @pl.when(position == count - 1)
+    def _():
+        out[...] = jnp.zeros_like(out)
+        out_state[...] = jnp.zeros_like(out_state)
+
+    @pl.when(position < count - 1)
+    def _():
+        for copy in copies:
+            copy.wait_recv()
+
+    @pl.when(position > 0)
+    def _():
+        for copy in copies:
+            copy.wait_send()
+
+
+def edges(own, own_state):
+    return pl.pallas_call(
+        functools.partial(edges_body, lax.axis_size("context") // 2),
+        out_shape=(
+            jax.ShapeDtypeStruct(own.shape, F32),
+            jax.ShapeDtypeStruct(own_state.shape, F32),
+        ),
+        in_specs=[VMEM_SPEC] * 2,
+        out_specs=[VMEM_SPEC] * 2,
+        scratch_shapes=[pltpu.SemaphoreType.DMA((2,)), pltpu.SemaphoreType.DMA((2,))],
+        compiler_params=params(collective_id=3, has_side_effects=True),
+        name="edges",
+    )(own, own_state)
+
+
+def reduce_body(
+    depth, gate, inner, small, token, taps, taps_state, gate_row, head_rows, skip_row, norm_row,
+    total, state_out, vector_out, token_out, state_own, vec_send, vec_land, vs, vl, ts, tl, ss, sl,
+    keep_sem, *scratch
+):
+    place = Place(depth)
+    x, y, z, c = place.x, place.y, place.z, place.c
+    wide = gate.shape[-1]
+    parts = [
+        (gate, slice(0, wide)),
+        (inner, slice(wide, 2 * wide)),
+        (small, slice(2 * wide, 2 * wide + WIDE)),
+    ]
+    reducing = Reducing(place, 0, parts, total, scratch[:8], scratch[8:])
+
+    vec_send[0] = jnp.zeros(vec_send.shape[1:], F32)
+    vec_send[0, : CONV + 1, : 2 * wide] = taps[: CONV + 1]
+    vec_send[0, : CONV + 1, 2 * wide :] = taps_state[: CONV + 1]
+    vec_send[0, 5:6, : 2 * wide] = gate_row[0:1]
+    vec_send[0, 5:6, 2 * wide : 2 * wide + LANES] = head_rows[0:1]
+    vec_send[0, 5:6, 2 * wide + LANES :] = skip_row[0:1]
+    model = norm_row.shape[1]
+    vec_send[0, 6:7, :model] = norm_row[0:1]
+    vec_send[0, 6:7, model : model + LANES] = head_rows[1:2]
+
+    place.greet([place.mate, place.x_peer, place.y_peer], (), True)
+    vec_targets = [place.mate, place.x_peer, place.y_peer]
+
+    def vec_copy(turn):
+        return remote(
+            vec_send.at[turn], vec_land.at[turn], vs.at[turn], vl.at[turn], vec_targets[turn]
+        )
+
+    def vec_far(away, lands_at):
+        return remote(
+            vec_send.at[3], vec_land.at[3 + lands_at], vs.at[3 + away], vl.at[3 + lands_at],
+            place.away(away),
+        )
+
+    share = token.shape[0] // depth
+
+    def token_copy(step):
+        at = pl.ds(pl.multiple_of(step * share, share), share)
+        return remote(token.at[at], token_out.at[y, at], ts.at[step], tl.at[step], place.y_peer)
+
+    token_keep = pltpu.make_async_copy(token, token_out.at[y], keep_sem.at[0])
+
+    vec_copy(0).start()
+    each(depth, reducing.start)
+    token_keep.start()
+
+    def step_all(step):
+        reducing.turn(step)
+
+        @pl.when(step >= 1)
+        def _():
+            token_copy(step - 1).start()
+
+        for turn in range(3):
+
+            @pl.when(step == turn)
+            def _():
+                vec_copy(turn).wait_recv()
+                vec_send[turn + 1] = vec_send[turn] + vec_land[turn]
+                if turn < 2:
+                    vec_copy(turn + 1).start()
+                else:
+                    each(depth, lambda s: vec_far(lax.rem(z + s, depth), z).start(), 1)
+                    vec_land[3 + z] = vec_send[3]
+
+    each(depth + 1, step_all)
+    reducing.close()
+    state_own[...] = total[:, 2 * wide : 2 * wide + NSTATE]
+    state_copy = remote(state_own, state_out.at[y], ss.at[0], sl.at[0], place.y_peer)
+    state_copy.start()
+    state_out[y] = state_own[...]
+
+    def vec_arrive(step):
+        away = lax.rem(z + step, depth)
+        vec_far(away, away).wait_recv()
+
+    each(depth, vec_arrive, 1)
+    vector_out[...] = vec_land[3]
+
+    def vec_add(step):
+        vector_out[...] += vec_land[3 + step]
+
+    each(depth, vec_add, 1)
+    for turn in range(3):
+        vec_copy(turn).wait_send()
+    each(depth, lambda s: vec_far(lax.rem(z + s, depth), z).wait_send(), 1)
+    reducing.finish()
+    each(depth, lambda step: token_copy(step).wait())
+    state_copy.wait()
+    token_keep.wait()
+
+
+def reduce_all(gate, inner, small, token, taps, taps_state, gate_row, head_rows, skip_row, norm_row):
+    count = lax.axis_size("context")
+    depth = count // 2
+    own_rows, wide = gate.shape[3:]
+    tall = 2 * wide + WIDE
+    shape = jax.ShapeDtypeStruct
+    sem = lambda *lead: pltpu.SemaphoreType.DMA(lead)
+    vector = (8, tall)
+    return pl.pallas_call(
+        functools.partial(reduce_body, depth),
+        out_shape=(
+            shape((own_rows, tall), F32),
+            shape((2, own_rows, NSTATE), F32),
+            shape(vector, F32),
+            shape((2,) + token.shape, LOW),
+        ),
+        in_specs=[ANY_SPEC] * 3 + [VMEM_SPEC] * 7,
+        out_specs=[VMEM_SPEC] * 3 + [ANY_SPEC],
+        scratch_shapes=[
+            pltpu.VMEM((own_rows, NSTATE), F32),
+            pltpu.VMEM((4,) + vector, F32),
+            pltpu.VMEM((3 + depth,) + vector, F32),
+            sem(3 + depth),
+            sem(3 + depth),
+            sem(depth),
+            sem(depth),
+            sem(1),
+            sem(1),
+            sem(1),
+        ]
+        + Reducing.scratch(depth, own_rows, tall),
+        compiler_params=params(collective_id=4, has_side_effects=True),
+        name="reduce_all",
+    )(gate, inner, small, token, taps, taps_state, gate_row, head_rows, skip_row, norm_row)
+
+
+def finish_body(
+    side_ref, mine, exits, state, vector, token, block_own, block_other, block_out, token_out,
+    norm_out, entry_out, state_out, step_out, kernel_out, filter_out, bias_out, decay_out, skip_out,
+    gate_out, exit_out
+):
+    side, spot = side_ref[0], side_ref[1]
+    token_out[...] = token[...].astype(F32)
+    first = side == 0
+    block_out[0] = jnp.where(first, block_own[...], block_other[...])
+    block_out[1] = jnp.where(first, block_other[...], block_own[...])
+
+    @pl.when(pl.program_id(0) == 0)
+    def _():
+        own_rows, _, wide = entry_out.shape
+        model = token.shape[2]
+        entry_out[:, 0] = mine[:, :wide]
+        entry_out[:, 1] = mine[:, wide : 2 * wide]
+        exit_out[...] = exits[...]
+        state_out[:, :NSTATE] = state[0]
+        state_out[:, NSTATE:] = state[1]
+
+        def twelve(value):
+            return jnp.where(first, value, pltpu.roll(value, LANES - 12, 1))[:, :12]
+
+        step_out[...] = twelve(mine[:, 2 * wide + NSTATE :])
+        left, right = vector[:, :wide], vector[:, wide : 2 * wide]
+        halves = jnp.where(first, left, right)
+        kernel_out[...] = halves[: CONV + 1]
+        gate_out[...] = halves[5:6]
+        filter_out[...] = vector[: CONV + 1, 2 * wide :]
+        bias_out[...] = twelve(vector[5:6, 2 * wide : 2 * wide + LANES])
+        skip_out[...] = twelve(vector[5:6, 2 * wide + LANES :])
+        decay_out[...] = twelve(vector[6:7, model : model + LANES])
+        turned = pltpu.roll(vector[:, :model], lax.rem(model - spot * own_rows, model), 1)
+        norm_out[...] = turned[6:7, :own_rows]
+
+
+def finish(side, mine, exits, state, vector, token, block_own, block_other):
+    own_rows, wide = exits.shape
+    _, rows, model = token.shape
+    share = rows // 4
+    shape = jax.ShapeDtypeStruct
+    outs = (
+        (shape((2, rows, model), LOW), pl.BlockSpec((2, share, model), lambda s, w: (0, s, 0))),
+        (shape((2, rows, model), F32), pl.BlockSpec((2, share, model), lambda s, w: (0, s, 0))),
+        (shape((1, own_rows), F32), None),
+        (shape((own_rows, 2, wide), F32), None),
+        (shape((own_rows, WIDE), F32), None),
+        (shape((own_rows, 12), F32), None),
+        (shape((CONV + 1, wide), F32), None),
+        (shape((CONV + 1, WIDE), F32), None),
+        (shape((1, 12), F32), None),
+        (shape((1, 12), F32), None),
+        (shape((1, 12), F32), None),
+        (shape((1, wide), F32), None),
+        (shape((own_rows, wide), F32), None),
+    )
+    return pl.pallas_call(
+        finish_body,
+        out_shape=[out[0] for out in outs],
+        grid_spec=pltpu.PrefetchScalarGridSpec(
+            num_scalar_prefetch=1,
+            grid=(4,),
+            in_specs=[
+                const(mine.shape),
+                const(exits.shape),
+                const(state.shape),
+                const(vector.shape),
+                pl.BlockSpec((2, share, model), lambda s, w: (0, s, 0)),
+                pl.BlockSpec((share, model), lambda s, w: (s, 0)),
+                pl.BlockSpec((share, model), lambda s, w: (s, 0)),
+            ],
+            out_specs=[out[1] if out[1] is not None else const(out[0].shape) for out in outs],
+        ),
+        compiler_params=params(),
+        name="finish",
+    )(side, mine, exits, state, vector, token, block_own, block_other)
 
 
 def body(
     tokens, documents, norm_gain, entry_weight, state_weight, step_weight, inner_kernel,
     state_filter, step_bias, decay_log, skip_gain, gate_gain, exit_weight, cotangent,
 ):
-    every = ("tensor", "dp", "context")
     seqs, rows, model = tokens.shape
     count = lax.axis_size("context")
     position, side = lax.axis_index("context"), lax.axis_index("tensor")
-    group_count = lax.axis_size("dp") * count
     own_rows = norm_gain.shape[0]
-    which = jnp.reshape(side, (1,)).astype(jnp.int32)
+    which = jnp.stack([side, lax.axis_index("dp") * count + position]).astype(jnp.int32)
     longest = rows * count // 4
-    hops = min(count - 1, -(-(longest - 1) // rows))
-
-    first = (side == 0).astype(F32)
-    state_half = jnp.where(side == 0, state_weight[:, :NSTATE], state_weight[:, NSTATE:])
-    packed = jnp.concatenate(
-        [
-            entry_weight[:, 0],
-            entry_weight[:, 1],
-            exit_weight,
-            state_half,
-            step_weight * first,
-            step_weight * (1.0 - first),
-            norm_gain[:, None],
-            jnp.zeros((own_rows, LANES - 25), F32),
-        ],
-        axis=1,
-    ).astype(LOW)
-    weights = lax.all_gather(packed, every, axis=0, tiled=True).reshape(2, model, -1)
-
-    def placed(v):
-        return jnp.concatenate([v * first, v * (1.0 - first), jnp.zeros((LANES - 24,), F32)])
-
-    row6 = jnp.concatenate(
-        [placed(step_bias), placed(decay_log), placed(skip_gain), jnp.zeros((model - 3 * LANES,))]
-    )
-    par_own = jnp.concatenate(
-        [inner_kernel, gate_gain[None], row6[None], jnp.zeros((1, model), F32)], axis=0
-    )
-    par = lax.all_gather(par_own, "tensor", axis=0)
-    par_heads = jnp.concatenate(
-        [(par[0, 6] + par[1, 6])[: 3 * LANES].reshape(3, LANES), jnp.zeros((5, LANES), F32)], axis=0
-    )
-    filt = jnp.concatenate([state_filter, jnp.zeros((3, WIDE), F32)], axis=0)
-
-    docs = lax.dynamic_index_in_dim(documents, side, 0, keepdims=False).astype(F32)
-    doc_col = jnp.broadcast_to(docs[:, None], (rows, LANES))
-    doc_row = jnp.broadcast_to(docs[None], (8, rows))
-    forward = [(i, i + 1) for i in range(count - 1)]
-    own_tokens = lax.dynamic_index_in_dim(tokens, side, 0, keepdims=False)
-    halo = lax.ppermute(own_tokens[-HALO:], "context", forward)
-    halo_docs = lax.ppermute(doc_col[-HALO:], "context", forward)
-    halo_docs = jnp.where(position == 0, -1.0, halo_docs)
-
+    rounds = min(count // 2 - 1, -(-(longest - 1) // (2 * rows)))
+
+    packed, packed_exit, par_own, doc_col, doc_row, edge_own = pack(
+        which, entry_weight, exit_weight, state_weight, step_weight, norm_gain, inner_kernel,
+        gate_gain, step_bias, decay_log, skip_gain, documents, tokens,
+    )
+    weights, par, par_heads, halo, halo_docs, cot_t = gather(
+        packed, par_own, edge_own, doc_col[-HALO:], cotangent
+    )
+    weights = weights.reshape(2, model, -1)
     (
-        hidden, cin, gate, pre, loc, fold, gain, cin_state, pre_state, bc, bct, score, mask, zst, dt,
-        sp, cumt, fac, match,
-    ) = front(which, tokens, halo, halo_docs, doc_col, doc_row, weights, par, par_heads, filt)
-    carry = chained(fold, gain, hops, False)
-    cot_t = lax.dynamic_index_in_dim(cotangent, side, 0, keepdims=False).T
+        hidden_t, cin, gate, pre, loc, fold, gain, cin_state, pre_state, bc, bct, score, mask, zst,
+        dt, sp, cumt, fac, match,
+    ) = front(which, tokens, halo, halo_docs, doc_col, doc_row, weights, par, par_heads, state_filter)
+    carry, exit_weights = chain(fold, gain, packed_exit, rounds)
+    exit_weights = exit_weights.reshape(2, model, -1)
     block_own, exit_part, dy, gpg, enter, gate_row, skip_row = middle(
-        which, tokens, cotangent, cot_t, pre, gate, loc, carry, weights, par, par_heads, bc, bct,
-        score, mask, sp, cumt, fac,
-    )
-    adj = chained(enter, gain, hops, True)
+        which, tokens, cotangent, cot_t, pre, gate, loc, carry, exit_weights, par, par_heads, bc,
+        bct, score, mask, sp, cumt, fac,
+    )
+    cut = lambda v: v.reshape(2, 2, count, own_rows, v.shape[-1])
+    adj, exit_mine = chain_back(enter, gain, cut(exit_part), rounds)
+    block_sent, adj = lax.optimization_barrier((block_own, adj))
+    block_other = lax.ppermute(block_sent, "tensor", [(0, 1), (1, 0)])
     cg, edge, taps, cg_state, edge_state, taps_state, srg, head_rows = scan_back(
-        pre, dy, loc, carry, adj, cin, par, par_heads, filt, cin_state, pre_state, bc, bct, score,
-        mask, sp, cumt, fac, match, zst, dt,
-    )
-    back = [(i + 1, i) for i in range(count - 1)]
-    edge, edge_state = lax.ppermute((edge, edge_state), "context", back)
+        pre, dy, loc, carry, adj, cin, par, par_heads, state_filter, cin_state, pre_state, bc, bct,
+        score, mask, sp, cumt, fac, match, zst, dt,
+    )
+    edge, edge_state = edges(edge, edge_state)
     gate_part, inner_part, small_part, token_own, norm_row = tail(
-        which, tokens, cotangent, hidden.T, gpg, cg, edge, cg_state, edge_state, srg, weights
-    )
-
-    small_both = jnp.stack([small_part, small_part])
-    parts = jnp.concatenate([gate_part, inner_part, exit_part, small_both], axis=2)
-    mine = lax.psum_scatter(
-        parts.reshape(2 * model, -1).astype(F32), every, scatter_dimension=0, tiled=True
-    )
-    smalls = lax.psum((taps, taps_state, gate_row, skip_row, head_rows, norm_row), every)
-    taps, taps_state, gate_row, skip_row, head_rows, norm_row = smalls
-    block_out = lax.all_gather(block_own, "tensor", axis=0)
-    token_grad = lax.all_gather(token_own, "tensor", axis=0)
-    wide = 3 * WIDE
-    at = lax.axis_index("dp") * count + position
-    half = lambda v: lax.dynamic_slice_in_dim(v, side * wide, wide, axis=-1)
-    twelve = lambda v: lax.dynamic_slice_in_dim(v[:24], side * 12, 12, axis=0)
-    step_grad = lax.dynamic_slice_in_dim(mine[:, 9 * WIDE + WIDE : 9 * WIDE + WIDE + 24], side * 12, 12, axis=1)
-    return (
-        block_out,
-        token_grad,
-        lax.dynamic_slice_in_dim(norm_row[0], at * own_rows, own_rows, axis=0),
-        jnp.stack([mine[:, :wide], mine[:, wide : 2 * wide]], axis=1),
-        mine[:, 9 * WIDE : 10 * WIDE],
-        step_grad,
-        half(taps[: CONV + 1]),
-        taps_state[: CONV + 1],
-        twelve(head_rows[0]),
-        twelve(head_rows[1]),
-        twelve(skip_row[0]),
-        half(gate_row[0]),
-        mine[:, 2 * wide : 3 * wide],
-    )
+        which, tokens, cotangent, hidden_t, gpg, cg, edge, cg_state, edge_state, srg, weights
+    )
+    mine, state_both, vector, token_both = reduce_all(
+        cut(gate_part), cut(inner_part), cut(small_part), token_own, taps, taps_state, gate_row,
+        head_rows, skip_row, norm_row,
+    )
+    outs = finish(which, mine, exit_mine, state_both, vector, token_both, block_own, block_other)
+    flat = (2, 8, 9, 10, 11)
+    return tuple(out[0] if index in flat else out for index, out in enumerate(outs))
 
 
 def solution(mesh):

time: 636 us -> 255 us (0.40)
  waiting for transfers between devices: 444 us -> 0.01 us
  Pallas kernels: 88.2 us -> 243 us
  other arithmetic: 27.8 us -> 1.88 us
  local copies, waits for them, and re-layouts: 30.8 us -> 6.23 us
  starting transfers between devices: 25 us -> 0.99 us
  between operations: 14 us -> 0.75 us
    reduce_scatter x1 -> x0, waiting for transfers between devices: 197 us -> none  [body(): lax.psum_scatter(parts.reshape(2 * model, -1).astype(F32), every, scatter...]
    pallas_call x0 -> x7, Pallas kernels: none -> 153 us  [the longest x1 51.5 us: reduce_all(): pl.pallas_call(functools.partial(reduce_body, depth), out_shape=(shape((o...]
    psum x1 -> x0, waiting for transfers between devices: 107 us -> none  [body(): lax.psum((taps, taps_state, gate_row, skip_row, head_rows, norm_row), every)]
    all_gather x3 -> x0, waiting for transfers between devices: 102 us -> none  [the longest x1 59.7 us: body(): lax.all_gather(packed, every, axis=0, tiled=True).reshape(2, model, -1)]
    ppermute x8 -> x1, waiting for transfers between devices: 37.8 us -> 0.01 us  [body(): block_other = lax.ppermute(block_sent, 'tensor', [(0, 1), (1, 0)])]
    ppermute x8 -> x1, starting transfers between devices: 24.8 us -> 0.99 us  [body(): block_other = lax.ppermute(block_sent, 'tensor', [(0, 1), (1, 0)])]
    convert_element_type x2 -> x0, other arithmetic: 10.8 us -> none  [the longest x1 10.1 us: body(): parts.reshape(2 * model, -1).astype(F32)]
    slice x11 -> x1, local copies, waits for them, and re-layouts: 8.65 us -> 1.3 us  [body(): doc_col[-HALO:]]
  transfers between devices with their start and end apart: 13 -> 1, of which waited for: 9 -> 0; matrix products, arithmetic and copies ran while one was open for 5% -> 0% of each run, Pallas kernels for 8% -> 43%
where the time goes in v3:
time: 255 us; the launch traced here: 253 us
  Pallas kernels  243 us (95%)
  local copies, waits for them, and re-layouts  6.23 us (2%)
    pallas_call x1, Pallas kernels, reduce_all(): pl.pallas_call(functools.partial(reduce_body, depth), out_shape=(shape((o...  51.5 us
    pallas_call x1, Pallas kernels, scan_back(): pl.pallas_call(scan_back_body, out_shape=[out[0] for out in outs], grid=(...  38.2 us
    pallas_call x1, Pallas kernels, gather(): pl.pallas_call(functools.partial(gather_body, depth), out_shape=(shape((2...  37.4 us
    pallas_call x1, Pallas kernels, chain(): pl.pallas_call(functools.partial(chain_body, depth, rounds), out_shape=(s...  27.7 us
    pallas_call x1, Pallas kernels, chain_back(): pl.pallas_call(functools.partial(chain_back_body, depth, rounds), out_sha...  24.6 us
    pallas_call x1, Pallas kernels, middle(): pl.pallas_call(middle_body, out_shape=[out[0] for out in outs], grid_spec...  22 us
    pallas_call x1, Pallas kernels, tail(): pl.pallas_call(tail_body, out_shape=[out[0] for out in outs], grid_spec=p...  15 us
    pallas_call x1, Pallas kernels, front(): pl.pallas_call(front_body, out_shape=[out[0] for out in outs], grid_spec=...  14.8 us
  transfers between devices with their start and end apart: 1, of which 0 were waited for; matrix products, arithmetic and copies ran while one was open for 0% of the time, Pallas kernels for 43%

profile of v3, /device:TPU:0, one launch (start us, length us, event | category | flops | bytes accessed | tf_op | source)
XLA Modules:
  0.0 253.3 jit_solution(7514211954609992656)
XLA Ops:
  0.6 1.3 broadcast_in_dim.16.gate_gain
  1.9 1.4 copy.27.steps
  3.3 0.6 pad_add_fusion.side_ref.which
  3.9 3.1 %pack.1 = (bf16[48,1792]{1,0:T(8,128)(2,1)}, bf16[48,768]{1,0:T(8,128)(2,1)}, f32[8,768]{1,0:T(8,128)}, f32[512,128]{1,0:T(8,128)}, f32[8,512]{1,0:T(8,128)}, /*index=5*/bf16[16,768]{1,0:T(8,128)(2,1)}) custom-call(s32[2]{0:T(128)} %pad_add_fusion.side_ref.which, f32[48,2,768]{2,1,0:T(2,128)} %entry.1, f32[48,768]{1,0:T(8,128)} %exits.1, f32[48,256]{1,0:T(8,128)} %state.1, ...), custom_call_target="tpu_custom_call" | custom-call | tf_op jit(solution)/shard_map/pack/pallas_call | solution.py:1262
  7.0 1.3 slice.3.docs_own
  8.3 37.4 %gather.1 = (bf16[2,2,8,48,1792]{4,3,2,1,0:T(8,128)(2,1)}, f32[2,8,768]{2,1,0:T(8,128)}, f32[8,128]{1,0:T(8,128)}, bf16[16,768]{1,0:T(8,128)(2,1)}, f32[16,128]{1,0:T(8,128)}, /*index=5*/bf16[768,512]{1,0:T(8,128)(2,1)}) custom-call(bf16[48,1792]{1,0:T(8,128)(2,1)} %get-tuple-element.89.packed, f32[8,768]{1,0:T(8,128)} %get-tuple-element.90.par_own, ...), custom_call_target="tpu_custom_call" | custom-call | tf_op jit(solution)/shard_map/gather/pallas_call | solution.py:1324
  45.7 14.8 %front.1 = (bf16[768,512]{1,0:T(8,128)(2,1)}, bf16[528,1536]{1,0:T(8,128)(2,1)}, f32[512,1536]{1,0:T(8,128)}, f32[512,1536]{1,0:T(8,128)}, f32[512,1536]{1,0:T(8...) custom-call(s32[2]{0:T(128)} %pad_add_fusion.side_ref.which, ...), custom_call_target="tpu_custom_call" | custom-call | tf_op jit(solution)/shard_map/front/pallas_call | solution.py:239
  60.5 27.7 %chain.1 = (bf16[128,1536]{1,0:T(8,128)(2,1)}, bf16[2,2,8,48,768]{4,3,2,1,0:T(8,128)(2,1)}) custom-call(f32[128,1536]{1,0:T(8,128)} %get-tuple-element.104.fold, f32[8,1536]{1,0:T(8,128)} %get-tuple-element.105.gain, bf16[48,768]{1,0:T(8,128)(2,1)} %get-tuple-element.106.packed), custom_call_target="tpu_custom_call" | custom-call | tf_op jit(solution)/shard_map/chain/pallas_call | solution.py:1372
  88.2 22.0 %middle.1 = (bf16[512,768]{1,0:T(8,128)(2,1)}, bf16[2,768,768]{2,1,0:T(8,128)(2,1)}, f32[512,1536]{1,0:T(8,128)}, bf16[512,1536]{1,0:T(8,128)(2,1)}, f32[128,153...) custom-call(s32[2]{0:T(128)} %pad_add_fusion.side_ref.which, bf16[2,512,768]{2,1,0:T(8,128)(2,1)} %tokens.5, ...), custom_call_target="tpu_custom_call" | custom-call | tf_op jit(solution)/shard_map/middle/pallas_call | solution.py:410
  110.2 0.0 copy-start
  110.2 24.6 %chain_back.1 = (bf16[128,1536]{1,0:T(8,128)(2,1)}, f32[48,768]{1,0:T(8,128)}) custom-call(f32[128,1536]{1,0:T(8,128)} %get-tuple-element.119.fold, f32[8,1536]{1,0:T(8,128)} %get-tuple-element.105.gain, bf16[2,2,8,48,768]{4,3,2,1,0:T(8,128)(2,1)} %bitcast.24), custom_call_target="tpu_custom_call" | custom-call | tf_op jit(solution)/shard_map/chain_back/pallas_call | solution.py:1407
  134.8 0.0 copy-done
  134.8 1.0 collective-permute-start
  135.8 38.2 %scan_back.1 = (f32[512,1536]{1,0:T(8,128)}, f32[8,1536]{1,0:T(8,128)}, f32[8,1536]{1,0:T(8,128)}, f32[512,256]{1,0:T(8,128)}, f32[8,256]{1,0:T(8,128)}, /*index...) custom-call(f32[512,1536]{1,0:T(8,128)} %get-tuple-element.101.pre_ref, ...), custom_call_target="tpu_custom_call" | custom-call | tf_op jit(solution)/shard_map/scan_back/pallas_call | solution.py:599
  174.0 3.5 %edges.1 = (f32[8,1536]{1,0:T(8,128)}, f32[8,256]{1,0:T(8,128)}) custom-call(f32[8,1536]{1,0:T(8,128)} %get-tuple-element.130.own, f32[8,256]{1,0:T(8,128)} %get-tuple-element.131.own_state), custom_call_target="tpu_custom_call" | custom-call | tf_op jit(solution)/shard_map/edges/pallas_call | solution.py:1451
  177.5 15.0 %tail.1 = (bf16[2,768,768]{2,1,0:T(8,128)(2,1)}, bf16[2,768,768]{2,1,0:T(8,128)(2,1)}, bf16[2,768,256]{2,1,0:T(8,128)(2,1)}, bf16[512,768]{1,0:T(8,128)(2,1)}, f32[8,768]{1,0:T(8,128)}) custom-call(s32[2]{0:T(128)} %pad_add_fusion.side_ref.which, bf16[2,512,768]{2,1,0:T(8,128)(2,1)} %tokens.5, bf16[2,512,768]{2,1,0:T(8,128)(2,1)} %cot.5, ...), custom_call_target="tpu_custom_call" | custom-call | tf_op jit(solution)/shard_map/tail/pallas_call | solution.py:703
  192.5 51.5 %reduce_all.1 = (f32[48,1792]{1,0:T(8,128)}, f32[2,48,128]{2,1,0:T(8,128)}, f32[8,1792]{1,0:T(8,128)}, bf16[2,512,768]{2,1,0:T(8,128)(2,1)}) custom-call(bf16[2,2,8,48,768]{4,3,2,1,0:T(8,128)(2,1)} %bitcast.22, bf16[2,2,8,48,768]{4,3,2,1,0:T(8,128)(2,1)} %bitcast.23, bf16[2,2,8,48,256]{4,3,2,1,0:T(8,128)(2,1)} %bitcast.26, ...), custom_call_target="tpu_custom_call" | custom-call | tf_op jit(solution)/shard_map/reduce_all/pallas_call | solution.py:1570
  244.0 0.0 collective-permute-done.block_other
  244.0 0.0 copy-start.1
  244.0 0.9 copy-done.1
  244.9 5.7 %finish.1 = (bf16[2,512,768]{2,1,0:T(8,128)(2,1)}, f32[2,512,768]{2,1,0:T(8,128)}, f32[1,48]{1,0:T(1,128)}, f32[48,2,768]{2,1,0:T(2,128)}, f32[48,256]{1,0:T(8,1...) custom-call(s32[2]{0:T(128)} %pad_add_fusion.side_ref.which, ...), custom_call_target="tpu_custom_call" | custom-call | tf_op jit(solution)/shard_map/finish/pallas_call | solution.py:1655
  250.6 1.4 copy.28
  252.0 1.3 reduce
Async XLA Ops:
  110.2 24.6 %copy-start = (bf16[512,768]{1,0:T(8,128)(2,1)S(1)}, bf16[512,768]{1,0:T(8,128)(2,1)}, u32[]{:S(2)}) copy-start(bf16[512,768]{1,0:T(8,128)(2,1)} %get-tuple-element.151.block_own) | copy-start | bytes 2359300
  134.8 109.2 %collective-permute-start = (bf16[512,768]{1,0:T(8,128)(2,1)S(1)}, bf16[512,768]{1,0:T(8,128)(2,1)S(1)}, u32[]{:S(2)}, u32[]{:S(2)}) collective-permute-start(bf16[512,768]{1,0:T(8,128)(2,1)S(1)} %copy-done), channel_id=1, source_target_pairs={{0,1},{1,0},{2,3},{3,2},{4,5},{5,4},{6,7},{7,6},{8,9},{9,8},{10,11... | collective-permute-start | bytes 2359304 | tf_op jit(solution)/shard_map/ppermute | solution.py:1710
  244.0 0.9 copy-start.1

commit v4 on v1

v4 whole, which is shorter than its diff:
```python
import functools
import jax
import jax.numpy as jnp
from jax import lax
from jax.experimental import pallas as pl
from jax.experimental.pallas import tpu as pltpu
from jax.sharding import PartitionSpec as P

HEAD = 64
NSTATE = 128
CONV = 4
EPSILON = 1e-05
Q = 128
HALO = 16
EDGE = 8
GROUPS = 6
BLOCK_CUTS = 8
LANES = 128
WIDE = 256
LOG2E = 1.4426950408889634
FAR = -1e30
LOW = jnp.bfloat16
F32 = jnp.float32
VMEM_LIMIT = 60 * 1024 * 1024


def mm(a, b):
    return lax.dot_general(a, b, (((1,), (0,)), ((), ())), preferred_element_type=F32)


def mm_nt(a, b):
    return lax.dot_general(a, b, (((1,), (1,)), ((), ())), preferred_element_type=F32)


def mm_tn(a, b):
    return lax.dot_general(a, b, (((0,), (0,)), ((), ())), preferred_element_type=F32)


def mm_exact(a, b):
    return lax.dot_general(
        a, b, (((1,), (0,)), ((), ())), precision=lax.Precision.HIGHEST, preferred_element_type=F32
    )


def split3(v):
    high = v.astype(LOW).astype(F32)
    rest = v - high
    mid = rest.astype(LOW).astype(F32)
    low = rest - mid
    return (high + pltpu.roll(mid, 32, 1) + pltpu.roll(low, 64, 1)).astype(LOW)


def iota(shape, dim):
    return lax.broadcasted_iota(jnp.int32, shape, dim)


def spreader(first_head, width, count):
    k = iota((LANES, width * count), 0)
    lane = iota((LANES, width * count), 1)
    hit = ((k & 31) == first_head + lane // width) & (k < 96)
    return hit.astype(F32).astype(LOW)


def gatherer(first_head, width, count):
    lane = iota((width * count, LANES), 0)
    k = iota((width * count, LANES), 1)
    return (k == first_head + lane // width).astype(F32).astype(LOW)


def head_sums(v, collect):
    high = v.astype(LOW)
    rest = (v - high.astype(F32)).astype(LOW)
    return mm(high, collect) + mm(rest, collect)


def sigmoid(v):
    return 1.0 / (1.0 + jnp.exp(-v))


def twice(v):
    return jnp.concatenate([v, v], axis=1)


def conv_forward(cin, taps, masks):
    rows = cin.shape[0] - HALO
    out = taps[CONV : CONV + 1] + taps[CONV - 1 : CONV] * cin[HALO:]
    for back in range(1, CONV):
        part = cin[HALO - back : HALO - back + rows]
        out = out + taps[CONV - 1 - back : CONV - back] * (part * twice(masks[back - 1]))
    return out


def conv_backward(pg, cin, taps, masks):
    rows, width = pg.shape
    sums = [None] * (CONV + 1)
    sums[CONV] = jnp.sum(pg, axis=0, keepdims=True)
    sums[CONV - 1] = jnp.sum(pg * cin[HALO:], axis=0, keepdims=True)
    pad = jnp.zeros((HALO, width), F32)
    grad = jnp.concatenate([pad, pg * taps[CONV - 1 : CONV]], axis=0)
    for back in range(1, CONV):
        masked = pg * twice(masks[back - 1])
        part = cin[HALO - back : HALO - back + rows]
        sums[CONV - 1 - back] = jnp.sum(masked * part, axis=0, keepdims=True)
        padded = jnp.concatenate([pad, masked * taps[CONV - 1 - back : CONV - back], pad], axis=0)
        grad = grad + padded[back : back + rows + HALO]
    return sums, grad


def const(shape):
    zeros = (0,) * len(shape)
    return pl.BlockSpec(shape, lambda *_: zeros)


def params(**extra):
    return pltpu.CompilerParams(vmem_limit_bytes=VMEM_LIMIT, **extra)


VMEM_SPEC = pl.BlockSpec(memory_space=pltpu.VMEM)
ANY_SPEC = pl.BlockSpec(memory_space=pl.ANY)


def side():
    return lax.axis_index("tensor")


def remote(src, dst, send_sem, recv_sem, target):
    return pltpu.make_async_remote_copy(
        src_ref=src,
        dst_ref=dst,
        send_sem=send_sem,
        recv_sem=recv_sem,
        device_id=target,
        device_id_type=pl.DeviceIdType.MESH,
    )


def each(count, run, first=0):
    def one(step, carry):
        run(step)
        return carry

    lax.fori_loop(first, count, one, 0)


class Place:
    def __init__(self, depth):
        position = lax.axis_index("context")
        self.depth = depth
        self.position = position
        self.x, self.y = lax.axis_index("dp"), lax.axis_index("tensor")
        self.z, self.c = position // 2, position % 2
        self.mate = self.at(self.x, self.y, self.z, 1 - self.c)
        self.x_peer = self.at(1 - self.x, self.y, self.z, self.c)
        self.y_peer = self.at(self.x, 1 - self.y, self.z, self.c)

    def at(self, x, y, z, c):
        return {"dp": x, "context": z * 2 + c, "tensor": y}

    def up(self):
        return self.at(self.x, self.y, self.z + 1, self.c)

    def down(self):
        return self.at(self.x, self.y, self.z - 1, self.c)

    def away(self, z):
        return self.at(self.x, self.y, z, self.c)

    def axes(self, turned):
        x, y, z, c = self.x, self.y, self.z, self.c
        x1, y1 = x + (1 - turned) * (1 - 2 * x), y + turned * (1 - 2 * y)
        x2, y2 = x + turned * (1 - 2 * x), y + (1 - turned) * (1 - 2 * y)
        return (x1, y1), (x2, y2)

    def around(self, run, first=0, last=None):
        z, depth = self.z, self.depth
        if first == 0:
            run(z)

        def step(away):
            @pl.when(z - away >= 0)
            def _():
                run(z - away)

            @pl.when(z + away < depth)
            def _():
                run(z + away)

        each(depth if last is None else last, step, max(first, 1))

    def greet(self, always, sometimes=(), column=False):
        barrier = pltpu.get_barrier_semaphore()
        kind = pl.DeviceIdType.MESH
        total = len(always)
        for target in always:
            pl.semaphore_signal(barrier, inc=1, device_id=target, device_id_type=kind)
        for holds, target in sometimes:

            @pl.when(holds)
            def _():
                pl.semaphore_signal(barrier, inc=1, device_id=target, device_id_type=kind)

            total = total + holds.astype(jnp.int32)
        if column:
            for_all = lambda step: pl.semaphore_signal(
                barrier,
                inc=1,
                device_id=self.away(lax.rem(self.z + step, self.depth)),
                device_id_type=kind,
            )
            each(self.depth, for_all, 1)
            total = total + (self.depth - 1)
        pl.semaphore_wait(barrier, total)


class Gathering:
    def __init__(self, place, own, full, sends, lands, local):
        self.place, self.own_ref, self.full = place, own, full
        self.sends, self.lands, self.local = sends, lands, local
        (self.x1, self.y1), (self.x2, self.y2) = place.axes(place.c)
        self.first = place.at(self.x1, self.y1, place.z, place.c)
        self.second = place.at(self.x2, self.y2, place.z, place.c)

    @staticmethod
    def scratch(depth):
        sem = pltpu.SemaphoreType.DMA
        return [sem((5, 4 * depth)), sem((8 * depth,)), sem((1,))]

    def copy(self, kind, index, x, y, z, c, target, own=False):
        chunk = self.full.at[y, x, z * 2 + c]
        mark = ((y * 2 + x) * self.place.depth + z) * 2 + c
        return remote(
            self.own_ref if own else chunk, chunk, self.sends.at[kind, index], self.lands.at[mark],
            target,
        )

    def arrive(self, x, y, z, c):
        self.copy(0, 0, x, y, z, c, self.place.mate).wait_recv()

    def kept(self):
        p = self.place
        return pltpu.make_async_copy(
            self.own_ref, self.full.at[p.y, p.x, p.z * 2 + p.c], self.local.at[0]
        )

    def own(self):
        p = self.place
        mine = (p.x, p.y, p.z, p.c)

        @pl.when(p.z + 1 < p.depth)
        def _():
            self.copy(3, p.z, *mine, p.up(), True).start()

        @pl.when(p.z > 0)
        def _():
            self.copy(4, p.z, *mine, p.down(), True).start()

        self.copy(1, p.z, *mine, self.first, True).start()
        self.copy(2, p.z, *mine, self.second, True).start()
        self.copy(0, p.z, *mine, p.mate, True).start()
        self.kept().start()

    def near(self, first=1, last=None):
        p = self.place

        def run(z):
            chunk = (p.x, p.y, z, p.c)
            self.arrive(*chunk)

            @pl.when((z < p.z) & (p.z + 1 < p.depth))
            def _():
                self.copy(3, z, *chunk, p.up()).start()

            @pl.when((z > p.z) & (p.z > 0))
            def _():
                self.copy(4, z, *chunk, p.down()).start()

            self.copy(1, z, *chunk, self.first).start()
            self.copy(2, z, *chunk, self.second).start()
            self.copy(0, z, *chunk, p.mate).start()

        p.around(run, first, last)

    def across(self):
        p = self.place

        def run(z):
            chunk = (self.x1, self.y1, z, p.c)
            self.arrive(*chunk)
            self.copy(2, p.depth + z, *chunk, self.second).start()
            self.copy(0, p.depth + z, *chunk, p.mate).start()

        p.around(run)

    def far(self):
        p = self.place

        def near_row(z):
            self.arrive(self.x2, self.y2, z, p.c)
            self.copy(0, 2 * p.depth + z, self.x2, self.y2, z, p.c, p.mate).start()

        def far_row(z):
            self.arrive(1 - p.x, 1 - p.y, z, p.c)
            self.copy(0, 3 * p.depth + z, 1 - p.x, 1 - p.y, z, p.c, p.mate).start()

        p.around(near_row)
        p.around(far_row)

    def finish(self):
        p = self.place

        def from_mate(z):
            for y in range(2):
                for x in range(2):
                    self.arrive(x, y, z, 1 - p.c)

        each(p.depth, from_mate)

        def sent(kind, index, target):
            self.copy(kind, index, p.x, p.y, p.z, p.c, target).wait_send()

        each(4 * p.depth, lambda step: sent(0, step, p.mate))
        each(p.depth, lambda step: sent(1, step, p.mate))
        each(2 * p.depth, lambda step: sent(2, step, p.mate))

        def chained(z):
            @pl.when((z <= p.z) & (p.z + 1 < p.depth))
            def _():
                sent(3, z, p.mate)

            @pl.when((z >= p.z) & (p.z > 0))
            def _():
                sent(4, z, p.mate)

        each(p.depth, chained)
        self.kept().wait()


class Reducing:
    def __init__(self, place, turned, parts, total, bufs, sems):
        self.place, self.parts, self.total = place, parts, total
        self.own, self.core, self.send1, self.land1 = bufs[:4]
        self.send2, self.land2, self.send3, self.land3 = bufs[4:]
        self.own_sem, self.core_send, self.core_land = sems[:3]
        self.s1, self.l1, self.s2, self.l2, self.s3, self.l3 = sems[3:]
        self.turned = turned
        (x1, y1), (x2, y2) = place.axes(turned)
        self.first = place.at(x1, y1, place.z, place.c)
        self.second = place.at(x2, y2, place.z, place.c)
        self.mine = place.y + turned * (place.x - place.y)

    @staticmethod
    def scratch(depth, rows, tall):
        buffer = lambda *lead: pltpu.VMEM(lead + (rows, tall), LOW)
        sem = lambda *lead: pltpu.SemaphoreType.DMA(lead)
        bufs = [
            buffer(2, 2, depth), buffer(2, 2, depth), buffer(depth, 2), buffer(depth, 2),
            buffer(depth), buffer(depth), buffer(depth), buffer(depth),
        ]
        return bufs + [sem(2, 2, depth)] * 3 + [sem(depth)] * 6

    def spot(self, step):
        return lax.rem(self.place.z + 1 + step, self.place.depth)

    def whole(self, y, x, z):
        return remote(
            self.core.at[y, x, z], self.core.at[y, x, z], self.core_send.at[y, x, z],
            self.core_land.at[y, x, z], self.place.mate,
        )

    def own_whole(self, y, x, z):
        return pltpu.make_async_copy(
            self.own.at[y, x, z], self.own.at[y, x, z], self.own_sem.at[y, x, z]
        )

    def start(self, step):
        p = self.place
        z = self.spot(step)
        for y in range(2):
            for x in range(2):
                for ref, cols in self.parts:
                    remote(
                        ref.at[y, x, z * 2 + 1 - p.c], self.core.at[y, x, z, :, cols],
                        self.core_send.at[y, x, z], self.core_land.at[y, x, z], p.mate,
                    ).start()
                    pltpu.make_async_copy(
                        ref.at[y, x, z * 2 + p.c], self.own.at[y, x, z, :, cols],
                        self.own_sem.at[y, x, z],
                    ).start()

    def base(self, y, x, z):
        return self.own[y, x, z].astype(F32) + self.core[y, x, z].astype(F32)

    def copy1(self, z):
        return remote(
            self.send1.at[z], self.land1.at[z], self.s1.at[z], self.l1.at[z], self.first
        )

    def copy2(self, z):
        return remote(
            self.send2.at[z], self.land2.at[z], self.s2.at[z], self.l2.at[z], self.second
        )

    def copy3(self, z, lands_at):
        return remote(
            self.send3.at[z], self.land3.at[lands_at], self.s3.at[z], self.l3.at[lands_at],
            self.place.away(z),
        )

    def stage1(self, step):
        p, turned = self.place, self.turned
        z = self.spot(step)
        for y in range(2):
            for x in range(2):
                self.whole(y, x, z).wait_recv()
                self.own_whole(y, x, z).wait()
        for index in range(2):
            x = (1 - turned) * (1 - p.x) + turned * index
            y = turned * (1 - p.y) + (1 - turned) * index
            self.send1[z, index] = self.base(y, x, z).astype(LOW)
        self.copy1(z).start()

    def stage2(self, step):
        p, turned = self.place, self.turned
        z = self.spot(step)
        self.copy1(z).wait_recv()
        other = 1 - self.mine
        x = (1 - turned) * p.x + turned * other
        y = turned * p.y + (1 - turned) * other
        self.send2[z] = (self.base(y, x, z) + self.land1[z, other].astype(F32)).astype(LOW)
        self.copy2(z).start()

    def final(self, z):
        p = self.place
        self.copy2(z).wait_recv()
        return (
            self.base(p.y, p.x, z)
            + self.land1[z, self.mine].astype(F32)
            + self.land2[z].astype(F32)
        )

    def stage3(self, step):
        z = self.spot(step)
        self.send3[z] = self.final(z).astype(LOW)
        self.copy3(z, self.place.z).start()

    def turn(self, step):
        depth = self.place.depth

        @pl.when(step < depth)
        def _():
            self.stage1(step)

        @pl.when((step >= 1) & (step <= depth))
        def _():
            self.stage2(step - 1)

        @pl.when((step >= 2) & (step <= depth))
        def _():
            self.stage3(step - 2)

    def close(self):
        p = self.place
        self.total[...] = self.final(p.z)

        def add(step):
            z = lax.rem(p.z + step, p.depth)
            self.copy3(z, z).wait_recv()
            self.total[...] += self.land3[z].astype(F32)

        each(p.depth, add, 1)

    def finish(self):
        p = self.place

        def sent(z):
            for y in range(2):
                for x in range(2):
                    self.whole(y, x, z).wait_send()
            self.copy1(z).wait_send()
            self.copy2(z).wait_send()

        each(p.depth, sent)
        each(p.depth, lambda step: self.copy3(lax.rem(p.z + step, p.depth), p.z).wait_send(), 1)


class Chaining:
    def __init__(self, place, rounds, backward, fold, gain, bufs, sems):
        self.place, self.rounds = place, rounds
        self.fold, self.gain = fold, gain
        self.from_mate, self.from_chip, self.to_mate, self.to_chip = bufs
        self.mate_send, self.mate_land, self.chip_send, self.chip_land = sems
        first = 1 if backward else 0
        by = -1 if backward else 1
        self.order = place.depth - 1 - place.z if backward else place.z
        self.leads = place.c == first
        self.after = place.at(place.x, place.y, place.z + by, first)
        self.before = place.at(place.x, place.y, place.z - by, 1 - first)
        self.linked_before = self.leads & (self.order > 0)
        self.linked_after = jnp.logical_not(self.leads) & (self.order < place.depth - 1)

    @staticmethod
    def scratch(rounds):
        slots = lambda turns: pltpu.VMEM((turns, GROUPS, NSTATE, WIDE), LOW)
        marks = lambda turns: pltpu.SemaphoreType.DMA((turns, GROUPS))
        return [
            slots(rounds + 1), slots(rounds), slots(rounds + 1), slots(rounds),
            marks(rounds + 1), marks(rounds + 1), marks(rounds), marks(rounds),
        ]

    def sometimes(self):
        return [(self.linked_before, self.before), (self.linked_after, self.after)]

    def mate_copy(self, turn, cut):
        return remote(
            self.to_mate.at[turn, cut], self.from_mate.at[turn, cut], self.mate_send.at[turn, cut],
            self.mate_land.at[turn, cut], self.place.mate,
        )

    def chip_copy(self, turn, cut):
        return remote(
            self.to_chip.at[turn, cut], self.from_chip.at[turn, cut], self.chip_send.at[turn, cut],
            self.chip_land.at[turn, cut], self.after,
        )

    def joined(self, cut, arrived):
        return (self.fold[cut] + self.gain[cut, 0:1] * arrived.astype(F32)).astype(LOW)

    def open(self, cut):
        @pl.when(self.leads)
        def _():
            self.to_mate[0, cut] = self.fold[cut].astype(LOW)
            self.mate_copy(0, cut).start()

    def pass_on(self, turn, cut):
        @pl.when(jnp.logical_not(self.leads))
        def _():
            self.mate_copy(turn, cut).wait_recv()

        @pl.when(self.linked_after)
        def _():
            self.to_chip[turn, cut] = self.joined(cut, self.from_mate[turn, cut])
            self.chip_copy(turn, cut).start()

    def relay(self, turn, cut):
        @pl.when(self.linked_before)
        def _():
            self.chip_copy(turn, cut).wait_recv()
            self.to_mate[turn + 1, cut] = self.joined(cut, self.from_chip[turn, cut])
            self.mate_copy(turn + 1, cut).start()

        @pl.when(self.leads & (self.order == 0))
        def _():
            self.to_mate[turn + 1, cut] = self.fold[cut].astype(LOW)
            self.mate_copy(turn + 1, cut).start()

    def later(self):
        for turn in range(1, self.rounds):
            for cut in range(GROUPS):
                self.pass_on(turn, cut)
            for cut in range(GROUPS):
                self.relay(turn, cut)

    def arrive(self, put):
        last = self.rounds - 1

        @pl.when(self.linked_before)
        def _():
            for cut in range(GROUPS):
                put(cut, self.from_chip[last, cut])

        @pl.when(self.leads & (self.order == 0))
        def _():
            for cut in range(GROUPS):
                put(cut, jnp.zeros((NSTATE, WIDE), LOW))

        @pl.when(jnp.logical_not(self.leads))
        def _():
            for cut in range(GROUPS):
                self.mate_copy(self.rounds, cut).wait_recv()
                put(cut, self.from_mate[self.rounds, cut])

    def finish(self):
        @pl.when(self.leads)
        def _():
            for turn in range(self.rounds + 1):
                for cut in range(GROUPS):
                    self.mate_copy(turn, cut).wait_send()

        @pl.when(self.linked_after)
        def _():
            for turn in range(self.rounds):
                for cut in range(GROUPS):
                    self.chip_copy(turn, cut).wait_send()


def front_body(
    depth, rounds, tokens, halo, halo_docs, doc_col, doc_row, w_gate, w_inner, w_small, par, par_heads,
    state_filter, packed_exit, hidden_out, cin_out, gate_out, pre_out, loc_out, carry_out,
    exit_weights, cin_state_out, pre_state_out, bc_out, bct_out, score_out, mask_out, zst_out, dt_out, sp_out,
    cumt_out, fac_out, match_out, hidden, sp_tail, facs, folds, gains, *scratch
):
    step = pl.program_id(0)
    rows = tokens.shape[1]
    spans = rows // Q
    place = Place(depth)
    chaining = Chaining(place, rounds, False, folds, gains, scratch[:4], scratch[4:8])
    gathering = Gathering(place, packed_exit, exit_weights, *scratch[8:])

    @pl.when(step == 0)
    def _():
        place.greet(
            [place.mate, place.x_peer, place.y_peer],
            [(place.z + 1 < depth, place.up()), (place.z > 0, place.down())] + chaining.sometimes(),
        )
        gathering.own()

    for away in range(1, 4):

        @pl.when(step == away)
        def _():
            gathering.near(away, away + 1 if away < 3 else None)

    @pl.when(step == 4)
    def _():
        gathering.across()

    @pl.when(step == 5)
    def _():
        gathering.far()

    for cut in range(GROUPS - 1):

        @pl.when(step == cut + 1)
        def _():
            chaining.pass_on(0, cut)

    for cut in range(GROUPS - 3):

        @pl.when(step == cut + 3)
        def _():
            chaining.relay(0, cut)

    @pl.when(step == 0)
    def _():
        gain_t = jnp.transpose(w_small[0, :, LANES : 2 * LANES].astype(F32))
        gain = gain_t[24:25]
        for ref, first, count in ((halo, 0, HALO), (tokens, HALO, rows)):
            value = (ref[...] if ref is halo else ref[0]).astype(F32)
            scale = lax.rsqrt(jnp.mean(value * value, axis=1, keepdims=True) + EPSILON)
            hidden[first : first + count] = (value * scale * gain).astype(LOW)
        hidden_out[...] = jnp.transpose(hidden[HALO:])
        both = [mm(hidden[...], w_small[index]) for index in range(2)]
        cin = jnp.concatenate([both[0][:, :LANES], both[1][:, :LANES]], axis=1).astype(LOW)
        cin_state_out[...] = cin
        docs = jnp.concatenate([halo_docs[...], doc_col[...]], axis=0)
        masks = []
        for back in range(1, CONV):
            match = (docs[HALO - back : HALO - back + rows] == docs[HALO:]).astype(F32)
            match_out[back - 1] = match
            masks.append(match)
        pre = conv_forward(cin.astype(F32), state_filter[...], masks)
        pre_state_out[...] = pre
        mixed = (pre * sigmoid(pre)).astype(LOW)
        bc_out[...] = mixed
        turned = jnp.transpose(mixed.astype(F32)).astype(LOW)
        bct_out[...] = turned
        heads = par_heads[...]
        used = iota((rows, LANES), 1) < 24
        raw = both[0][HALO:, LANES:] + both[1][HALO:, LANES:]
        zst = jnp.where(used, raw, 0.0) + heads[0:1]
        zst_out[...] = zst
        dt = jnp.where(used, jnp.maximum(zst, 0.0) + jnp.log1p(jnp.exp(-jnp.abs(zst))), 0.0)
        dt_out[...] = dt
        decay = -dt * jnp.exp(heads[1:2])
        t_at, u_at = iota((Q, Q), 0), iota((Q, Q), 1)
        lower = (t_at >= u_at).astype(F32)
        fac_rows = []
        for index in range(spans):
            at = slice(index * Q, (index + 1) * Q)
            cum = mm_exact(lower, decay[at])
            final = cum[Q - 1 : Q]
            before = docs[HALO + index * Q - 1 : HALO + index * Q]
            here = doc_col[at]
            last = here[Q - 1 : Q]
            opened = (here == before).astype(F32)
            tail = (here == last).astype(F32) * jnp.exp(final - cum)
            fac_rows.append((last == before).astype(F32) * jnp.exp(final))
            cum2 = cum * LOG2E
            turned_cum = jnp.transpose(cum2)
            for group in range(6):
                cumt_out[group, 0:4, at] = turned_cum[4 * group : 4 * group + 4]
            sp_out[0, at] = split3(dt[at])
            sp_out[1, at] = split3(cum2)
            lanes_used = iota((Q, LANES), 1) < 24
            sp_out[2, at] = split3(jnp.where(lanes_used, opened * jnp.exp(cum), 0.0))
            sp_out[3, at] = split3(jnp.where(lanes_used, tail, 0.0))
            sp_tail[at] = split3(jnp.where(lanes_used, tail * dt[at], 0.0))
            same = (t_at >= u_at) & (here == doc_row[0:1, at])
            mask_out[at] = jnp.where(same, 0.0, FAR)
            score_out[at] = mm_nt(mixed[at, LANES:], mixed[at, :LANES])
        gain_total = fac_rows[0]
        for row in fac_rows[1:]:
            gain_total = gain_total * row
        rows8 = jnp.concatenate(
            fac_rows + [gain_total] + [jnp.zeros((1, LANES), F32)] * (7 - spans), axis=0
        )
        rows8 = jnp.where(iota((8, LANES), 1) < 24, rows8, 0.0)
        fac_out[...] = rows8
        facs[...] = split3(rows8)

    cin = mm(hidden[...], w_inner[0]).astype(LOW)
    cin_out[...] = cin
    gate_out[...] = mm(hidden[HALO:], w_gate[0])
    masks = [match_out[back] for back in range(CONV - 1)]
    pre = conv_forward(cin.astype(F32), par[0], masks)
    pre_out[...] = pre
    spread = spreader(4 * step, HEAD, 4)
    value = (pre * sigmoid(pre) * mm(sp_tail[...], spread)).astype(LOW)
    facx = mm(facs[...], spread)
    fold = jnp.zeros((NSTATE, WIDE), F32)
    for index in range(spans):
        at = slice(index * Q, (index + 1) * Q)
        loc = mm(bct_out[:NSTATE, at], value[at])
        loc_out[at] = loc
        fold = facx[index : index + 1] * fold + loc
    folds[step] = fold
    gains[step] = jnp.broadcast_to(facx[spans : spans + 1], (8, WIDE))
    for cut in range(GROUPS):

        @pl.when(step == cut)
        def _():
            chaining.open(cut)

    @pl.when(step == GROUPS - 1)
    def _():
        chaining.pass_on(0, GROUPS - 1)
        for cut in range(GROUPS - 3, GROUPS):
            chaining.relay(0, cut)
        chaining.later()

        def put(cut, value):
            carry_out[:, cut * WIDE : (cut + 1) * WIDE] = value

        chaining.arrive(put)
        gathering.finish()
        chaining.finish()


def front(
    tokens, halo, halo_docs, doc_col, doc_row, weights, par, par_heads, state_filter, packed_exit,
    rounds
):
    rows, model = tokens.shape[1:]
    count = lax.axis_size("context")
    depth = count // 2
    wide = 2 * 3 * WIDE
    ext = rows + HALO
    shape = jax.ShapeDtypeStruct
    outs = (
        (shape((model, rows), LOW), const((model, rows))),
        (shape((ext, wide), LOW), pl.BlockSpec((ext, WIDE), lambda s: (0, s))),
        (shape((rows, wide), F32), pl.BlockSpec((rows, WIDE), lambda s: (0, s))),
        (shape((rows, wide), F32), pl.BlockSpec((rows, WIDE), lambda s: (0, s))),
        (shape((rows, wide), F32), pl.BlockSpec((rows, WIDE), lambda s: (0, s))),
        (shape((NSTATE, wide), LOW), const((NSTATE, wide))),
        (shape((2, 2, count) + packed_exit.shape, LOW), ANY_SPEC),
        (shape((ext, WIDE), LOW), const((ext, WIDE))),
        (shape((rows, WIDE), F32), const((rows, WIDE))),
        (shape((rows, WIDE), LOW), const((rows, WIDE))),
        (shape((WIDE, rows), LOW), const((WIDE, rows))),
        (shape((rows, Q), F32), const((rows, Q))),
        (shape((rows, Q), F32), const((rows, Q))),
        (shape((rows, LANES), F32), const((rows, LANES))),
        (shape((rows, LANES), F32), const((rows, LANES))),
        (shape((4, rows, LANES), LOW), const((4, rows, LANES))),
        (shape((6, 8, rows), F32), const((6, 8, rows))),
        (shape((8, LANES), F32), const((8, LANES))),
        (shape((CONV - 1, rows, LANES), F32), const((CONV - 1, rows, LANES))),
    )
    return pl.pallas_call(
        functools.partial(front_body, depth, rounds),
        out_shape=[out[0] for out in outs],
        grid=(GROUPS,),
        in_specs=[
            pl.BlockSpec((1, rows, model), lambda s: (side(), 0, 0)),
            const((HALO, model)),
            const((HALO, LANES)),
            const((rows, LANES)),
            const((8, rows)),
            pl.BlockSpec((1, model, WIDE), lambda s: (s // 3, 0, s % 3)),
            pl.BlockSpec((1, model, WIDE), lambda s: (s // 3, 0, 3 + s % 3)),
            pl.BlockSpec((2, model, WIDE), lambda s: (0, 0, 6)),
            pl.BlockSpec((1, 8, WIDE), lambda s: (s // 3, 0, s % 3)),
            const((8, LANES)),
            const((CONV + 1, WIDE)),
            VMEM_SPEC,
        ],
        out_specs=[out[1] for out in outs],
        scratch_shapes=[
            pltpu.VMEM((ext, model), LOW),
            pltpu.VMEM((rows, LANES), LOW),
            pltpu.VMEM((8, LANES), LOW),
            pltpu.VMEM((GROUPS, NSTATE, WIDE), F32),
            pltpu.VMEM((GROUPS, 8, WIDE), F32),
        ]
        + Chaining.scratch(rounds)
        + Gathering.scratch(depth),
        compiler_params=params(collective_id=1, has_side_effects=True),
        name="front",
    )(
        tokens, halo, halo_docs, doc_col, doc_row, weights, weights, weights, par, par_heads,
        state_filter, packed_exit,
    )


def middle_body(
    tokens, cot, cot_t, hidden_t, pre_ref, gate_ref, loc_ref, carry_ref, w_exit, par, par_heads, bc,
    bct, score, mask, sp, cumt, fac, block_out, exit_out, gate_part_out, dy_out, gpg_out, enter_out, row_out,
    skip_out, outputs, gates, unit_grads, mixes, sums, total
):
    step = pl.program_id(0)
    rows = pre_ref.shape[0]
    spans = rows // Q
    wide = 6 * WIDE

    @pl.when(step == 0)
    def _():
        sums[...] = jnp.zeros_like(sums)
        total[...] = jnp.zeros_like(total)
        skip_out[...] = jnp.zeros_like(skip_out)

    @pl.when(step < 6)
    def _():
        group = step
        spread = spreader(4 * group, HEAD, 4)
        pre = pre_ref[...]
        mix = pre * sigmoid(pre)
        mixes[group] = mix
        value = mix * mm(sp[0], spread)
        growth = mm(sp[2], spread)
        facx = mm(split3(fac[...]), spread)
        cums = mm(sp[1], spreader(4 * group, LANES, 4))
        skipx = mm(split3(par_heads[...]), spread)[2:3]
        state = carry_ref[...].astype(F32)
        half = iota((Q, LANES), 1) < HEAD
        for index in range(spans):
            at = slice(index * Q, (index + 1) * Q)
            carried = mm(bc[at, LANES:], state.astype(LOW)) * growth[at]
            parts = []
            for pair in range(2):
                lanes = slice(pair * LANES, (pair + 1) * LANES)
                local = None
                for side in range(2):
                    head = 2 * pair + side
                    across = cumt[group, head : head + 1, at]
                    spread_at = cums[at, head * LANES : (head + 1) * LANES] - across + mask[at]
                    weight = (jnp.exp2(spread_at) * score[at]).astype(LOW)
                    keep = half if side == 0 else jnp.logical_not(half)
                    seen = jnp.where(keep, value[at, lanes], 0.0).astype(LOW)
                    part = mm(weight, seen)
                    local = part if local is None else local + part
                parts.append(local)
            out = jnp.concatenate(parts, axis=1) + carried + skipx * mix[at]
            outputs[group, at] = out
            state = facx[index : index + 1] * state + loc_ref[at]
        gate = gate_ref[...]
        gates[group] = gate
        gated = outputs[group] * (gate * sigmoid(gate))
        unit_grad = mm(cot[0], w_exit[0])
        unit_grads[group] = unit_grad
        square = gated * gated
        cross = unit_grad * par[0, 5:6] * gated
        sums[0] += square[:, :LANES] + square[:, LANES:]
        sums[1] += cross[:, :LANES] + cross[:, LANES:]

    @pl.when(step == 5)
    def _():
        square = jnp.sum(sums[0], axis=1, keepdims=True)
        cross = jnp.sum(sums[1], axis=1, keepdims=True)
        normal = lax.rsqrt(square / wide + EPSILON)
        sums[0] = jnp.broadcast_to(normal, (rows, LANES))
        sums[1] = jnp.broadcast_to(normal * normal * normal * cross / wide, (rows, LANES))

    @pl.when(step >= 6)
    def _():
        group = step - 6
        spread = spreader(4 * group, HEAD, 4)
        normal = twice(sums[0])
        pull = twice(sums[1])
        gain = par[0, 5:6]
        gate = gates[group]
        out = outputs[group]
        unit_grad = unit_grads[group]
        sigma = sigmoid(gate)
        act = gate * sigma
        gated = out * act
        scaled_in = gated * normal
        unit = (scaled_in * gain).astype(LOW)
        total[...] += mm_nt(unit, w_exit[0])
        exit_out[0] = mm(cot_t[...], unit).astype(LOW)
        gate_sum = jnp.sum(unit_grad * scaled_in, axis=0, keepdims=True)
        gated_grad = normal * (unit_grad * gain) - pull * gated
        dy = gated_grad * act
        dy_out[...] = dy
        gate_grad = (gated_grad * out * sigma * (1.0 + gate * (1.0 - sigma))).astype(LOW)
        gpg_out[...] = gate_grad
        gate_part_out[0] = mm(hidden_t[...], gate_grad).astype(LOW)
        skip_sum = jnp.sum(dy * mixes[group], axis=0, keepdims=True)
        row_out[...] = jnp.broadcast_to(gate_sum, (8, WIDE))
        skip_out[...] += head_sums(
            jnp.broadcast_to(skip_sum, (8, WIDE)), gatherer(4 * group, HEAD, 4)
        )
        facx = mm(split3(fac[...]), spread)
        pushed = (dy * mm(sp[2], spread)).astype(LOW)
        enter = jnp.zeros((NSTATE, WIDE), F32)
        for index in reversed(range(spans)):
            at = slice(index * Q, (index + 1) * Q)
            enter = facx[index : index + 1] * enter + mm(bct[NSTATE:, at], pushed[at])
        enter_out[...] = enter

    @pl.when(step == 11)
    def _():
        block_out[...] = (tokens[0].astype(F32) + total[...]).astype(LOW)


def middle(
    tokens, cot, cot_t, hidden_t, pre, gate, loc, carry, weights, par, par_heads, bc, bct, score, mask,
    sp, cumt, fac
):
    rows, model = tokens.shape[1:]
    wide = 6 * WIDE
    shape = jax.ShapeDtypeStruct

    def early(s):
        return jnp.minimum(s, 5)

    def late(s):
        return jnp.maximum(s - 6, 0)

    def group(s):
        return s % 6

    outs = (
        (shape((rows, model), LOW), const((rows, model))),
        (
            shape((2, model, 3 * WIDE), LOW),
            pl.BlockSpec((1, model, WIDE), lambda s: (late(s) // 3, 0, late(s) % 3)),
        ),
        (
            shape((2, model, 3 * WIDE), LOW),
            pl.BlockSpec((1, model, WIDE), lambda s: (late(s) // 3, 0, late(s) % 3)),
        ),
        (shape((rows, wide), F32), pl.BlockSpec((rows, WIDE), lambda s: (0, late(s)))),
        (shape((rows, wide), LOW), pl.BlockSpec((rows, WIDE), lambda s: (0, late(s)))),
        (shape((NSTATE, wide), F32), pl.BlockSpec((NSTATE, WIDE), lambda s: (0, late(s)))),
        (shape((8, wide), F32), pl.BlockSpec((8, WIDE), lambda s: (0, late(s)))),
        (shape((8, LANES), F32), const((8, LANES))),
    )
    return pl.pallas_call(
        middle_body,
        out_shape=[out[0] for out in outs],
        grid=(12,),
        in_specs=[
                pl.BlockSpec((1, rows, model), lambda s: (side(), 0, 0)),
                pl.BlockSpec((1, rows, model), lambda s: (side(), 0, 0)),
                const((model, rows)),
                const((model, rows)),
                pl.BlockSpec((rows, WIDE), lambda s: (0, early(s))),
                pl.BlockSpec((rows, WIDE), lambda s: (0, early(s))),
                pl.BlockSpec((rows, WIDE), lambda s: (0, early(s))),
                pl.BlockSpec((NSTATE, WIDE), lambda s: (0, early(s))),
                pl.BlockSpec((1, model, WIDE), lambda s: (group(s) // 3, 0, group(s) % 3)),
                pl.BlockSpec((1, 8, WIDE), lambda s: (group(s) // 3, 0, group(s) % 3)),
                const((8, LANES)),
                const((rows, WIDE)),
                const((WIDE, rows)),
                const((rows, Q)),
                const((rows, Q)),
                const((4, rows, LANES)),
                const((6, 8, rows)),
                const((8, LANES)),
        ],
        out_specs=[out[1] for out in outs],
        scratch_shapes=[
                pltpu.VMEM((6, rows, WIDE), F32),
                pltpu.VMEM((6, rows, WIDE), F32),
                pltpu.VMEM((6, rows, WIDE), F32),
                pltpu.VMEM((6, rows, WIDE), F32),
                pltpu.VMEM((2, rows, LANES), F32),
                pltpu.VMEM((rows, model), F32),
        ],
        compiler_params=params(),
        name="middle",
    )(
        tokens, cot, cot_t, hidden_t, pre, gate, loc, carry, weights, par, par_heads, bc, bct, score,
        mask, sp, cumt, fac,
    )


def scan_back_body(
    depth, rounds, pre_ref, dy_ref, loc_ref, carry_ref, enter, cin_ref, par, par_heads,
    state_filter, cin_state, pre_state, bc, bct, score, mask, sp, cumt, fac, match, zst, dt_ref,
    exits, gate_part, block_own, tokens, cot, hidden_t, gpg, w_gate, w_inner, w_small, tap_out,
    tap_state_out, small_out, mine, block_out, inner_part, small_part, token_out, norm_out, d_bc,
    d_score, d_cum, heads, local_value, enters, gains, adjoints, edge_own, edge_in, grads, total, es,
    el, bs, bl, block_keep, *scratch
):
    group = pl.program_id(0)
    blocks = BLOCK_CUTS
    rows = pre_ref.shape[0]
    spans = rows // Q
    place = Place(depth)
    wide = exits.shape[-1]
    chaining = Chaining(place, rounds, True, enters, gains, scratch[:4], scratch[4:8])
    reducing = Reducing(
        place, 0, [(exits, slice(0, wide)), (gate_part, slice(wide, 2 * wide))], mine,
        scratch[8:16], scratch[16:],
    )
    position = place.position
    has_before, has_after = position > 0, position < 2 * depth - 1
    before, after = {"context": position - 1}, {"context": position + 1}
    share = rows // blocks

    def block_copy(index):
        at = pl.ds(pl.multiple_of(index * share, share), share)
        return remote(
            block_own.at[at], block_out.at[place.y, at], bs.at[index], bl.at[index], place.y_peer
        )

    block_local = pltpu.make_async_copy(block_own, block_out.at[place.y], block_keep.at[0])

    def edge_copy(index):
        return remote(edge_own.at[index], edge_in.at[index], es.at[index], el.at[index], before)

    def edge_wait(index):
        @pl.when(has_after)
        def _():
            edge_copy(index).wait_recv()

    def joined(index):
        grad = grads[...]
        return jnp.concatenate(
            [grad[: rows - EDGE], grad[rows - EDGE :] + edge_in[index]], axis=0
        ).astype(LOW)

    @pl.when(group == 0)
    def _():
        d_bc[...] = jnp.zeros_like(d_bc)
        d_score[...] = jnp.zeros_like(d_score)
        d_cum[...] = jnp.zeros_like(d_cum)
        heads[...] = jnp.zeros_like(heads)
        grads[...] = jnp.zeros_like(grads)
        total[...] = jnp.zeros_like(total)
        edge_in[GROUPS + 1] = jnp.zeros((EDGE, WIDE), F32)

        @pl.when(jnp.logical_not(has_after))
        def _():
            edge_in[...] = jnp.zeros_like(edge_in)

        place.greet(
            [place.mate, place.x_peer, place.y_peer],
            chaining.sometimes() + [(has_before, before), (has_after, after)],
            True,
        )
        facs = split3(fac[...])
        for cut in range(GROUPS):
            enters[cut] = enter[:, cut * WIDE : (cut + 1) * WIDE]
            chaining.open(cut)
        for cut in range(GROUPS):
            rows8 = mm(facs, spreader(4 * cut, HEAD, 4))
            gains[cut] = jnp.broadcast_to(rows8[spans : spans + 1], (8, WIDE))
        each(depth, reducing.start)
        block_local.start()
        each(3, lambda index: block_copy(index).start())
        for cut in range(GROUPS):
            chaining.pass_on(0, cut)

    @pl.when(group < GROUPS)
    def _():
        spread = spreader(4 * group, HEAD, 4)
        collect = gatherer(4 * group, HEAD, 4)
        pre = pre_ref[...]
        sigma = sigmoid(pre)
        mix = pre * sigma
        dtx = mm(sp[0], spread)
        growth = mm(sp[2], spread)
        facx = mm(split3(fac[...]), spread)
        cums = mm(sp[1], spreader(4 * group, LANES, 4))
        half = iota((Q, LANES), 1) < HEAD
        ones = jnp.ones((8, Q), F32).astype(LOW)
        states = [carry_ref[...].astype(F32)]
        for index in range(spans - 1):
            at = slice(index * Q, (index + 1) * Q)
            states.append(facx[index : index + 1] * states[-1] + loc_ref[at])
        for index in range(spans):
            at = slice(index * Q, (index + 1) * Q)
            dy = dy_ref[at]
            value = mix[at] * dtx[at]
            parts = []
            sum_score = None
            for pair in range(2):
                lanes = slice(pair * LANES, (pair + 1) * LANES)
                value_low = value[:, lanes].astype(LOW)
                local = None
                for part_of in range(2):
                    head = 2 * pair + part_of
                    across = cumt[group, head : head + 1, at]
                    spread_at = cums[at, head * LANES : (head + 1) * LANES] - across + mask[at]
                    decay = jnp.exp2(spread_at)
                    keep = half if part_of == 0 else jnp.logical_not(half)
                    dy_low = jnp.where(keep, dy[:, lanes], 0.0).astype(LOW)
                    inner = decay * mm_nt(dy_low, value_low)
                    sum_score = inner if sum_score is None else sum_score + inner
                    moved = (inner * score[at]).astype(LOW)
                    turn = mm_nt(ones, moved) - mm(ones, moved)
                    d_cum[group, head : head + 1, at] = turn[0:1]
                    part = mm_tn((decay * score[at]).astype(LOW), dy_low)
                    local = part if local is None else local + part
                parts.append(local)
            d_score[at] += sum_score
            local_value[at] = jnp.concatenate(parts, axis=1)
            pushed = dy * growth[at]
            state_low = states[index].astype(LOW)
            carried = mm(bc[at, LANES:], state_low)
            d_bc[at, LANES:] += mm_nt(pushed.astype(LOW), state_low)
            heads[1, at] += head_sums(pushed * carried, collect)

    @pl.when(group == 0)
    def _():
        for cut in range(GROUPS):
            chaining.relay(0, cut)
        chaining.later()

        def put(cut, value):
            adjoints[cut] = value

        chaining.arrive(put)
        chaining.finish()

    for turn in range(5):

        @pl.when(group == turn)
        def _():
            each(turn + 1 if turn < 4 else depth + 1, reducing.turn, turn)
            block_copy(turn + 3).start()

    @pl.when(group == 5)
    def _():
        reducing.close()

    @pl.when((group > 0) & (group < GROUPS))
    def _():
        edge_wait(group - 1)

    @pl.when(group < GROUPS)
    def _():
        spread = spreader(4 * group, HEAD, 4)
        collect = gatherer(4 * group, HEAD, 4)
        pre = pre_ref[...]
        sigma = sigmoid(pre)
        mix = pre * sigma
        dtx = mm(sp[0], spread)
        growth = mm(sp[2], spread)
        facx = mm(split3(fac[...]), spread)
        states = [carry_ref[...].astype(F32)]
        for index in range(spans - 1):
            at = slice(index * Q, (index + 1) * Q)
            states.append(facx[index : index + 1] * states[-1] + loc_ref[at])
        arrived = jnp.where(group > 0, group - 1, GROUPS + 1)
        grad = joined(arrived)
        gate_grad = gpg[...]
        inner_part[0] = mm(hidden_t[...], grad).astype(LOW)
        total[...] += mm_nt(gate_grad, w_gate[0]) + mm_nt(grad, w_inner[0])
        tails = mm(sp[3], spread)
        skipx = mm(split3(par_heads[...]), spread)[2:3]
        adjoint = adjoints[group].astype(F32)
        masks = [match[back] for back in range(CONV - 1)]
        pgs = [None] * spans
        for index in reversed(range(spans)):
            at = slice(index * Q, (index + 1) * Q)
            dy = dy_ref[at]
            value = mix[at] * dtx[at]
            adj_low = adjoint.astype(LOW)
            reached = mm(bc[at, :LANES], adj_low) * tails[at]
            d_bc[at, :LANES] += mm_nt((value * tails[at]).astype(LOW), adj_low)
            heads[0, at] += head_sums(value * reached, collect)
            fac_part = jnp.sum(adjoint * states[index], axis=0, keepdims=True)
            heads[3, index * 8 : index * 8 + 8] += head_sums(
                jnp.broadcast_to(fac_part, (8, WIDE)), collect
            )
            pushed_low = (dy * growth[at]).astype(LOW)
            adjoint = facx[index : index + 1] * adjoint + mm(bct[NSTATE:, at], pushed_low)
            d_value = local_value[at] + reached
            heads[2, at] += head_sums(mix[at] * d_value, collect)
            d_mix = dtx[at] * d_value + skipx * dy
            s = sigma[at]
            pgs[index] = d_mix * s * (1.0 + pre[at] * (1.0 - s))
        pg = jnp.concatenate(pgs, axis=0)
        sums, grad = conv_backward(pg, cin_ref[...].astype(F32), par[0], masks)
        tap_out[...] = jnp.concatenate(sums + [jnp.zeros((3, WIDE), F32)], axis=0)
        grads[...] = grad[HALO:]
        edge_own[group] = grad[HALO - EDGE : HALO]

        @pl.when(has_before)
        def _():
            edge_copy(group).start()

    @pl.when(group == GROUPS)
    def _():
        masks = [match[back] for back in range(CONV - 1)]
        edge_wait(GROUPS - 1)
        grad = joined(GROUPS - 1)
        inner_part[0] = mm(hidden_t[...], grad).astype(LOW)
        total[...] += mm_nt(grad, w_inner[0])
        t_at, u_at = iota((Q, Q), 0), iota((Q, Q), 1)
        onward = (t_at <= u_at).astype(F32)
        earlier = (t_at > u_at).astype(F32)
        rate = jnp.exp(par_heads[1:2])
        raws = []
        bias_sum = jnp.zeros((1, LANES), F32)
        decay_sum = jnp.zeros((1, LANES), F32)
        used = iota((Q, LANES), 1) < 24
        for index in range(spans):
            at = slice(index * Q, (index + 1) * Q)
            pieces = [d_cum[piece, 0:4, at] for piece in range(6)]
            pieces.append(jnp.zeros((LANES - 24, Q), F32))
            cum_col = jnp.transpose(jnp.concatenate(pieces, axis=0))
            fac_row = fac[index : index + 1] * heads[3, index * 8 : index * 8 + 1]
            d_decay = (
                mm_exact(onward, cum_col + heads[1, at]) + mm_exact(earlier, heads[0, at]) + fac_row
            )
            dt = dt_ref[at]
            raw = (heads[2, at] - d_decay * rate) * sigmoid(zst[at])
            raw = jnp.where(used, raw, 0.0)
            raws.append(raw.astype(LOW))
            bias_sum += jnp.sum(raw, axis=0, keepdims=True)
            decay_sum -= jnp.sum(
                jnp.where(used, d_decay * dt * rate, 0.0), axis=0, keepdims=True
            )
            score_low = d_score[at].astype(LOW)
            d_bc[at, :LANES] += mm_tn(score_low, bc[at, LANES:])
            d_bc[at, LANES:] += mm(score_low, bc[at, :LANES])
        small_out[...] = jnp.concatenate(
            [bias_sum, decay_sum, jnp.zeros((6, LANES), F32)], axis=0
        )
        pre = pre_state[...]
        s = sigmoid(pre)
        pg = d_bc[...] * s * (1.0 + pre * (1.0 - s))
        sums, grad = conv_backward(pg, cin_state[...].astype(F32), state_filter[...], masks)
        tap_state_out[...] = jnp.concatenate(sums + [jnp.zeros((3, WIDE), F32)], axis=0)
        grads[...] = grad[HALO:]
        edge_own[GROUPS] = grad[HALO - EDGE : HALO]

        @pl.when(has_before)
        def _():
            edge_copy(GROUPS).start()

        steps = jnp.concatenate(raws, axis=0)
        turned = hidden_t[...]
        step_part = mm(turned, steps).astype(LOW)
        small_part[0, :, LANES:] = step_part
        small_part[1, :, LANES:] = step_part
        total[...] += mm_nt(steps, w_small[0, :, LANES:]) + mm_nt(steps, w_small[1, :, LANES:])
        edge_wait(GROUPS)
        state = joined(GROUPS)
        state_part = mm(turned, state).astype(LOW)
        small_part[0, :, :LANES] = state_part[:, :LANES]
        small_part[1, :, :LANES] = state_part[:, LANES:]
        value = tokens[0].astype(F32)
        scale = lax.rsqrt(jnp.mean(value * value, axis=1, keepdims=True) + EPSILON)
        hidden_grad = (
            total[...]
            + mm_nt(state[:, :LANES], w_small[0, :, :LANES])
            + mm_nt(state[:, LANES:], w_small[1, :, :LANES])
        )
        norm_sum = jnp.sum(hidden_grad * (value * scale), axis=0, keepdims=True)
        norm_out[...] = jnp.broadcast_to(norm_sum, norm_out.shape)
        gain = jnp.transpose(w_small[0, :, LANES : 2 * LANES].astype(F32))[24:25]
        normed = hidden_grad * gain
        pull = jnp.sum(normed * value, axis=1, keepdims=True) / value.shape[1]
        token_out[...] = (
            cot[0].astype(F32) + scale * normed - (scale * scale * scale) * value * pull
        ).astype(LOW)
        reducing.finish()
        each(blocks, lambda index: block_copy(index).wait())
        block_local.wait()

        @pl.when(has_before)
        def _():
            each(GROUPS + 1, lambda index: edge_copy(index).wait_send())


def scan_back(
    pre, dy, loc, carry, enter, cin, par, par_heads, state_filter, cin_state, pre_state, bc, bct,
    score, mask, sp, cumt, fac, match, zst, dt, exits, gate_part, block_own, tokens, cot, hidden_t,
    gpg, weights, rounds
):
    rows, wide = pre.shape
    ext = rows + HALO
    depth = lax.axis_size("context") // 2
    own_rows, half_wide = exits.shape[3:]
    shape = jax.ShapeDtypeStruct
    sem = lambda *lead: pltpu.SemaphoreType.DMA(lead)
    model = tokens.shape[2]
    now = lambda s: jnp.minimum(s, GROUPS - 1)
    lag = lambda s: jnp.maximum(s - 1, 0)
    column = lambda count: pl.BlockSpec((count, WIDE), lambda s: (0, now(s)))
    outs = (
        (shape((8, wide), F32), column(8)),
        (shape((8, WIDE), F32), const((8, WIDE))),
        (shape((8, LANES), F32), const((8, LANES))),
        (shape((own_rows, 2 * half_wide), F32), const((own_rows, 2 * half_wide))),
        (shape((2,) + block_own.shape, LOW), ANY_SPEC),
        (
            shape((2, model, 3 * WIDE), LOW),
            pl.BlockSpec((1, model, WIDE), lambda s: (lag(s) // 3, 0, lag(s) % 3)),
        ),
        (shape((2, model, WIDE), LOW), const((2, model, WIDE))),
        (shape((rows, model), LOW), const((rows, model))),
        (shape((8, model), F32), const((8, model))),
    )
    return pl.pallas_call(
        functools.partial(scan_back_body, depth, rounds),
        out_shape=[out[0] for out in outs],
        grid=(GROUPS + 1,),
        in_specs=[
            column(rows),
            column(rows),
            column(rows),
            column(NSTATE),
            const((NSTATE, wide)),
            column(ext),
            pl.BlockSpec((1, 8, WIDE), lambda s: (now(s) // 3, 0, now(s) % 3)),
            const((8, LANES)),
            const((CONV + 1, WIDE)),
            const((ext, WIDE)),
            const((rows, WIDE)),
            const((rows, WIDE)),
            const((WIDE, rows)),
            const((rows, Q)),
            const((rows, Q)),
            const((4, rows, LANES)),
            const((6, 8, rows)),
            const((8, LANES)),
            const((CONV - 1, rows, LANES)),
            const((rows, LANES)),
            const((rows, LANES)),
            ANY_SPEC,
            ANY_SPEC,
            VMEM_SPEC,
            pl.BlockSpec((1, rows, model), lambda s: (side(), 0, 0)),
            pl.BlockSpec((1, rows, model), lambda s: (side(), 0, 0)),
            const((model, rows)),
            column(rows),
            pl.BlockSpec((1, model, WIDE), lambda s: (now(s) // 3, 0, now(s) % 3)),
            pl.BlockSpec((1, model, WIDE), lambda s: (lag(s) // 3, 0, 3 + lag(s) % 3)),
            pl.BlockSpec((2, model, WIDE), lambda s: (0, 0, 6)),
        ],
        out_specs=[out[1] for out in outs],
        scratch_shapes=[
            pltpu.VMEM((rows, WIDE), F32),
            pltpu.VMEM((rows, Q), F32),
            pltpu.VMEM((6, 8, rows), F32),
            pltpu.VMEM((4, rows, LANES), F32),
            pltpu.VMEM((rows, WIDE), F32),
            pltpu.VMEM((GROUPS, NSTATE, WIDE), F32),
            pltpu.VMEM((GROUPS, 8, WIDE), F32),
            pltpu.VMEM((GROUPS, NSTATE, WIDE), LOW),
            pltpu.VMEM((GROUPS + 1, EDGE, WIDE), F32),
            pltpu.VMEM((GROUPS + 2, EDGE, WIDE), F32),
            pltpu.VMEM((rows, WIDE), F32),
            pltpu.VMEM((rows, model), F32),
            sem(GROUPS + 1),
            sem(GROUPS + 1),
            sem(BLOCK_CUTS),
            sem(BLOCK_CUTS),
            sem(1),
        ]
        + Chaining.scratch(rounds)
        + Reducing.scratch(depth, own_rows, 2 * half_wide),
        compiler_params=params(collective_id=2, has_side_effects=True),
        name="scan_back",
    )(
        pre, dy, loc, carry, enter, cin, par, par_heads, state_filter, cin_state, pre_state, bc,
        bct, score, mask, sp, cumt, fac, match, zst, dt, exits, gate_part, block_own, tokens, cot,
        hidden_t, gpg, weights, weights, weights,
    )


def pack_body(
    side_ref, entry, exits, state, steps, gain, inner_kernel, gate_gain, bias, decay, skip, docs,
    tail_tokens, packed, packed_exit, par, doc_col, doc_row, edge
):
    side = side_ref[0]
    rows = entry.shape[0]
    wide = entry.shape[2]

    def placed(value):
        filled = jnp.concatenate(
            [value, jnp.zeros((value.shape[0], LANES - value.shape[1]), F32)], axis=1
        )
        return jnp.where(side == 0, filled, pltpu.roll(filled, value.shape[1], 1))

    packed[:, :wide] = entry[:, 0].astype(LOW)
    packed[:, wide : 2 * wide] = entry[:, 1].astype(LOW)
    half = jnp.where(side == 0, state[:, :NSTATE], state[:, NSTATE:])
    packed[:, 2 * wide : 2 * wide + NSTATE] = half.astype(LOW)
    gain_row = jnp.concatenate([gain[...], jnp.zeros((1, LANES - rows), F32)], axis=1)
    gain_col = jnp.transpose(jnp.broadcast_to(gain_row, (LANES, LANES)))[:rows]
    lane = iota((rows, LANES), 1)
    small = jnp.where(lane == 24, gain_col, placed(steps[...]))
    packed[:, 2 * wide + NSTATE :] = small.astype(LOW)
    packed_exit[...] = exits[...].astype(LOW)
    par[0 : CONV + 1] = inner_kernel[...]
    par[CONV + 1 : CONV + 2] = gate_gain[...]
    par[CONV + 2 : CONV + 4] = jnp.zeros((2, wide), F32)
    for index, ref in enumerate((bias, decay, skip)):
        par[CONV + 2 : CONV + 3, index * LANES : (index + 1) * LANES] = placed(ref[...])
    own = jnp.where(side == 0, docs[0:1], docs[1:2]).astype(F32)
    doc_row[...] = jnp.broadcast_to(own, doc_row.shape)
    doc_col[...] = jnp.transpose(jnp.broadcast_to(own, (LANES, own.shape[1])))
    edge[...] = tail_tokens[0]


def pack(
    which, entry, exits, state, steps, gain, inner_kernel, gate_gain, bias, decay, skip, docs, tokens
):
    own_rows, _, wide = entry.shape
    rows, model = tokens.shape[1:]
    shape = jax.ShapeDtypeStruct
    arrays = (
        entry, exits, state, steps, gain[None], inner_kernel, gate_gain[None], bias[None],
        decay[None], skip[None], docs,
    )
    outs = (
        shape((own_rows, 2 * wide + WIDE), LOW),
        shape((own_rows, wide), LOW),
        shape((8, wide), F32),
        shape((rows, LANES), F32),
        shape((8, rows), F32),
        shape((HALO, model), LOW),
    )
    return pl.pallas_call(
        pack_body,
        out_shape=outs,
        grid_spec=pltpu.PrefetchScalarGridSpec(
            num_scalar_prefetch=1,
            grid=(1,),
            in_specs=[const(array.shape) for array in arrays]
            + [pl.BlockSpec((1, HALO, model), lambda s, w: (w[0], rows // HALO - 1, 0))],
            out_specs=[const(out.shape) for out in outs],
        ),
        compiler_params=params(),
        name="pack",
    )(which, *arrays, tokens)


def gather_body(
    depth, packed, par_own, edge_own, docs_own, cot, weights, par, heads, edge, docs, cot_t, docs_in,
    cot_in, side_send, side_land, local, *scratch
):
    place = Place(depth)
    count = 2 * depth
    onward = {"context": lax.rem(place.position + 1, count)}
    behind = {"context": lax.rem(place.position + count - 1, count)}
    x, y, z, c = place.x, place.y, place.z, place.c
    place.greet(
        [place.mate, place.x_peer, place.y_peer, onward, behind],
        [(z + 1 < depth, place.up()), (z > 0, place.down())],
    )
    gathering = Gathering(place, packed, weights, *scratch)
    sides = [
        remote(edge_own, edge, side_send.at[0], side_land.at[0], onward),
        remote(docs_own, docs_in, side_send.at[1], side_land.at[1], onward),
        remote(par_own, par.at[y], side_send.at[2], side_land.at[2], place.y_peer),
    ]
    for copy in sides:
        copy.start()
    gathering.own()
    cot_copy = pltpu.make_async_copy(cot.at[y], cot_in, local.at[1])
    cot_copy.start()
    par_keep = pltpu.make_async_copy(par_own, par.at[y], local.at[0])
    par_keep.start()
    cot_copy.wait()
    cot_t[...] = jnp.transpose(cot_in[...])
    gathering.near()
    gathering.across()
    for copy in sides:
        copy.wait()
    docs[...] = jnp.where(place.position == 0, -1.0, docs_in[...])
    par_keep.wait()
    both = par[0, CONV + 2 : CONV + 3] + par[1, CONV + 2 : CONV + 3]
    heads[...] = jnp.zeros_like(heads)
    for index in range(3):
        heads[index : index + 1] = both[:, index * LANES : (index + 1) * LANES]
    gathering.far()
    gathering.finish()


def gather(packed, par_own, edge_own, docs_own, cot):
    count = lax.axis_size("context")
    depth = count // 2
    rows, model = cot.shape[1:]
    shape = jax.ShapeDtypeStruct
    return pl.pallas_call(
        functools.partial(gather_body, depth),
        out_shape=(
            shape((2, 2, count) + packed.shape, LOW),
            shape((2,) + par_own.shape, F32),
            shape((8, LANES), F32),
            shape(edge_own.shape, LOW),
            shape(docs_own.shape, F32),
            shape((model, rows), LOW),
        ),
        in_specs=[VMEM_SPEC] * 4 + [ANY_SPEC],
        out_specs=[ANY_SPEC] + [VMEM_SPEC] * 5,
        scratch_shapes=[
            pltpu.VMEM(docs_own.shape, F32),
            pltpu.VMEM((rows, model), LOW),
            pltpu.SemaphoreType.DMA((3,)),
            pltpu.SemaphoreType.DMA((3,)),
            pltpu.SemaphoreType.DMA((2,)),
        ]
        + Gathering.scratch(depth),
        compiler_params=params(collective_id=0, has_side_effects=True),
        name="gather",
    )(packed, par_own, edge_own, docs_own, cot)


def reduce_body(
    depth, inner, small, token, taps, taps_state, gate_row, head_rows, skip_row, norm_row,
    total, state_out, vector_out, token_out, state_own, vec_send, vec_land, vs, vl, ts, tl, ss, sl,
    keep_sem, *scratch
):
    place = Place(depth)
    x, y, z, c = place.x, place.y, place.z, place.c
    wide = inner.shape[-1]
    parts = [(inner, slice(0, wide)), (small, slice(wide, wide + WIDE))]
    reducing = Reducing(place, 0, parts, total, scratch[:8], scratch[8:])

    vec_send[0] = jnp.zeros(vec_send.shape[1:], F32)
    vec_send[0, : CONV + 1, : 2 * wide] = taps[: CONV + 1]
    vec_send[0, : CONV + 1, 2 * wide :] = taps_state[: CONV + 1]
    vec_send[0, 5:6, : 2 * wide] = gate_row[0:1]
    vec_send[0, 5:6, 2 * wide : 2 * wide + LANES] = head_rows[0:1]
    vec_send[0, 5:6, 2 * wide + LANES :] = skip_row[0:1]
    model = norm_row.shape[1]
    vec_send[0, 6:7, :model] = norm_row[0:1]
    vec_send[0, 6:7, model : model + LANES] = head_rows[1:2]

    place.greet([place.mate, place.x_peer, place.y_peer], (), True)
    vec_targets = [place.mate, place.x_peer, place.y_peer]

    def vec_copy(turn):
        return remote(
            vec_send.at[turn], vec_land.at[turn], vs.at[turn], vl.at[turn], vec_targets[turn]
        )

    def vec_far(away, lands_at):
        return remote(
            vec_send.at[3], vec_land.at[3 + lands_at], vs.at[3 + away], vl.at[3 + lands_at],
            place.away(away),
        )

    share = token.shape[0] // depth

    def token_copy(step):
        at = pl.ds(pl.multiple_of(step * share, share), share)
        return remote(token.at[at], token_out.at[y, at], ts.at[step], tl.at[step], place.y_peer)

    token_keep = pltpu.make_async_copy(token, token_out.at[y], keep_sem.at[0])

    vec_copy(0).start()
    each(depth, reducing.start)
    token_keep.start()

    def step_all(step):
        reducing.turn(step)

        @pl.when(step >= 1)
        def _():
            token_copy(step - 1).start()

        for turn in range(3):

            @pl.when(step == turn)
            def _():
                vec_copy(turn).wait_recv()
                vec_send[turn + 1] = vec_send[turn] + vec_land[turn]
                if turn < 2:
                    vec_copy(turn + 1).start()
                else:
                    each(depth, lambda s: vec_far(lax.rem(z + s, depth), z).start(), 1)
                    vec_land[3 + z] = vec_send[3]

    each(depth + 1, step_all)
    reducing.close()
    state_own[...] = total[:, wide : wide + NSTATE]
    state_copy = remote(state_own, state_out.at[y], ss.at[0], sl.at[0], place.y_peer)
    state_copy.start()
    state_out[y] = state_own[...]

    def vec_arrive(step):
        away = lax.rem(z + step, depth)
        vec_far(away, away).wait_recv()

    each(depth, vec_arrive, 1)
    vector_out[...] = vec_land[3]

    def vec_add(step):
        vector_out[...] += vec_land[3 + step]

    each(depth, vec_add, 1)
    for turn in range(3):
        vec_copy(turn).wait_send()
    each(depth, lambda s: vec_far(lax.rem(z + s, depth), z).wait_send(), 1)
    reducing.finish()
    each(depth, lambda step: token_copy(step).wait())
    state_copy.wait()
    token_keep.wait()


def reduce_all(inner, small, token, taps, taps_state, gate_row, head_rows, skip_row, norm_row):
    count = lax.axis_size("context")
    depth = count // 2
    own_rows, wide = inner.shape[3:]
    tall = wide + WIDE
    shape = jax.ShapeDtypeStruct
    sem = lambda *lead: pltpu.SemaphoreType.DMA(lead)
    vector = (8, 2 * wide + WIDE)
    return pl.pallas_call(
        functools.partial(reduce_body, depth),
        out_shape=(
            shape((own_rows, tall), F32),
            shape((2, own_rows, NSTATE), F32),
            shape(vector, F32),
            shape((2,) + token.shape, LOW),
        ),
        in_specs=[ANY_SPEC] * 2 + [VMEM_SPEC] * 7,
        out_specs=[VMEM_SPEC] * 3 + [ANY_SPEC],
        scratch_shapes=[
            pltpu.VMEM((own_rows, NSTATE), F32),
            pltpu.VMEM((4,) + vector, F32),
            pltpu.VMEM((3 + depth,) + vector, F32),
            sem(3 + depth),
            sem(3 + depth),
            sem(depth),
            sem(depth),
            sem(1),
            sem(1),
            sem(1),
        ]
        + Reducing.scratch(depth, own_rows, tall),
        compiler_params=params(collective_id=4, has_side_effects=True),
        name="reduce_all",
    )(inner, small, token, taps, taps_state, gate_row, head_rows, skip_row, norm_row)


def finish_body(
    side_ref, mine, exits, state, vector, token, block, block_out, token_out,
    norm_out, entry_out, state_out, step_out, kernel_out, filter_out, bias_out, decay_out, skip_out,
    gate_out, exit_out
):
    side, spot = side_ref[0], side_ref[1]
    token_out[...] = token[...].astype(F32)
    first = side == 0
    block_out[...] = block[...]

    @pl.when(pl.program_id(0) == 0)
    def _():
        own_rows, _, wide = entry_out.shape
        model = token.shape[2]
        entry_out[:, 0] = exits[:, wide:]
        entry_out[:, 1] = mine[:, :wide]
        exit_out[...] = exits[:, :wide]
        state_out[:, :NSTATE] = state[0]
        state_out[:, NSTATE:] = state[1]

        def twelve(value):
            return jnp.where(first, value, pltpu.roll(value, LANES - 12, 1))[:, :12]

        step_out[...] = twelve(mine[:, wide + NSTATE :])
        left, right = vector[:, :wide], vector[:, wide : 2 * wide]
        halves = jnp.where(first, left, right)
        kernel_out[...] = halves[: CONV + 1]
        gate_out[...] = halves[5:6]
        filter_out[...] = vector[: CONV + 1, 2 * wide :]
        bias_out[...] = twelve(vector[5:6, 2 * wide : 2 * wide + LANES])
        skip_out[...] = twelve(vector[5:6, 2 * wide + LANES :])
        decay_out[...] = twelve(vector[6:7, model : model + LANES])
        turned = pltpu.roll(vector[:, :model], lax.rem(model - spot * own_rows, model), 1)
        norm_out[...] = turned[6:7, :own_rows]


def finish(side, mine, exits, state, vector, token, block):
    own_rows, wide = exits.shape[0], exits.shape[1] // 2
    _, rows, model = token.shape
    share = rows // 4
    shape = jax.ShapeDtypeStruct
    outs = (
        (shape((2, rows, model), LOW), pl.BlockSpec((2, share, model), lambda s, w: (0, s, 0))),
        (shape((2, rows, model), F32), pl.BlockSpec((2, share, model), lambda s, w: (0, s, 0))),
        (shape((1, own_rows), F32), None),
        (shape((own_rows, 2, wide), F32), None),
        (shape((own_rows, WIDE), F32), None),
        (shape((own_rows, 12), F32), None),
        (shape((CONV + 1, wide), F32), None),
        (shape((CONV + 1, WIDE), F32), None),
        (shape((1, 12), F32), None),
        (shape((1, 12), F32), None),
        (shape((1, 12), F32), None),
        (shape((1, wide), F32), None),
        (shape((own_rows, wide), F32), None),
    )
    return pl.pallas_call(
        finish_body,
        out_shape=[out[0] for out in outs],
        grid_spec=pltpu.PrefetchScalarGridSpec(
            num_scalar_prefetch=1,
            grid=(4,),
            in_specs=[
                const(mine.shape),
                const(exits.shape),
                const(state.shape),
                const(vector.shape),
                pl.BlockSpec((2, share, model), lambda s, w: (0, s, 0)),
                pl.BlockSpec((2, share, model), lambda s, w: (0, s, 0)),
            ],
            out_specs=[out[1] if out[1] is not None else const(out[0].shape) for out in outs],
        ),
        compiler_params=params(),
        name="finish",
    )(side, mine, exits, state, vector, token, block)


def body(
    tokens, documents, norm_gain, entry_weight, state_weight, step_weight, inner_kernel,
    state_filter, step_bias, decay_log, skip_gain, gate_gain, exit_weight, cotangent,
):
    seqs, rows, model = tokens.shape
    count = lax.axis_size("context")
    position, side = lax.axis_index("context"), lax.axis_index("tensor")
    own_rows = norm_gain.shape[0]
    which = jnp.stack([side, lax.axis_index("dp") * count + position]).astype(jnp.int32)
    longest = rows * count // 4
    rounds = min(count // 2 - 1, -(-(longest - 1) // (2 * rows)))

    packed, packed_exit, par_own, doc_col, doc_row, edge_own = pack(
        which, entry_weight, exit_weight, state_weight, step_weight, norm_gain, inner_kernel,
        gate_gain, step_bias, decay_log, skip_gain, documents, tokens,
    )
    weights, par, par_heads, halo, halo_docs, cot_t = gather(
        packed, par_own, edge_own, doc_col[-HALO:], cotangent
    )
    weights = weights.reshape(2, model, -1)
    (
        hidden_t, cin, gate, pre, loc, carry, exit_weights, cin_state, pre_state, bc, bct, score,
        mask, zst, dt, sp, cumt, fac, match,
    ) = front(
        tokens, halo, halo_docs, doc_col, doc_row, weights, par, par_heads, state_filter,
        packed_exit, rounds,
    )
    exit_weights = exit_weights.reshape(2, model, -1)
    block_own, exit_part, gate_part, dy, gpg, enter, gate_row, skip_row = middle(
        tokens, cotangent, cot_t, hidden_t, pre, gate, loc, carry, exit_weights, par, par_heads, bc,
        bct, score, mask, sp, cumt, fac,
    )
    cut = lambda v: v.reshape(2, 2, count, own_rows, v.shape[-1])
    (
        taps, taps_state, head_rows, exit_mine, block_both, inner_part, small_part, token_own,
        norm_row,
    ) = scan_back(
        pre, dy, loc, carry, enter, cin, par, par_heads, state_filter, cin_state, pre_state, bc, bct,
        score, mask, sp, cumt, fac, match, zst, dt, cut(exit_part), cut(gate_part), block_own,
        tokens, cotangent, hidden_t, gpg, weights, rounds,
    )
    mine, state_both, vector, token_both = reduce_all(
        cut(inner_part), cut(small_part), token_own, taps, taps_state, gate_row, head_rows, skip_row,
        norm_row,
    )
    outs = finish(which, mine, exit_mine, state_both, vector, token_both, block_both)
    flat = (2, 8, 9, 10, 11)
    return tuple(out[0] if index in flat else out for index, out in enumerate(outs))


def solution(mesh):
    in_specs = (
        P("dp", "context", None),
        P("dp", "context"),
        P(("dp", "context")),
        P(("dp", "context"), None, "tensor"),
        P(("dp", "context"), None),
        P(("dp", "context"), "tensor"),
        P(None, "tensor"),
        P(),
        P("tensor"),
        P("tensor"),
        P("tensor"),
        P("tensor"),
        P(("dp", "context"), "tensor"),
        P("dp", "context", None),
    )
    out_specs = (
        P("dp", "context", None),
        P("dp", "context", None),
        P(("dp", "context")),
        P(("dp", "context"), None, "tensor"),
        P(("dp", "context"), None),
        P(("dp", "context"), "tensor"),
        P(None, "tensor"),
        P(),
        P("tensor"),
        P("tensor"),
        P("tensor"),
        P("tensor"),
        P(("dp", "context"), "tensor"),
    )
    return jax.shard_map(body, mesh=mesh, in_specs=in_specs, out_specs=out_specs, check_vma=False)
```

time: 636 us -> 218 us (0.34)
  waiting for transfers between devices: 444 us -> 0 us
  Pallas kernels: 88.2 us -> 209 us
  other arithmetic: 27.8 us -> 1.95 us
  local copies, waits for them, and re-layouts: 30.8 us -> 5.36 us
  starting transfers between devices: 25 us -> 0 us
  between operations: 14 us -> 0.7 us
    reduce_scatter x1 -> x0, waiting for transfers between devices: 197 us -> none  [body(): lax.psum_scatter(parts.reshape(2 * model, -1).astype(F32), every, scatter...]
    pallas_call x4 -> x7, Pallas kernels: 88.2 us -> 209 us  [the longest x1 69.4 us: scan_back(): pl.pallas_call(functools.partial(scan_back_body, depth, rounds), out_shap...]
    psum x1 -> x0, waiting for transfers between devices: 107 us -> none  [body(): lax.psum((taps, taps_state, gate_row, skip_row, head_rows, norm_row), every)]
    all_gather x3 -> x0, waiting for transfers between devices: 102 us -> none  [the longest x1 59.7 us: body(): lax.all_gather(packed, every, axis=0, tiled=True).reshape(2, model, -1)]
    ppermute x8 -> x0, waiting for transfers between devices: 37.8 us -> none  [the longest x4 27.2 us: chained(): carry = lax.ppermute(fold + gain[0:1] * carry, 'context', pairs)]
    ppermute x8 -> x0, starting transfers between devices: 24.8 us -> none  [the longest x4 15.3 us: chained(): carry = lax.ppermute(fold + gain[0:1] * carry, 'context', pairs)]
    convert_element_type x2 -> x0, other arithmetic: 10.8 us -> none  [the longest x1 10.1 us: body(): parts.reshape(2 * model, -1).astype(F32)]
    slice x11 -> x1, local copies, waits for them, and re-layouts: 8.65 us -> 1.3 us  [body(): doc_col[-HALO:]]
  transfers between devices with their start and end apart: 13 -> 0, of which waited for: 9 -> 0; matrix products, arithmetic and copies ran while one was open for 5% -> 0% of each run, Pallas kernels for 8% -> 0%
where the time goes in v4:
time: 218 us; the launch traced here: 217 us
  Pallas kernels  209 us (96%)
  local copies, waits for them, and re-layouts  5.36 us (2%)
    pallas_call x1, Pallas kernels, scan_back(): pl.pallas_call(functools.partial(scan_back_body, depth, rounds), out_shap...  69.4 us
    pallas_call x1, Pallas kernels, reduce_all(): pl.pallas_call(functools.partial(reduce_body, depth), out_shape=(shape((o...  41.7 us
    pallas_call x1, Pallas kernels, gather(): pl.pallas_call(functools.partial(gather_body, depth), out_shape=(shape((2...  37.5 us
    pallas_call x1, Pallas kernels, front(): pl.pallas_call(functools.partial(front_body, depth, rounds), out_shape=[o...  29 us
    pallas_call x1, Pallas kernels, middle(): pl.pallas_call(middle_body, out_shape=[out[0] for out in outs], grid=(12,...  23 us
    pallas_call x1, Pallas kernels, finish(): pl.pallas_call(finish_body, out_shape=[out[0] for out in outs], grid_spec...  5.69 us

profile of v4, /device:TPU:0, one launch (start us, length us, event | category | flops | bytes accessed | tf_op | source)
XLA Modules:
  0.0 217.3 jit_solution(8040752071505860055)
XLA Ops:
  0.6 0.7 pad_add_fusion.side_ref
  1.3 1.3 broadcast_in_dim.16.gate_gain
  2.6 1.4 copy.27.steps
  4.0 3.1 %pack.1 = (bf16[48,1792]{1,0:T(8,128)(2,1)}, bf16[48,768]{1,0:T(8,128)(2,1)}, f32[8,768]{1,0:T(8,128)}, f32[512,128]{1,0:T(8,128)}, f32[8,512]{1,0:T(8,128)}, /*index=5*/bf16[16,768]{1,0:T(8,128)(2,1)}) custom-call(s32[2]{0:T(128)} %pad_add_fusion.side_ref, f32[48,2,768]{2,1,0:T(2,128)} %entry.1, f32[48,768]{1,0:T(8,128)} %exits.1, f32[48,256]{1,0:T(8,128)} %state.1, ...), custom_call_target="tpu_custom_call" | custom-call | tf_op jit(solution)/shard_map/pack/pallas_call | solution.py:1443
  7.0 1.3 slice.3.docs_own
  8.3 37.5 %gather.1 = (bf16[2,2,8,48,1792]{4,3,2,1,0:T(8,128)(2,1)}, f32[2,8,768]{2,1,0:T(8,128)}, f32[8,128]{1,0:T(8,128)}, bf16[16,768]{1,0:T(8,128)(2,1)}, f32[16,128]{1,0:T(8,128)}, /*index=5*/bf16[768,512]{1,0:T(8,128)(2,1)}) custom-call(bf16[48,1792]{1,0:T(8,128)(2,1)} %get-tuple-element.78.packed, f32[8,768]{1,0:T(8,128)} %get-tuple-element.79.par_own, ...), custom_call_target="tpu_custom_call" | custom-call | tf_op jit(solution)/shard_map/gather/pallas_call | solution.py:1505
  45.8 29.0 %front.1 = (bf16[768,512]{1,0:T(8,128)(2,1)}, bf16[528,1536]{1,0:T(8,128)(2,1)}, f32[512,1536]{1,0:T(8,128)}, f32[512,1536]{1,0:T(8,128)}, f32[512,1536]{1,0:T(8...) custom-call(bf16[2,512,768]{2,1,0:T(8,128)(2,1)} %tokens.5, ...), custom_call_target="tpu_custom_call" | custom-call | tf_op jit(solution)/shard_map/front/pallas_call | solution.py:780
  74.8 23.0 %middle.1 = (bf16[512,768]{1,0:T(8,128)(2,1)}, bf16[2,768,768]{2,1,0:T(8,128)(2,1)}, bf16[2,768,768]{2,1,0:T(8,128)(2,1)}, f32[512,1536]{1,0:T(8,128)}, bf16[512...) custom-call(bf16[2,512,768]{2,1,0:T(8,128)(2,1)} %tokens.5, ...), custom_call_target="tpu_custom_call" | custom-call | tf_op jit(solution)/shard_map/middle/pallas_call | solution.py:959
  97.7 69.4 %scan_back.1 = (f32[8,1536]{1,0:T(8,128)}, f32[8,256]{1,0:T(8,128)}, f32[8,128]{1,0:T(8,128)}, f32[48,1536]{1,0:T(8,128)}, bf16[2,512,768]{2,1,0:T(8,128)(2,1)},...) custom-call(f32[512,1536]{1,0:T(8,128)} %get-tuple-element.89.pre_ref, ...), custom_call_target="tpu_custom_call" | custom-call | tf_op jit(solution)/shard_map/scan_back/pallas_call | solution.py:1322
  167.1 41.7 %reduce_all.1 = (f32[48,1024]{1,0:T(8,128)}, f32[2,48,128]{2,1,0:T(8,128)}, f32[8,1792]{1,0:T(8,128)}, bf16[2,512,768]{2,1,0:T(8,128)(2,1)}) custom-call(bf16[2,2,8,48,768]{4,3,2,1,0:T(8,128)(2,1)} %bitcast.25, bf16[2,2,8,48,256]{4,3,2,1,0:T(8,128)(2,1)} %bitcast.26, bf16[512,768]{1,0:T(8,128)(2,1)} %get-tuple-element.117.token, ...), custom_call_target="tpu_custom_call" | custom-call | tf_op jit(solution)/shard_map/reduce_all/pallas_call | solution.py:1631
  208.9 5.7 %finish.1 = (bf16[2,512,768]{2,1,0:T(8,128)(2,1)}, f32[2,512,768]{2,1,0:T(8,128)}, f32[1,48]{1,0:T(1,128)}, f32[48,2,768]{2,1,0:T(2,128)}, f32[48,256]{1,0:T(8,1...) custom-call(s32[2]{0:T(128)} %pad_add_fusion.side_ref, ...), custom_call_target="tpu_custom_call" | custom-call | tf_op jit(solution)/shard_map/finish/pallas_call | solution.py:1715
  214.6 1.3 reduce
  215.9 1.4 copy.28

commit v5 on v4

--- a/solution.py
+++ b/solution.py
@@ -15,6 +15,7 @@
 EDGE = 8
 GROUPS = 6
 BLOCK_CUTS = 8
+ORDER = (0, 3, 1, 4, 2, 5)
 LANES = 128
 WIDE = 256
 LOG2E = 1.4426950408889634
@@ -216,6 +217,7 @@
     def __init__(self, place, own, full, sends, lands, local):
         self.place, self.own_ref, self.full = place, own, full
         self.sends, self.lands, self.local = sends, lands, local
+        self.starts = [first * place.depth for first in (0, 4, 5, 7, 8)]
         (self.x1, self.y1), (self.x2, self.y2) = place.axes(place.c)
         self.first = place.at(self.x1, self.y1, place.z, place.c)
         self.second = place.at(self.x2, self.y2, place.z, place.c)
@@ -223,14 +225,14 @@
     @staticmethod
     def scratch(depth):
         sem = pltpu.SemaphoreType.DMA
-        return [sem((5, 4 * depth)), sem((8 * depth,)), sem((1,))]
+        return [sem((9 * depth,)), sem((8 * depth,)), sem((1,))]
 
     def copy(self, kind, index, x, y, z, c, target, own=False):
         chunk = self.full.at[y, x, z * 2 + c]
         mark = ((y * 2 + x) * self.place.depth + z) * 2 + c
         return remote(
-            self.own_ref if own else chunk, chunk, self.sends.at[kind, index], self.lands.at[mark],
-            target,
+            self.own_ref if own else chunk, chunk, self.sends.at[self.starts[kind] + index],
+            self.lands.at[mark], target,
         )
 
     def arrive(self, x, y, z, c):
@@ -305,7 +307,7 @@
         p.around(near_row)
         p.around(far_row)
 
-    def finish(self):
+    def mates(self):
         p = self.place
 
         def from_mate(z):
@@ -314,6 +316,10 @@
                     self.arrive(x, y, z, 1 - p.c)
 
         each(p.depth, from_mate)
+        self.kept().wait()
+
+    def finish(self):
+        p = self.place
 
         def sent(kind, index, target):
             self.copy(kind, index, p.x, p.y, p.z, p.c, target).wait_send()
@@ -332,7 +338,6 @@
                 sent(4, z, p.mate)
 
         each(p.depth, chained)
-        self.kept().wait()
 
 
 class Reducing:
@@ -593,78 +598,83 @@
                     self.chip_copy(turn, cut).wait_send()
 
 
-def front_body(
-    depth, rounds, tokens, halo, halo_docs, doc_col, doc_row, w_gate, w_inner, w_small, par, par_heads,
-    state_filter, packed_exit, hidden_out, cin_out, gate_out, pre_out, loc_out, carry_out,
-    exit_weights, cin_state_out, pre_state_out, bc_out, bct_out, score_out, mask_out, zst_out, dt_out, sp_out,
-    cumt_out, fac_out, match_out, hidden, sp_tail, facs, folds, gains, *scratch
-):
+def turn_of(step):
+    index = jnp.maximum(step - 1, 0)
+    half, part = index % 2, index // 2
+    return half * 3 + part, half, part
+
+
+def entry_body(depth, rounds, fused, *refs):
     step = pl.program_id(0)
-    rows = tokens.shape[1]
+    tokens, doc_col, doc_row, state_filter = refs[:4]
+    if fused:
+        own_small, own_parts, own_exit, own_par, own_edge, own_docs, cot = refs[4:11]
+    else:
+        w_gate, w_inner, w_small, par, heads_ref, edge, halo_docs = refs[4:11]
+    (
+        hidden_out, cin_out, gate_out, pre_out, loc_out, carry_out, cin_state_out, pre_state_out,
+        bc_out, bct_out, score_out, mask_out, zst_out, dt_out, sp_out, cumt_out, fac_out, match_out,
+    ) = refs[11:29]
+    refs = refs[29:]
+    if fused:
+        small_out, parts_out, exit_out, par, heads_ref, cot_t = refs[:6]
+        refs = refs[6:]
+    hidden, normed, sp_tail, facs, folds, gains = refs[:6]
+    rows, model = tokens.shape[1:]
     spans = rows // Q
     place = Place(depth)
-    chaining = Chaining(place, rounds, False, folds, gains, scratch[:4], scratch[4:8])
-    gathering = Gathering(place, packed_exit, exit_weights, *scratch[8:])
-
-    @pl.when(step == 0)
-    def _():
-        place.greet(
-            [place.mate, place.x_peer, place.y_peer],
-            [(place.z + 1 < depth, place.up()), (place.z > 0, place.down())] + chaining.sometimes(),
-        )
-        gathering.own()
-
-    for away in range(1, 4):
-
-        @pl.when(step == away)
-        def _():
-            gathering.near(away, away + 1 if away < 3 else None)
-
-    @pl.when(step == 4)
-    def _():
-        gathering.across()
-
-    @pl.when(step == 5)
-    def _():
-        gathering.far()
-
-    for cut in range(GROUPS - 1):
-
-        @pl.when(step == cut + 1)
-        def _():
-            chaining.pass_on(0, cut)
-
-    for cut in range(GROUPS - 3):
-
-        @pl.when(step == cut + 3)
-        def _():
-            chaining.relay(0, cut)
-
-    @pl.when(step == 0)
-    def _():
-        gain_t = jnp.transpose(w_small[0, :, LANES : 2 * LANES].astype(F32))
-        gain = gain_t[24:25]
-        for ref, first, count in ((halo, 0, HALO), (tokens, HALO, rows)):
-            value = (ref[...] if ref is halo else ref[0]).astype(F32)
+    chaining = Chaining(place, rounds, False, folds, gains, refs[6:10], refs[10:14])
+    group, half, part = turn_of(step)
+    x, y, z, c = place.x, place.y, place.z, place.c
+    meets = [(z + 1 < depth, place.up()), (z > 0, place.down())]
+    if fused:
+        v_small, v_parts, edge, halo_docs, docs_in, cot_in, par_in = refs[14:21]
+        side_send, side_land, local, out_sem = refs[21:25]
+        marks = refs[25:]
+        own = [own_small, own_parts.at[0], own_parts.at[1], own_parts.at[2], own_exit]
+        full = [v_small, v_parts.at[0], v_parts.at[1], v_parts.at[2], exit_out]
+        pieces = [
+            Gathering(place, own[i], full[i], *marks[3 * i : 3 * i + 3]) for i in range(5)
+        ]
+        stores = [pltpu.make_async_copy(v_small, small_out, out_sem.at[0])]
+        for index in range(3):
+            stores.append(
+                pltpu.make_async_copy(
+                    v_parts.at[index], parts_out.at[index], out_sem.at[index + 1]
+                )
+            )
+
+    def before_weights():
+        for ref, first, count in ((edge, 0, HALO), (tokens, HALO, rows)):
+            value = (ref[...] if ref is edge else ref[0]).astype(F32)
             scale = lax.rsqrt(jnp.mean(value * value, axis=1, keepdims=True) + EPSILON)
-            hidden[first : first + count] = (value * scale * gain).astype(LOW)
+            normed[first : first + count] = value * scale
+        docs = jnp.concatenate([halo_docs[...], doc_col[...]], axis=0)
+        for back in range(1, CONV):
+            match = (docs[HALO - back : HALO - back + rows] == docs[HALO:]).astype(F32)
+            match_out[back - 1] = match
+        t_at, u_at = iota((Q, Q), 0), iota((Q, Q), 1)
+        for index in range(spans):
+            at = slice(index * Q, (index + 1) * Q)
+            same = (t_at >= u_at) & (doc_col[at] == doc_row[0:1, at])
+            mask_out[at] = jnp.where(same, 0.0, FAR)
+
+    def after_weights(small):
+        gain = jnp.transpose(small[0][:, LANES:].astype(F32))[24:25]
+        hidden[...] = (normed[...] * gain).astype(LOW)
         hidden_out[...] = jnp.transpose(hidden[HALO:])
-        both = [mm(hidden[...], w_small[index]) for index in range(2)]
+        both = [mm(hidden[...], small[index]) for index in range(2)]
         cin = jnp.concatenate([both[0][:, :LANES], both[1][:, :LANES]], axis=1).astype(LOW)
         cin_state_out[...] = cin
         docs = jnp.concatenate([halo_docs[...], doc_col[...]], axis=0)
-        masks = []
-        for back in range(1, CONV):
-            match = (docs[HALO - back : HALO - back + rows] == docs[HALO:]).astype(F32)
-            match_out[back - 1] = match
-            masks.append(match)
+        masks = [match_out[back] for back in range(CONV - 1)]
         pre = conv_forward(cin.astype(F32), state_filter[...], masks)
         pre_state_out[...] = pre
         mixed = (pre * sigmoid(pre)).astype(LOW)
         bc_out[...] = mixed
         turned = jnp.transpose(mixed.astype(F32)).astype(LOW)
         bct_out[...] = turned
-        heads = par_heads[...]
+        heads = heads_ref[...]
         used = iota((rows, LANES), 1) < 24
         raw = both[0][HALO:, LANES:] + both[1][HALO:, LANES:]
         zst = jnp.where(used, raw, 0.0) + heads[0:1]
@@ -695,8 +705,6 @@
             sp_out[2, at] = split3(jnp.where(lanes_used, opened * jnp.exp(cum), 0.0))
             sp_out[3, at] = split3(jnp.where(lanes_used, tail, 0.0))
             sp_tail[at] = split3(jnp.where(lanes_used, tail * dt[at], 0.0))
-            same = (t_at >= u_at) & (here == doc_row[0:1, at])
-            mask_out[at] = jnp.where(same, 0.0, FAR)
             score_out[at] = mm_nt(mixed[at, LANES:], mixed[at, :LANES])
         gain_total = fac_rows[0]
         for row in fac_rows[1:]:
@@ -708,30 +716,138 @@
         fac_out[...] = rows8
         facs[...] = split3(rows8)
 
-    cin = mm(hidden[...], w_inner[0]).astype(LOW)
-    cin_out[...] = cin
-    gate_out[...] = mm(hidden[HALO:], w_gate[0])
-    masks = [match_out[back] for back in range(CONV - 1)]
-    pre = conv_forward(cin.astype(F32), par[0], masks)
-    pre_out[...] = pre
-    spread = spreader(4 * step, HEAD, 4)
-    value = (pre * sigmoid(pre) * mm(sp_tail[...], spread)).astype(LOW)
-    facx = mm(facs[...], spread)
-    fold = jnp.zeros((NSTATE, WIDE), F32)
-    for index in range(spans):
-        at = slice(index * Q, (index + 1) * Q)
-        loc = mm(bct_out[:NSTATE, at], value[at])
-        loc_out[at] = loc
-        fold = facx[index : index + 1] * fold + loc
-    folds[step] = fold
-    gains[step] = jnp.broadcast_to(facx[spans : spans + 1], (8, WIDE))
+    if fused:
+
+        @pl.when(step == 0)
+        def _():
+            count = 2 * depth
+            onward = {"context": lax.rem(place.position + 1, count)}
+            behind = {"context": lax.rem(place.position + count - 1, count)}
+            place.greet(
+                [place.mate, place.x_peer, place.y_peer, onward, behind],
+                meets + chaining.sometimes(),
+            )
+            sides = [
+                remote(own_edge, edge, side_send.at[0], side_land.at[0], onward),
+                remote(own_docs, docs_in, side_send.at[1], side_land.at[1], onward),
+                remote(own_par, par_in.at[y], side_send.at[2], side_land.at[2], place.y_peer),
+            ]
+            for copy in sides:
+                copy.start()
+            for piece in pieces:
+                piece.own()
+            cot_copy = pltpu.make_async_copy(cot.at[y], cot_in, local.at[0])
+            par_keep = pltpu.make_async_copy(own_par, par_in.at[y], local.at[1])
+            cot_copy.start()
+            par_keep.start()
+            for copy in sides:
+                copy.wait()
+            par_keep.wait()
+            pieces[0].near()
+            pieces[1].near()
+            halo_docs[...] = jnp.where(place.position == 0, -1.0, docs_in[...])
+            par[...] = par_in[...]
+            both = par[0, CONV + 2 : CONV + 3] + par[1, CONV + 2 : CONV + 3]
+            heads_ref[...] = jnp.zeros_like(heads_ref)
+            for index in range(3):
+                heads_ref[index : index + 1] = both[:, index * LANES : (index + 1) * LANES]
+            before_weights()
+            pieces[0].across()
+            pieces[2].near()
+            pieces[1].across()
+            pieces[0].far()
+            cot_copy.wait()
+            cot_t[...] = jnp.transpose(cot_in[...])
+            pieces[0].mates()
+            stores[0].start()
+            after_weights([v_small[index].reshape(model, WIDE) for index in range(2)])
+
+        @pl.when(step == 1)
+        def _():
+            pieces[3].near()
+            pieces[2].across()
+            pieces[1].far()
+            pieces[1].mates()
+            stores[1].start()
+
+        @pl.when(step == 2)
+        def _():
+            pieces[4].near()
+
+        @pl.when(step == 3)
+        def _():
+            pieces[3].across()
+            pieces[2].far()
+            pieces[2].mates()
+            stores[2].start()
+
+        @pl.when(step == 4)
+        def _():
+            pieces[4].across()
+
+        @pl.when(step == 5)
+        def _():
+            pieces[3].far()
+            pieces[3].mates()
+            stores[3].start()
+
+        @pl.when(step == 6)
+        def _():
+            pieces[4].far()
+
+    else:
+
+        @pl.when(step == 0)
+        def _():
+            place.greet([place.mate], chaining.sometimes())
+            before_weights()
+            after_weights([w_small[index] for index in range(2)])
+
+    for cut in range(GROUPS - 1):
+
+        @pl.when(step == cut + 2)
+        def _():
+            chaining.pass_on(0, cut)
+
+    for cut in range(GROUPS - 3):
+
+        @pl.when(step == cut + 4)
+        def _():
+            chaining.relay(0, cut)
+
+    @pl.when(step > 0)
+    def _():
+        if fused:
+            gate_low = v_parts[part, half, :, :, :, :WIDE].reshape(model, WIDE)
+            inner_low = v_parts[part, half, :, :, :, WIDE:].reshape(model, WIDE)
+        else:
+            gate_low, inner_low = w_gate[0, 0], w_inner[0, 0]
+        taps = par[half, :, pl.ds(pl.multiple_of(part * WIDE, WIDE), WIDE)]
+        cin = mm(hidden[...], inner_low).astype(LOW)
+        cin_out[...] = cin
+        gate_out[...] = mm(hidden[HALO:], gate_low)
+        masks = [match_out[back] for back in range(CONV - 1)]
+        pre = conv_forward(cin.astype(F32), taps, masks)
+        pre_out[...] = pre
+        spread = spreader(4 * group, HEAD, 4)
+        value = (pre * sigmoid(pre) * mm(sp_tail[...], spread)).astype(LOW)
+        facx = mm(facs[...], spread)
+        fold = jnp.zeros((NSTATE, WIDE), F32)
+        for index in range(spans):
+            at = slice(index * Q, (index + 1) * Q)
+            loc = mm(bct_out[:NSTATE, at], value[at])
+            loc_out[at] = loc
+            fold = facx[index : index + 1] * fold + loc
+        folds[step - 1] = fold
+        gains[step - 1] = jnp.broadcast_to(facx[spans : spans + 1], (8, WIDE))
+
     for cut in range(GROUPS):
 
-        @pl.when(step == cut)
+        @pl.when(step == cut + 1)
         def _():
             chaining.open(cut)
 
-    @pl.when(step == GROUPS - 1)
+    @pl.when(step == GROUPS)
     def _():
         chaining.pass_on(0, GROUPS - 1)
         for cut in range(GROUPS - 3, GROUPS):
@@ -739,77 +855,118 @@
         chaining.later()
 
         def put(cut, value):
-            carry_out[:, cut * WIDE : (cut + 1) * WIDE] = value
+            at = ORDER[cut] * WIDE
+            carry_out[:, at : at + WIDE] = value
 
         chaining.arrive(put)
-        gathering.finish()
+        if fused:
+            pieces[4].mates()
+            for piece in pieces:
+                piece.finish()
+            for store in stores:
+                store.wait()
         chaining.finish()
 
 
-def front(
-    tokens, halo, halo_docs, doc_col, doc_row, weights, par, par_heads, state_filter, packed_exit,
-    rounds
-):
+def entry(tokens, doc_col, doc_row, state_filter, packs, cot, rounds):
+    own_small, own_parts, own_exit, own_par, own_edge, own_docs = packs
     rows, model = tokens.shape[1:]
     count = lax.axis_size("context")
     depth = count // 2
-    wide = 2 * 3 * WIDE
+    wide = GROUPS * WIDE
     ext = rows + HALO
+    fused = own_small.shape[0] % 16 == 0
     shape = jax.ShapeDtypeStruct
-    outs = (
-        (shape((model, rows), LOW), const((model, rows))),
-        (shape((ext, wide), LOW), pl.BlockSpec((ext, WIDE), lambda s: (0, s))),
-        (shape((rows, wide), F32), pl.BlockSpec((rows, WIDE), lambda s: (0, s))),
-        (shape((rows, wide), F32), pl.BlockSpec((rows, WIDE), lambda s: (0, s))),
-        (shape((rows, wide), F32), pl.BlockSpec((rows, WIDE), lambda s: (0, s))),
-        (shape((NSTATE, wide), LOW), const((NSTATE, wide))),
-        (shape((2, 2, count) + packed_exit.shape, LOW), ANY_SPEC),
-        (shape((ext, WIDE), LOW), const((ext, WIDE))),
-        (shape((rows, WIDE), F32), const((rows, WIDE))),
-        (shape((rows, WIDE), LOW), const((rows, WIDE))),
-        (shape((WIDE, rows), LOW), const((WIDE, rows))),
-        (shape((rows, Q), F32), const((rows, Q))),
-        (shape((rows, Q), F32), const((rows, Q))),
-        (shape((rows, LANES), F32), const((rows, LANES))),
-        (shape((rows, LANES), F32), const((rows, LANES))),
-        (shape((4, rows, LANES), LOW), const((4, rows, LANES))),
-        (shape((6, 8, rows), F32), const((6, 8, rows))),
-        (shape((8, LANES), F32), const((8, LANES))),
-        (shape((CONV - 1, rows, LANES), F32), const((CONV - 1, rows, LANES))),
-    )
-    return pl.pallas_call(
-        functools.partial(front_body, depth, rounds),
+    sem = lambda *lead: pltpu.SemaphoreType.DMA(lead)
+    column = lambda count: pl.BlockSpec((count, WIDE), lambda s: (0, turn_of(s)[0]))
+    whole = lambda *dims, dtype=F32: (shape(dims, dtype), const(dims))
+    outs = [
+        whole(model, rows, dtype=LOW),
+        (shape((ext, wide), LOW), column(ext)),
+        (shape((rows, wide), F32), column(rows)),
+        (shape((rows, wide), F32), column(rows)),
+        (shape((rows, wide), F32), column(rows)),
+        whole(NSTATE, wide, dtype=LOW),
+        whole(ext, WIDE, dtype=LOW),
+        whole(rows, WIDE),
+        whole(rows, WIDE, dtype=LOW),
+        whole(WIDE, rows, dtype=LOW),
+        whole(rows, Q),
+        whole(rows, Q),
+        whole(rows, LANES),
+        whole(rows, LANES),
+        whole(4, rows, LANES, dtype=LOW),
+        whole(6, 8, rows),
+        whole(8, LANES),
+        whole(CONV - 1, rows, LANES),
+    ]
+    scratch = [
+        pltpu.VMEM((ext, model), LOW),
+        pltpu.VMEM((ext, model), F32),
+        pltpu.VMEM((rows, LANES), LOW),
+        pltpu.VMEM((8, LANES), LOW),
+        pltpu.VMEM((GROUPS, NSTATE, WIDE), F32),
+        pltpu.VMEM((GROUPS, 8, WIDE), F32),
+    ] + Chaining.scratch(rounds)
+    in_specs = [
+        pl.BlockSpec((1, rows, model), lambda s: (side(), 0, 0)),
+        const((rows, LANES)),
+        const((8, rows)),
+        const((CONV + 1, WIDE)),
+    ]
+    args = [tokens, doc_col, doc_row, state_filter]
+    full = lambda own: (2, 2, count) + own.shape[-2:]
+    if fused:
+        outs += [
+            (shape(full(own_small), LOW), ANY_SPEC),
+            (shape((3,) + full(own_parts), LOW), ANY_SPEC),
+            (shape(full(own_exit), LOW), ANY_SPEC),
+            (shape((2,) + own_par.shape, F32), VMEM_SPEC),
+            (shape((8, LANES), F32), VMEM_SPEC),
+            (shape((model, rows), LOW), VMEM_SPEC),
+        ]
+        scratch += [
+            pltpu.VMEM(full(own_small), LOW),
+            pltpu.VMEM((3,) + full(own_parts), LOW),
+            pltpu.VMEM(own_edge.shape, LOW),
+            pltpu.VMEM(own_docs.shape, F32),
+            pltpu.VMEM(own_docs.shape, F32),
+            pltpu.VMEM((rows, model), LOW),
+            pltpu.VMEM((2,) + own_par.shape, F32),
+            sem(3),
+            sem(3),
+            sem(2),
+            sem(4),
+        ] + Gathering.scratch(depth) * 5
+        in_specs += [VMEM_SPEC] * 6 + [ANY_SPEC]
+        args += [own_small, own_parts, own_exit, own_par, own_edge, own_docs, cot]
+    else:
+        small, parts, exits, par, heads, edge, docs, cot_t = gather(*packs, cot)
+        weights = parts.reshape(3, 2, model, 2 * WIDE)
+        block = lambda at: pl.BlockSpec(
+            (1, 1, model, WIDE), lambda s: (turn_of(s)[2], turn_of(s)[1], 0, at)
+        )
+        in_specs += [block(0), block(1), const((2, model, WIDE))] + [VMEM_SPEC] * 4
+        args += [weights, weights, small.reshape(2, model, WIDE), par, heads, edge, docs]
+    results = pl.pallas_call(
+        functools.partial(entry_body, depth, rounds, fused),
         out_shape=[out[0] for out in outs],
-        grid=(GROUPS,),
-        in_specs=[
-            pl.BlockSpec((1, rows, model), lambda s: (side(), 0, 0)),
-            const((HALO, model)),
-            const((HALO, LANES)),
-            const((rows, LANES)),
-            const((8, rows)),
-            pl.BlockSpec((1, model, WIDE), lambda s: (s // 3, 0, s % 3)),
-            pl.BlockSpec((1, model, WIDE), lambda s: (s // 3, 0, 3 + s % 3)),
-            pl.BlockSpec((2, model, WIDE), lambda s: (0, 0, 6)),
-            pl.BlockSpec((1, 8, WIDE), lambda s: (s // 3, 0, s % 3)),
-            const((8, LANES)),
-            const((CONV + 1, WIDE)),
-            VMEM_SPEC,
-        ],
+        grid=(GROUPS + 1,),
+        in_specs=in_specs,
         out_specs=[out[1] for out in outs],
-        scratch_shapes=[
-            pltpu.VMEM((ext, model), LOW),
-            pltpu.VMEM((rows, LANES), LOW),
-            pltpu.VMEM((8, LANES), LOW),
-            pltpu.VMEM((GROUPS, NSTATE, WIDE), F32),
-            pltpu.VMEM((GROUPS, 8, WIDE), F32),
-        ]
-        + Chaining.scratch(rounds)
-        + Gathering.scratch(depth),
+        scratch_shapes=scratch,
         compiler_params=params(collective_id=1, has_side_effects=True),
-        name="front",
-    )(
-        tokens, halo, halo_docs, doc_col, doc_row, weights, weights, weights, par, par_heads,
-        state_filter, packed_exit,
+        name="entry",
+    )(*args)
+    if fused:
+        small, parts, exits, par, heads, cot_t = results[18:]
+    return tuple(results[:18]), (
+        small.reshape(2, model, WIDE),
+        parts.reshape(3, 2, model, 2 * WIDE),
+        exits.reshape(2, model, -1),
+        par,
+        heads,
+        cot_t,
     )
 
 
@@ -1170,7 +1327,7 @@
         grad = joined(arrived)
         gate_grad = gpg[...]
         inner_part[0] = mm(hidden_t[...], grad).astype(LOW)
-        total[...] += mm_nt(gate_grad, w_gate[0]) + mm_nt(grad, w_inner[0])
+        total[...] += mm_nt(gate_grad, w_gate[0, 0]) + mm_nt(grad, w_inner[0, 0])
         tails = mm(sp[3], spread)
         skipx = mm(split3(par_heads[...]), spread)[2:3]
         adjoint = adjoints[group].astype(F32)
@@ -1211,7 +1368,7 @@
         edge_wait(GROUPS - 1)
         grad = joined(GROUPS - 1)
         inner_part[0] = mm(hidden_t[...], grad).astype(LOW)
-        total[...] += mm_nt(grad, w_inner[0])
+        total[...] += mm_nt(grad, w_inner[0, 0])
         t_at, u_at = iota((Q, Q), 0), iota((Q, Q), 1)
         onward = (t_at <= u_at).astype(F32)
         earlier = (t_at > u_at).astype(F32)
@@ -1293,7 +1450,7 @@
 def scan_back(
     pre, dy, loc, carry, enter, cin, par, par_heads, state_filter, cin_state, pre_state, bc, bct,
     score, mask, sp, cumt, fac, match, zst, dt, exits, gate_part, block_own, tokens, cot, hidden_t,
-    gpg, weights, rounds
+    gpg, parts, small, rounds
 ):
     rows, wide = pre.shape
     ext = rows + HALO
@@ -1352,9 +1509,9 @@
             pl.BlockSpec((1, rows, model), lambda s: (side(), 0, 0)),
             const((model, rows)),
             column(rows),
-            pl.BlockSpec((1, model, WIDE), lambda s: (now(s) // 3, 0, now(s) % 3)),
-            pl.BlockSpec((1, model, WIDE), lambda s: (lag(s) // 3, 0, 3 + lag(s) % 3)),
-            pl.BlockSpec((2, model, WIDE), lambda s: (0, 0, 6)),
+            pl.BlockSpec((1, 1, model, WIDE), lambda s: (now(s) % 3, now(s) // 3, 0, 0)),
+            pl.BlockSpec((1, 1, model, WIDE), lambda s: (lag(s) % 3, lag(s) // 3, 0, 1)),
+            const((2, model, WIDE)),
         ],
         out_specs=[out[1] for out in outs],
         scratch_shapes=[
@@ -1383,13 +1540,13 @@
     )(
         pre, dy, loc, carry, enter, cin, par, par_heads, state_filter, cin_state, pre_state, bc,
         bct, score, mask, sp, cumt, fac, match, zst, dt, exits, gate_part, block_own, tokens, cot,
-        hidden_t, gpg, weights, weights, weights,
+        hidden_t, gpg, parts, parts, small,
     )
 
 
 def pack_body(
     side_ref, entry, exits, state, steps, gain, inner_kernel, gate_gain, bias, decay, skip, docs,
-    tail_tokens, packed, packed_exit, par, doc_col, doc_row, edge
+    tail_tokens, packed_small, packed_parts, packed_exit, par, doc_col, doc_row, edge, docs_own
 ):
     side = side_ref[0]
     rows = entry.shape[0]
@@ -1401,15 +1558,17 @@
         )
         return jnp.where(side == 0, filled, pltpu.roll(filled, value.shape[1], 1))
 
-    packed[:, :wide] = entry[:, 0].astype(LOW)
-    packed[:, wide : 2 * wide] = entry[:, 1].astype(LOW)
+    for part in range(3):
+        at = slice(part * WIDE, (part + 1) * WIDE)
+        packed_parts[part, :, :WIDE] = entry[:, 0, at].astype(LOW)
+        packed_parts[part, :, WIDE:] = entry[:, 1, at].astype(LOW)
     half = jnp.where(side == 0, state[:, :NSTATE], state[:, NSTATE:])
-    packed[:, 2 * wide : 2 * wide + NSTATE] = half.astype(LOW)
+    packed_small[:, :NSTATE] = half.astype(LOW)
     gain_row = jnp.concatenate([gain[...], jnp.zeros((1, LANES - rows), F32)], axis=1)
     gain_col = jnp.transpose(jnp.broadcast_to(gain_row, (LANES, LANES)))[:rows]
     lane = iota((rows, LANES), 1)
     small = jnp.where(lane == 24, gain_col, placed(steps[...]))
-    packed[:, 2 * wide + NSTATE :] = small.astype(LOW)
+    packed_small[:, NSTATE:] = small.astype(LOW)
     packed_exit[...] = exits[...].astype(LOW)
     par[0 : CONV + 1] = inner_kernel[...]
     par[CONV + 1 : CONV + 2] = gate_gain[...]
@@ -1419,6 +1578,7 @@
     own = jnp.where(side == 0, docs[0:1], docs[1:2]).astype(F32)
     doc_row[...] = jnp.broadcast_to(own, doc_row.shape)
     doc_col[...] = jnp.transpose(jnp.broadcast_to(own, (LANES, own.shape[1])))
+    docs_own[...] = doc_col[own.shape[1] - HALO :]
     edge[...] = tail_tokens[0]
 
 
@@ -1433,12 +1593,14 @@
         decay[None], skip[None], docs,
     )
     outs = (
-        shape((own_rows, 2 * wide + WIDE), LOW),
+        shape((own_rows, WIDE), LOW),
+        shape((3, own_rows, 2 * WIDE), LOW),
         shape((own_rows, wide), LOW),
         shape((8, wide), F32),
         shape((rows, LANES), F32),
         shape((8, rows), F32),
         shape((HALO, model), LOW),
+        shape((HALO, LANES), F32),
     )
     return pl.pallas_call(
         pack_body,
@@ -1456,19 +1618,21 @@
 
 
 def gather_body(
-    depth, packed, par_own, edge_own, docs_own, cot, weights, par, heads, edge, docs, cot_t, docs_in,
-    cot_in, side_send, side_land, local, *scratch
+    depth, own_small, own_parts, own_exit, par_own, edge_own, docs_own, cot, small, parts, exits, par,
+    heads, edge, docs, cot_t, docs_in, cot_in, side_send, side_land, local, *marks
 ):
     place = Place(depth)
     count = 2 * depth
     onward = {"context": lax.rem(place.position + 1, count)}
     behind = {"context": lax.rem(place.position + count - 1, count)}
-    x, y, z, c = place.x, place.y, place.z, place.c
+    y, z = place.y, place.z
     place.greet(
         [place.mate, place.x_peer, place.y_peer, onward, behind],
         [(z + 1 < depth, place.up()), (z > 0, place.down())],
     )
-    gathering = Gathering(place, packed, weights, *scratch)
+    own = [own_small, own_parts.at[0], own_parts.at[1], own_parts.at[2], own_exit]
+    full = [small, parts.at[0], parts.at[1], parts.at[2], exits]
+    pieces = [Gathering(place, own[i], full[i], *marks[3 * i : 3 * i + 3]) for i in range(5)]
     sides = [
         remote(edge_own, edge, side_send.at[0], side_land.at[0], onward),
         remote(docs_own, docs_in, side_send.at[1], side_land.at[1], onward),
@@ -1476,15 +1640,18 @@
     ]
     for copy in sides:
         copy.start()
-    gathering.own()
     cot_copy = pltpu.make_async_copy(cot.at[y], cot_in, local.at[1])
     cot_copy.start()
     par_keep = pltpu.make_async_copy(par_own, par.at[y], local.at[0])
     par_keep.start()
+    for piece in pieces:
+        piece.own()
     cot_copy.wait()
     cot_t[...] = jnp.transpose(cot_in[...])
-    gathering.near()
-    gathering.across()
+    for piece in pieces:
+        piece.near()
+        piece.across()
+        piece.far()
     for copy in sides:
         copy.wait()
     docs[...] = jnp.where(place.position == 0, -1.0, docs_in[...])
@@ -1493,27 +1660,31 @@
     heads[...] = jnp.zeros_like(heads)
     for index in range(3):
         heads[index : index + 1] = both[:, index * LANES : (index + 1) * LANES]
-    gathering.far()
-    gathering.finish()
-
-
-def gather(packed, par_own, edge_own, docs_own, cot):
+    for piece in pieces:
+        piece.mates()
+        piece.finish()
+
+
+def gather(own_small, own_parts, own_exit, par_own, edge_own, docs_own, cot):
     count = lax.axis_size("context")
     depth = count // 2
     rows, model = cot.shape[1:]
     shape = jax.ShapeDtypeStruct
+    full = lambda own: (2, 2, count) + own.shape[-2:]
     return pl.pallas_call(
         functools.partial(gather_body, depth),
         out_shape=(
-            shape((2, 2, count) + packed.shape, LOW),
+            shape(full(own_small), LOW),
+            shape((3,) + full(own_parts), LOW),
+            shape(full(own_exit), LOW),
             shape((2,) + par_own.shape, F32),
             shape((8, LANES), F32),
             shape(edge_own.shape, LOW),
             shape(docs_own.shape, F32),
             shape((model, rows), LOW),
         ),
-        in_specs=[VMEM_SPEC] * 4 + [ANY_SPEC],
-        out_specs=[ANY_SPEC] + [VMEM_SPEC] * 5,
+        in_specs=[VMEM_SPEC] * 6 + [ANY_SPEC],
+        out_specs=[ANY_SPEC] * 3 + [VMEM_SPEC] * 5,
         scratch_shapes=[
             pltpu.VMEM(docs_own.shape, F32),
             pltpu.VMEM((rows, model), LOW),
@@ -1521,10 +1692,10 @@
             pltpu.SemaphoreType.DMA((3,)),
             pltpu.SemaphoreType.DMA((2,)),
         ]
-        + Gathering.scratch(depth),
+        + Gathering.scratch(depth) * 5,
         compiler_params=params(collective_id=0, has_side_effects=True),
         name="gather",
-    )(packed, par_own, edge_own, docs_own, cot)
+    )(own_small, own_parts, own_exit, par_own, edge_own, docs_own, cot)
 
 
 def reduce_body(
@@ -1577,9 +1748,9 @@
     def step_all(step):
         reducing.turn(step)
 
-        @pl.when(step >= 1)
-        def _():
-            token_copy(step - 1).start()
+        @pl.when(step < depth)
+        def _():
+            token_copy(step).start()
 
         for turn in range(3):
 
@@ -1745,22 +1916,17 @@
     longest = rows * count // 4
     rounds = min(count // 2 - 1, -(-(longest - 1) // (2 * rows)))
 
-    packed, packed_exit, par_own, doc_col, doc_row, edge_own = pack(
+    own_small, own_parts, own_exit, own_par, doc_col, doc_row, own_edge, own_docs = pack(
         which, entry_weight, exit_weight, state_weight, step_weight, norm_gain, inner_kernel,
         gate_gain, step_bias, decay_log, skip_gain, documents, tokens,
     )
-    weights, par, par_heads, halo, halo_docs, cot_t = gather(
-        packed, par_own, edge_own, doc_col[-HALO:], cotangent
+    packs = (own_small, own_parts, own_exit, own_par, own_edge, own_docs)
+    (
+        hidden_t, cin, gate, pre, loc, carry, cin_state, pre_state, bc, bct, score, mask, zst, dt, sp,
+        cumt, fac, match,
+    ), (small, parts, exit_weights, par, par_heads, cot_t) = entry(
+        tokens, doc_col, doc_row, state_filter, packs, cotangent, rounds
     )
-    weights = weights.reshape(2, model, -1)
-    (
-        hidden_t, cin, gate, pre, loc, carry, exit_weights, cin_state, pre_state, bc, bct, score,
-        mask, zst, dt, sp, cumt, fac, match,
-    ) = front(
-        tokens, halo, halo_docs, doc_col, doc_row, weights, par, par_heads, state_filter,
-        packed_exit, rounds,
-    )
-    exit_weights = exit_weights.reshape(2, model, -1)
     block_own, exit_part, gate_part, dy, gpg, enter, gate_row, skip_row = middle(
         tokens, cotangent, cot_t, hidden_t, pre, gate, loc, carry, exit_weights, par, par_heads, bc,
         bct, score, mask, sp, cumt, fac,
@@ -1772,7 +1938,7 @@
     ) = scan_back(
         pre, dy, loc, carry, enter, cin, par, par_heads, state_filter, cin_state, pre_state, bc, bct,
         score, mask, sp, cumt, fac, match, zst, dt, cut(exit_part), cut(gate_part), block_own,
-        tokens, cotangent, hidden_t, gpg, weights, rounds,
+        tokens, cotangent, hidden_t, gpg, parts, small, rounds,
     )
     mine, state_both, vector, token_both = reduce_all(
         cut(inner_part), cut(small_part), token_own, taps, taps_state, gate_row, head_rows, skip_row,

time: 218 us -> 207 us (0.950)
  Pallas kernels: 209 us -> 200 us
    pallas_call x2 -> x1, Pallas kernels: 66.4 us -> 58.7 us  [entry(): pl.pallas_call(functools.partial(entry_body, depth, rounds, fused), out_s...]
where the time goes in v5:
time: 207 us
  Pallas kernels  200 us (97%)
  local copies, waits for them, and re-layouts  4.06 us (2%)
    pallas_call x1, Pallas kernels, scan_back(): pl.pallas_call(functools.partial(scan_back_body, depth, rounds), out_shap...  70 us
    pallas_call x1, Pallas kernels, entry(): pl.pallas_call(functools.partial(entry_body, depth, rounds, fused), out_s...  58.7 us
    pallas_call x1, Pallas kernels, reduce_all(): pl.pallas_call(functools.partial(reduce_body, depth), out_shape=(shape((o...  39.7 us
    pallas_call x1, Pallas kernels, middle(): pl.pallas_call(middle_body, out_shape=[out[0] for out in outs], grid=(12,...  22.9 us
    pallas_call x1, Pallas kernels, finish(): pl.pallas_call(finish_body, out_shape=[out[0] for out in outs], grid_spec...  5.69 us

profile of v5, /device:TPU:0, one launch (start us, length us, event | category | flops | bytes accessed | tf_op | source)
XLA Modules:
  0.0 206.7 jit_solution(14741595113038947533)
XLA Ops:
  0.6 0.6 pad_add_fusion.side_ref
  1.3 1.3 broadcast_in_dim.16.gate_gain
  2.6 1.4 copy.27.steps
  4.0 3.0 %pack.1 = (bf16[48,256]{1,0:T(8,128)(2,1)}, bf16[3,48,512]{2,1,0:T(8,128)(2,1)}, bf16[48,768]{1,0:T(8,128)(2,1)}, f32[8,768]{1,0:T(8,128)}, f32[512,128]{1,0:T(8...) custom-call(s32[2]{0:T(128)} %pad_add_fusion.side_ref, f32[48,2,768]{2,1,0:T(2,128)} %entry.2, ...), custom_call_target="tpu_custom_call" | custom-call | tf_op jit(solution)/shard_map/pack/pallas_call | solution.py:1605
  6.9 58.7 %entry.3 = (bf16[768,512]{1,0:T(8,128)(2,1)}, bf16[528,1536]{1,0:T(8,128)(2,1)}, f32[512,1536]{1,0:T(8,128)}, f32[512,1536]{1,0:T(8,128)}, f32[512,1536]{1,0:T(8...) custom-call(bf16[2,512,768]{2,1,0:T(8,128)(2,1)} %tokens.3, ...), custom_call_target="tpu_custom_call" | custom-call | tf_op jit(solution)/shard_map/entry/pallas_call | solution.py:951
  65.7 22.9 %middle.1 = (bf16[512,768]{1,0:T(8,128)(2,1)}, bf16[2,768,768]{2,1,0:T(8,128)(2,1)}, bf16[2,768,768]{2,1,0:T(8,128)(2,1)}, f32[512,1536]{1,0:T(8,128)}, bf16[512...) custom-call(bf16[2,512,768]{2,1,0:T(8,128)(2,1)} %tokens.3, ...), custom_call_target="tpu_custom_call" | custom-call | tf_op jit(solution)/shard_map/middle/pallas_call | solution.py:1116
  88.6 70.0 %scan_back.1 = (f32[8,1536]{1,0:T(8,128)}, f32[8,256]{1,0:T(8,128)}, f32[8,128]{1,0:T(8,128)}, f32[48,1536]{1,0:T(8,128)}, bf16[2,512,768]{2,1,0:T(8,128)(2,1)},...) custom-call(f32[512,1536]{1,0:T(8,128)} %get-tuple-element.87.pre_ref, ...), custom_call_target="tpu_custom_call" | custom-call | tf_op jit(solution)/shard_map/scan_back/pallas_call | solution.py:1479
  158.6 39.7 %reduce_all.1 = (f32[48,1024]{1,0:T(8,128)}, f32[2,48,128]{2,1,0:T(8,128)}, f32[8,1792]{1,0:T(8,128)}, bf16[2,512,768]{2,1,0:T(8,128)(2,1)}) custom-call(bf16[2,2,8,48,768]{4,3,2,1,0:T(8,128)(2,1)} %bitcast.22, bf16[2,2,8,48,256]{4,3,2,1,0:T(8,128)(2,1)} %bitcast.23, bf16[512,768]{1,0:T(8,128)(2,1)} %get-tuple-element.119.token, ...), custom_call_target="tpu_custom_call" | custom-call | tf_op jit(solution)/shard_map/reduce_all/pallas_call | solution.py:1802
  198.3 5.7 %finish.1 = (bf16[2,512,768]{2,1,0:T(8,128)(2,1)}, f32[2,512,768]{2,1,0:T(8,128)}, f32[1,48]{1,0:T(1,128)}, f32[48,2,768]{2,1,0:T(2,128)}, f32[48,256]{1,0:T(8,1...) custom-call(s32[2]{0:T(128)} %pad_add_fusion.side_ref, ...), custom_call_target="tpu_custom_call" | custom-call | tf_op jit(solution)/shard_map/finish/pallas_call | solution.py:1886
  204.0 1.3 reduce
  205.3 1.4 copy.28

commit v6 on v5

--- a/solution.py
+++ b/solution.py
@@ -157,12 +157,6 @@
     def at(self, x, y, z, c):
         return {"dp": x, "context": z * 2 + c, "tensor": y}
 
-    def up(self):
-        return self.at(self.x, self.y, self.z + 1, self.c)
-
-    def down(self):
-        return self.at(self.x, self.y, self.z - 1, self.c)
-
     def away(self, z):
         return self.at(self.x, self.y, z, self.c)
 
@@ -217,7 +211,7 @@
     def __init__(self, place, own, full, sends, lands, local):
         self.place, self.own_ref, self.full = place, own, full
         self.sends, self.lands, self.local = sends, lands, local
-        self.starts = [first * place.depth for first in (0, 4, 5, 7, 8)]
+        self.starts = [first * place.depth for first in (0, 4, 5, 7)]
         (self.x1, self.y1), (self.x2, self.y2) = place.axes(place.c)
         self.first = place.at(self.x1, self.y1, place.z, place.c)
         self.second = place.at(self.x2, self.y2, place.z, place.c)
@@ -225,7 +219,7 @@
     @staticmethod
     def scratch(depth):
         sem = pltpu.SemaphoreType.DMA
-        return [sem((9 * depth,)), sem((8 * depth,)), sem((1,))]
+        return [sem((8 * depth,)), sem((8 * depth,)), sem((1,))]
 
     def copy(self, kind, index, x, y, z, c, target, own=False):
         chunk = self.full.at[y, x, z * 2 + c]
@@ -248,14 +242,10 @@
         p = self.place
         mine = (p.x, p.y, p.z, p.c)
 
-        @pl.when(p.z + 1 < p.depth)
-        def _():
-            self.copy(3, p.z, *mine, p.up(), True).start()
-
-        @pl.when(p.z > 0)
-        def _():
-            self.copy(4, p.z, *mine, p.down(), True).start()
-
+        def far_z(z):
+            self.copy(3, z, *mine, p.away(z), True).start()
+
+        p.around(far_z, 1)
         self.copy(1, p.z, *mine, self.first, True).start()
         self.copy(2, p.z, *mine, self.second, True).start()
         self.copy(0, p.z, *mine, p.mate, True).start()
@@ -267,14 +257,6 @@
         def run(z):
             chunk = (p.x, p.y, z, p.c)
             self.arrive(*chunk)
-
-            @pl.when((z < p.z) & (p.z + 1 < p.depth))
-            def _():
-                self.copy(3, z, *chunk, p.up()).start()
-
-            @pl.when((z > p.z) & (p.z > 0))
-            def _():
-                self.copy(4, z, *chunk, p.down()).start()
 
             self.copy(1, z, *chunk, self.first).start()
             self.copy(2, z, *chunk, self.second).start()
@@ -328,16 +310,7 @@
         each(p.depth, lambda step: sent(1, step, p.mate))
         each(2 * p.depth, lambda step: sent(2, step, p.mate))
 
-        def chained(z):
-            @pl.when((z <= p.z) & (p.z + 1 < p.depth))
-            def _():
-                sent(3, z, p.mate)
-
-            @pl.when((z >= p.z) & (p.z > 0))
-            def _():
-                sent(4, z, p.mate)
-
-        each(p.depth, chained)
+        p.around(lambda z: sent(3, z, p.mate), 1)
 
 
 class Reducing:
@@ -625,8 +598,7 @@
     place = Place(depth)
     chaining = Chaining(place, rounds, False, folds, gains, refs[6:10], refs[10:14])
     group, half, part = turn_of(step)
-    x, y, z, c = place.x, place.y, place.z, place.c
-    meets = [(z + 1 < depth, place.up()), (z > 0, place.down())]
+    y = place.y
     if fused:
         v_small, v_parts, edge, halo_docs, docs_in, cot_in, par_in = refs[14:21]
         side_send, side_land, local, out_sem = refs[21:25]
@@ -724,8 +696,7 @@
             onward = {"context": lax.rem(place.position + 1, count)}
             behind = {"context": lax.rem(place.position + count - 1, count)}
             place.greet(
-                [place.mate, place.x_peer, place.y_peer, onward, behind],
-                meets + chaining.sometimes(),
+                [place.mate, place.x_peer, place.y_peer, onward, behind], chaining.sometimes(), True
             )
             sides = [
                 remote(own_edge, edge, side_send.at[0], side_land.at[0], onward),
@@ -1545,37 +1516,47 @@
 
 
 def pack_body(
-    side_ref, entry, exits, state, steps, gain, inner_kernel, gate_gain, bias, decay, skip, docs,
+    entry, exits, state, steps, gain, inner_kernel, gate_gain, bias, decay, skip, docs,
     tail_tokens, packed_small, packed_parts, packed_exit, par, doc_col, doc_row, edge, docs_own
 ):
-    side = side_ref[0]
+    half_of = side()
     rows = entry.shape[0]
     wide = entry.shape[2]
 
-    def placed(value):
-        filled = jnp.concatenate(
+    def placed(filled, used):
+        return jnp.where(half_of == 0, filled, pltpu.roll(filled, used, 1))
+
+    def widened(value):
+        return jnp.concatenate(
             [value, jnp.zeros((value.shape[0], LANES - value.shape[1]), F32)], axis=1
         )
-        return jnp.where(side == 0, filled, pltpu.roll(filled, value.shape[1], 1))
 
     for part in range(3):
         at = slice(part * WIDE, (part + 1) * WIDE)
         packed_parts[part, :, :WIDE] = entry[:, 0, at].astype(LOW)
         packed_parts[part, :, WIDE:] = entry[:, 1, at].astype(LOW)
-    half = jnp.where(side == 0, state[:, :NSTATE], state[:, NSTATE:])
+    half = jnp.where(half_of == 0, state[:, :NSTATE], state[:, NSTATE:])
     packed_small[:, :NSTATE] = half.astype(LOW)
     gain_row = jnp.concatenate([gain[...], jnp.zeros((1, LANES - rows), F32)], axis=1)
     gain_col = jnp.transpose(jnp.broadcast_to(gain_row, (LANES, LANES)))[:rows]
     lane = iota((rows, LANES), 1)
-    small = jnp.where(lane == 24, gain_col, placed(steps[...]))
+    heads_here = steps.shape[0]
+    step_rows = jnp.concatenate([steps[...], jnp.zeros((heads_here, LANES - rows), F32)], axis=1)
+    step_rows = jnp.concatenate([step_rows, jnp.zeros((LANES - heads_here, LANES), F32)], axis=0)
+    step_cols = jnp.transpose(step_rows)[:rows]
+    small = jnp.where(lane == 24, gain_col, placed(step_cols, heads_here))
     packed_small[:, NSTATE:] = small.astype(LOW)
     packed_exit[...] = exits[...].astype(LOW)
     par[0 : CONV + 1] = inner_kernel[...]
-    par[CONV + 1 : CONV + 2] = gate_gain[...]
+    for index in range(wide // LANES):
+        at = slice(index * LANES, (index + 1) * LANES)
+        par[CONV + 1 : CONV + 2, at] = gate_gain[index : index + 1]
     par[CONV + 2 : CONV + 4] = jnp.zeros((2, wide), F32)
     for index, ref in enumerate((bias, decay, skip)):
-        par[CONV + 2 : CONV + 3, index * LANES : (index + 1) * LANES] = placed(ref[...])
-    own = jnp.where(side == 0, docs[0:1], docs[1:2]).astype(F32)
+        par[CONV + 2 : CONV + 3, index * LANES : (index + 1) * LANES] = placed(
+            widened(ref[...]), ref.shape[1]
+        )
+    own = jnp.where(half_of == 0, docs[0:1], docs[1:2]).astype(F32)
     doc_row[...] = jnp.broadcast_to(own, doc_row.shape)
     doc_col[...] = jnp.transpose(jnp.broadcast_to(own, (LANES, own.shape[1])))
     docs_own[...] = doc_col[own.shape[1] - HALO :]
@@ -1583,13 +1564,13 @@
 
 
 def pack(
-    which, entry, exits, state, steps, gain, inner_kernel, gate_gain, bias, decay, skip, docs, tokens
+    entry, exits, state, steps, gain, inner_kernel, gate_gain, bias, decay, skip, docs, tokens
 ):
     own_rows, _, wide = entry.shape
     rows, model = tokens.shape[1:]
     shape = jax.ShapeDtypeStruct
     arrays = (
-        entry, exits, state, steps, gain[None], inner_kernel, gate_gain[None], bias[None],
+        entry, exits, state, steps.T, gain[None], inner_kernel, gate_gain.reshape(-1, LANES), bias[None],
         decay[None], skip[None], docs,
     )
     outs = (
@@ -1605,16 +1586,13 @@
     return pl.pallas_call(
         pack_body,
         out_shape=outs,
-        grid_spec=pltpu.PrefetchScalarGridSpec(
-            num_scalar_prefetch=1,
-            grid=(1,),
-            in_specs=[const(array.shape) for array in arrays]
-            + [pl.BlockSpec((1, HALO, model), lambda s, w: (w[0], rows // HALO - 1, 0))],
-            out_specs=[const(out.shape) for out in outs],
-        ),
+        grid=(1,),
+        in_specs=[const(array.shape) for array in arrays]
+        + [pl.BlockSpec((1, HALO, model), lambda s: (side(), rows // HALO - 1, 0))],
+        out_specs=[const(out.shape) for out in outs],
         compiler_params=params(),
         name="pack",
-    )(which, *arrays, tokens)
+    )(*arrays, tokens)
 
 
 def gather_body(
@@ -1625,11 +1603,8 @@
     count = 2 * depth
     onward = {"context": lax.rem(place.position + 1, count)}
     behind = {"context": lax.rem(place.position + count - 1, count)}
-    y, z = place.y, place.z
-    place.greet(
-        [place.mate, place.x_peer, place.y_peer, onward, behind],
-        [(z + 1 < depth, place.up()), (z > 0, place.down())],
-    )
+    y = place.y
+    place.greet([place.mate, place.x_peer, place.y_peer, onward, behind], (), True)
     own = [own_small, own_parts.at[0], own_parts.at[1], own_parts.at[2], own_exit]
     full = [small, parts.at[0], parts.at[1], parts.at[2], exits]
     pieces = [Gathering(place, own[i], full[i], *marks[3 * i : 3 * i + 3]) for i in range(5)]
@@ -1828,13 +1803,14 @@
 
 
 def finish_body(
-    side_ref, mine, exits, state, vector, token, block, block_out, token_out,
+    mine, exits, state, vector, token, block, block_out, token_out,
     norm_out, entry_out, state_out, step_out, kernel_out, filter_out, bias_out, decay_out, skip_out,
     gate_out, exit_out
 ):
-    side, spot = side_ref[0], side_ref[1]
+    half_of = side()
+    spot = lax.axis_index("dp") * lax.axis_size("context") + lax.axis_index("context")
     token_out[...] = token[...].astype(F32)
-    first = side == 0
+    first = half_of == 0
     block_out[...] = block[...]
 
     @pl.when(pl.program_id(0) == 0)
@@ -1850,11 +1826,14 @@
         def twelve(value):
             return jnp.where(first, value, pltpu.roll(value, LANES - 12, 1))[:, :12]
 
-        step_out[...] = twelve(mine[:, wide + NSTATE :])
+        steps = jnp.where(first, mine[:, wide + NSTATE :], pltpu.roll(mine[:, wide + NSTATE :], LANES - 12, 1))
+        steps = jnp.concatenate([steps, jnp.zeros((LANES - own_rows, LANES), F32)], axis=0)
+        step_out[...] = jnp.transpose(steps)[:12, :own_rows]
         left, right = vector[:, :wide], vector[:, wide : 2 * wide]
         halves = jnp.where(first, left, right)
         kernel_out[...] = halves[: CONV + 1]
-        gate_out[...] = halves[5:6]
+        for index in range(wide // LANES):
+            gate_out[index : index + 1] = halves[5:6, index * LANES : (index + 1) * LANES]
         filter_out[...] = vector[: CONV + 1, 2 * wide :]
         bias_out[...] = twelve(vector[5:6, 2 * wide : 2 * wide + LANES])
         skip_out[...] = twelve(vector[5:6, 2 * wide + LANES :])
@@ -1863,45 +1842,42 @@
         norm_out[...] = turned[6:7, :own_rows]
 
 
-def finish(side, mine, exits, state, vector, token, block):
+def finish(mine, exits, state, vector, token, block):
     own_rows, wide = exits.shape[0], exits.shape[1] // 2
     _, rows, model = token.shape
     share = rows // 4
     shape = jax.ShapeDtypeStruct
     outs = (
-        (shape((2, rows, model), LOW), pl.BlockSpec((2, share, model), lambda s, w: (0, s, 0))),
-        (shape((2, rows, model), F32), pl.BlockSpec((2, share, model), lambda s, w: (0, s, 0))),
+        (shape((2, rows, model), LOW), pl.BlockSpec((2, share, model), lambda s: (0, s, 0))),
+        (shape((2, rows, model), F32), pl.BlockSpec((2, share, model), lambda s: (0, s, 0))),
         (shape((1, own_rows), F32), None),
         (shape((own_rows, 2, wide), F32), None),
         (shape((own_rows, WIDE), F32), None),
-        (shape((own_rows, 12), F32), None),
+        (shape((12, own_rows), F32), None),
         (shape((CONV + 1, wide), F32), None),
         (shape((CONV + 1, WIDE), F32), None),
         (shape((1, 12), F32), None),
         (shape((1, 12), F32), None),
         (shape((1, 12), F32), None),
-        (shape((1, wide), F32), None),
+        (shape((wide // LANES, LANES), F32), None),
         (shape((own_rows, wide), F32), None),
     )
     return pl.pallas_call(
         finish_body,
         out_shape=[out[0] for out in outs],
-        grid_spec=pltpu.PrefetchScalarGridSpec(
-            num_scalar_prefetch=1,
-            grid=(4,),
-            in_specs=[
-                const(mine.shape),
-                const(exits.shape),
-                const(state.shape),
-                const(vector.shape),
-                pl.BlockSpec((2, share, model), lambda s, w: (0, s, 0)),
-                pl.BlockSpec((2, share, model), lambda s, w: (0, s, 0)),
-            ],
-            out_specs=[out[1] if out[1] is not None else const(out[0].shape) for out in outs],
-        ),
+        grid=(4,),
+        in_specs=[
+            const(mine.shape),
+            const(exits.shape),
+            const(state.shape),
+            const(vector.shape),
+            pl.BlockSpec((2, share, model), lambda s: (0, s, 0)),
+            pl.BlockSpec((2, share, model), lambda s: (0, s, 0)),
+        ],
+        out_specs=[out[1] if out[1] is not None else const(out[0].shape) for out in outs],
         compiler_params=params(),
         name="finish",
-    )(side, mine, exits, state, vector, token, block)
+    )(mine, exits, state, vector, token, block)
 
 
 def body(
@@ -1910,14 +1886,12 @@
 ):
     seqs, rows, model = tokens.shape
     count = lax.axis_size("context")
-    position, side = lax.axis_index("context"), lax.axis_index("tensor")
     own_rows = norm_gain.shape[0]
-    which = jnp.stack([side, lax.axis_index("dp") * count + position]).astype(jnp.int32)
     longest = rows * count // 4
     rounds = min(count // 2 - 1, -(-(longest - 1) // (2 * rows)))
 
     own_small, own_parts, own_exit, own_par, doc_col, doc_row, own_edge, own_docs = pack(
-        which, entry_weight, exit_weight, state_weight, step_weight, norm_gain, inner_kernel,
+        entry_weight, exit_weight, state_weight, step_weight, norm_gain, inner_kernel,
         gate_gain, step_bias, decay_log, skip_gain, documents, tokens,
     )
     packs = (own_small, own_parts, own_exit, own_par, own_edge, own_docs)
@@ -1944,9 +1918,12 @@
         cut(inner_part), cut(small_part), token_own, taps, taps_state, gate_row, head_rows, skip_row,
         norm_row,
     )
-    outs = finish(which, mine, exit_mine, state_both, vector, token_both, block_both)
-    flat = (2, 8, 9, 10, 11)
-    return tuple(out[0] if index in flat else out for index, out in enumerate(outs))
+    outs = list(finish(mine, exit_mine, state_both, vector, token_both, block_both))
+    for index in (2, 8, 9, 10):
+        outs[index] = outs[index][0]
+    outs[5] = outs[5].T
+    outs[11] = outs[11].reshape(-1)
+    return tuple(outs)
 
 
 def solution(mesh):

time: 207 us -> 197 us (0.952)
  local copies, waits for them, and re-layouts: 4.06 us -> 0 us
  Pallas kernels: 200 us -> 196 us
    pallas_call x1, Pallas kernels: 58.7 us -> 55.3 us  [entry(): pl.pallas_call(functools.partial(entry_body, depth, rounds, fused), out_s...]
    unnamed x2 -> x0, local copies, waits for them, and re-layouts: 2.8 us -> none
where the time goes in v6:
time: 197 us; the launch traced here: 196 us
  Pallas kernels  196 us (99%)
    pallas_call x1, Pallas kernels, scan_back(): pl.pallas_call(functools.partial(scan_back_body, depth, rounds), out_shap...  70.2 us
    pallas_call x1, Pallas kernels, entry(): pl.pallas_call(functools.partial(entry_body, depth, rounds, fused), out_s...  55.3 us
    pallas_call x1, Pallas kernels, reduce_all(): pl.pallas_call(functools.partial(reduce_body, depth), out_shape=(shape((o...  39.7 us
    pallas_call x1, Pallas kernels, middle(): pl.pallas_call(middle_body, out_shape=[out[0] for out in outs], grid=(12,...  22.9 us
    pallas_call x1, Pallas kernels, finish(): pl.pallas_call(finish_body, out_shape=[out[0] for out in outs], grid=(4,)...  5.06 us

profile of v6, /device:TPU:0, one launch (start us, length us, event | category | flops | bytes accessed | tf_op | source)
XLA Modules:
  0.0 196.5 jit_solution(4768161202108721512)
XLA Ops:
  0.6 2.4 %pack.1 = (bf16[48,256]{1,0:T(8,128)(2,1)}, bf16[3,48,512]{2,1,0:T(8,128)(2,1)}, bf16[48,768]{1,0:T(8,128)(2,1)}, f32[8,768]{1,0:T(8,128)}, f32[512,128]{1,0:T(8...) custom-call(f32[48,2,768]{2,1,0:T(2,128)} %entry.2, f32[48,768]{1,0:T(8,128)} %exits.1, ...), custom_call_target="tpu_custom_call" | custom-call | tf_op jit(solution)/shard_map/pack/pallas_call | solution.py:1586
  3.1 55.3 %entry.3 = (bf16[768,512]{1,0:T(8,128)(2,1)}, bf16[528,1536]{1,0:T(8,128)(2,1)}, f32[512,1536]{1,0:T(8,128)}, f32[512,1536]{1,0:T(8,128)}, f32[512,1536]{1,0:T(8...) custom-call(bf16[2,512,768]{2,1,0:T(8,128)(2,1)} %tokens.3, ...), custom_call_target="tpu_custom_call" | custom-call | tf_op jit(solution)/shard_map/entry/pallas_call | solution.py:922
  58.4 22.9 %middle.1 = (bf16[512,768]{1,0:T(8,128)(2,1)}, bf16[2,768,768]{2,1,0:T(8,128)(2,1)}, bf16[2,768,768]{2,1,0:T(8,128)(2,1)}, f32[512,1536]{1,0:T(8,128)}, bf16[512...) custom-call(bf16[2,512,768]{2,1,0:T(8,128)(2,1)} %tokens.3, ...), custom_call_target="tpu_custom_call" | custom-call | tf_op jit(solution)/shard_map/middle/pallas_call | solution.py:1087
  81.4 70.2 %scan_back.1 = (f32[8,1536]{1,0:T(8,128)}, f32[8,256]{1,0:T(8,128)}, f32[8,128]{1,0:T(8,128)}, f32[48,1536]{1,0:T(8,128)}, bf16[2,512,768]{2,1,0:T(8,128)(2,1)},...) custom-call(f32[512,1536]{1,0:T(8,128)} %get-tuple-element.87.pre_ref, ...), custom_call_target="tpu_custom_call" | custom-call | tf_op jit(solution)/shard_map/scan_back/pallas_call | solution.py:1450
  151.6 39.7 %reduce_all.1 = (f32[48,1024]{1,0:T(8,128)}, f32[2,48,128]{2,1,0:T(8,128)}, f32[8,1792]{1,0:T(8,128)}, bf16[2,512,768]{2,1,0:T(8,128)(2,1)}) custom-call(bf16[2,2,8,48,768]{4,3,2,1,0:T(8,128)(2,1)} %bitcast.24, bf16[2,2,8,48,256]{4,3,2,1,0:T(8,128)(2,1)} %bitcast.25, bf16[512,768]{1,0:T(8,128)(2,1)} %get-tuple-element.119.token, ...), custom_call_target="tpu_custom_call" | custom-call | tf_op jit(solution)/shard_map/reduce_all/pallas_call | solution.py:1777
  191.3 5.1 %finish.1 = (bf16[2,512,768]{2,1,0:T(8,128)(2,1)}, f32[2,512,768]{2,1,0:T(8,128)}, f32[1,48]{1,0:T(1,128)}, f32[48,2,768]{2,1,0:T(2,128)}, f32[48,256]{1,0:T(8,1...) custom-call(f32[48,1024]{1,0:T(8,128)} %get-tuple-element.126.mine, ...), custom_call_target="tpu_custom_call" | custom-call | tf_op jit(solution)/shard_map/finish/pallas_call | solution.py:1865

commit v7 on v6

--- a/solution.py
+++ b/solution.py
@@ -571,10 +571,116 @@
                     self.chip_copy(turn, cut).wait_send()
 
 
-def turn_of(step):
-    index = jnp.maximum(step - 1, 0)
+class Closing:
+    def __init__(self, place, token, token_out, refs):
+        self.place, self.token, self.token_out = place, token, token_out
+        self.state_own, self.state_in, self.send, self.land = refs[:4]
+        self.vs, self.vl, self.ts, self.tl, self.ss, self.sl, self.keep_sem = refs[4:]
+        self.targets = [place.mate, place.y_peer, place.x_peer]
+
+    @staticmethod
+    def scratch(depth, own_rows, vector):
+        sem = lambda *lead: pltpu.SemaphoreType.DMA(lead)
+        return [
+            pltpu.VMEM((own_rows, NSTATE), F32),
+            pltpu.VMEM((2, own_rows, NSTATE), F32),
+            pltpu.VMEM((4,) + vector, F32),
+            pltpu.VMEM((3 + depth,) + vector, F32),
+            sem(3 + depth), sem(3 + depth), sem(depth), sem(depth), sem(1), sem(1), sem(1),
+        ]
+
+    def vec_copy(self, turn):
+        return remote(
+            self.send.at[turn], self.land.at[turn], self.vs.at[turn], self.vl.at[turn],
+            self.targets[turn],
+        )
+
+    def vec_far(self, away, lands_at):
+        return remote(
+            self.send.at[3], self.land.at[3 + lands_at], self.vs.at[3 + away],
+            self.vl.at[3 + lands_at], self.place.away(away),
+        )
+
+    def token_copy(self, step):
+        p = self.place
+        share = self.token.shape[0] // p.depth
+        at = pl.ds(pl.multiple_of(step * share, share), share)
+        return remote(
+            self.token.at[at], self.token_out.at[p.y, at], self.ts.at[step], self.tl.at[step],
+            p.y_peer,
+        )
+
+    def run(self, reducing, width, state_out, vector_out, first, pending=None):
+        p = self.place
+        depth, z = p.depth, p.z
+        keep = pltpu.make_async_copy(self.token, self.token_out.at[p.y], self.keep_sem.at[0])
+        keep.start()
+        self.vec_copy(0).start()
+
+        def step_all(step):
+            if pending is not None:
+
+                @pl.when(step + 3 <= depth)
+                def _():
+                    pending.turn(step + 3)
+
+            reducing.turn(step)
+
+            @pl.when(step < depth)
+            def _():
+                self.token_copy(step).start()
+
+            for turn in range(3):
+
+                @pl.when(step == turn)
+                def _():
+                    self.vec_copy(turn).wait_recv()
+                    self.send[turn + 1] = self.send[turn] + self.land[turn]
+                    if turn < 2:
+                        self.vec_copy(turn + 1).start()
+                    else:
+                        each(depth, lambda s: self.vec_far(lax.rem(z + s, depth), z).start(), 1)
+                        self.land[3 + z] = self.send[3]
+
+        each(depth + 1, step_all)
+        if pending is not None:
+            pending.close()
+        reducing.close()
+        self.state_own[...] = reducing.total[:, first : first + width]
+        state_copy = remote(
+            self.state_own, self.state_in.at[p.y], self.ss.at[0], self.sl.at[0], p.y_peer
+        )
+        state_copy.start()
+        self.state_in[p.y] = self.state_own[...]
+
+        def vec_arrive(step):
+            away = lax.rem(z + step, depth)
+            self.vec_far(away, away).wait_recv()
+
+        each(depth, vec_arrive, 1)
+        vector_out[...] = self.land[3]
+
+        def vec_add(step):
+            vector_out[...] += self.land[3 + step]
+
+        each(depth, vec_add, 1)
+        for turn in range(3):
+            self.vec_copy(turn).wait_send()
+        each(depth, lambda s: self.vec_far(lax.rem(z + s, depth), z).wait_send(), 1)
+        reducing.finish()
+        each(depth, lambda step: self.token_copy(step).wait())
+        state_copy.wait()
+        state_out[...] = self.state_in[...]
+        keep.wait()
+
+
+def group_of(index):
     half, part = index % 2, index // 2
     return half * 3 + part, half, part
+
+
+def turn_of(step):
+    return group_of(jnp.maximum(step - 1, 0))
 
 
 def entry_body(depth, rounds, fused, *refs):
@@ -1125,15 +1231,27 @@
     )
 
 
-def scan_back_body(
-    depth, rounds, pre_ref, dy_ref, loc_ref, carry_ref, enter, cin_ref, par, par_heads,
-    state_filter, cin_state, pre_state, bc, bct, score, mask, sp, cumt, fac, match, zst, dt_ref,
-    exits, gate_part, block_own, tokens, cot, hidden_t, gpg, w_gate, w_inner, w_small, tap_out,
-    tap_state_out, small_out, mine, block_out, inner_part, small_part, token_out, norm_out, d_bc,
-    d_score, d_cum, heads, local_value, enters, gains, adjoints, edge_own, edge_in, grads, total, es,
-    el, bs, bl, block_keep, *scratch
-):
-    group = pl.program_id(0)
+def scan_back_body(depth, rounds, fused, *refs):
+    (
+        pre_ref, dy_ref, loc_ref, carry_ref, enter, cin_ref, par, par_heads, state_filter, cin_state,
+        pre_state, bc, bct, score, mask, sp, cumt, fac, match, zst, dt_ref, exits, gate_part,
+        block_own, tokens, cot, hidden_t, gpg, w_gate, w_inner, w_small, gate_row, skip_row,
+    ) = refs[:33]
+    mine, block_out = refs[33:35]
+    if fused:
+        mine2, mine3, state_out, vector_out, token_both = refs[35:40]
+        refs = refs[40:]
+    else:
+        tap_out, tap_state_out, small_out, inner_part, small_part, token_out, norm_out = refs[35:42]
+        refs = refs[42:]
+    (
+        d_bc, d_score, d_cum, heads, local_value, enters, gains, adjoints, edge_own, edge_in, grads,
+        total, es, el, bs, bl, block_keep,
+    ) = refs[:17]
+    scratch = refs[17:42]
+    step = pl.program_id(0)
+    group, half_at, part_at = group_of(jnp.minimum(step, GROUPS - 1))
+    last_group, last_half, last_part = group_of(jnp.maximum(step - 1, 0))
     blocks = BLOCK_CUTS
     rows = pre_ref.shape[0]
     spans = rows // Q
@@ -1142,8 +1260,20 @@
     chaining = Chaining(place, rounds, True, enters, gains, scratch[:4], scratch[4:8])
     reducing = Reducing(
         place, 0, [(exits, slice(0, wide)), (gate_part, slice(wide, 2 * wide))], mine,
-        scratch[8:16], scratch[16:],
+        scratch[8:16], scratch[16:25],
     )
+    if fused:
+        inner_v, small_v, token_v, taps_v = refs[42:46]
+        buffers = refs[46:]
+        second = Reducing(
+            place, 0, [(inner_v.at[0], slice(0, WIDE)), (inner_v.at[1], slice(WIDE, 2 * WIDE))],
+            mine2, buffers[:8], buffers[8:17],
+        )
+        third = Reducing(
+            place, 0, [(inner_v.at[2], slice(0, WIDE)), (small_v, slice(WIDE, 2 * WIDE))], mine3,
+            buffers[17:25], buffers[25:34],
+        )
+        closing = Closing(place, token_v, token_both, buffers[34:])
     position = place.position
     has_before, has_after = position > 0, position < 2 * depth - 1
     before, after = {"context": position - 1}, {"context": position + 1}
@@ -1164,6 +1294,12 @@
         @pl.when(has_after)
         def _():
             edge_copy(index).wait_recv()
+
+    def put_inner(value):
+        if fused:
+            inner_v[last_part, last_half] = value.reshape(inner_v.shape[2:])
+        else:
+            inner_part[0] = value
 
     def joined(index):
         grad = grads[...]
@@ -1171,7 +1307,7 @@
             [grad[: rows - EDGE], grad[rows - EDGE :] + edge_in[index]], axis=0
         ).astype(LOW)
 
-    @pl.when(group == 0)
+    @pl.when(step == 0)
     def _():
         d_bc[...] = jnp.zeros_like(d_bc)
         d_score[...] = jnp.zeros_like(d_score)
@@ -1203,7 +1339,13 @@
         for cut in range(GROUPS):
             chaining.pass_on(0, cut)
 
-    @pl.when(group < GROUPS)
+    if fused:
+
+        @pl.when(step == 5)
+        def _():
+            each(depth, second.start)
+
+    @pl.when(step < GROUPS)
     def _():
         spread = spreader(4 * group, HEAD, 4)
         collect = gatherer(4 * group, HEAD, 4)
@@ -1253,7 +1395,7 @@
             d_bc[at, LANES:] += mm_nt(pushed.astype(LOW), state_low)
             heads[1, at] += head_sums(pushed * carried, collect)
 
-    @pl.when(group == 0)
+    @pl.when(step == 0)
     def _():
         for cut in range(GROUPS):
             chaining.relay(0, cut)
@@ -1267,20 +1409,22 @@
 
     for turn in range(5):
 
-        @pl.when(group == turn)
+        @pl.when(step == turn)
         def _():
             each(turn + 1 if turn < 4 else depth + 1, reducing.turn, turn)
             block_copy(turn + 3).start()
 
-    @pl.when(group == 5)
+    @pl.when(step == 5)
     def _():
         reducing.close()
-
-    @pl.when((group > 0) & (group < GROUPS))
+        if fused:
+            second.turn(0)
+
+    @pl.when((step > 0) & (step < GROUPS))
     def _():
-        edge_wait(group - 1)
-
-    @pl.when(group < GROUPS)
+        edge_wait(last_group)
+
+    @pl.when(step < GROUPS)
     def _():
         spread = spreader(4 * group, HEAD, 4)
         collect = gatherer(4 * group, HEAD, 4)
@@ -1294,10 +1438,10 @@
         for index in range(spans - 1):
             at = slice(index * Q, (index + 1) * Q)
             states.append(facx[index : index + 1] * states[-1] + loc_ref[at])
-        arrived = jnp.where(group > 0, group - 1, GROUPS + 1)
+        arrived = jnp.where(step > 0, last_group, GROUPS + 1)
         grad = joined(arrived)
         gate_grad = gpg[...]
-        inner_part[0] = mm(hidden_t[...], grad).astype(LOW)
+        put_inner(mm(hidden_t[...], grad).astype(LOW))
         total[...] += mm_nt(gate_grad, w_gate[0, 0]) + mm_nt(grad, w_inner[0, 0])
         tails = mm(sp[3], spread)
         skipx = mm(split3(par_heads[...]), spread)[2:3]
@@ -1325,7 +1469,11 @@
             pgs[index] = d_mix * s * (1.0 + pre[at] * (1.0 - s))
         pg = jnp.concatenate(pgs, axis=0)
         sums, grad = conv_backward(pg, cin_ref[...].astype(F32), par[0], masks)
-        tap_out[...] = jnp.concatenate(sums + [jnp.zeros((3, WIDE), F32)], axis=0)
+        taps8 = jnp.concatenate(sums + [jnp.zeros((3, WIDE), F32)], axis=0)
+        if fused:
+            taps_v[group] = taps8
+        else:
+            tap_out[...] = taps8
         grads[...] = grad[HALO:]
         edge_own[group] = grad[HALO - EDGE : HALO]
 
@@ -1333,12 +1481,14 @@
         def _():
             edge_copy(group).start()
 
-    @pl.when(group == GROUPS)
+    @pl.when(step == GROUPS)
     def _():
+        if fused:
+            second.turn(1)
         masks = [match[back] for back in range(CONV - 1)]
         edge_wait(GROUPS - 1)
         grad = joined(GROUPS - 1)
-        inner_part[0] = mm(hidden_t[...], grad).astype(LOW)
+        put_inner(mm(hidden_t[...], grad).astype(LOW))
         total[...] += mm_nt(grad, w_inner[0, 0])
         t_at, u_at = iota((Q, Q), 0), iota((Q, Q), 1)
         onward = (t_at <= u_at).astype(F32)
@@ -1368,14 +1518,21 @@
             score_low = d_score[at].astype(LOW)
             d_bc[at, :LANES] += mm_tn(score_low, bc[at, LANES:])
             d_bc[at, LANES:] += mm(score_low, bc[at, :LANES])
-        small_out[...] = jnp.concatenate(
-            [bias_sum, decay_sum, jnp.zeros((6, LANES), F32)], axis=0
-        )
+        if not fused:
+            small_out[...] = jnp.concatenate(
+                [bias_sum, decay_sum, jnp.zeros((6, LANES), F32)], axis=0
+            )
+        if fused:
+            second.turn(2)
         pre = pre_state[...]
         s = sigmoid(pre)
         pg = d_bc[...] * s * (1.0 + pre * (1.0 - s))
         sums, grad = conv_backward(pg, cin_state[...].astype(F32), state_filter[...], masks)
-        tap_state_out[...] = jnp.concatenate(sums + [jnp.zeros((3, WIDE), F32)], axis=0)
+        taps8 = jnp.concatenate(sums + [jnp.zeros((3, WIDE), F32)], axis=0)
+        if fused:
+            taps_v[GROUPS] = taps8
+        else:
+            tap_state_out[...] = taps8
         grads[...] = grad[HALO:]
         edge_own[GROUPS] = grad[HALO - EDGE : HALO]
 
@@ -1386,14 +1543,19 @@
         steps = jnp.concatenate(raws, axis=0)
         turned = hidden_t[...]
         step_part = mm(turned, steps).astype(LOW)
-        small_part[0, :, LANES:] = step_part
-        small_part[1, :, LANES:] = step_part
         total[...] += mm_nt(steps, w_small[0, :, LANES:]) + mm_nt(steps, w_small[1, :, LANES:])
         edge_wait(GROUPS)
         state = joined(GROUPS)
         state_part = mm(turned, state).astype(LOW)
-        small_part[0, :, :LANES] = state_part[:, :LANES]
-        small_part[1, :, :LANES] = state_part[:, LANES:]
+        for index in range(2):
+            state_half = state_part[:, index * LANES : (index + 1) * LANES]
+            value = jnp.concatenate([state_half, step_part], axis=1)
+            if fused:
+                small_v[index] = value.reshape(small_v.shape[1:])
+            else:
+                small_part[index] = value
+        if fused:
+            each(depth, third.start)
         value = tokens[0].astype(F32)
         scale = lax.rsqrt(jnp.mean(value * value, axis=1, keepdims=True) + EPSILON)
         hidden_grad = (
@@ -1402,13 +1564,31 @@
             + mm_nt(state[:, LANES:], w_small[1, :, :LANES])
         )
         norm_sum = jnp.sum(hidden_grad * (value * scale), axis=0, keepdims=True)
-        norm_out[...] = jnp.broadcast_to(norm_sum, norm_out.shape)
+        if not fused:
+            norm_out[...] = jnp.broadcast_to(norm_sum, norm_out.shape)
         gain = jnp.transpose(w_small[0, :, LANES : 2 * LANES].astype(F32))[24:25]
         normed = hidden_grad * gain
         pull = jnp.sum(normed * value, axis=1, keepdims=True) / value.shape[1]
-        token_out[...] = (
+        token_low = (
             cot[0].astype(F32) + scale * normed - (scale * scale * scale) * value * pull
         ).astype(LOW)
+        if fused:
+            token_v[...] = token_low
+            for index in range(GROUPS + 1):
+                at = slice(index * WIDE, (index + 1) * WIDE)
+                closing.send[0, : CONV + 1, at] = taps_v[index, : CONV + 1]
+            high = GROUPS * WIDE
+            closing.send[0, CONV + 1 :] = jnp.zeros((8 - CONV - 1, high + WIDE), F32)
+            closing.send[0, 5:6, :high] = gate_row[0:1]
+            closing.send[0, 5:6, high : high + LANES] = bias_sum
+            closing.send[0, 5:6, high + LANES :] = skip_row[0:1]
+            model = norm_sum.shape[1]
+            closing.send[0, 6:7, :model] = norm_sum
+            closing.send[0, 6:7, model : model + LANES] = decay_sum
+            closing.run(third, NSTATE, state_out, vector_out, WIDE, second)
+            second.finish()
+        else:
+            token_out[...] = token_low
         reducing.finish()
         each(blocks, lambda index: block_copy(index).wait())
         block_local.wait()
@@ -1421,7 +1601,7 @@
 def scan_back(
     pre, dy, loc, carry, enter, cin, par, par_heads, state_filter, cin_state, pre_state, bc, bct,
     score, mask, sp, cumt, fac, match, zst, dt, exits, gate_part, block_own, tokens, cot, hidden_t,
-    gpg, parts, small, rounds
+    gpg, parts, small, gate_row, skip_row, rounds
 ):
     rows, wide = pre.shape
     ext = rows + HALO
@@ -1430,25 +1610,50 @@
     shape = jax.ShapeDtypeStruct
     sem = lambda *lead: pltpu.SemaphoreType.DMA(lead)
     model = tokens.shape[2]
-    now = lambda s: jnp.minimum(s, GROUPS - 1)
-    lag = lambda s: jnp.maximum(s - 1, 0)
-    column = lambda count: pl.BlockSpec((count, WIDE), lambda s: (0, now(s)))
-    outs = (
-        (shape((8, wide), F32), column(8)),
-        (shape((8, WIDE), F32), const((8, WIDE))),
-        (shape((8, LANES), F32), const((8, LANES))),
-        (shape((own_rows, 2 * half_wide), F32), const((own_rows, 2 * half_wide))),
+    count = 2 * depth
+    fused = own_rows % 16 == 0
+    now = lambda s: group_of(jnp.minimum(s, GROUPS - 1))
+    lag = lambda s: group_of(jnp.maximum(s - 1, 0))
+    column = lambda count: pl.BlockSpec((count, WIDE), lambda s: (0, now(s)[0]))
+    whole = lambda *dims, dtype=F32: (shape(dims, dtype), const(dims))
+    outs = [
+        whole(own_rows, 2 * half_wide),
         (shape((2,) + block_own.shape, LOW), ANY_SPEC),
-        (
-            shape((2, model, 3 * WIDE), LOW),
-            pl.BlockSpec((1, model, WIDE), lambda s: (lag(s) // 3, 0, lag(s) % 3)),
-        ),
-        (shape((2, model, WIDE), LOW), const((2, model, WIDE))),
-        (shape((rows, model), LOW), const((rows, model))),
-        (shape((8, model), F32), const((8, model))),
-    )
+    ]
+    if fused:
+        outs += [
+            whole(own_rows, 2 * WIDE),
+            whole(own_rows, 2 * WIDE),
+            whole(2, own_rows, NSTATE),
+            whole(8, wide + WIDE),
+            (shape((2, rows, model), LOW), ANY_SPEC),
+        ]
+        extra = (
+            [
+                pltpu.VMEM((3, 2, 2, count, own_rows, WIDE), LOW),
+                pltpu.VMEM((2, 2, count, own_rows, WIDE), LOW),
+                pltpu.VMEM((rows, model), LOW),
+                pltpu.VMEM((GROUPS + 1, 8, WIDE), F32),
+            ]
+            + Reducing.scratch(depth, own_rows, 2 * WIDE) * 2
+            + Closing.scratch(depth, own_rows, (8, wide + WIDE))
+        )
+    else:
+        outs += [
+            (shape((8, wide), F32), column(8)),
+            whole(8, WIDE),
+            whole(8, LANES),
+            (
+                shape((2, model, 3 * WIDE), LOW),
+                pl.BlockSpec((1, model, WIDE), lambda s: (lag(s)[1], 0, lag(s)[2])),
+            ),
+            whole(2, model, WIDE, dtype=LOW),
+            whole(rows, model, dtype=LOW),
+            whole(8, model),
+        ]
+        extra = []
     return pl.pallas_call(
-        functools.partial(scan_back_body, depth, rounds),
+        functools.partial(scan_back_body, depth, rounds, fused),
         out_shape=[out[0] for out in outs],
         grid=(GROUPS + 1,),
         in_specs=[
@@ -1458,7 +1663,7 @@
             column(NSTATE),
             const((NSTATE, wide)),
             column(ext),
-            pl.BlockSpec((1, 8, WIDE), lambda s: (now(s) // 3, 0, now(s) % 3)),
+            pl.BlockSpec((1, 8, WIDE), lambda s: (now(s)[1], 0, now(s)[2])),
             const((8, LANES)),
             const((CONV + 1, WIDE)),
             const((ext, WIDE)),
@@ -1480,9 +1685,11 @@
             pl.BlockSpec((1, rows, model), lambda s: (side(), 0, 0)),
             const((model, rows)),
             column(rows),
-            pl.BlockSpec((1, 1, model, WIDE), lambda s: (now(s) % 3, now(s) // 3, 0, 0)),
-            pl.BlockSpec((1, 1, model, WIDE), lambda s: (lag(s) % 3, lag(s) // 3, 0, 1)),
+            pl.BlockSpec((1, 1, model, WIDE), lambda s: (now(s)[2], now(s)[1], 0, 0)),
+            pl.BlockSpec((1, 1, model, WIDE), lambda s: (lag(s)[2], lag(s)[1], 0, 1)),
             const((2, model, WIDE)),
+            const((8, wide)),
+            const((8, LANES)),
         ],
         out_specs=[out[1] for out in outs],
         scratch_shapes=[
@@ -1505,13 +1712,14 @@
             sem(1),
         ]
         + Chaining.scratch(rounds)
-        + Reducing.scratch(depth, own_rows, 2 * half_wide),
+        + Reducing.scratch(depth, own_rows, 2 * half_wide)
+        + extra,
         compiler_params=params(collective_id=2, has_side_effects=True),
         name="scan_back",
     )(
         pre, dy, loc, carry, enter, cin, par, par_heads, state_filter, cin_state, pre_state, bc,
         bct, score, mask, sp, cumt, fac, match, zst, dt, exits, gate_part, block_own, tokens, cot,
-        hidden_t, gpg, parts, parts, small,
+        hidden_t, gpg, parts, parts, small, gate_row, skip_row,
     )
 
 
@@ -1674,105 +1882,34 @@
 
 
 def reduce_body(
-    depth, inner, small, token, taps, taps_state, gate_row, head_rows, skip_row, norm_row,
-    total, state_out, vector_out, token_out, state_own, vec_send, vec_land, vs, vl, ts, tl, ss, sl,
-    keep_sem, *scratch
+    depth, inner, small, token, taps, taps_state, gate_row, head_rows, skip_row, norm_row, mine,
+    state_out, vector_out, token_out, *scratch
 ):
     place = Place(depth)
-    x, y, z, c = place.x, place.y, place.z, place.c
     wide = inner.shape[-1]
     parts = [(inner, slice(0, wide)), (small, slice(wide, wide + WIDE))]
-    reducing = Reducing(place, 0, parts, total, scratch[:8], scratch[8:])
-
-    vec_send[0] = jnp.zeros(vec_send.shape[1:], F32)
-    vec_send[0, : CONV + 1, : 2 * wide] = taps[: CONV + 1]
-    vec_send[0, : CONV + 1, 2 * wide :] = taps_state[: CONV + 1]
-    vec_send[0, 5:6, : 2 * wide] = gate_row[0:1]
-    vec_send[0, 5:6, 2 * wide : 2 * wide + LANES] = head_rows[0:1]
-    vec_send[0, 5:6, 2 * wide + LANES :] = skip_row[0:1]
+    reducing = Reducing(place, 0, parts, mine, scratch[:8], scratch[8:17])
+    closing = Closing(place, token, token_out, scratch[17:])
+    vec = closing.send
+    vec[0] = jnp.zeros(vec.shape[1:], F32)
+    vec[0, : CONV + 1, : 2 * wide] = taps[: CONV + 1]
+    vec[0, : CONV + 1, 2 * wide :] = taps_state[: CONV + 1]
+    vec[0, 5:6, : 2 * wide] = gate_row[0:1]
+    vec[0, 5:6, 2 * wide : 2 * wide + LANES] = head_rows[0:1]
+    vec[0, 5:6, 2 * wide + LANES :] = skip_row[0:1]
     model = norm_row.shape[1]
-    vec_send[0, 6:7, :model] = norm_row[0:1]
-    vec_send[0, 6:7, model : model + LANES] = head_rows[1:2]
-
+    vec[0, 6:7, :model] = norm_row[0:1]
+    vec[0, 6:7, model : model + LANES] = head_rows[1:2]
     place.greet([place.mate, place.x_peer, place.y_peer], (), True)
-    vec_targets = [place.mate, place.x_peer, place.y_peer]
-
-    def vec_copy(turn):
-        return remote(
-            vec_send.at[turn], vec_land.at[turn], vs.at[turn], vl.at[turn], vec_targets[turn]
-        )
-
-    def vec_far(away, lands_at):
-        return remote(
-            vec_send.at[3], vec_land.at[3 + lands_at], vs.at[3 + away], vl.at[3 + lands_at],
-            place.away(away),
-        )
-
-    share = token.shape[0] // depth
-
-    def token_copy(step):
-        at = pl.ds(pl.multiple_of(step * share, share), share)
-        return remote(token.at[at], token_out.at[y, at], ts.at[step], tl.at[step], place.y_peer)
-
-    token_keep = pltpu.make_async_copy(token, token_out.at[y], keep_sem.at[0])
-
-    vec_copy(0).start()
     each(depth, reducing.start)
-    token_keep.start()
-
-    def step_all(step):
-        reducing.turn(step)
-
-        @pl.when(step < depth)
-        def _():
-            token_copy(step).start()
-
-        for turn in range(3):
-
-            @pl.when(step == turn)
-            def _():
-                vec_copy(turn).wait_recv()
-                vec_send[turn + 1] = vec_send[turn] + vec_land[turn]
-                if turn < 2:
-                    vec_copy(turn + 1).start()
-                else:
-                    each(depth, lambda s: vec_far(lax.rem(z + s, depth), z).start(), 1)
-                    vec_land[3 + z] = vec_send[3]
-
-    each(depth + 1, step_all)
-    reducing.close()
-    state_own[...] = total[:, wide : wide + NSTATE]
-    state_copy = remote(state_own, state_out.at[y], ss.at[0], sl.at[0], place.y_peer)
-    state_copy.start()
-    state_out[y] = state_own[...]
-
-    def vec_arrive(step):
-        away = lax.rem(z + step, depth)
-        vec_far(away, away).wait_recv()
-
-    each(depth, vec_arrive, 1)
-    vector_out[...] = vec_land[3]
-
-    def vec_add(step):
-        vector_out[...] += vec_land[3 + step]
-
-    each(depth, vec_add, 1)
-    for turn in range(3):
-        vec_copy(turn).wait_send()
-    each(depth, lambda s: vec_far(lax.rem(z + s, depth), z).wait_send(), 1)
-    reducing.finish()
-    each(depth, lambda step: token_copy(step).wait())
-    state_copy.wait()
-    token_keep.wait()
+    closing.run(reducing, NSTATE, state_out, vector_out, wide)
 
 
 def reduce_all(inner, small, token, taps, taps_state, gate_row, head_rows, skip_row, norm_row):
-    count = lax.axis_size("context")
-    depth = count // 2
+    depth = lax.axis_size("context") // 2
     own_rows, wide = inner.shape[3:]
     tall = wide + WIDE
     shape = jax.ShapeDtypeStruct
-    sem = lambda *lead: pltpu.SemaphoreType.DMA(lead)
     vector = (8, 2 * wide + WIDE)
     return pl.pallas_call(
         functools.partial(reduce_body, depth),
@@ -1784,26 +1921,15 @@
         ),
         in_specs=[ANY_SPEC] * 2 + [VMEM_SPEC] * 7,
         out_specs=[VMEM_SPEC] * 3 + [ANY_SPEC],
-        scratch_shapes=[
-            pltpu.VMEM((own_rows, NSTATE), F32),
-            pltpu.VMEM((4,) + vector, F32),
-            pltpu.VMEM((3 + depth,) + vector, F32),
-            sem(3 + depth),
-            sem(3 + depth),
-            sem(depth),
-            sem(depth),
-            sem(1),
-            sem(1),
-            sem(1),
-        ]
-        + Reducing.scratch(depth, own_rows, tall),
+        scratch_shapes=Reducing.scratch(depth, own_rows, tall)
+        + Closing.scratch(depth, own_rows, vector),
         compiler_params=params(collective_id=4, has_side_effects=True),
         name="reduce_all",
     )(inner, small, token, taps, taps_state, gate_row, head_rows, skip_row, norm_row)
 
 
 def finish_body(
-    mine, exits, state, vector, token, block, block_out, token_out,
+    mine, mine_last, exits, state, vector, token, block, block_out, token_out,
     norm_out, entry_out, state_out, step_out, kernel_out, filter_out, bias_out, decay_out, skip_out,
     gate_out, exit_out
 ):
@@ -1818,7 +1944,8 @@
         own_rows, _, wide = entry_out.shape
         model = token.shape[2]
         entry_out[:, 0] = exits[:, wide:]
-        entry_out[:, 1] = mine[:, :wide]
+        entry_out[:, 1, : 2 * WIDE] = mine[...]
+        entry_out[:, 1, 2 * WIDE :] = mine_last[:, :WIDE]
         exit_out[...] = exits[:, :wide]
         state_out[:, :NSTATE] = state[0]
         state_out[:, NSTATE:] = state[1]
@@ -1826,7 +1953,7 @@
         def twelve(value):
             return jnp.where(first, value, pltpu.roll(value, LANES - 12, 1))[:, :12]
 
-        steps = jnp.where(first, mine[:, wide + NSTATE :], pltpu.roll(mine[:, wide + NSTATE :], LANES - 12, 1))
+        steps = jnp.where(first, mine_last[:, WIDE + NSTATE :], pltpu.roll(mine_last[:, WIDE + NSTATE :], LANES - 12, 1))
         steps = jnp.concatenate([steps, jnp.zeros((LANES - own_rows, LANES), F32)], axis=0)
         step_out[...] = jnp.transpose(steps)[:12, :own_rows]
         left, right = vector[:, :wide], vector[:, wide : 2 * wide]
@@ -1842,7 +1969,7 @@
         norm_out[...] = turned[6:7, :own_rows]
 
 
-def finish(mine, exits, state, vector, token, block):
+def finish(mine, mine_last, exits, state, vector, token, block):
     own_rows, wide = exits.shape[0], exits.shape[1] // 2
     _, rows, model = token.shape
     share = rows // 4
@@ -1868,6 +1995,7 @@
         grid=(4,),
         in_specs=[
             const(mine.shape),
+            const(mine_last.shape),
             const(exits.shape),
             const(state.shape),
             const(vector.shape),
@@ -1877,7 +2005,7 @@
         out_specs=[out[1] if out[1] is not None else const(out[0].shape) for out in outs],
         compiler_params=params(),
         name="finish",
-    )(mine, exits, state, vector, token, block)
+    )(mine, mine_last, exits, state, vector, token, block)
 
 
 def body(
@@ -1906,19 +2034,21 @@
         bct, score, mask, sp, cumt, fac,
     )
     cut = lambda v: v.reshape(2, 2, count, own_rows, v.shape[-1])
-    (
-        taps, taps_state, head_rows, exit_mine, block_both, inner_part, small_part, token_own,
-        norm_row,
-    ) = scan_back(
+    exit_mine, block_both, *others = scan_back(
         pre, dy, loc, carry, enter, cin, par, par_heads, state_filter, cin_state, pre_state, bc, bct,
         score, mask, sp, cumt, fac, match, zst, dt, cut(exit_part), cut(gate_part), block_own,
-        tokens, cotangent, hidden_t, gpg, parts, small, rounds,
+        tokens, cotangent, hidden_t, gpg, parts, small, gate_row, skip_row, rounds,
     )
-    mine, state_both, vector, token_both = reduce_all(
-        cut(inner_part), cut(small_part), token_own, taps, taps_state, gate_row, head_rows, skip_row,
-        norm_row,
-    )
-    outs = list(finish(mine, exit_mine, state_both, vector, token_both, block_both))
+    if len(others) == 5:
+        mine, mine_last, state_both, vector, token_both = others
+    else:
+        taps, taps_state, head_rows, inner_part, small_part, token_own, norm_row = others
+        mine, state_both, vector, token_both = reduce_all(
+            cut(inner_part), cut(small_part), token_own, taps, taps_state, gate_row, head_rows,
+            skip_row, norm_row,
+        )
+        mine, mine_last = mine[:, : 2 * WIDE], mine[:, 2 * WIDE :]
+    outs = list(finish(mine, mine_last, exit_mine, state_both, vector, token_both, block_both))
     for index in (2, 8, 9, 10):
         outs[index] = outs[index][0]
     outs[5] = outs[5].T

time: 197 us -> 190 us (0.964)
  Pallas kernels: 196 us -> 189 us
    pallas_call x2 -> x1, Pallas kernels: 110 us -> 103 us  [scan_back(): pl.pallas_call(functools.partial(scan_back_body, depth, rounds, fused), o...]
where the time goes in v7:
time: 190 us
  Pallas kernels  189 us (99%)
    pallas_call x1, Pallas kernels, scan_back(): pl.pallas_call(functools.partial(scan_back_body, depth, rounds, fused), o...  103 us
    pallas_call x1, Pallas kernels, entry(): pl.pallas_call(functools.partial(entry_body, depth, rounds, fused), out_s...  55.4 us
    pallas_call x1, Pallas kernels, middle(): pl.pallas_call(middle_body, out_shape=[out[0] for out in outs], grid=(12,...  22.9 us
    pallas_call x1, Pallas kernels, finish(): pl.pallas_call(finish_body, out_shape=[out[0] for out in outs], grid=(4,)...  5.1 us

profile of v7, /device:TPU:0, one launch (start us, length us, event | category | flops | bytes accessed | tf_op | source)
XLA Modules:
  0.0 189.8 jit_solution(8045280619618050184)
XLA Ops:
  0.6 2.4 %pack.1 = (bf16[48,256]{1,0:T(8,128)(2,1)}, bf16[3,48,512]{2,1,0:T(8,128)(2,1)}, bf16[48,768]{1,0:T(8,128)(2,1)}, f32[8,768]{1,0:T(8,128)}, f32[512,128]{1,0:T(8...) custom-call(f32[48,2,768]{2,1,0:T(2,128)} %entry.2, f32[48,768]{1,0:T(8,128)} %exits.1, ...), custom_call_target="tpu_custom_call" | custom-call | tf_op jit(solution)/shard_map/pack/pallas_call | solution.py:1794
  3.1 55.4 %entry.3 = (bf16[768,512]{1,0:T(8,128)(2,1)}, bf16[528,1536]{1,0:T(8,128)(2,1)}, f32[512,1536]{1,0:T(8,128)}, f32[512,1536]{1,0:T(8,128)}, f32[512,1536]{1,0:T(8...) custom-call(bf16[2,512,768]{2,1,0:T(8,128)(2,1)} %refs_24_.1, ...), custom_call_target="tpu_custom_call" | custom-call | tf_op jit(solution)/shard_map/entry/pallas_call | solution.py:1028
  58.5 22.9 %middle.1 = (bf16[512,768]{1,0:T(8,128)(2,1)}, bf16[2,768,768]{2,1,0:T(8,128)(2,1)}, bf16[2,768,768]{2,1,0:T(8,128)(2,1)}, f32[512,1536]{1,0:T(8,128)}, bf16[512...) custom-call(bf16[2,512,768]{2,1,0:T(8,128)(2,1)} %refs_24_.1, ...), custom_call_target="tpu_custom_call" | custom-call | tf_op jit(solution)/shard_map/middle/pallas_call | solution.py:1193
  81.5 103.1 %scan_back.1 = (f32[48,1536]{1,0:T(8,128)}, bf16[2,512,768]{2,1,0:T(8,128)(2,1)}, f32[48,512]{1,0:T(8,128)}, f32[48,512]{1,0:T(8,128)}, f32[2,48,128]{2,1,0:T(8,...) custom-call(f32[512,1536]{1,0:T(8,128)} %get-tuple-element.81.pre_ref.refs_0_, ...), custom_call_target="tpu_custom_call" | custom-call | tf_op jit(solution)/shard_map/scan_back/pallas_call | solution.py:1655
  184.6 5.1 %finish.1 = (bf16[2,512,768]{2,1,0:T(8,128)(2,1)}, f32[2,512,768]{2,1,0:T(8,128)}, f32[1,48]{1,0:T(1,128)}, f32[48,2,768]{2,1,0:T(2,128)}, f32[48,256]{1,0:T(8,1...) custom-call(f32[48,512]{1,0:T(8,128)} %get-tuple-element.113.mine, ...), custom_call_target="tpu_custom_call" | custom-call | tf_op jit(solution)/shard_map/finish/pallas_call | solution.py:1992

commit v8 on v7

--- a/solution.py
+++ b/solution.py
@@ -1048,17 +1048,27 @@
 
 
 def middle_body(
-    tokens, cot, cot_t, hidden_t, pre_ref, gate_ref, loc_ref, carry_ref, w_exit, par, par_heads, bc,
+    tokens_far, cot, cot_t_far, hidden_far, pre_ref, gate_ref, loc_ref, carry_ref, w_exit, par, par_heads, bc,
     bct, score, mask, sp, cumt, fac, block_out, exit_out, gate_part_out, dy_out, gpg_out, enter_out, row_out,
-    skip_out, outputs, gates, unit_grads, mixes, sums, total
+    skip_out, outputs, gates, unit_grads, mixes, sums, total,
+    tokens, cot_t, hidden_t, late_sem
 ):
     step = pl.program_id(0)
     rows = pre_ref.shape[0]
     spans = rows // Q
     wide = 6 * WIDE
 
+    late = [
+        pltpu.make_async_copy(src, dst, late_sem.at[index])
+        for index, (src, dst) in enumerate(
+            ((cot_t_far, cot_t), (hidden_far, hidden_t), (tokens_far.at[side()], tokens))
+        )
+    ]
+
     @pl.when(step == 0)
     def _():
+        for copy in late:
+            copy.start()
         sums[...] = jnp.zeros_like(sums)
         total[...] = jnp.zeros_like(total)
         skip_out[...] = jnp.zeros_like(skip_out)
@@ -1083,16 +1093,14 @@
             parts = []
             for pair in range(2):
                 lanes = slice(pair * LANES, (pair + 1) * LANES)
-                local = None
-                for side in range(2):
-                    head = 2 * pair + side
+                weights, seen = [], []
+                for head in (2 * pair, 2 * pair + 1):
                     across = cumt[group, head : head + 1, at]
                     spread_at = cums[at, head * LANES : (head + 1) * LANES] - across + mask[at]
-                    weight = (jnp.exp2(spread_at) * score[at]).astype(LOW)
-                    keep = half if side == 0 else jnp.logical_not(half)
-                    seen = jnp.where(keep, value[at, lanes], 0.0).astype(LOW)
-                    part = mm(weight, seen)
-                    local = part if local is None else local + part
+                    weights.append((jnp.exp2(spread_at) * score[at]).astype(LOW))
+                    keep = half if head % 2 == 0 else jnp.logical_not(half)
+                    seen.append(jnp.where(keep, value[at, lanes], 0.0).astype(LOW))
+                local = mm(jnp.concatenate(weights, axis=1), jnp.concatenate(seen, axis=0))
                 parts.append(local)
             out = jnp.concatenate(parts, axis=1) + carried + skipx * mix[at]
             outputs[group, at] = out
@@ -1109,6 +1117,8 @@
 
     @pl.when(step == 5)
     def _():
+        for copy in late:
+            copy.wait()
         square = jnp.sum(sums[0], axis=1, keepdims=True)
         cross = jnp.sum(sums[1], axis=1, keepdims=True)
         normal = lax.rsqrt(square / wide + EPSILON)
@@ -1154,7 +1164,7 @@
 
     @pl.when(step == 11)
     def _():
-        block_out[...] = (tokens[0].astype(F32) + total[...]).astype(LOW)
+        block_out[...] = (tokens[...].astype(F32) + total[...]).astype(LOW)
 
 
 def middle(
@@ -1195,10 +1205,10 @@
         out_shape=[out[0] for out in outs],
         grid=(12,),
         in_specs=[
+                ANY_SPEC,
                 pl.BlockSpec((1, rows, model), lambda s: (side(), 0, 0)),
-                pl.BlockSpec((1, rows, model), lambda s: (side(), 0, 0)),
-                const((model, rows)),
-                const((model, rows)),
+                ANY_SPEC,
+                ANY_SPEC,
                 pl.BlockSpec((rows, WIDE), lambda s: (0, early(s))),
                 pl.BlockSpec((rows, WIDE), lambda s: (0, early(s))),
                 pl.BlockSpec((rows, WIDE), lambda s: (0, early(s))),
@@ -1222,6 +1232,10 @@
                 pltpu.VMEM((6, rows, WIDE), F32),
                 pltpu.VMEM((2, rows, LANES), F32),
                 pltpu.VMEM((rows, model), F32),
+                pltpu.VMEM((rows, model), LOW),
+                pltpu.VMEM((model, rows), LOW),
+                pltpu.VMEM((model, rows), LOW),
+                pltpu.SemaphoreType.DMA((3,)),
         ],
         compiler_params=params(),
         name="middle",
@@ -1233,9 +1247,10 @@
 
 def scan_back_body(depth, rounds, fused, *refs):
     (
-        pre_ref, dy_ref, loc_ref, carry_ref, enter, cin_ref, par, par_heads, state_filter, cin_state,
-        pre_state, bc, bct, score, mask, sp, cumt, fac, match, zst, dt_ref, exits, gate_part,
-        block_own, tokens, cot, hidden_t, gpg, w_gate, w_inner, w_small, gate_row, skip_row,
+        pre_ref, dy_ref, loc_ref, carry_ref, enter, cin_ref, par, par_heads, state_filter, cin_far,
+        pre_far, bc, bct, score, mask, sp, cumt, fac, match_far, zst_far, dt_far, exits, gate_part,
+        block_far, tokens_far, cot_far, hidden_far, gpg, w_gate, w_inner, small_far, gate_row,
+        skip_row,
     ) = refs[:33]
     mine, block_out = refs[33:35]
     if fused:
@@ -1244,6 +1259,19 @@
     else:
         tap_out, tap_state_out, small_out, inner_part, small_part, token_out, norm_out = refs[35:42]
         refs = refs[42:]
+    block_own, hidden_t, match, tokens, cot, w_small, pre_state, cin_state, zst, dt_ref = refs[:10]
+    late_sem = refs[10]
+    refs = refs[11:]
+    late = [
+        pltpu.make_async_copy(src, dst, late_sem.at[index])
+        for index, (src, dst) in enumerate(
+            (
+                (block_far, block_own), (hidden_far, hidden_t), (match_far, match),
+                (tokens_far.at[side()], tokens), (cot_far.at[side()], cot), (small_far, w_small),
+                (pre_far, pre_state), (cin_far, cin_state), (zst_far, zst), (dt_far, dt_ref),
+            )
+        )
+    ]
     (
         d_bc, d_score, d_cum, heads, local_value, enters, gains, adjoints, edge_own, edge_in, grads,
         total, es, el, bs, bl, block_keep,
@@ -1309,6 +1337,8 @@
 
     @pl.when(step == 0)
     def _():
+        for copy in late:
+            copy.start()
         d_bc[...] = jnp.zeros_like(d_bc)
         d_score[...] = jnp.zeros_like(d_score)
         d_cum[...] = jnp.zeros_like(d_cum)
@@ -1334,6 +1364,7 @@
             rows8 = mm(facs, spreader(4 * cut, HEAD, 4))
             gains[cut] = jnp.broadcast_to(rows8[spans : spans + 1], (8, WIDE))
         each(depth, reducing.start)
+        late[0].wait()
         block_local.start()
         each(3, lambda index: block_copy(index).start())
         for cut in range(GROUPS):
@@ -1356,7 +1387,6 @@
         growth = mm(sp[2], spread)
         facx = mm(split3(fac[...]), spread)
         cums = mm(sp[1], spreader(4 * group, LANES, 4))
-        half = iota((Q, LANES), 1) < HEAD
         ones = jnp.ones((8, Q), F32).astype(LOW)
         states = [carry_ref[...].astype(F32)]
         for index in range(spans - 1):
@@ -1366,34 +1396,44 @@
             at = slice(index * Q, (index + 1) * Q)
             dy = dy_ref[at]
             value = mix[at] * dtx[at]
+            value_low = value.astype(LOW)
+            lane = iota((Q, WIDE), 1) // HEAD
+            dy_heads = [jnp.where(lane == head, dy, 0.0).astype(LOW) for head in range(4)]
+            d_weight = mm_nt(jnp.concatenate(dy_heads, axis=0), value_low)
             parts = []
             sum_score = None
+            row_sums = None
             for pair in range(2):
                 lanes = slice(pair * LANES, (pair + 1) * LANES)
-                value_low = value[:, lanes].astype(LOW)
-                local = None
-                for part_of in range(2):
-                    head = 2 * pair + part_of
+                moved, weights = [], []
+                for head in (2 * pair, 2 * pair + 1):
                     across = cumt[group, head : head + 1, at]
                     spread_at = cums[at, head * LANES : (head + 1) * LANES] - across + mask[at]
                     decay = jnp.exp2(spread_at)
-                    keep = half if part_of == 0 else jnp.logical_not(half)
-                    dy_low = jnp.where(keep, dy[:, lanes], 0.0).astype(LOW)
-                    inner = decay * mm_nt(dy_low, value_low)
+                    inner = decay * d_weight[head * Q : (head + 1) * Q]
                     sum_score = inner if sum_score is None else sum_score + inner
-                    moved = (inner * score[at]).astype(LOW)
-                    turn = mm_nt(ones, moved) - mm(ones, moved)
-                    d_cum[group, head : head + 1, at] = turn[0:1]
-                    part = mm_tn((decay * score[at]).astype(LOW), dy_low)
-                    local = part if local is None else local + part
-                parts.append(local)
+                    moved.append((inner * score[at]).astype(LOW))
+                    weights.append((decay * score[at]).astype(LOW))
+                both = jnp.concatenate(moved, axis=1)
+                column_sums = mm(ones, both)
+                for index_in in range(2):
+                    head = 2 * pair + index_in
+                    d_cum[group, head : head + 1, at] = -column_sums[
+                        0:1, index_in * Q : (index_in + 1) * Q
+                    ]
+                part = mm(both, gatherer(4 * group + 2 * pair, LANES, 2))
+                row_sums = part if row_sums is None else row_sums + part
+                pushed_heads = [dy_heads[2 * pair][:, lanes], dy_heads[2 * pair + 1][:, lanes]]
+                parts.append(
+                    mm_tn(jnp.concatenate(weights, axis=0), jnp.concatenate(pushed_heads, axis=0))
+                )
             d_score[at] += sum_score
             local_value[at] = jnp.concatenate(parts, axis=1)
             pushed = dy * growth[at]
             state_low = states[index].astype(LOW)
             carried = mm(bc[at, LANES:], state_low)
             d_bc[at, LANES:] += mm_nt(pushed.astype(LOW), state_low)
-            heads[1, at] += head_sums(pushed * carried, collect)
+            heads[1, at] += head_sums(pushed * carried, collect) + row_sums
 
     @pl.when(step == 0)
     def _():
@@ -1406,6 +1446,8 @@
 
         chaining.arrive(put)
         chaining.finish()
+        late[1].wait()
+        late[2].wait()
 
     for turn in range(5):
 
@@ -1483,6 +1525,8 @@
 
     @pl.when(step == GROUPS)
     def _():
+        for copy in late[3:]:
+            copy.wait()
         if fused:
             second.turn(1)
         masks = [match[back] for back in range(CONV - 1)]
@@ -1556,7 +1600,7 @@
                 small_part[index] = value
         if fused:
             each(depth, third.start)
-        value = tokens[0].astype(F32)
+        value = tokens[...].astype(F32)
         scale = lax.rsqrt(jnp.mean(value * value, axis=1, keepdims=True) + EPSILON)
         hidden_grad = (
             total[...]
@@ -1570,7 +1614,7 @@
         normed = hidden_grad * gain
         pull = jnp.sum(normed * value, axis=1, keepdims=True) / value.shape[1]
         token_low = (
-            cot[0].astype(F32) + scale * normed - (scale * scale * scale) * value * pull
+            cot[...].astype(F32) + scale * normed - (scale * scale * scale) * value * pull
         ).astype(LOW)
         if fused:
             token_v[...] = token_low
@@ -1666,8 +1710,8 @@
             pl.BlockSpec((1, 8, WIDE), lambda s: (now(s)[1], 0, now(s)[2])),
             const((8, LANES)),
             const((CONV + 1, WIDE)),
-            const((ext, WIDE)),
-            const((rows, WIDE)),
+            ANY_SPEC,
+            ANY_SPEC,
             const((rows, WIDE)),
             const((WIDE, rows)),
             const((rows, Q)),
@@ -1675,24 +1719,35 @@
             const((4, rows, LANES)),
             const((6, 8, rows)),
             const((8, LANES)),
-            const((CONV - 1, rows, LANES)),
-            const((rows, LANES)),
-            const((rows, LANES)),
             ANY_SPEC,
             ANY_SPEC,
-            VMEM_SPEC,
-            pl.BlockSpec((1, rows, model), lambda s: (side(), 0, 0)),
-            pl.BlockSpec((1, rows, model), lambda s: (side(), 0, 0)),
-            const((model, rows)),
+            ANY_SPEC,
+            ANY_SPEC,
+            ANY_SPEC,
+            ANY_SPEC,
+            ANY_SPEC,
+            ANY_SPEC,
+            ANY_SPEC,
             column(rows),
             pl.BlockSpec((1, 1, model, WIDE), lambda s: (now(s)[2], now(s)[1], 0, 0)),
             pl.BlockSpec((1, 1, model, WIDE), lambda s: (lag(s)[2], lag(s)[1], 0, 1)),
-            const((2, model, WIDE)),
+            ANY_SPEC,
             const((8, wide)),
             const((8, LANES)),
         ],
         out_specs=[out[1] for out in outs],
         scratch_shapes=[
+            pltpu.VMEM((rows, model), LOW),
+            pltpu.VMEM((model, rows), LOW),
+            pltpu.VMEM((CONV - 1, rows, LANES), F32),
+            pltpu.VMEM((rows, model), LOW),
+            pltpu.VMEM((rows, model), LOW),
+            pltpu.VMEM((2, model, WIDE), LOW),
+            pltpu.VMEM((rows, WIDE), F32),
+            pltpu.VMEM((ext, WIDE), LOW),
+            pltpu.VMEM((rows, LANES), F32),
+            pltpu.VMEM((rows, LANES), F32),
+            sem(10),
             pltpu.VMEM((rows, WIDE), F32),
             pltpu.VMEM((rows, Q), F32),
             pltpu.VMEM((6, 8, rows), F32),

time: 190 us -> 185 us (0.974)
  Pallas kernels: 189 us -> 184 us
    pallas_call x1, Pallas kernels: 103 us -> 99.1 us  [scan_back(): pl.pallas_call(functools.partial(scan_back_body, depth, rounds, fused), o...]
where the time goes in v8:
time: 185 us
  Pallas kernels  184 us (99%)
    pallas_call x1, Pallas kernels, scan_back(): pl.pallas_call(functools.partial(scan_back_body, depth, rounds, fused), o...  99.1 us
    pallas_call x1, Pallas kernels, entry(): pl.pallas_call(functools.partial(entry_body, depth, rounds, fused), out_s...  55.4 us
    pallas_call x1, Pallas kernels, middle(): pl.pallas_call(middle_body, out_shape=[out[0] for out in outs], grid=(12,...  21.8 us
    pallas_call x1, Pallas kernels, finish(): pl.pallas_call(finish_body, out_shape=[out[0] for out in outs], grid=(4,)...  5.1 us

profile of v8, /device:TPU:0, one launch (start us, length us, event | category | flops | bytes accessed | tf_op | source)
XLA Modules:
  0.0 184.7 jit_solution(8382930837616789503)
XLA Ops:
  0.6 2.4 %pack.1 = (bf16[48,256]{1,0:T(8,128)(2,1)}, bf16[3,48,512]{2,1,0:T(8,128)(2,1)}, bf16[48,768]{1,0:T(8,128)(2,1)}, f32[8,768]{1,0:T(8,128)}, f32[512,128]{1,0:T(8...) custom-call(f32[48,2,768]{2,1,0:T(2,128)} %entry.2, f32[48,768]{1,0:T(8,128)} %exits.1, ...), custom_call_target="tpu_custom_call" | custom-call | tf_op jit(solution)/shard_map/pack/pallas_call | solution.py:1849
  3.1 55.4 %entry.3 = (bf16[768,512]{1,0:T(8,128)(2,1)}, bf16[528,1536]{1,0:T(8,128)(2,1)}, f32[512,1536]{1,0:T(8,128)}, f32[512,1536]{1,0:T(8,128)}, f32[512,1536]{1,0:T(8...) custom-call(bf16[2,512,768]{2,1,0:T(8,128)(2,1)} %refs_24_.1, ...), custom_call_target="tpu_custom_call" | custom-call | tf_op jit(solution)/shard_map/entry/pallas_call | solution.py:1028
  58.5 21.8 %middle.1 = (bf16[512,768]{1,0:T(8,128)(2,1)}, bf16[2,768,768]{2,1,0:T(8,128)(2,1)}, bf16[2,768,768]{2,1,0:T(8,128)(2,1)}, f32[512,1536]{1,0:T(8,128)}, bf16[512...) custom-call(bf16[2,512,768]{2,1,0:T(8,128)(2,1)} %refs_24_.1, ...), custom_call_target="tpu_custom_call" | custom-call | tf_op jit(solution)/shard_map/middle/pallas_call | solution.py:1203
  80.4 99.1 %scan_back.1 = (f32[48,1536]{1,0:T(8,128)}, bf16[2,512,768]{2,1,0:T(8,128)(2,1)}, f32[48,512]{1,0:T(8,128)}, f32[48,512]{1,0:T(8,128)}, f32[2,48,128]{2,1,0:T(8,...) custom-call(f32[512,1536]{1,0:T(8,128)} %get-tuple-element.81.pre_ref.refs_0_, ...), custom_call_target="tpu_custom_call" | custom-call | tf_op jit(solution)/shard_map/scan_back/pallas_call | solution.py:1699
  179.4 5.1 %finish.1 = (bf16[2,512,768]{2,1,0:T(8,128)(2,1)}, f32[2,512,768]{2,1,0:T(8,128)}, f32[1,48]{1,0:T(1,128)}, f32[48,2,768]{2,1,0:T(2,128)}, f32[48,256]{1,0:T(8,1...) custom-call(f32[48,512]{1,0:T(8,128)} %get-tuple-element.113.mine, ...), custom_call_target="tpu_custom_call" | custom-call | tf_op jit(solution)/shard_map/finish/pallas_call | solution.py:2047

commit v9 on v8

--- a/solution.py
+++ b/solution.py
@@ -112,6 +112,11 @@
     return pl.BlockSpec(shape, lambda *_: zeros)
 
 
+def fixed(shape):
+    zeros = (0,) * len(shape)
+    return pl.BlockSpec(shape, lambda *_: zeros, pipeline_mode=pl.Buffered(1))
+
+
 def params(**extra):
     return pltpu.CompilerParams(vmem_limit_bytes=VMEM_LIMIT, **extra)
 
@@ -693,8 +698,9 @@
     (
         hidden_out, cin_out, gate_out, pre_out, loc_out, carry_out, cin_state_out, pre_state_out,
         bc_out, bct_out, score_out, mask_out, zst_out, dt_out, sp_out, cumt_out, fac_out, match_out,
-    ) = refs[11:29]
-    refs = refs[29:]
+        local_out,
+    ) = refs[11:30]
+    refs = refs[30:]
     if fused:
         small_out, parts_out, exit_out, par, heads_ref, cot_t = refs[:6]
         refs = refs[6:]
@@ -907,14 +913,31 @@
         pre = conv_forward(cin.astype(F32), taps, masks)
         pre_out[...] = pre
         spread = spreader(4 * group, HEAD, 4)
-        value = (pre * sigmoid(pre) * mm(sp_tail[...], spread)).astype(LOW)
+        mix = pre * sigmoid(pre)
+        value = (mix * mm(sp_tail[...], spread)).astype(LOW)
         facx = mm(facs[...], spread)
+        cums = mm(sp_out[1], spreader(4 * group, LANES, 4))
+        skipx = mm(split3(heads_ref[...]), spread)[2:3]
+        stepped = mix * mm(sp_out[0], spread)
+        first_half = iota((Q, LANES), 1) < HEAD
         fold = jnp.zeros((NSTATE, WIDE), F32)
         for index in range(spans):
             at = slice(index * Q, (index + 1) * Q)
             loc = mm(bct_out[:NSTATE, at], value[at])
             loc_out[at] = loc
             fold = facx[index : index + 1] * fold + loc
+            parts = []
+            for pair in range(2):
+                lanes = slice(pair * LANES, (pair + 1) * LANES)
+                weights, seen = [], []
+                for head in (2 * pair, 2 * pair + 1):
+                    across = cumt_out[group, head : head + 1, at]
+                    spread_at = cums[at, head * LANES : (head + 1) * LANES] - across + mask_out[at]
+                    weights.append((jnp.exp2(spread_at) * score_out[at]).astype(LOW))
+                    keep = first_half if head % 2 == 0 else jnp.logical_not(first_half)
+                    seen.append(jnp.where(keep, stepped[at, lanes], 0.0).astype(LOW))
+                parts.append(mm(jnp.concatenate(weights, axis=1), jnp.concatenate(seen, axis=0)))
+            local_out[at] = jnp.concatenate(parts, axis=1) + skipx * mix[at]
         folds[step - 1] = fold
         gains[step - 1] = jnp.broadcast_to(facx[spans : spans + 1], (8, WIDE))
 
@@ -976,6 +999,7 @@
         whole(6, 8, rows),
         whole(8, LANES),
         whole(CONV - 1, rows, LANES),
+        (shape((rows, wide), F32), column(rows)),
     ]
     scratch = [
         pltpu.VMEM((ext, model), LOW),
@@ -987,9 +1011,9 @@
     ] + Chaining.scratch(rounds)
     in_specs = [
         pl.BlockSpec((1, rows, model), lambda s: (side(), 0, 0)),
-        const((rows, LANES)),
-        const((8, rows)),
-        const((CONV + 1, WIDE)),
+        fixed((rows, LANES)),
+        fixed((8, rows)),
+        fixed((CONV + 1, WIDE)),
     ]
     args = [tokens, doc_col, doc_row, state_filter]
     full = lambda own: (2, 2, count) + own.shape[-2:]
@@ -1023,7 +1047,7 @@
         block = lambda at: pl.BlockSpec(
             (1, 1, model, WIDE), lambda s: (turn_of(s)[2], turn_of(s)[1], 0, at)
         )
-        in_specs += [block(0), block(1), const((2, model, WIDE))] + [VMEM_SPEC] * 4
+        in_specs += [block(0), block(1), fixed((2, model, WIDE))] + [VMEM_SPEC] * 4
         args += [weights, weights, small.reshape(2, model, WIDE), par, heads, edge, docs]
     results = pl.pallas_call(
         functools.partial(entry_body, depth, rounds, fused),
@@ -1036,8 +1060,8 @@
         name="entry",
     )(*args)
     if fused:
-        small, parts, exits, par, heads, cot_t = results[18:]
-    return tuple(results[:18]), (
+        small, parts, exits, par, heads, cot_t = results[19:]
+    return tuple(results[:19]), (
         small.reshape(2, model, WIDE),
         parts.reshape(3, 2, model, 2 * WIDE),
         exits.reshape(2, model, -1),
@@ -1048,8 +1072,8 @@
 
 
 def middle_body(
-    tokens_far, cot, cot_t_far, hidden_far, pre_ref, gate_ref, loc_ref, carry_ref, w_exit, par, par_heads, bc,
-    bct, score, mask, sp, cumt, fac, block_out, exit_out, gate_part_out, dy_out, gpg_out, enter_out, row_out,
+    tokens_far, cot, cot_t_far, hidden_far, pre_ref, gate_ref, loc_ref, local_ref, carry_ref, w_exit,
+    par, bc, bct, sp, fac, block_out, exit_out, gate_part_out, dy_out, gpg_out, enter_out, row_out,
     skip_out, outputs, gates, unit_grads, mixes, sums, total,
     tokens, cot_t, hidden_t, late_sem
 ):
@@ -1080,29 +1104,13 @@
         pre = pre_ref[...]
         mix = pre * sigmoid(pre)
         mixes[group] = mix
-        value = mix * mm(sp[0], spread)
         growth = mm(sp[2], spread)
         facx = mm(split3(fac[...]), spread)
-        cums = mm(sp[1], spreader(4 * group, LANES, 4))
-        skipx = mm(split3(par_heads[...]), spread)[2:3]
         state = carry_ref[...].astype(F32)
-        half = iota((Q, LANES), 1) < HEAD
         for index in range(spans):
             at = slice(index * Q, (index + 1) * Q)
             carried = mm(bc[at, LANES:], state.astype(LOW)) * growth[at]
-            parts = []
-            for pair in range(2):
-                lanes = slice(pair * LANES, (pair + 1) * LANES)
-                weights, seen = [], []
-                for head in (2 * pair, 2 * pair + 1):
-                    across = cumt[group, head : head + 1, at]
-                    spread_at = cums[at, head * LANES : (head + 1) * LANES] - across + mask[at]
-                    weights.append((jnp.exp2(spread_at) * score[at]).astype(LOW))
-                    keep = half if head % 2 == 0 else jnp.logical_not(half)
-                    seen.append(jnp.where(keep, value[at, lanes], 0.0).astype(LOW))
-                local = mm(jnp.concatenate(weights, axis=1), jnp.concatenate(seen, axis=0))
-                parts.append(local)
-            out = jnp.concatenate(parts, axis=1) + carried + skipx * mix[at]
+            out = local_ref[at] + carried
             outputs[group, at] = out
             state = facx[index : index + 1] * state + loc_ref[at]
         gate = gate_ref[...]
@@ -1168,8 +1176,7 @@
 
 
 def middle(
-    tokens, cot, cot_t, hidden_t, pre, gate, loc, carry, weights, par, par_heads, bc, bct, score, mask,
-    sp, cumt, fac
+    tokens, cot, cot_t, hidden_t, pre, gate, loc, local, carry, weights, par, bc, bct, sp, fac
 ):
     rows, model = tokens.shape[1:]
     wide = 6 * WIDE
@@ -1212,17 +1219,14 @@
                 pl.BlockSpec((rows, WIDE), lambda s: (0, early(s))),
                 pl.BlockSpec((rows, WIDE), lambda s: (0, early(s))),
                 pl.BlockSpec((rows, WIDE), lambda s: (0, early(s))),
+                pl.BlockSpec((rows, WIDE), lambda s: (0, early(s))),
                 pl.BlockSpec((NSTATE, WIDE), lambda s: (0, early(s))),
                 pl.BlockSpec((1, model, WIDE), lambda s: (group(s) // 3, 0, group(s) % 3)),
                 pl.BlockSpec((1, 8, WIDE), lambda s: (group(s) // 3, 0, group(s) % 3)),
-                const((8, LANES)),
-                const((rows, WIDE)),
-                const((WIDE, rows)),
-                const((rows, Q)),
-                const((rows, Q)),
-                const((4, rows, LANES)),
-                const((6, 8, rows)),
-                const((8, LANES)),
+                fixed((rows, WIDE)),
+                fixed((WIDE, rows)),
+                fixed((4, rows, LANES)),
+                fixed((8, LANES)),
         ],
         out_specs=[out[1] for out in outs],
         scratch_shapes=[
@@ -1239,10 +1243,7 @@
         ],
         compiler_params=params(),
         name="middle",
-    )(
-        tokens, cot, cot_t, hidden_t, pre, gate, loc, carry, weights, par, par_heads, bc, bct, score,
-        mask, sp, cumt, fac,
-    )
+    )(tokens, cot, cot_t, hidden_t, pre, gate, loc, local, carry, weights, par, bc, bct, sp, fac)
 
 
 def scan_back_body(depth, rounds, fused, *refs):
@@ -1705,20 +1706,20 @@
             column(rows),
             column(rows),
             column(NSTATE),
-            const((NSTATE, wide)),
+            fixed((NSTATE, wide)),
             column(ext),
             pl.BlockSpec((1, 8, WIDE), lambda s: (now(s)[1], 0, now(s)[2])),
-            const((8, LANES)),
-            const((CONV + 1, WIDE)),
+            fixed((8, LANES)),
+            fixed((CONV + 1, WIDE)),
             ANY_SPEC,
             ANY_SPEC,
-            const((rows, WIDE)),
-            const((WIDE, rows)),
-            const((rows, Q)),
-            const((rows, Q)),
-            const((4, rows, LANES)),
-            const((6, 8, rows)),
-            const((8, LANES)),
+            fixed((rows, WIDE)),
+            fixed((WIDE, rows)),
+            fixed((rows, Q)),
+            fixed((rows, Q)),
+            fixed((4, rows, LANES)),
+            fixed((6, 8, rows)),
+            fixed((8, LANES)),
             ANY_SPEC,
             ANY_SPEC,
             ANY_SPEC,
@@ -1732,8 +1733,8 @@
             pl.BlockSpec((1, 1, model, WIDE), lambda s: (now(s)[2], now(s)[1], 0, 0)),
             pl.BlockSpec((1, 1, model, WIDE), lambda s: (lag(s)[2], lag(s)[1], 0, 1)),
             ANY_SPEC,
-            const((8, wide)),
-            const((8, LANES)),
+            fixed((8, wide)),
+            fixed((8, LANES)),
         ],
         out_specs=[out[1] for out in outs],
         scratch_shapes=[
@@ -1850,7 +1851,7 @@
         pack_body,
         out_shape=outs,
         grid=(1,),
-        in_specs=[const(array.shape) for array in arrays]
+        in_specs=[fixed(array.shape) for array in arrays]
         + [pl.BlockSpec((1, HALO, model), lambda s: (side(), rows // HALO - 1, 0))],
         out_specs=[const(out.shape) for out in outs],
         compiler_params=params(),
@@ -2027,7 +2028,7 @@
 def finish(mine, mine_last, exits, state, vector, token, block):
     own_rows, wide = exits.shape[0], exits.shape[1] // 2
     _, rows, model = token.shape
-    share = rows // 4
+    share = rows // 2
     shape = jax.ShapeDtypeStruct
     outs = (
         (shape((2, rows, model), LOW), pl.BlockSpec((2, share, model), lambda s: (0, s, 0))),
@@ -2047,13 +2048,13 @@
     return pl.pallas_call(
         finish_body,
         out_shape=[out[0] for out in outs],
-        grid=(4,),
+        grid=(2,),
         in_specs=[
-            const(mine.shape),
-            const(mine_last.shape),
-            const(exits.shape),
-            const(state.shape),
-            const(vector.shape),
+            fixed(mine.shape),
+            fixed(mine_last.shape),
+            fixed(exits.shape),
+            fixed(state.shape),
+            fixed(vector.shape),
             pl.BlockSpec((2, share, model), lambda s: (0, s, 0)),
             pl.BlockSpec((2, share, model), lambda s: (0, s, 0)),
         ],
@@ -2080,13 +2081,13 @@
     packs = (own_small, own_parts, own_exit, own_par, own_edge, own_docs)
     (
         hidden_t, cin, gate, pre, loc, carry, cin_state, pre_state, bc, bct, score, mask, zst, dt, sp,
-        cumt, fac, match,
+        cumt, fac, match, local,
     ), (small, parts, exit_weights, par, par_heads, cot_t) = entry(
         tokens, doc_col, doc_row, state_filter, packs, cotangent, rounds
     )
     block_own, exit_part, gate_part, dy, gpg, enter, gate_row, skip_row = middle(
-        tokens, cotangent, cot_t, hidden_t, pre, gate, loc, carry, exit_weights, par, par_heads, bc,
-        bct, score, mask, sp, cumt, fac,
+        tokens, cotangent, cot_t, hidden_t, pre, gate, loc, local, carry, exit_weights, par, bc, bct,
+        sp, fac,
     )
     cut = lambda v: v.reshape(2, 2, count, own_rows, v.shape[-1])
     exit_mine, block_both, *others = scan_back(

time: 185 us -> 184 us (level)
  no operation moved by 1% of the time
where the time goes in v9:
time: 184 us
  Pallas kernels  183 us (99%)
    pallas_call x1, Pallas kernels, scan_back(): pl.pallas_call(functools.partial(scan_back_body, depth, rounds, fused), o...  99.3 us
    pallas_call x1, Pallas kernels, entry(): pl.pallas_call(functools.partial(entry_body, depth, rounds, fused), out_s...  55.9 us
    pallas_call x1, Pallas kernels, middle(): pl.pallas_call(middle_body, out_shape=[out[0] for out in outs], grid=(12,...  21 us
    pallas_call x1, Pallas kernels, finish(): pl.pallas_call(finish_body, out_shape=[out[0] for out in outs], grid=(2,)...  4.22 us

profile of v9, /device:TPU:0, one launch (start us, length us, event | category | flops | bytes accessed | tf_op | source)
XLA Modules:
  0.0 183.6 jit_solution(15675124962986861409)
XLA Ops:
  0.6 2.4 %pack.1 = (bf16[48,256]{1,0:T(8,128)(2,1)}, bf16[3,48,512]{2,1,0:T(8,128)(2,1)}, bf16[48,768]{1,0:T(8,128)(2,1)}, f32[8,768]{1,0:T(8,128)}, f32[512,128]{1,0:T(8...) custom-call(f32[48,2,768]{2,1,0:T(2,128)} %entry.2, f32[48,768]{1,0:T(8,128)} %exits.1, ...), custom_call_target="tpu_custom_call" | custom-call | tf_op jit(solution)/shard_map/pack/pallas_call | solution.py:1850
  3.1 55.9 %entry.3 = (bf16[768,512]{1,0:T(8,128)(2,1)}, bf16[528,1536]{1,0:T(8,128)(2,1)}, f32[512,1536]{1,0:T(8,128)}, f32[512,1536]{1,0:T(8,128)}, f32[512,1536]{1,0:T(8...) custom-call(bf16[2,512,768]{2,1,0:T(8,128)(2,1)} %refs_24_.1, ...), custom_call_target="tpu_custom_call" | custom-call | tf_op jit(solution)/shard_map/entry/pallas_call | solution.py:1052
  59.0 21.0 %middle.1 = (bf16[512,768]{1,0:T(8,128)(2,1)}, bf16[2,768,768]{2,1,0:T(8,128)(2,1)}, bf16[2,768,768]{2,1,0:T(8,128)(2,1)}, f32[512,1536]{1,0:T(8,128)}, bf16[512...) custom-call(bf16[2,512,768]{2,1,0:T(8,128)(2,1)} %refs_24_.1, ...), custom_call_target="tpu_custom_call" | custom-call | tf_op jit(solution)/shard_map/middle/pallas_call | solution.py:1210
  80.0 99.3 %scan_back.1 = (f32[48,1536]{1,0:T(8,128)}, bf16[2,512,768]{2,1,0:T(8,128)(2,1)}, f32[48,512]{1,0:T(8,128)}, f32[48,512]{1,0:T(8,128)}, f32[2,48,128]{2,1,0:T(8,...) custom-call(f32[512,1536]{1,0:T(8,128)} %get-tuple-element.82.pre_ref.refs_0_, ...), custom_call_target="tpu_custom_call" | custom-call | tf_op jit(solution)/shard_map/scan_back/pallas_call | solution.py:1700
  179.2 4.2 %finish.1 = (bf16[2,512,768]{2,1,0:T(8,128)(2,1)}, f32[2,512,768]{2,1,0:T(8,128)}, f32[1,48]{1,0:T(1,128)}, f32[48,2,768]{2,1,0:T(2,128)}, f32[48,256]{1,0:T(8,1...) custom-call(f32[48,512]{1,0:T(8,128)} %get-tuple-element.115.mine, ...), custom_call_target="tpu_custom_call" | custom-call | tf_op jit(solution)/shard_map/finish/pallas_call | solution.py:2048

commit v10 on v9

--- a/solution.py
+++ b/solution.py
@@ -690,17 +690,19 @@
 
 def entry_body(depth, rounds, fused, *refs):
     step = pl.program_id(0)
-    tokens, doc_col, doc_row, state_filter = refs[:4]
+    tokens, state_filter = refs[:2]
     if fused:
-        own_small, own_parts, own_exit, own_par, own_edge, own_docs, cot = refs[4:11]
+        raw, cot = refs[2:13], refs[13]
+        refs = refs[14:]
     else:
-        w_gate, w_inner, w_small, par, heads_ref, edge, halo_docs = refs[4:11]
+        doc_col, doc_row, w_gate, w_inner, w_small, par, heads_ref, edge, halo_docs = refs[2:11]
+        refs = refs[11:]
     (
         hidden_out, cin_out, gate_out, pre_out, loc_out, carry_out, cin_state_out, pre_state_out,
         bc_out, bct_out, score_out, mask_out, zst_out, dt_out, sp_out, cumt_out, fac_out, match_out,
         local_out,
-    ) = refs[11:30]
-    refs = refs[30:]
+    ) = refs[:19]
+    refs = refs[19:]
     if fused:
         small_out, parts_out, exit_out, par, heads_ref, cot_t = refs[:6]
         refs = refs[6:]
@@ -714,7 +716,9 @@
     if fused:
         v_small, v_parts, edge, halo_docs, docs_in, cot_in, par_in = refs[14:21]
         side_send, side_land, local, out_sem = refs[21:25]
-        marks = refs[25:]
+        packed = refs[25:33]
+        own_small, own_parts, own_exit, own_par, doc_col, doc_row, own_edge, own_docs = packed
+        marks = refs[33:]
         own = [own_small, own_parts.at[0], own_parts.at[1], own_parts.at[2], own_exit]
         full = [v_small, v_parts.at[0], v_parts.at[1], v_parts.at[2], exit_out]
         pieces = [
@@ -807,6 +811,7 @@
             count = 2 * depth
             onward = {"context": lax.rem(place.position + 1, count)}
             behind = {"context": lax.rem(place.position + count - 1, count)}
+            pack_body(*raw, tokens.at[:, rows - HALO :], *packed)
             place.greet(
                 [place.mate, place.x_peer, place.y_peer, onward, behind], chaining.sometimes(), True
             )
@@ -968,9 +973,11 @@
         chaining.finish()
 
 
-def entry(tokens, doc_col, doc_row, state_filter, packs, cot, rounds):
-    own_small, own_parts, own_exit, own_par, own_edge, own_docs = packs
+def entry(tokens, raw, state_filter, cot, rounds):
     rows, model = tokens.shape[1:]
+    own_small, own_parts, own_exit, own_par, doc_col, doc_row, own_edge, own_docs = pack_shapes(
+        raw[0].shape[0], raw[0].shape[2], rows, model
+    )
     count = lax.axis_size("context")
     depth = count // 2
     wide = GROUPS * WIDE
@@ -1011,11 +1018,9 @@
     ] + Chaining.scratch(rounds)
     in_specs = [
         pl.BlockSpec((1, rows, model), lambda s: (side(), 0, 0)),
-        fixed((rows, LANES)),
-        fixed((8, rows)),
         fixed((CONV + 1, WIDE)),
     ]
-    args = [tokens, doc_col, doc_row, state_filter]
+    args = [tokens, state_filter]
     full = lambda own: (2, 2, count) + own.shape[-2:]
     if fused:
         outs += [
@@ -1038,11 +1043,16 @@
             sem(3),
             sem(2),
             sem(4),
-        ] + Gathering.scratch(depth) * 5
-        in_specs += [VMEM_SPEC] * 6 + [ANY_SPEC]
-        args += [own_small, own_parts, own_exit, own_par, own_edge, own_docs, cot]
+        ]
+        own = (own_small, own_parts, own_exit, own_par, doc_col, doc_row, own_edge, own_docs)
+        scratch += [pltpu.VMEM(one.shape, one.dtype) for one in own] + Gathering.scratch(depth) * 5
+        in_specs += [fixed(one.shape) for one in raw] + [ANY_SPEC]
+        args += [*raw, cot]
     else:
-        small, parts, exits, par, heads, edge, docs, cot_t = gather(*packs, cot)
+        *packs, doc_col, doc_row, edge, docs = pack(raw, tokens)
+        small, parts, exits, par, heads, edge, docs, cot_t = gather(*packs, edge, docs, cot)
+        in_specs += [fixed((rows, LANES)), fixed((8, rows))]
+        args += [doc_col, doc_row]
         weights = parts.reshape(3, 2, model, 2 * WIDE)
         block = lambda at: pl.BlockSpec(
             (1, 1, model, WIDE), lambda s: (turn_of(s)[2], turn_of(s)[1], 0, at)
@@ -1827,17 +1837,9 @@
     edge[...] = tail_tokens[0]
 
 
-def pack(
-    entry, exits, state, steps, gain, inner_kernel, gate_gain, bias, decay, skip, docs, tokens
-):
-    own_rows, _, wide = entry.shape
-    rows, model = tokens.shape[1:]
+def pack_shapes(own_rows, wide, rows, model):
     shape = jax.ShapeDtypeStruct
-    arrays = (
-        entry, exits, state, steps.T, gain[None], inner_kernel, gate_gain.reshape(-1, LANES), bias[None],
-        decay[None], skip[None], docs,
-    )
-    outs = (
+    return (
         shape((own_rows, WIDE), LOW),
         shape((3, own_rows, 2 * WIDE), LOW),
         shape((own_rows, wide), LOW),
@@ -1847,6 +1849,12 @@
         shape((HALO, model), LOW),
         shape((HALO, LANES), F32),
     )
+
+
+def pack(arrays, tokens):
+    own_rows, _, wide = arrays[0].shape
+    rows, model = tokens.shape[1:]
+    outs = pack_shapes(own_rows, wide, rows, model)
     return pl.pallas_call(
         pack_body,
         out_shape=outs,
@@ -2074,16 +2082,15 @@
     longest = rows * count // 4
     rounds = min(count // 2 - 1, -(-(longest - 1) // (2 * rows)))
 
-    own_small, own_parts, own_exit, own_par, doc_col, doc_row, own_edge, own_docs = pack(
-        entry_weight, exit_weight, state_weight, step_weight, norm_gain, inner_kernel,
-        gate_gain, step_bias, decay_log, skip_gain, documents, tokens,
+    raw = (
+        entry_weight, exit_weight, state_weight, step_weight.T, norm_gain[None], inner_kernel,
+        gate_gain.reshape(-1, LANES), step_bias[None], decay_log[None], skip_gain[None], documents,
     )
-    packs = (own_small, own_parts, own_exit, own_par, own_edge, own_docs)
     (
         hidden_t, cin, gate, pre, loc, carry, cin_state, pre_state, bc, bct, score, mask, zst, dt, sp,
         cumt, fac, match, local,
     ), (small, parts, exit_weights, par, par_heads, cot_t) = entry(
-        tokens, doc_col, doc_row, state_filter, packs, cotangent, rounds
+        tokens, raw, state_filter, cotangent, rounds
     )
     block_own, exit_part, gate_part, dy, gpg, enter, gate_row, skip_row = middle(
         tokens, cotangent, cot_t, hidden_t, pre, gate, loc, local, carry, exit_weights, par, bc, bct,

time: 184 us -> 182 us (0.989)
  Pallas kernels: 183 us -> 181 us
    pallas_call x1 -> x0, Pallas kernels: 2.42 us -> none  [pack(): pl.pallas_call(pack_body, out_shape=outs, grid=(1,), in_specs=[fixed(arra...]
where the time goes in v10:
time: 182 us
  Pallas kernels  181 us (99%)
    pallas_call x1, Pallas kernels, scan_back(): pl.pallas_call(functools.partial(scan_back_body, depth, rounds, fused), o...  99.3 us
    pallas_call x1, Pallas kernels, entry(): pl.pallas_call(functools.partial(entry_body, depth, rounds, fused), out_s...  56.5 us
    pallas_call x1, Pallas kernels, middle(): pl.pallas_call(middle_body, out_shape=[out[0] for out in outs], grid=(12,...  21 us
    pallas_call x1, Pallas kernels, finish(): pl.pallas_call(finish_body, out_shape=[out[0] for out in outs], grid=(2,)...  4.22 us

profile of v10, /device:TPU:0, one launch (start us, length us, event | category | flops | bytes accessed | tf_op | source)
XLA Modules:
  0.0 181.8 jit_solution(13540210315378582087)
XLA Ops:
  0.6 56.5 %entry.1 = (bf16[768,512]{1,0:T(8,128)(2,1)}, bf16[528,1536]{1,0:T(8,128)(2,1)}, f32[512,1536]{1,0:T(8,128)}, f32[512,1536]{1,0:T(8,128)}, f32[512,1536]{1,0:T(8...) custom-call(bf16[2,512,768]{2,1,0:T(8,128)(2,1)} %refs_24_.1, ...), custom_call_target="tpu_custom_call" | custom-call | tf_op jit(solution)/shard_map/entry/pallas_call | solution.py:1062
  57.1 21.0 %middle.1 = (bf16[512,768]{1,0:T(8,128)(2,1)}, bf16[2,768,768]{2,1,0:T(8,128)(2,1)}, bf16[2,768,768]{2,1,0:T(8,128)(2,1)}, f32[512,1536]{1,0:T(8,128)}, bf16[512...) custom-call(bf16[2,512,768]{2,1,0:T(8,128)(2,1)} %refs_24_.1, ...), custom_call_target="tpu_custom_call" | custom-call | tf_op jit(solution)/shard_map/middle/pallas_call | solution.py:1220
  78.1 99.3 %scan_back.1 = (f32[48,1536]{1,0:T(8,128)}, bf16[2,512,768]{2,1,0:T(8,128)(2,1)}, f32[48,512]{1,0:T(8,128)}, f32[48,512]{1,0:T(8,128)}, f32[2,48,128]{2,1,0:T(8,...) custom-call(f32[512,1536]{1,0:T(8,128)} %get-tuple-element.66.pre_ref.refs_0_, ...), custom_call_target="tpu_custom_call" | custom-call | tf_op jit(solution)/shard_map/scan_back/pallas_call | solution.py:1710
  177.4 4.2 %finish.1 = (bf16[2,512,768]{2,1,0:T(8,128)(2,1)}, f32[2,512,768]{2,1,0:T(8,128)}, f32[1,48]{1,0:T(1,128)}, f32[48,2,768]{2,1,0:T(2,128)}, f32[48,256]{1,0:T(8,1...) custom-call(f32[48,512]{1,0:T(8,128)} %get-tuple-element.99.mine, ...), custom_call_target="tpu_custom_call" | custom-call | tf_op jit(solution)/shard_map/finish/pallas_call | solution.py:2056

commit v11 on v10

--- a/solution.py
+++ b/solution.py
@@ -99,11 +99,10 @@
     pad = jnp.zeros((HALO, width), F32)
     grad = jnp.concatenate([pad, pg * taps[CONV - 1 : CONV]], axis=0)
     for back in range(1, CONV):
-        masked = pg * twice(masks[back - 1])
-        part = cin[HALO - back : HALO - back + rows]
-        sums[CONV - 1 - back] = jnp.sum(masked * part, axis=0, keepdims=True)
-        padded = jnp.concatenate([pad, masked * taps[CONV - 1 - back : CONV - back], pad], axis=0)
-        grad = grad + padded[back : back + rows + HALO]
+        padded = jnp.concatenate([pad, pg * twice(masks[back - 1]), pad], axis=0)
+        moved = padded[back : back + rows + HALO]
+        sums[CONV - 1 - back] = jnp.sum(moved * cin, axis=0, keepdims=True)
+        grad = grad + moved * taps[CONV - 1 - back : CONV - back]
     return sums, grad
 
 

time: 182 us -> 183 us (level)
  no operation moved by 1% of the time
where the time goes in v11:
time: 183 us; the launch traced here: 182 us
  Pallas kernels  182 us (99%)
    pallas_call x1, Pallas kernels, scan_back(): pl.pallas_call(functools.partial(scan_back_body, depth, rounds, fused), o...  100 us
    pallas_call x1, Pallas kernels, entry(): pl.pallas_call(functools.partial(entry_body, depth, rounds, fused), out_s...  56.5 us
    pallas_call x1, Pallas kernels, middle(): pl.pallas_call(middle_body, out_shape=[out[0] for out in outs], grid=(12,...  21 us
    pallas_call x1, Pallas kernels, finish(): pl.pallas_call(finish_body, out_shape=[out[0] for out in outs], grid=(2,)...  4.22 us

profile of v11, /device:TPU:0, one launch (start us, length us, event | category | flops | bytes accessed | tf_op | source)
XLA Modules:
  0.0 182.5 jit_solution(15942838510470491337)
XLA Ops:
  0.6 56.5 %entry.1 = (bf16[768,512]{1,0:T(8,128)(2,1)}, bf16[528,1536]{1,0:T(8,128)(2,1)}, f32[512,1536]{1,0:T(8,128)}, f32[512,1536]{1,0:T(8,128)}, f32[512,1536]{1,0:T(8...) custom-call(bf16[2,512,768]{2,1,0:T(8,128)(2,1)} %refs_24_.1, ...), custom_call_target="tpu_custom_call" | custom-call | tf_op jit(solution)/shard_map/entry/pallas_call | solution.py:1061
  57.1 21.0 %middle.1 = (bf16[512,768]{1,0:T(8,128)(2,1)}, bf16[2,768,768]{2,1,0:T(8,128)(2,1)}, bf16[2,768,768]{2,1,0:T(8,128)(2,1)}, f32[512,1536]{1,0:T(8,128)}, bf16[512...) custom-call(bf16[2,512,768]{2,1,0:T(8,128)(2,1)} %refs_24_.1, ...), custom_call_target="tpu_custom_call" | custom-call | tf_op jit(solution)/shard_map/middle/pallas_call | solution.py:1219
  78.1 100.0 %scan_back.1 = (f32[48,1536]{1,0:T(8,128)}, bf16[2,512,768]{2,1,0:T(8,128)(2,1)}, f32[48,512]{1,0:T(8,128)}, f32[48,512]{1,0:T(8,128)}, f32[2,48,128]{2,1,0:T(8,...) custom-call(f32[512,1536]{1,0:T(8,128)} %get-tuple-element.66.pre_ref.refs_0_, ...), custom_call_target="tpu_custom_call" | custom-call | tf_op jit(solution)/shard_map/scan_back/pallas_call | solution.py:1709
  178.1 4.2 %finish.1 = (bf16[2,512,768]{2,1,0:T(8,128)(2,1)}, f32[2,512,768]{2,1,0:T(8,128)}, f32[1,48]{1,0:T(1,128)}, f32[48,2,768]{2,1,0:T(2,128)}, f32[48,256]{1,0:T(8,1...) custom-call(f32[48,512]{1,0:T(8,128)} %get-tuple-element.99.mine, ...), custom_call_target="tpu_custom_call" | custom-call | tf_op jit(solution)/shard_map/finish/pallas_call | solution.py:2055
